TPU v7x, 32 devices: a whole 2x2x4 slice. The times are simulated.
32 devices in a mesh: wide: 8 (over z, y), narrow: 4 (over x, core).
Axes of the slice: x: 2, y: 2, z: 4, core: 2. Of those that a mesh axis runs over, the one named last changes fastest.
Arguments:
- cond_fields: bfloat16 [4, 6824, 172], P(None, 'wide'), may hold values from -6 to 6
- target: float32 [4, 6824, 84], P(None, 'wide'), may hold values from -6 to 6
- noise_draw: float32 [4, 6824, 84], P(None, 'wide'), may hold values from -6 to 6
- noise_sigma: float32 [4], replicated, may hold values from 0.3 to 10
- grid_to_mesh: int32 [4096, 8], P('wide'), may hold values from 0 to 6823, as said below
- mesh_edges: int32 [4096, 16], P('wide'), may hold values from -1 to 4095, as said below
- mesh_to_grid: int32 [6824, 3], P('wide'), may hold values from 0 to 4095, as said below
- latitude_row: int32 [6824], P('wide'), may hold values from 0 to 180
- level_index: int32 [84], replicated, may hold values from 0 to 12
- encoder: float32 [256, 512], P('wide', 'narrow'), may hold values from -0.375 to 0.375
- up_proj: float32 [512, 3584], P('wide', 'narrow'), may hold values from -0.25 to 0.25
- down_proj: float32 [2560, 512], P('narrow', 'wide'), may hold values from -0.25 to 0.25
- readout: float32 [512, 86], P(('narrow', 'wide')), may hold values from -1 to 1.5
- encoder_moment: float32 [256, 512], P('wide', 'narrow'), may hold values from -9.536743e-07 to 9.536743e-07
- up_moment: float32 [512, 3584], P('wide', 'narrow'), may hold values from -9.536743e-07 to 9.536743e-07
- down_moment: float32 [2560, 512], P('narrow', 'wide'), may hold values from -9.536743e-07 to 9.536743e-07
- readout_moment: float32 [512, 86], P(('narrow', 'wide')), may hold values from -9.536743e-07 to 9.536743e-07
- encoder_second: float32 [256, 512], P('wide', 'narrow'), may hold values from 1.5056467e-16 to 2.4090348e-15
- up_second: float32 [512, 3584], P('wide', 'narrow'), may hold values from 1.5056467e-16 to 2.4090348e-15
- down_second: float32 [2560, 512], P('narrow', 'wide'), may hold values from 1.5056467e-16 to 2.4090348e-15
- readout_second: float32 [512, 86], P(('narrow', 'wide')), may hold values from 1.5056467e-16 to 2.4090348e-15
- encoder_average: float32 [256, 512], P('wide', 'narrow'), may hold values from -0.375 to 0.375
- up_average: float32 [512, 3584], P('wide', 'narrow'), may hold values from -0.25 to 0.25
- down_average: float32 [2560, 512], P('narrow', 'wide'), may hold values from -0.25 to 0.25
- readout_average: float32 [512, 86], P(('narrow', 'wide')), may hold values from -1 to 1.5
Outputs:
- loss_value: float32 [], replicated
- grad_norm: float32 [], replicated
- next_encoder_moment: float32 [256, 512], P('wide', 'narrow')
- next_encoder_second: float32 [256, 512], P('wide', 'narrow')
- next_encoder: float32 [256, 512], P('wide', 'narrow')
- next_encoder_average: float32 [256, 512], P('wide', 'narrow')
- encoder_copy: bfloat16 [256, 512], P('wide', 'narrow')
- next_up_moment: float32 [512, 3584], P('wide', 'narrow')
- next_up_second: float32 [512, 3584], P('wide', 'narrow')
- next_up_proj: float32 [512, 3584], P('wide', 'narrow')
- next_up_average: float32 [512, 3584], P('wide', 'narrow')
- up_copy: bfloat16 [512, 3584], P('wide', 'narrow')
- next_down_moment: float32 [2560, 512], P('narrow', 'wide')
- next_down_second: float32 [2560, 512], P('narrow', 'wide')
- next_down_proj: float32 [2560, 512], P('narrow', 'wide')
- next_down_average: float32 [2560, 512], P('narrow', 'wide')
- down_copy: bfloat16 [2560, 512], P('narrow', 'wide')
- next_readout_moment: float32 [512, 86], P(('narrow', 'wide'))
- next_readout_second: float32 [512, 86], P(('narrow', 'wide'))
- next_readout: float32 [512, 86], P(('narrow', 'wide'))
- next_readout_average: float32 [512, 86], P(('narrow', 'wide'))
- readout_copy: bfloat16 [512, 86], P(('narrow', 'wide'))
Inputs may be any that keep to these rules, and one draw needn't show every extreme that they name: `grid_to_mesh`: row i names grid points of pixel block i // 512, pixels 853 b to 853 (b + 1) - 1. `mesh_edges`: slot 0 of node i is i itself; used slots name nodes j with (j - i) mod 4096 or (i - j) mod 4096 at most 512; unused slots (-1) end a row; a row uses at least 8 slots. `mesh_to_grid`: row p names mesh nodes of node block p // 853, nodes 512 b to 512 (b + 1) - 1.
All inputs are finite; a program needn't handle non-finite values.
Results may differ from a plain program's by a relative error of at most 0.0062.
The roundings to bfloat16 on the way count: a program that leaves them out, or rounds other values in their place, can miss the bound.
Values may be sent and summed in bfloat16 or wider, within the bound.
No kernel may reach another device: no remote copies, remote signals or barrier semaphores. Data moves between devices by JAX's collectives and lax.ppermute only.
A program may use at most 192 MiB of HBM per device.

v0:
```python
import math

import jax
import jax.numpy as jnp
from jax import lax
from jax.sharding import PartitionSpec as P

D = 512
HEAD_DIM = 128
OUT = 84
IN = 256
LEVELS = 13
KM = 16
KG = 8
KD = 3
STEPS_DONE = 7
MB = 4


HIGH = lax.Precision.HIGHEST
clip_norm = 0.001
beta_one = 0.9
beta_two = 0.999
epsilon = 1e-08
learn_rate = 0.04
weight_decay = 0.1
average_decay = 0.9


def padded(array, sides, width):
    for axis, dim in sides:
        peers, length = (lax.axis_size(axis), array.shape[dim])
        up = [(i, (i + 1) % peers) for i in range(peers)]
        down = [(j, i) for i, j in up]
        last = lax.slice_in_dim(array, length - width, length, axis=dim)
        first = lax.slice_in_dim(array, 0, width, axis=dim)
        before = lax.ppermute(last, axis, up)
        after = lax.ppermute(first, axis, down)
        array = jnp.concatenate([before, array, after], axis=dim)
    return array


def from_behind(array, axis, by):
    peers = lax.axis_size(axis)
    return lax.ppermute(array, axis, [(i, (i + by) % peers) for i in range(peers)])


def matmul(left, right):
    return jnp.dot(left, right, preferred_element_type=jnp.float32)


def left_trans(left, right):
    return lax.dot_general(
        left, right, (((0,), (0,)), ((), ())), preferred_element_type=jnp.float32
    )


def right_trans(left, right):
    return lax.dot_general(
        left, right, (((1,), (1,)), ((), ())), preferred_element_type=jnp.float32
    )


def norm_rows(values, gain):
    center = values - jnp.mean(values, axis=-1, keepdims=True)
    inverse = lax.rsqrt(jnp.mean(center * center, axis=-1, keepdims=True) + 1e-05)
    normal = center * inverse
    return (normal * gain, normal, inverse)


def norm_back(grad_out, normal, inverse, gain):
    gain_grad = jnp.sum(grad_out * normal, axis=0)
    scaled = grad_out * gain
    inner = (
        scaled
        - jnp.mean(scaled, axis=-1, keepdims=True)
        - normal * jnp.mean(scaled * normal, axis=-1, keepdims=True)
    )
    return (inner * inverse, gain_grad)


def gather_rows(state, gain):
    return (
        lax.all_gather(state.astype(jnp.bfloat16), "narrow", axis=1, tiled=True),
        lax.all_gather(gain, "narrow", axis=0, tiled=True),
    )


def return_rows(grad_rows, gain_grad):
    return (
        lax.psum_scatter(
            grad_rows.astype(jnp.bfloat16), "narrow", scatter_dimension=1, tiled=True
        ).astype(jnp.float32),
        lax.psum_scatter(
            gain_grad.astype(jnp.bfloat16), "narrow", scatter_dimension=0, tiled=True
        ).astype(jnp.float32),
    )


def finish_branch(partial_value):
    return lax.psum_scatter(
        partial_value.astype(jnp.bfloat16), "narrow", scatter_dimension=1, tiled=True
    ).astype(jnp.float32)


def branch_grad(grad_state):
    return lax.all_gather(grad_state.astype(jnp.bfloat16), "narrow", axis=1, tiled=True)


def adam_update(grad_raw, factor, fix_one, fix_two, weight, moment, second, average):
    grad = grad_raw * factor
    moment_new = beta_one * moment + (1.0 - beta_one) * grad
    second_new = beta_two * second + (1.0 - beta_two) * grad * grad
    weight_new = weight - learn_rate * (
        moment_new / fix_one / (jnp.sqrt(second_new / fix_two) + epsilon) + weight_decay * weight
    )
    average_new = average_decay * average + (1.0 - average_decay) * weight_new
    return [moment_new, second_new, weight_new, average_new, weight_new.astype(jnp.bfloat16)]


def body(
    cond_fields,
    target,
    noise_draw,
    noise_sigma,
    grid_to_mesh,
    mesh_edges,
    mesh_to_grid,
    latitude_row,
    level_index,
    encoder,
    up_proj,
    down_proj,
    readout,
    encoder_moment,
    up_moment,
    down_moment,
    readout_moment,
    encoder_second,
    up_second,
    down_second,
    readout_second,
    encoder_average,
    up_average,
    down_average,
    readout_average,
):
    enc_full, up_full, down_full, read_full = (
        lax.all_gather(encoder.astype(jnp.bfloat16), "wide", axis=0, tiled=True),
        lax.all_gather(up_proj.astype(jnp.bfloat16), "wide", axis=0, tiled=True),
        lax.all_gather(down_proj.astype(jnp.bfloat16), "wide", axis=1, tiled=True),
        lax.all_gather(readout.astype(jnp.bfloat16), "wide", axis=0, tiled=True),
    )
    nodes = mesh_edges.shape[0]
    pixels = cond_fields.shape[1]
    feat = enc_full.shape[1]
    heads_here = feat // HEAD_DIM
    wide_index = lax.axis_index("wide")
    wide_count = lax.axis_size("wide")
    narrow_index = lax.axis_index("narrow")
    all_nodes = nodes * wide_count
    local_grid = grid_to_mesh - wide_index * pixels
    local_mesh = mesh_to_grid - wide_index * nodes
    valid = mesh_edges >= 0
    slot_rows = jnp.where(
        valid, (mesh_edges - wide_index * nodes + nodes + all_nodes) % all_nodes, nodes
    )
    lat_weight = jnp.cos((latitude_row.astype(jnp.float32) - 90.0) * (math.pi / 180.0))
    level_weight = (level_index.astype(jnp.float32) + 1.0) / LEVELS
    pix_weight = lat_weight[:, None] * level_weight[None, :]
    pix_total = jnp.sum(pix_weight)
    early_total = lax.psum(pix_total, "wide")
    w_qkv = up_full[:, : 3 * feat]
    w_hidden = up_full[:, 3 * feat :]
    w_output = down_full[:feat]
    w_down = down_full[feat:]
    w_dec = read_full[:, :OUT]
    gain_att = read_full[:, OUT]
    gain_mlp = read_full[:, OUT + 1]
    scale = HEAD_DIM ** (-0.5)
    grad_enc = jnp.zeros(enc_full.shape, jnp.float32)
    grad_qkv_w = jnp.zeros(w_qkv.shape, jnp.float32)
    grad_hidden_w = jnp.zeros(w_hidden.shape, jnp.float32)
    grad_output_w = jnp.zeros(w_output.shape, jnp.float32)
    grad_down_w = jnp.zeros(w_down.shape, jnp.float32)
    grad_dec = jnp.zeros(w_dec.shape, jnp.float32)
    grad_gain_att = jnp.zeros((feat,), jnp.float32)
    grad_gain_mlp = jnp.zeros((feat,), jnp.float32)
    loss_sum = jnp.zeros((), jnp.float32)
    for globe in range(MB):
        sigma = noise_sigma[globe]
        square = sigma * sigma
        c_in = lax.rsqrt(square + 1.0)
        c_skip = 1.0 / (square + 1.0)
        c_out = sigma * c_in
        noisy = target[globe] + sigma * noise_draw[globe]
        grid = jnp.concatenate([cond_fields[globe], (c_in * noisy).astype(jnp.bfloat16)], axis=1)
        embed = matmul(grid, enc_full)
        state0 = jnp.sum(embed[local_grid], axis=1) / KG
        rows_att, gain_full_att = gather_rows(state0, gain_att)
        normed, normal_att, inverse_att = norm_rows(
            rows_att.astype(jnp.float32), gain_full_att.astype(jnp.float32)
        )
        normed_att = normed.astype(jnp.bfloat16)
        qkv = matmul(normed_att, w_qkv).astype(jnp.bfloat16)
        query = qkv[:, :feat].reshape(nodes, heads_here, HEAD_DIM)
        extended = padded(qkv[:, feat:], (("wide", 0),), nodes)
        picked = extended[slot_rows]
        keys = picked[:, :, :feat].reshape(nodes, KM, heads_here, HEAD_DIM)
        values_wide = (
            picked[:, :, feat:].astype(jnp.float32).reshape(nodes, KM, heads_here, HEAD_DIM)
        )
        scores = (
            jnp.einsum("nhd,nkhd->nhk", query, keys, preferred_element_type=jnp.float32) * scale
        )
        scores = jnp.where(valid[:, None, :], scores, -1e30)
        top = jnp.max(scores, axis=-1, keepdims=True)
        expo = jnp.exp(scores - top)
        probs = expo / jnp.sum(expo, axis=-1, keepdims=True)
        mixed = jnp.einsum("nhk,nkhd->nhd", probs, values_wide, precision=HIGH)
        mixed_low = mixed.reshape(nodes, feat).astype(jnp.bfloat16)
        state1 = state0 + finish_branch(matmul(mixed_low, w_output))
        rows_mlp, gain_full_mlp = gather_rows(state1, gain_mlp)
        normed, normal_mlp, inverse_mlp = norm_rows(
            rows_mlp.astype(jnp.float32), gain_full_mlp.astype(jnp.float32)
        )
        normed_mlp = normed.astype(jnp.bfloat16)
        pre = matmul(normed_mlp, w_hidden)
        act = jax.nn.silu(pre).astype(jnp.bfloat16)
        state2 = state1 + finish_branch(matmul(act, w_down))
        pooled = (jnp.sum(state2[local_mesh], axis=1) / KD).astype(jnp.bfloat16)
        pred = lax.psum(matmul(pooled, w_dec).astype(jnp.bfloat16), "narrow").astype(jnp.float32)
        error = c_skip * noisy + c_out * pred - target[globe]
        weighted = (square + 1.0) / square * pix_weight
        loss_sum = loss_sum + jnp.sum(weighted * error * error)
        grad_pred = (2.0 * c_out * weighted * error).astype(jnp.bfloat16)
        grad_dec = grad_dec + left_trans(pooled, grad_pred)
        grad_pooled = right_trans(grad_pred, w_dec) / KD
        grad_state = (
            jnp.zeros((nodes, feat), jnp.float32)
            .at[local_mesh.reshape(-1)]
            .add(jnp.repeat(grad_pooled, KD, axis=0))
        )
        grad_rows = branch_grad(grad_state)
        grad_down_w = grad_down_w + left_trans(act, grad_rows)
        grad_act = right_trans(grad_rows, w_down)
        logistic = jax.nn.sigmoid(pre)
        grad_pre = (grad_act * logistic * (1.0 + pre * (1.0 - logistic))).astype(jnp.bfloat16)
        grad_hidden_w = grad_hidden_w + left_trans(normed_mlp, grad_pre)
        part_rows, part_gain = norm_back(
            right_trans(grad_pre, w_hidden),
            normal_mlp,
            inverse_mlp,
            gain_full_mlp.astype(jnp.float32),
        )
        back_rows, back_gain = return_rows(part_rows, part_gain)
        grad_gain_mlp = grad_gain_mlp + back_gain
        grad_state = grad_state + back_rows
        grad_rows = branch_grad(grad_state)
        grad_output_w = grad_output_w + left_trans(mixed_low, grad_rows)
        grad_mixed = right_trans(grad_rows, w_output).reshape(nodes, heads_here, HEAD_DIM)
        grad_probs = jnp.einsum("nhd,nkhd->nhk", grad_mixed, values_wide, precision=HIGH)
        grad_scores = (
            probs * (grad_probs - jnp.sum(probs * grad_probs, axis=-1, keepdims=True)) * scale
        )
        grad_query = jnp.einsum(
            "nhk,nkhd->nhd", grad_scores, keys.astype(jnp.float32), precision=HIGH
        )
        grad_keys = jnp.einsum(
            "nhk,nhd->nkhd", grad_scores, query.astype(jnp.float32), precision=HIGH
        )
        grad_values = jnp.einsum("nhk,nhd->nkhd", probs, grad_mixed, precision=HIGH)
        grad_pairs = jnp.concatenate(
            [grad_keys.reshape(nodes, KM, feat), grad_values.reshape(nodes, KM, feat)], axis=-1
        )
        grad_ext = (
            jnp.zeros((3 * nodes, 2 * feat), jnp.float32)
            .at[slot_rows.reshape(-1)]
            .add(grad_pairs.reshape(nodes * KM, 2 * feat))
        )
        from_next = from_behind(grad_ext[:nodes].astype(jnp.bfloat16), "wide", -1).astype(
            jnp.float32
        )
        from_prev = from_behind(grad_ext[2 * nodes :].astype(jnp.bfloat16), "wide", 1).astype(
            jnp.float32
        )
        grad_pair_own = (grad_ext[nodes : 2 * nodes] + from_next + from_prev).astype(jnp.bfloat16)
        grad_qkv = jnp.concatenate(
            [grad_query.reshape(nodes, feat).astype(jnp.bfloat16), grad_pair_own], axis=1
        )
        grad_qkv_w = grad_qkv_w + left_trans(normed_att, grad_qkv)
        part_rows, part_gain = norm_back(
            right_trans(grad_qkv, w_qkv), normal_att, inverse_att, gain_full_att.astype(jnp.float32)
        )
        back_rows, back_gain = return_rows(part_rows, part_gain)
        grad_gain_att = grad_gain_att + back_gain
        grad_state = grad_state + back_rows
        grad_embed = (
            jnp.zeros((pixels, feat), jnp.float32)
            .at[local_grid.reshape(-1)]
            .add(jnp.repeat(grad_state / KG, KG, axis=0))
        )
        grad_enc = grad_enc + left_trans(grid, grad_embed.astype(jnp.bfloat16))
    grad_up = jnp.concatenate([grad_qkv_w, grad_hidden_w], axis=1)
    grad_downs = jnp.concatenate([grad_output_w, grad_down_w], axis=0)
    grad_read = jnp.concatenate([grad_dec, grad_gain_att[:, None], grad_gain_mlp[:, None]], axis=1)
    summed = lax.psum((grad_enc, grad_up, grad_downs, grad_read), "wide")
    share_enc = lax.dynamic_slice_in_dim(
        summed[0], wide_index * (IN // wide_count), IN // wide_count, 0
    )
    share_up = lax.dynamic_slice_in_dim(
        summed[1], wide_index * (D // wide_count), D // wide_count, 0
    )
    share_down = lax.dynamic_slice_in_dim(
        summed[2], wide_index * (D // wide_count), D // wide_count, 1
    )
    share_read = lax.dynamic_slice_in_dim(
        summed[3], wide_index * (feat // wide_count), feat // wide_count, 0
    )
    shares = [share_enc, share_up, share_down, share_read]
    square_sum = (
        jnp.sum(share_enc * share_enc)
        + jnp.sum(share_up * share_up)
        + jnp.sum(share_down * share_down)
        + jnp.sum(share_read * share_read)
    )
    narrow_first = (narrow_index == 0).astype(jnp.float32)
    square_all, loss_all = lax.psum((square_sum, loss_sum * narrow_first), ("wide", "narrow"))
    total = early_total * MB
    norm_value = jnp.sqrt(square_all) / total
    factor = jnp.minimum(1.0, clip_norm / norm_value) / total
    step = jnp.asarray(STEPS_DONE, jnp.float32)
    fix_one = 1.0 - jnp.power(beta_one, step)
    fix_two = 1.0 - jnp.power(beta_two, step)
    states = [
        (encoder, encoder_moment, encoder_second, encoder_average),
        (up_proj, up_moment, up_second, up_average),
        (down_proj, down_moment, down_second, down_average),
        (readout, readout_moment, readout_second, readout_average),
    ]
    outputs = [loss_all / total, norm_value]
    for share, (weight, moment, second, average) in zip(shares, states):
        outputs.extend(
            adam_update(share, factor, fix_one, fix_two, weight, moment, second, average)
        )
    return tuple(outputs)


def solution(mesh):
    placed = (
        P(None, "wide", None),
        P(None, "wide", None),
        P(None, "wide", None),
        P(),
        P("wide", None),
        P("wide", None),
        P("wide", None),
        P("wide"),
        P(),
        P("wide", "narrow"),
        P("wide", "narrow"),
        P("narrow", "wide"),
        P(("narrow", "wide"), None),
        P("wide", "narrow"),
        P("wide", "narrow"),
        P("narrow", "wide"),
        P(("narrow", "wide"), None),
        P("wide", "narrow"),
        P("wide", "narrow"),
        P("narrow", "wide"),
        P(("narrow", "wide"), None),
        P("wide", "narrow"),
        P("wide", "narrow"),
        P("narrow", "wide"),
        P(("narrow", "wide"), None),
    )
    return jax.shard_map(
        body,
        mesh=mesh,
        in_specs=placed,
        out_specs=(
            P(),
            P(),
            P("wide", "narrow"),
            P("wide", "narrow"),
            P("wide", "narrow"),
            P("wide", "narrow"),
            P("wide", "narrow"),
            P("wide", "narrow"),
            P("wide", "narrow"),
            P("wide", "narrow"),
            P("wide", "narrow"),
            P("wide", "narrow"),
            P("narrow", "wide"),
            P("narrow", "wide"),
            P("narrow", "wide"),
            P("narrow", "wide"),
            P("narrow", "wide"),
            P(("narrow", "wide"), None),
            P(("narrow", "wide"), None),
            P(("narrow", "wide"), None),
            P(("narrow", "wide"), None),
            P(("narrow", "wide"), None),
        ),
        check_vma=False,
    )
```

profile of v0, /device:TPU:0, one launch (start us, length us, event | category | flops | bytes accessed | tf_op | source)
XLA Modules:
  0.0 1628.5 jit_solution(12360319729996108475)
XLA Ops:
  12.7 32.2 %all_gather.74 = bf16[128,86]{1,0:T(8,128)(2,1)S(1)} all-gather(bf16[16,86]{1,0:T(8,128)(2,1)S(1)} %convert_element_type.485), channel_id=1, replica_groups=mesh['wide'=8,'narrow'=4] {'wide'}, dimensions={0}, use_global_device_ids=true | all-gather | bytes 24768 | tf_op jit(solution)/shard_map/all_gather | solution.py:152
  44.9 30.5 %all_gather.72 = bf16[256,128]{1,0:T(8,128)(2,1)S(1)} all-gather(bf16[32,128]{1,0:T(8,128)(2,1)S(1)} %convert_element_type.482), channel_id=1, replica_groups=mesh['wide'=8,'narrow'=4] {'wide'}, dimensions={0}, use_global_device_ids=true | all-gather | bytes 73728 | tf_op jit(solution)/shard_map/all_gather | solution.py:149
  83.0 32.3 %all_gather.76 = bf16[512,896]{1,0:T(8,128)(2,1)S(1)} all-gather(bf16[64,896]{1,0:T(8,128)(2,1)S(1)} %convert_element_type.488), channel_id=1, replica_groups=mesh['wide'=8,'narrow'=4] {'wide'}, dimensions={0}, use_global_device_ids=true | all-gather | bytes 1032192 | tf_op jit(solution)/shard_map/all_gather | solution.py:150
  129.5 14.1 gather_fusion.3
  145.9 7.2 all_gather.80
  164.1 14.1 gather_fusion.9
  197.9 14.1 gather_fusion
  215.0 7.4 all_gather.73
  230.4 14.1 gather_fusion.6
  258.4 32.2 %all_gather.77 = bf16[640,512]{0,1:T(8,128)(2,1)S(1)} all-gather(bf16[640,64]{0,1:T(8,128)(2,1)S(1)} %convert_element_type.491), channel_id=1, replica_groups=mesh['wide'=8,'narrow'=4] {'wide'}, dimensions={1}, use_global_device_ids=true | all-gather | bytes 737280 | tf_op jit(solution)/shard_map/all_gather | solution.py:151
  296.4 33.0 %gather_fusion.10 = bf16[8192,256]{1,0:T(8,128)(2,1)} fusion(bf16[1536,256]{1,0:T(8,128)(2,1)S(1)} %pad_maximum_fusion.5, s32[8192]{0:T(1024)S(1)} %broadcast_clamp_fusion), kind=kCustom, calls=%fused_computation.10 | custom fusion | bytes 8421376 | tf_op jit(solution)/shard_map/gather | solution.py:208
  333.6 32.9 %gather_fusion.1 = bf16[8192,256]{1,0:T(8,128)(2,1)} fusion(bf16[1536,256]{1,0:T(8,128)(2,1)S(1)} %pad_maximum_fusion.2, s32[8192]{0:T(1024)S(1)} %broadcast_clamp_fusion), kind=kCustom, calls=%fused_computation.1 | custom fusion | bytes 8421376 | tf_op jit(solution)/shard_map/gather | solution.py:208
  370.6 33.0 %gather_fusion.7 = bf16[8192,256]{1,0:T(8,128)(2,1)} fusion(bf16[1536,256]{1,0:T(8,128)(2,1)S(1)} %pad_maximum_fusion.4, s32[8192]{0:T(1024)S(1)} %broadcast_clamp_fusion), kind=kCustom, calls=%fused_computation.7 | custom fusion | bytes 8421376 | tf_op jit(solution)/shard_map/gather | solution.py:208
  407.7 33.0 %gather_fusion.4 = bf16[8192,256]{1,0:T(8,128)(2,1)} fusion(bf16[1536,256]{1,0:T(8,128)(2,1)S(1)} %pad_maximum_fusion.3, s32[8192]{0:T(1024)S(1)} %broadcast_clamp_fusion), kind=kCustom, calls=%fused_computation.4 | custom fusion | bytes 8421376 | tf_op jit(solution)/shard_map/gather | solution.py:208
  477.7 7.3 all_gather.85
  485.1 11.1 reduce-scatter.53.cloned.1.call-done
  508.7 11.7 reduce-scatter.57.cloned.1.call-done
  535.5 9.2 reduce-scatter.49.cloned.1.call-done
  558.6 10.1 reduce-scatter.55.cloned.1.call-done
  571.4 21.4 %reduce-scatter.63.cloned.1.call-done = bf16[128,512]{1,0:T(8,128)(2,1)} async-done(((bf16[512,512]{1,0:T(8,128)(2,1)}), bf16[128,512]{1,0:T(8,128)(2,1)}) %reduce-scatter.63.cloned.1.call-update) | async-done | bytes 131088
  595.6 21.4 %reduce-scatter.59.cloned.1.call-done = bf16[128,512]{1,0:T(8,128)(2,1)} async-done(((bf16[512,512]{1,0:T(8,128)(2,1)}), bf16[128,512]{1,0:T(8,128)(2,1)}) %reduce-scatter.59.cloned.1.call-update) | async-done | bytes 131088
  618.2 23.1 %reduce-scatter.51.cloned.1.call-done = bf16[128,512]{1,0:T(8,128)(2,1)} async-done(((bf16[512,512]{1,0:T(8,128)(2,1)}), bf16[128,512]{1,0:T(8,128)(2,1)}) %reduce-scatter.51.cloned.1.call-update) | async-done | bytes 131088
  697.8 32.2 %all-reduce.18.cloned.1.call-done = (bf16[853,84]{0,1:T(8,128)(2,1)}, bf16[853,84]{0,1:T(8,128)(2,1)}, bf16[853,84]{0,1:T(8,128)(2,1)}, bf16[853,84]{0,1:T(8,128)(2,1)}) async-done(((bf16[853,84]{0,1:T(8,128)(2,1)}, bf16[853,84]{0,1:T(8,128)(2,1)}, bf16[853,84]{0,1:T(8,128)(2,1)}, bf16[853,84]{0,1:T(8,128)(2,1)}), (bf16[853,84]{0,1:T(8,128)(2,1)}, bf16[853,84]{0,1:T(8,128)(2,1)}, bf16[853,84]{0,1:T(8,128)(2,1)}, ...) | async-done | bytes 573232 | tf_op jit(solution)/shard_map/psum | solution.py:232
  742.2 14.6 scatter_custom_fusion
  772.9 14.6 scatter_custom_fusion.3
  787.5 7.5 all_gather.88
  804.4 14.6 scatter_custom_fusion.6
  819.1 7.3 all_gather.90
  836.1 15.2 scatter_custom_fusion.9
  852.3 7.3 all_gather.92
  897.8 7.3 all_gather.93
  918.9 7.7 all_gather.91
  939.8 7.3 all_gather.89
  987.9 45.6 %scatter_custom_fusion.1 = f32[1536,256]{1,0:T(8,128)S(1)} fusion(s32[8192]{0:T(1024)} %bitcast.449, f32[8192,128]{1,0:T(8,128)} %bitcast.390, f32[]{:T(128)} %constant.173.clone.1, f32[8192,128]{1,0:T(8,128)} %bitcast.394, f32[]{:T(128)} %constant.162.clone.1), kind=kCustom, calls=%fused_computation.24 | custom fusion | flops 4194304 | bytes 9962496 | tf_op jit(solution)/shard_map/scatter-add | solution.py:279
  1047.2 45.6 %scatter_custom_fusion.4 = f32[1536,256]{1,0:T(8,128)S(1)} fusion(s32[8192]{0:T(1024)} %bitcast.450, f32[8192,128]{1,0:T(8,128)} %bitcast.391, f32[]{:T(128)} %constant.173.clone.1, f32[8192,128]{1,0:T(8,128)} %bitcast.395, f32[]{:T(128)} %constant.162.clone.1), kind=kCustom, calls=%fused_computation.28 | custom fusion | flops 4194304 | bytes 9962496 | tf_op jit(solution)/shard_map/scatter-add | solution.py:279
  1106.6 45.6 %scatter_custom_fusion.7 = f32[1536,256]{1,0:T(8,128)S(1)} fusion(s32[8192]{0:T(1024)} %bitcast.451, f32[8192,128]{1,0:T(8,128)} %bitcast.392, f32[]{:T(128)} %constant.173.clone.1, f32[8192,128]{1,0:T(8,128)} %bitcast.396, f32[]{:T(128)} %constant.162.clone.1), kind=kCustom, calls=%fused_computation.32 | custom fusion | flops 4194304 | bytes 9962496 | tf_op jit(solution)/shard_map/scatter-add | solution.py:279
  1166.5 45.6 %scatter_custom_fusion.10 = f32[1536,256]{1,0:T(8,128)S(1)} fusion(s32[8192]{0:T(1024)} %bitcast.452, f32[8192,128]{1,0:T(8,128)} %bitcast.389, f32[]{:T(128)} %constant.173.clone.1, f32[8192,128]{1,0:T(8,128)} %bitcast.393, f32[]{:T(128)} %constant.162.clone.1), kind=kCustom, calls=%fused_computation.36 | custom fusion | flops 4194304 | bytes 9962496 | tf_op jit(solution)/shard_map/scatter-add | solution.py:279
  1222.8 8.8 collective-permute-done.14
  1259.7 23.1 %reduce-scatter.75.cloned.1.call-done = bf16[128,512]{1,0:T(8,128)(2,1)} async-done(((bf16[512,512]{1,0:T(8,128)(2,1)}), bf16[128,512]{1,0:T(8,128)(2,1)}) %reduce-scatter.75.cloned.1.call-update) | async-done | bytes 131088
  1283.9 22.9 %reduce-scatter.71.cloned.1.call-done = bf16[128,512]{1,0:T(8,128)(2,1)} async-done(((bf16[512,512]{1,0:T(8,128)(2,1)}), bf16[128,512]{1,0:T(8,128)(2,1)}) %reduce-scatter.71.cloned.1.call-update) | async-done | bytes 131088
  1307.9 23.1 %reduce-scatter.67.cloned.1.call-done = bf16[128,512]{1,0:T(8,128)(2,1)} async-done(((bf16[512,512]{1,0:T(8,128)(2,1)}), bf16[128,512]{1,0:T(8,128)(2,1)}) %reduce-scatter.67.cloned.1.call-update) | async-done | bytes 131088
  1332.1 22.6 %scatter_custom_fusion.2 = f32[853,128]{1,0:T(8,128)S(1)} fusion(s32[4096]{0:T(1024)} %bitcast.453, f32[512,128]{1,0:T(8,128)S(1)} %copy.502, f32[]{:T(128)} %constant.162.clone.1), kind=kCustom, calls=%fused_computation.46 | custom fusion | flops 524288 | bytes 699392 | tf_op jit(solution)/shard_map/scatter-add | solution.py:301
  1355.7 22.7 %scatter_custom_fusion.5 = f32[853,128]{1,0:T(8,128)S(1)} fusion(s32[4096]{0:T(1024)} %bitcast.454, f32[512,128]{1,0:T(8,128)S(1)} %copy.510, f32[]{:T(128)} %constant.162.clone.1), kind=kCustom, calls=%fused_computation.44 | custom fusion | flops 524288 | bytes 699392 | tf_op jit(solution)/shard_map/scatter-add | solution.py:301
  1378.4 22.6 %scatter_custom_fusion.8 = f32[853,128]{1,0:T(8,128)S(1)} fusion(s32[4096]{0:T(1024)} %bitcast.455, f32[512,128]{1,0:T(8,128)S(1)} %copy.518, f32[]{:T(128)} %constant.162.clone.1), kind=kCustom, calls=%fused_computation.42 | custom fusion | flops 524288 | bytes 699392 | tf_op jit(solution)/shard_map/scatter-add | solution.py:301
  1401.0 22.8 %scatter_custom_fusion.11 = f32[853,128]{1,0:T(8,128)S(1)} fusion(s32[4096]{0:T(1024)} %bitcast.456, f32[512,128]{1,0:T(8,128)S(1)} %copy.526, f32[]{:T(128)} %constant.162.clone.1), kind=kCustom, calls=%fused_computation.40 | custom fusion | flops 524288 | bytes 699392 | tf_op jit(solution)/shard_map/scatter-add | solution.py:301
  1438.7 41.9 %all-reduce.9 = (f32[128,86]{1,0:T(8,128)S(1)}, f32[]{:T(128)}) all-reduce(f32[128,86]{1,0:T(8,128)S(1)} %pad_maximum_fusion.30, f32[]{:T(128)} %get-tuple-element.164), channel_id=1, replica_groups=mesh['wide'=8,'narrow'=4] {'wide'}, use_global_device_ids=true, to_apply=%region_113.114 | all-reduce | flops 11009 | bytes 88072 | tf_op jit(solution)/shard_map/psum | solution.py:307
  1481.9 80.3 %all-reduce.16.cloned.1.call-done = (f32[256,128]{1,0:T(8,128)}, f32[512,896]{1,0:T(8,128)}, f32[640,512]{0,1:T(8,128)}) async-done(((f32[256,128]{1,0:T(8,128)}, f32[512,896]{1,0:T(8,128)}, f32[640,512]{0,1:T(8,128)}), (f32[256,128]{1,0:T(8,128)}, f32[512,896]{1,0:T(8,128)}, f32[640,512]{0,1:T(8,128)})) %all-reduce.16.cloned.1.call-update) | async-done | bytes 3276816 | tf_op jit(solution)/shard_map/psum | solution.py:307
  1570.0 39.2 %all-reduce.8 = (f32[]{:T(128)}, f32[]{:T(128)}) all-reduce(f32[]{:T(128)S(6)} %mul.1020, f32[]{:T(128)S(6)} %add.653), channel_id=1, replica_groups=mesh['wide'=8,'narrow'=4] {'wide','narrow'}, use_global_device_ids=true, to_apply=%region_48.49 | all-reduce | flops 2 | bytes 16 | tf_op jit(solution)/shard_map/psum | solution.py:328
  (965 shorter events, 497.8 us)
Async XLA Ops:
  7.2 469.6 %reduce-scatter.61.cloned.1.call-start = ((), (), s32[]{:S(2)}) async-start(), calls=%async_computation.22 | async-start | bytes 655360
  145.8 350.4 %copy-start.28 = (f32[512,128]{0,1:T(8,128)}, f32[512,128]{0,1:T(8,128)S(1)}, u32[]{:S(2)}) copy-start(f32[512,128]{0,1:T(8,128)S(1)} %copy.474) | copy-start | bytes 786436
  154.7 251.7 %collective-permute-start.3 = (bf16[512,256]{1,0:T(8,128)(2,1)}, bf16[512,256]{1,0:T(8,128)(2,1)}, u32[]{:S(2)}, u32[]{:S(2)}) collective-permute-start(bf16[512,256]{1,0:T(8,128)(2,1)} %slice.252), channel_id=1, source_target_pairs={{4,0},{8,4},{12,8},{16,12},{20,16},{24,20},{28,24},{0,28},{5,1},{9... | collective-permute-start | bytes 786440 | tf_op jit(solution)/shard_map/ppermute | solution.py:38
  159.2 247.3 %collective-permute-start.2 = (bf16[512,256]{1,0:T(8,128)(2,1)}, bf16[512,256]{1,0:T(8,128)(2,1)}, u32[]{:S(2)}, u32[]{:S(2)}) collective-permute-start(bf16[512,256]{1,0:T(8,128)(2,1)} %slice.252), channel_id=1, source_target_pairs={{0,4},{4,8},{8,12},{12,16},{16,20},{20,24},{24,28},{28,0},{1,5},{5... | collective-permute-start | bytes 786440 | tf_op jit(solution)/shard_map/ppermute | solution.py:37
  180.5 296.3 %copy-start.30 = (f32[512,128]{0,1:T(8,128)}, f32[512,128]{0,1:T(8,128)S(1)}, u32[]{:S(2)}) copy-start(f32[512,128]{0,1:T(8,128)S(1)} %copy.488) | copy-start | bytes 786436
  189.2 101.3 %collective-permute-start.7 = (bf16[512,256]{1,0:T(8,128)(2,1)}, bf16[512,256]{1,0:T(8,128)(2,1)}, u32[]{:S(2)}, u32[]{:S(2)}) collective-permute-start(bf16[512,256]{1,0:T(8,128)(2,1)} %slice.260), channel_id=1, source_target_pairs={{4,0},{8,4},{12,8},{16,12},{20,16},{24,20},{28,24},{0,28},{5,1},{9... | collective-permute-start | bytes 786440 | tf_op jit(solution)/shard_map/ppermute | solution.py:38
  193.6 96.9 %collective-permute-start.6 = (bf16[512,256]{1,0:T(8,128)(2,1)}, bf16[512,256]{1,0:T(8,128)(2,1)}, u32[]{:S(2)}, u32[]{:S(2)}) collective-permute-start(bf16[512,256]{1,0:T(8,128)(2,1)} %slice.260), channel_id=1, source_target_pairs={{0,4},{4,8},{8,12},{12,16},{16,20},{20,24},{24,28},{28,0},{1,5},{5... | collective-permute-start | bytes 786440 | tf_op jit(solution)/shard_map/ppermute | solution.py:37
  223.9 108.4 %collective-permute-start.1 = (bf16[512,256]{1,0:T(8,128)(2,1)}, bf16[512,256]{1,0:T(8,128)(2,1)}, u32[]{:S(2)}, u32[]{:S(2)}) collective-permute-start(bf16[512,256]{1,0:T(8,128)(2,1)} %slice.243), channel_id=1, source_target_pairs={{4,0},{8,4},{12,8},{16,12},{20,16},{24,20},{28,24},{0,28},{5,1},{9... | collective-permute-start | bytes 786440 | tf_op jit(solution)/shard_map/ppermute | solution.py:38
  290.5 240.5 %copy-start.23 = (bf16[640,512]{0,1:T(8,128)(2,1)}, bf16[640,512]{0,1:T(8,128)(2,1)S(1)}, u32[]{:S(2)}) copy-start(bf16[640,512]{0,1:T(8,128)(2,1)S(1)} %all_gather.77) | copy-start | bytes 1966084
  290.5 41.9 %collective-permute-start = (bf16[512,256]{1,0:T(8,128)(2,1)}, bf16[512,256]{1,0:T(8,128)(2,1)}, u32[]{:S(2)}, u32[]{:S(2)}) collective-permute-start(bf16[512,256]{1,0:T(8,128)(2,1)} %slice.243), channel_id=1, source_target_pairs={{0,4},{4,8},{8,12},{12,16},{16,20},{20,24},{24,28},{28,0},{1,5},{5... | collective-permute-start | bytes 786440 | tf_op jit(solution)/shard_map/ppermute | solution.py:37
  290.5 78.9 %collective-permute-start.5 = (bf16[512,256]{1,0:T(8,128)(2,1)S(1)}, bf16[512,256]{1,0:T(8,128)(2,1)}, u32[]{:S(2)}, u32[]{:S(2)}) collective-permute-start(bf16[512,256]{1,0:T(8,128)(2,1)S(1)} %slice.256), channel_id=1, source_target_pairs={{4,0},{8,4},{12,8},{16,12},{20,16},{24,20},{28,24},{0,28},{5,1},{9... | collective-permute-start | bytes 786440 | tf_op jit(solution)/shard_map/ppermute | solution.py:38
  332.3 37.1 %collective-permute-start.4 = (bf16[512,256]{1,0:T(8,128)(2,1)S(1)}, bf16[512,256]{1,0:T(8,128)(2,1)}, u32[]{:S(2)}, u32[]{:S(2)}) collective-permute-start(bf16[512,256]{1,0:T(8,128)(2,1)S(1)} %slice.256), channel_id=1, source_target_pairs={{0,4},{4,8},{8,12},{12,16},{16,20},{20,24},{24,28},{28,0},{1,5},{5... | collective-permute-start | bytes 786440 | tf_op jit(solution)/shard_map/ppermute | solution.py:37
  448.6 47.7 %reduce-scatter.53.cloned.1.call-start = ((), (), s32[]{:S(2)}) async-start(), calls=%async_computation.18 | async-start | bytes 655360
  454.2 66.2 %reduce-scatter.57.cloned.1.call-start = ((), (), s32[]{:S(2)}) async-start(), calls=%async_computation.20 | async-start | bytes 655360
  459.5 85.2 %reduce-scatter.49.cloned.1.call-start = ((), (), s32[]{:S(2)}) async-start(), calls=%async_computation.16 | async-start | bytes 655360
  476.7 92.0 %reduce-scatter.55.cloned.1.call-start = ((), (), s32[]{:S(2)}) async-start(), calls=%async_computation.19 | async-start | bytes 655360
  508.7 84.2 %reduce-scatter.63.cloned.1.call-start = ((), (), s32[]{:S(2)}) async-start(), calls=%async_computation.23 | async-start | bytes 655360
  530.4 86.6 %reduce-scatter.59.cloned.1.call-start = ((), (), s32[]{:S(2)}) async-start(), calls=%async_computation.21 | async-start | bytes 655360
  552.5 88.9 %reduce-scatter.51.cloned.1.call-start = ((), (), s32[]{:S(2)}) async-start(), calls=%async_computation.17 | async-start | bytes 655360
  557.8 172.2 %all-reduce.18.cloned.1.call-start = ((), (), s32[]{:S(2)}) async-start(), calls=%async_computation.33 | async-start | bytes 1261568 | tf_op jit(solution)/shard_map/psum | solution.py:232
  696.0 200.8 %reduce-scatter.77.cloned.1.call-start = ((), (), s32[]{:S(2)}) async-start(), calls=%async_computation.30 | async-start | bytes 655360
  866.7 51.3 %reduce-scatter.73.cloned.1.call-start = ((), (), s32[]{:S(2)}) async-start(), calls=%async_computation.28 | async-start | bytes 655360
  874.7 64.1 %reduce-scatter.69.cloned.1.call-start = ((), (), s32[]{:S(2)}) async-start(), calls=%async_computation.26 | async-start | bytes 655360
  887.6 74.4 %reduce-scatter.65.cloned.1.call-start = ((), (), s32[]{:S(2)}) async-start(), calls=%async_computation.24 | async-start | bytes 655360
  896.7 361.9 %reduce-scatter.79.cloned.1.call-start = ((), (), s32[]{:S(2)}) async-start(), calls=%async_computation.31 | async-start | bytes 655360
  1034.4 177.8 %collective-permute-start.8 = (bf16[512,256]{1,0:T(8,128)(2,1)}, bf16[512,256]{1,0:T(8,128)(2,1)}, u32[]{:S(2)}, u32[]{:S(2)}) collective-permute-start(bf16[512,256]{1,0:T(8,128)(2,1)} %get-tuple-element.233), channel_id=1, source_target_pairs={{0,28},{4,0},{8,4},{12,8},{16,12},{20,16},{24,20},{28,24},{1,29},{... | collective-permute-start | bytes 786440 | tf_op jit(solution)/shard_map/ppermute | solution.py:45
  1038.6 174.6 %collective-permute-start.9 = (bf16[512,256]{1,0:T(8,128)(2,1)}, bf16[512,256]{1,0:T(8,128)(2,1)}, u32[]{:S(2)}, u32[]{:S(2)}) collective-permute-start(bf16[512,256]{1,0:T(8,128)(2,1)} %get-tuple-element.234), channel_id=1, source_target_pairs={{0,4},{4,8},{8,12},{12,16},{16,20},{20,24},{24,28},{28,0},{1,5},{5... | collective-permute-start | bytes 786440 | tf_op jit(solution)/shard_map/ppermute | solution.py:45
  1093.7 126.0 %collective-permute-start.10 = (bf16[512,256]{1,0:T(8,128)(2,1)}, bf16[512,256]{1,0:T(8,128)(2,1)}, u32[]{:S(2)}, u32[]{:S(2)}) collective-permute-start(bf16[512,256]{1,0:T(8,128)(2,1)} %get-tuple-element.231), channel_id=1, source_target_pairs={{0,28},{4,0},{8,4},{12,8},{16,12},{20,16},{24,20},{28,24},{1,29},{... | collective-permute-start | bytes 786440 | tf_op jit(solution)/shard_map/ppermute | solution.py:45
  1098.3 121.6 %collective-permute-start.11 = (bf16[512,256]{1,0:T(8,128)(2,1)}, bf16[512,256]{1,0:T(8,128)(2,1)}, u32[]{:S(2)}, u32[]{:S(2)}) collective-permute-start(bf16[512,256]{1,0:T(8,128)(2,1)} %get-tuple-element.232), channel_id=1, source_target_pairs={{0,4},{4,8},{8,12},{12,16},{16,20},{20,24},{24,28},{28,0},{1,5},{5... | collective-permute-start | bytes 786440 | tf_op jit(solution)/shard_map/ppermute | solution.py:45
  1153.2 81.6 %collective-permute-start.12 = (bf16[512,256]{1,0:T(8,128)(2,1)}, bf16[512,256]{1,0:T(8,128)(2,1)}, u32[]{:S(2)}, u32[]{:S(2)}) collective-permute-start(bf16[512,256]{1,0:T(8,128)(2,1)} %get-tuple-element.229), channel_id=1, source_target_pairs={{0,28},{4,0},{8,4},{12,8},{16,12},{20,16},{24,20},{28,24},{1,29},{... | collective-permute-start | bytes 786440 | tf_op jit(solution)/shard_map/ppermute | solution.py:45
  1213.2 21.6 %collective-permute-start.13 = (bf16[512,256]{1,0:T(8,128)(2,1)S(1)}, bf16[512,256]{1,0:T(8,128)(2,1)S(1)}, u32[]{:S(2)}, u32[]{:S(2)}) collective-permute-start(bf16[512,256]{1,0:T(8,128)(2,1)S(1)} %copy-done.171), channel_id=1, source_target_pairs={{0,4},{4,8},{8,12},{12,16},{16,20},{20,24},{24,28},{28,0},{1,5},{5... | collective-permute-start | bytes 786440 | tf_op jit(solution)/shard_map/ppermute | solution.py:45
  1213.2 18.4 %collective-permute-start.14 = (bf16[512,256]{1,0:T(8,128)(2,1)S(1)}, bf16[512,256]{1,0:T(8,128)(2,1)S(1)}, u32[]{:S(2)}, u32[]{:S(2)}) collective-permute-start(bf16[512,256]{1,0:T(8,128)(2,1)S(1)} %get-tuple-element.227), channel_id=1, source_target_pairs={{0,28},{4,0},{8,4},{12,8},{16,12},{20,16},{24,20},{28,24},{1,29},{... | collective-permute-start | bytes 786440 | tf_op jit(solution)/shard_map/ppermute | solution.py:45
  1219.8 11.8 collective-permute-start.15
  1239.9 42.9 %reduce-scatter.75.cloned.1.call-start = ((), (), s32[]{:S(2)}) async-start(), calls=%async_computation.29 | async-start | bytes 655360
  1244.1 62.8 %reduce-scatter.71.cloned.1.call-start = ((), (), s32[]{:S(2)}) async-start(), calls=%async_computation.27 | async-start | bytes 655360
  1249.2 81.7 %reduce-scatter.67.cloned.1.call-start = ((), (), s32[]{:S(2)}) async-start(), calls=%async_computation.25 | async-start | bytes 655360
  1255.0 307.3 %all-reduce.16.cloned.1.call-start = ((), (), s32[]{:S(2)}) async-start(), calls=%async_computation.32 | async-start | bytes 6553600 | tf_op jit(solution)/shard_map/psum | solution.py:307
  1431.0 181.5 %copy-start.150 = (f32[640,64]{0,1:T(8,128)S(1)}, f32[640,64]{0,1:T(8,128)}, u32[]{:S(2)}) copy-start(f32[640,64]{0,1:T(8,128)} %param.36) | copy-start | bytes 491524
  1431.0 181.5 %copy-start.176 = (f32[640,64]{0,1:T(8,128)S(1)}, f32[640,64]{0,1:T(8,128)}, u32[]{:S(2)}) copy-start(f32[640,64]{0,1:T(8,128)} %param.44) | copy-start | bytes 491524
  1431.7 182.7 %copy-start.188 = (f32[32,128]{1,0:T(8,128)S(1)}, f32[32,128]{1,0:T(8,128)}, u32[]{:S(2)}) copy-start(f32[32,128]{1,0:T(8,128)} %param.34) | copy-start | bytes 49156
  1431.7 182.7 %copy-start.237 = (f32[32,128]{1,0:T(8,128)S(1)}, f32[32,128]{1,0:T(8,128)}, u32[]{:S(2)}) copy-start(f32[32,128]{1,0:T(8,128)} %param.42) | copy-start | bytes 49156
  1431.7 182.7 %copy-start.238 = (f32[32,128]{1,0:T(8,128)S(1)}, f32[32,128]{1,0:T(8,128)}, u32[]{:S(2)}) copy-start(f32[32,128]{1,0:T(8,128)} %param.38) | copy-start | bytes 49156
  1431.7 184.1 %copy-start.197 = (f32[16,86]{1,0:T(8,128)S(1)}, f32[16,86]{1,0:T(8,128)}, u32[]{:S(2)}) copy-start(f32[16,86]{1,0:T(8,128)} %param.37) | copy-start | bytes 16516
  1431.8 184.1 %copy-start.248 = (f32[16,86]{1,0:T(8,128)S(1)}, f32[16,86]{1,0:T(8,128)}, u32[]{:S(2)}) copy-start(f32[16,86]{1,0:T(8,128)} %param.45) | copy-start | bytes 16516
  1431.8 184.1 %copy-start.249 = (f32[16,86]{1,0:T(8,128)S(1)}, f32[16,86]{1,0:T(8,128)}, u32[]{:S(2)}) copy-start(f32[16,86]{1,0:T(8,128)} %param.41) | copy-start | bytes 16516
  1431.8 184.7 %copy-start.250 = (f32[16,86]{1,0:T(8,128)S(1)}, f32[16,86]{1,0:T(8,128)}, u32[]{:S(2)}) copy-start(f32[16,86]{1,0:T(8,128)} %param.49) | copy-start | bytes 16516
  1431.8 185.3 %copy-start.239 = (f32[32,128]{1,0:T(8,128)S(1)}, f32[32,128]{1,0:T(8,128)}, u32[]{:S(2)}) copy-start(f32[32,128]{1,0:T(8,128)} %param.46) | copy-start | bytes 49156
  1431.8 185.9 %copy-start.175 = (f32[640,64]{0,1:T(8,128)S(1)}, f32[640,64]{0,1:T(8,128)}, u32[]{:S(2)}) copy-start(f32[640,64]{0,1:T(8,128)} %param.48) | copy-start | bytes 491524
  (257 other events, 3914.8 us)
Sparse Core Ops, SparseCore 0:
  448.7 23.2 reduce-scatter.60
  474.6 21.6 reduce-scatter.52
  498.7 21.6 reduce-scatter.56
  522.9 21.6 reduce-scatter.48
  547.0 21.6 reduce-scatter.54
  571.1 21.6 reduce-scatter.62
  595.3 21.6 reduce-scatter.58
  619.7 21.6 reduce-scatter.50
  696.1 33.8 all-reduce.17
  866.8 22.3 reduce-scatter.76
  891.8 21.6 reduce-scatter.72
  915.9 21.7 reduce-scatter.68
  940.3 21.6 reduce-scatter.64
  1240.0 18.5 reduce-scatter.78
  1261.1 21.6 reduce-scatter.74
  1285.1 21.6 reduce-scatter.70
  1309.3 21.6 reduce-scatter.66
  1426.5 135.7 all-reduce.15
where the time goes:
time: 1650 us; the launch traced here: 1630 us
  other arithmetic  475 us (29%)
  blocking collectives  340 us (21%)
  local copies, waits for them, and re-layouts  313 us (19%)
  waiting for transfers between devices  304 us (18%)
  matrix products  120 us (7%)
  starting transfers between devices  38.9 us (2%)
  between operations  37.5 us (2%)
    unnamed x34, waiting for transfers between devices  183 us
    scatter-add x4, other arithmetic, body(): grad_ext = jnp.zeros((3 * nodes, 2 * feat), jnp.float32).at[slot_rows.res...  182 us
    gather x4, local copies, waits for them, and re-layouts, body(): picked = extended[slot_rows]  132 us
    scatter-add x4, other arithmetic, body(): grad_embed = jnp.zeros((pixels, feat), jnp.float32).at[local_grid.reshape...  90.7 us
    psum x1, waiting for transfers between devices, body(): summed = lax.psum((grad_enc, grad_up, grad_downs, grad_read), 'wide')  80.3 us
    scatter-add x4, other arithmetic, body(): grad_state = jnp.zeros((nodes, feat), jnp.float32).at[local_mesh.reshape(...  59.1 us
    all_gather x8, blocking collectives, branch_grad(): lax.all_gather(grad_state.astype(jnp.bfloat16), 'narrow', axis=1, tiled=T...  57.9 us
    gather x4, local copies, waits for them, and re-layouts, body(): state0 = jnp.sum(embed[local_grid], axis=1) / KG  56.5 us
  transfers between devices with their start and end apart: 34, of which 15 were waited for; matrix products, arithmetic and copies ran while one was open for 29% of the time, Pallas kernels for 0%

commit v1 on v0

v1 whole, which is shorter than its diff:
```python
import functools
import math

import jax
import jax.numpy as jnp
from jax import lax
from jax.experimental import pallas as pl
from jax.experimental.pallas import tpu as pltpu
from jax.sharding import PartitionSpec as P

D = 512
HEADS = 4
HEAD_DIM = 128
OUT = 84
IN = 256
LEVELS = 13
KM = 16
KG = 8
KD = 3
STEPS_DONE = 7
MB = 4
GROUPS = 4
HID = 512
ROWS = 8
LINES = 64
EARLY = 512
LATE = 1152
BAND = 256
WINDOW = 1280
NEAR = 1536

clip_norm = 0.001
beta_one = 0.9
beta_two = 0.999
epsilon = 1e-08
learn_rate = 0.04
weight_decay = 0.1
average_decay = 0.9

BF = jnp.bfloat16
F32 = jnp.float32
BIG = 60 * 1024 * 1024


def mm(left, right):
    return jnp.dot(left, right, preferred_element_type=F32)


def mm_nt(left, right):
    return lax.dot_general(left, right, (((1,), (1,)), ((), ())), preferred_element_type=F32)


def mm_tn(left, right):
    return lax.dot_general(left, right, (((0,), (0,)), ((), ())), preferred_element_type=F32)


def split_two(value):
    high = value.astype(BF)
    return high, (value - high.astype(F32)).astype(BF)


def norm_parts(rows_low):
    values = rows_low.astype(F32)
    center = values - jnp.mean(values, axis=-1, keepdims=True)
    inverse = lax.rsqrt(jnp.mean(center * center, axis=-1, keepdims=True) + 1e-05)
    return center * inverse, inverse


def norm_pull(grad_out, normal, inverse, gain):
    scaled = grad_out * gain
    inner = (
        scaled
        - jnp.mean(scaled, axis=-1, keepdims=True)
        - normal * jnp.mean(scaled * normal, axis=-1, keepdims=True)
    )
    return inner * inverse, jnp.sum(grad_out * normal, axis=0, keepdims=True)


def prepare_kernel(grid_ref, pixels_ref, slots_ref, up_ref, across_ref, sums_ref, bias_ref, pool_ref, pull_ref, count_ref):
    nodes = sums_ref.shape[0]
    width = grid_ref.shape[0]
    step = 32

    def count_pixels(i, _):
        at = pl.multiple_of(i * step, step)
        picks = pixels_ref[pl.ds(at, step), :]
        lanes = lax.broadcasted_iota(jnp.int32, (step, width), 1)
        total = jnp.zeros((step, width), jnp.int32)
        for k in range(KG):
            total = total + (picks[:, k : k + 1] == lanes).astype(jnp.int32)
        count_ref[pl.ds(at, step), :] = total.astype(F32).astype(BF)
        return 0

    lax.fori_loop(0, nodes // step, count_pixels, 0)
    sums_ref[...] = mm(count_ref[...], grid_ref[...])

    def count_slots(i, _):
        at = pl.multiple_of(i * step, step)
        band = (i * step) // BAND
        picks = slots_ref[pl.ds(at, step), :] - band * BAND
        lanes = lax.broadcasted_iota(jnp.int32, (step, WINDOW), 1)
        total = jnp.zeros((step, WINDOW), jnp.int32)
        for k in range(KM):
            total = total + (picks[:, k : k + 1] == lanes).astype(jnp.int32)
        bias_ref[pl.ds(at, step), :] = jnp.where(
            total > 0, jnp.log2(total.astype(F32)), -1e30
        )
        return 0

    lax.fori_loop(0, nodes // step, count_slots, 0)

    def count_up(i, _):
        at = pl.multiple_of(i * step, step)
        picks = up_ref[pl.ds(at, step), :]
        lanes = lax.broadcasted_iota(jnp.int32, (step, nodes), 1)
        total = jnp.zeros((step, nodes), jnp.int32)
        for k in range(KD):
            total = total + (picks[:, k : k + 1] == lanes).astype(jnp.int32)
        pool_ref[pl.ds(at, step), :] = total.astype(F32).astype(BF)
        return 0

    lax.fori_loop(0, width // step, count_up, 0)

    def count_across(i, _):
        at = pl.multiple_of(i * step, step)
        rows = lax.broadcasted_iota(jnp.int32, (step, width), 0) + at
        total = jnp.zeros((step, width), jnp.int32)
        for k in range(KD):
            total = total + (across_ref[k : k + 1, :] == rows).astype(jnp.int32)
        pull_ref[pl.ds(at, step), :] = total.astype(F32).astype(BF)
        return 0

    lax.fori_loop(0, nodes // step, count_across, 0)


def prepare(grid, pixel_rows, slot_rows, up_rows, across_rows):
    nodes, width = slot_rows.shape[0], grid.shape[0]
    return pl.pallas_call(
        prepare_kernel,
        out_shape=(
            jax.ShapeDtypeStruct((nodes, IN), F32),
            jax.ShapeDtypeStruct((nodes, WINDOW), F32),
            jax.ShapeDtypeStruct((width, nodes), BF),
            jax.ShapeDtypeStruct((nodes, width), BF),
        ),
        scratch_shapes=[pltpu.VMEM((nodes, width), BF)],
        compiler_params=pltpu.CompilerParams(vmem_limit_bytes=32 * 1024 * 1024),
        cost_estimate=pl.CostEstimate(flops=400_000_000, bytes_accessed=6_000_000, transcendentals=700_000),
        name="prepare",
    )(grid, pixel_rows, slot_rows, up_rows, across_rows)


def copies_of(pairs, sems):
    return [pltpu.make_async_copy(source, target, sems.at[i]) for i, (source, target) in enumerate(pairs)]


def early_weights(early_ref, enc, wq, wkv, dec):
    pairs = []
    for n in range(GROUPS):
        if enc is not None:
            pairs.append((early_ref.at[:, n, 0:32, 384:512], enc.at[:, :, n * 128 : n * 128 + 128]))
        pairs.append((early_ref.at[:, n, :, 0:128], wq.at[:, :, n * 128 : n * 128 + 128]))
        pairs.append((early_ref.at[:, n, :, 128:256], wkv.at[:, :, n * 128 : n * 128 + 128]))
        pairs.append((early_ref.at[:, n, :, 256:384], wkv.at[:, :, 512 + n * 128 : 640 + n * 128]))
        pairs.append((early_ref.at[:, n, 32:48, 384:512], dec.at[n]))
    return pairs


def attend_kernel(
    early_ref, sums_ref, bias_ref,
    state_ref, rows_ref, normed_ref, query_ref, pair_ref, mixed_ref, probs_ref,
    enc, wq, wkv, dec, sems,
):
    copies = copies_of(early_weights(early_ref, enc, wq, wkv, dec), sems)
    for copy in copies:
        copy.start()
    for copy in copies:
        copy.wait()
    gain = dec[...].reshape(D, 128).astype(F32).T[OUT : OUT + 1, :]
    enc_full = enc[...].reshape(IN, D)
    pair_full = wkv[...].reshape(D, 2 * D)
    step = 256

    def encode(i, _):
        at = pl.multiple_of(i * step, step)
        high, low = split_two(sums_ref[pl.ds(at, step), :])
        state = (mm(high, enc_full) + mm(low, enc_full)) * (1.0 / KG)
        rows = state.astype(BF)
        rows_ref[pl.ds(at, step), :] = rows
        normal, _inverse = norm_parts(rows)
        normed = (normal * gain).astype(BF)
        normed_ref[pl.ds(at, step), :] = normed
        pair_ref[pl.ds(at, step), :] = mm(normed, pair_full).astype(BF)

        @pl.when((i >= 2) & (i < 4))
        def _():
            state_ref[pl.ds(pl.multiple_of(at - 512, step), step), :] = state

        return 0

    lax.fori_loop(0, NEAR // step, encode, 0)
    query_ref[...] = mm(normed_ref[512:1024, :], wq[...].reshape(D, D)).astype(BF)
    factor = HEAD_DIM ** (-0.5) * math.log2(math.e)

    def head(h, _):
        lane = pl.multiple_of(h * HEAD_DIM, HEAD_DIM)
        for band in range(2):
            at = band * BAND
            query = query_ref[at : at + BAND, pl.ds(lane, HEAD_DIM)]
            keys = pair_ref[at : at + WINDOW, pl.ds(lane, HEAD_DIM)]
            values = pair_ref[at : at + WINDOW, pl.ds(lane + D, HEAD_DIM)]
            scores = mm_nt(query, keys) * factor + bias_ref[at : at + BAND, :]
            top = jnp.max(scores, axis=-1, keepdims=True)
            expo = jnp.exp2(scores - top)
            inverse = 1.0 / jnp.sum(expo, axis=-1, keepdims=True)
            mixed_ref[at : at + BAND, pl.ds(lane, HEAD_DIM)] = (
                mm(expo.astype(BF), values) * inverse
            ).astype(BF)
            probs_ref[h, at : at + BAND, :] = (expo * inverse).astype(BF)
        return 0

    lax.fori_loop(0, HEADS, head, 0)


def attend(early, sums, bias):
    nodes = bias.shape[0]
    return pl.pallas_call(
        attend_kernel,
        in_specs=[
            pl.BlockSpec(memory_space=pl.ANY),
            pl.BlockSpec(memory_space=pltpu.VMEM),
            pl.BlockSpec(memory_space=pltpu.VMEM),
        ],
        out_shape=(
            jax.ShapeDtypeStruct((nodes, D), F32),
            jax.ShapeDtypeStruct((NEAR, D), BF),
            jax.ShapeDtypeStruct((NEAR, D), BF),
            jax.ShapeDtypeStruct((nodes, D), BF),
            jax.ShapeDtypeStruct((NEAR, 2 * D), BF),
            jax.ShapeDtypeStruct((nodes, D), BF),
            jax.ShapeDtypeStruct((HEADS, nodes, WINDOW), BF),
        ),
        scratch_shapes=[
            pltpu.VMEM((8, 32, D), BF),
            pltpu.VMEM((8, 64, D), BF),
            pltpu.VMEM((8, 64, 2 * D), BF),
            pltpu.VMEM((GROUPS, 8, 16, 128), BF),
            pltpu.SemaphoreType.DMA((20,)),
        ],
        compiler_params=pltpu.CompilerParams(vmem_limit_bytes=BIG),
        cost_estimate=pl.CostEstimate(flops=5_000_000_000, bytes_accessed=18_000_000, transcendentals=3_000_000),
        name="attend",
    )(early, sums, bias)


def feed_kernel(
    place_ref, scalars_ref, late_ref, early_ref, state_ref, mixed_ref, pool_ref, pull_ref, noisy_ref, target_ref, lat_ref, level_ref,
    keep_ref, send_ref, grad_state_ref, grad_mixed_ref, grad_dec_ref, loss_ref,
    w_hid, w_out, w_down, dec, pre_ref, act_ref, grad_pred_ref, sems,
):
    pairs = []
    for n in range(GROUPS):
        pairs.append((late_ref.at[:, n, :, 512:640], w_out.at[:, :, n * 128 : n * 128 + 128]))
        pairs.append((early_ref.at[:, n, 32:48, 384:512], dec.at[n]))
        pairs.append((late_ref.at[:, n, :, 0:512], w_hid.at[:, :, n * HID : (n + 1) * HID]))
        pairs.append((late_ref.at[:, n, :, 640:1152], w_down.at[:, :, n * HID : (n + 1) * HID]))
    copies = copies_of(pairs, sems)
    for copy in copies:
        copy.start()
    for copy in copies:
        copy.wait()
    dec_full = dec[...].reshape(D, 128)
    gain = dec_full.astype(F32).T[OUT + 1 : OUT + 2, :]
    out_full = w_out[...].reshape(D, D)
    mixed = mixed_ref[...]
    state1 = state_ref[...] + mm_nt(mixed, out_full)
    normal, inverse = norm_parts(state1.astype(BF))
    normed = (normal * gain).astype(BF)

    def forward(n, state):
        lane = pl.multiple_of(n * HID, HID)
        pre = mm(normed, w_hid[:, :, pl.ds(lane, HID)].reshape(D, HID))
        pre_ref[n] = pre
        act = (pre / (1.0 + jnp.exp(-pre))).astype(BF)
        act_ref[n] = act
        return state + mm_nt(act, w_down[:, :, pl.ds(lane, HID)].reshape(D, HID))

    state2 = lax.fori_loop(0, GROUPS, forward, state1)
    high, low = split_two(state2)
    pool = pool_ref[...]
    pooled = ((mm(pool, high) + mm(pool, low)) / KD).astype(BF)
    pixels = noisy_ref.shape[0]
    pred = mm(pooled, dec_full)[:pixels, :OUT]
    c_skip, c_out, lam = scalars_ref[0], scalars_ref[1], scalars_ref[2]
    error = c_skip * noisy_ref[...] + c_out * pred - target_ref[...]
    weighted = lam * (lat_ref[...] * level_ref[...])
    loss_ref[...] = jnp.broadcast_to(jnp.sum(weighted * error * error), loss_ref.shape)
    grad_pred_ref[...] = jnp.zeros_like(grad_pred_ref)
    grad_pred_ref[:pixels, :OUT] = 2.0 * c_out * weighted * error
    grad_pred = grad_pred_ref[...].astype(BF)
    grad_dec_ref[...] = mm_tn(grad_pred, pooled)
    up_high, up_low = split_two(mm(pull_ref[...], grad_pred))
    lanes = lax.broadcasted_iota(jnp.int32, (1, 128), 1)
    dec_only = jnp.where(lanes < OUT, dec_full.astype(F32), 0.0).astype(BF)
    grad_state2 = (mm_nt(up_high, dec_only) + mm_nt(up_low, dec_only)) / KD
    grad_low = grad_state2.astype(BF)

    own_wide, own_narrow = place_ref[0], place_ref[1]

    def put(out_ref, side, part, first, value):
        done = 0
        while done < value.shape[1]:
            colour, column = divmod(first + done, 384)
            count = min(384 - column, value.shape[1] - done)
            for w in range(8):
                out_ref[colour, part, w ^ own_wide, :, column : column + count] = value[
                    w * LINES : (w + 1) * LINES, done : done + count
                ]
            done += count

    def backward(part, grad_n, out_ref, side):
        n = (part * 2 + side) ^ own_narrow
        lane = pl.multiple_of(n * HID, HID)
        act = act_ref[n]
        pre = pre_ref[n]
        put(out_ref, side, part, 640, mm_tn(grad_low, act).astype(BF))
        grad_act = mm(grad_low, w_down[:, :, pl.ds(lane, HID)].reshape(D, HID))
        logistic = 1.0 / (1.0 + jnp.exp(-pre))
        grad_pre = (grad_act * logistic * (1.0 + pre * (1.0 - logistic))).astype(BF)
        put(out_ref, side, part, 0, mm_tn(normed, grad_pre).astype(BF))
        return grad_n + mm_nt(grad_pre, w_hid[:, :, pl.ds(lane, HID)].reshape(D, HID))

    grad_n = jnp.zeros((D, D), F32)
    for side, out_ref in ((1, send_ref), (0, keep_ref)):
        grad_n = lax.fori_loop(0, 2, functools.partial(backward, out_ref=out_ref, side=side), grad_n)
    back, gain_grad = norm_pull(grad_n, normal, inverse, gain)
    grad_dec_ref[OUT + 1 : OUT + 2, :] = gain_grad
    grad_state1 = grad_state2 + back
    grad_state_ref[...] = grad_state1
    grad_low1 = grad_state1.astype(BF)
    act_ref[0] = mixed
    for side, out_ref in ((1, send_ref), (0, keep_ref)):
        for part in range(2):
            lane = pl.multiple_of(((part * 2 + side) ^ own_narrow) * 128, 128)
            put(out_ref, side, part, 512, mm_tn(grad_low1, act_ref[0, :, pl.ds(lane, 128)]).astype(BF))
    grad_mixed_ref[...] = mm(grad_low1, out_full)


def feed(place, scalars, late, early, state0, mixed, pool, pull, noisy, target, lat, level):
    nodes = state0.shape[0]
    width = pool.shape[0]
    vmem = pl.BlockSpec(memory_space=pltpu.VMEM)
    anywhere = pl.BlockSpec(memory_space=pl.ANY)
    return pl.pallas_call(
        feed_kernel,
        in_specs=[pl.BlockSpec(memory_space=pltpu.SMEM)] * 2 + [anywhere, anywhere] + [vmem] * 8,
        out_shape=(
            jax.ShapeDtypeStruct((3, 2, 8, LINES, 384), BF),
            jax.ShapeDtypeStruct((3, 2, 8, LINES, 384), BF),
            jax.ShapeDtypeStruct((nodes, D), F32),
            jax.ShapeDtypeStruct((nodes, D), F32),
            jax.ShapeDtypeStruct((128, D), F32),
            jax.ShapeDtypeStruct((8, 128), F32),
        ),
        scratch_shapes=[
            pltpu.VMEM((8, LINES, GROUPS * HID), BF),
            pltpu.VMEM((8, LINES, D), BF),
            pltpu.VMEM((8, LINES, GROUPS * HID), BF),
            pltpu.VMEM((GROUPS, 8, 16, 128), BF),
            pltpu.VMEM((GROUPS, nodes, HID), F32),
            pltpu.VMEM((GROUPS, nodes, HID), BF),
            pltpu.VMEM((width, 128), F32),
            pltpu.SemaphoreType.DMA((16,)),
        ],
        compiler_params=pltpu.CompilerParams(vmem_limit_bytes=BIG),
        cost_estimate=pl.CostEstimate(flops=9_000_000_000, bytes_accessed=20_000_000, transcendentals=3_000_000),
        name="feed",
    )(place, scalars, late, early, state0, mixed, pool, pull, noisy, target, lat, level)


def return_kernel(
    place_ref, early_ref, probs_ref, query_ref, pair_ref, grad_mixed_ref, grad_state_ref, rows_ref, normed_ref, sums_ref, grad_dec_ref,
    keep_ref, send_ref,
    wq, wkv, dec, grad_query, grad_pair, turned, turn_query, turn_mixed, grad_weight, sems,
):
    copies = copies_of(early_weights(early_ref, None, wq, wkv, dec), sems)
    for copy in copies:
        copy.start()
    scale = HEAD_DIM ** (-0.5)
    turned[...] = jnp.zeros_like(turned)
    turn_query[...] = query_ref[...].astype(F32).T.astype(BF)
    turn_mixed[...] = grad_mixed_ref[...].T.astype(BF)

    def head(h, _):
        lane = pl.multiple_of(h * HEAD_DIM, HEAD_DIM)
        for band in range(2):
            at = band * BAND
            grad_low = grad_mixed_ref[at : at + BAND, pl.ds(lane, HEAD_DIM)].astype(BF)
            keys = pair_ref[at : at + WINDOW, pl.ds(lane, HEAD_DIM)]
            values = pair_ref[at : at + WINDOW, pl.ds(lane + D, HEAD_DIM)]
            probs_low = probs_ref[h, at : at + BAND, :]
            probs = probs_low.astype(F32)
            grad_probs = mm_nt(grad_low, values)
            part = probs * grad_probs
            inner = jnp.sum(part, axis=-1, keepdims=True)
            grad_scores = ((part - probs * inner) * scale).astype(BF)
            grad_query[at : at + BAND, pl.ds(lane, HEAD_DIM)] = mm(grad_scores, keys).astype(BF)
            turned[pl.ds(lane, HEAD_DIM), at : at + WINDOW] += mm(
                turn_query[pl.ds(lane, HEAD_DIM), at : at + BAND], grad_scores
            )
            turned[pl.ds(lane + D, HEAD_DIM), at : at + WINDOW] += mm(
                turn_mixed[pl.ds(lane, HEAD_DIM), at : at + BAND], probs_low
            )
        return 0

    lax.fori_loop(0, HEADS, head, 0)

    def turn(h, _):
        lane = pl.multiple_of(h * HEAD_DIM, HEAD_DIM)
        grad_pair[:, pl.ds(lane, HEAD_DIM)] = turned[pl.ds(lane, HEAD_DIM), :].T.astype(BF)
        return 0

    lax.fori_loop(0, 2 * HEADS, turn, 0)
    for copy in copies:
        copy.wait()
    gain = dec[...].reshape(D, 128).astype(F32).T[OUT : OUT + 1, :]
    grad_query_w = mm_tn(normed_ref[512:1024, :], grad_query[...]).astype(BF)
    grad_pair_w = mm_tn(normed_ref[...], grad_pair[...]).astype(BF)
    own_wide, own_narrow = place_ref[0], place_ref[1]
    grad_weight[:, :D] = grad_query_w
    grad_weight[:, D:] = grad_pair_w
    for side, out_ref in ((1, send_ref), (0, keep_ref)):
        for part in range(2):
            n = (part * 2 + side) ^ own_narrow
            for kind in range(3):
                lane = pl.multiple_of(n * 128 + kind * D, 128)
                value = grad_weight[:, pl.ds(lane, 128)]
                for w in range(8):
                    out_ref[part, w ^ own_wide, :, kind * 128 : kind * 128 + 128] = value[w * LINES : (w + 1) * LINES, :]
    grad_enc = jnp.zeros((IN, D), F32)
    gain_grad = jnp.zeros((1, D), F32)
    for block in range(3):
        at = block * 512
        grad_n = mm_nt(grad_pair[at : at + 512, :], wkv[...].reshape(D, 2 * D))
        if block == 1:
            grad_n = grad_n + mm_nt(grad_query[...], wq[...].reshape(D, D))
        normal, inverse = norm_parts(rows_ref[at : at + 512, :])
        back, gain_part = norm_pull(grad_n, normal, inverse, gain)
        gain_grad = gain_grad + gain_part
        if block == 1:
            back = back + grad_state_ref[...]
        back_low = (back * (1.0 / KG)).astype(BF)
        high, low = split_two(sums_ref[at : at + 512, :])
        grad_enc = grad_enc + mm_tn(high, back_low) + mm_tn(low, back_low)
    grad_enc = grad_enc.astype(BF)
    rows = lax.broadcasted_iota(jnp.int32, (128, 1), 0)
    grad_dec = jnp.where(rows == OUT, gain_grad, grad_dec_ref[...]).T.astype(BF)
    grad_weight[0:IN, :D] = grad_enc
    grad_weight[:, D : D + 128] = grad_dec
    for side, out_ref in ((1, send_ref), (0, keep_ref)):
        for part in range(2):
            n = (part * 2 + side) ^ own_narrow
            enc_part = grad_weight[0:IN, pl.ds(pl.multiple_of(n * 128, 128), 128)]
            dec_part = grad_weight[pl.ds(pl.multiple_of(n * 128, 128), 128), D : D + 128]
            for w in range(8):
                out_ref[part, w ^ own_wide, :, 384:512] = jnp.concatenate(
                    [enc_part[w * 32 : w * 32 + 32, :], dec_part[w * 16 : w * 16 + 16, :], jnp.zeros((16, 128), BF)], axis=0
                )


def give_back(place, early, probs, query, pair, grad_mixed, grad_state, rows, normed, sums, grad_dec):
    nodes = query.shape[0]
    vmem = pl.BlockSpec(memory_space=pltpu.VMEM)
    return pl.pallas_call(
        return_kernel,
        in_specs=[pl.BlockSpec(memory_space=pltpu.SMEM), pl.BlockSpec(memory_space=pl.ANY)] + [vmem] * 9,
        out_shape=(
            jax.ShapeDtypeStruct((2, 8, LINES, EARLY), BF),
            jax.ShapeDtypeStruct((2, 8, LINES, EARLY), BF),
        ),
        scratch_shapes=[
            pltpu.VMEM((8, 64, D), BF),
            pltpu.VMEM((8, 64, 2 * D), BF),
            pltpu.VMEM((GROUPS, 8, 16, 128), BF),
            pltpu.VMEM((nodes, D), BF),
            pltpu.VMEM((NEAR, 2 * D), BF),
            pltpu.VMEM((2 * D, NEAR), F32),
            pltpu.VMEM((D, nodes), BF),
            pltpu.VMEM((D, nodes), BF),
            pltpu.VMEM((D, 3 * D), BF),
            pltpu.SemaphoreType.DMA((16,)),
        ],
        compiler_params=pltpu.CompilerParams(vmem_limit_bytes=BIG),
        cost_estimate=pl.CostEstimate(flops=9_000_000_000, bytes_accessed=20_000_000, transcendentals=0),
        name="give_back",
    )(place, early, probs, query, pair, grad_mixed, grad_state, rows, normed, sums, grad_dec)


def adam_update(grad_raw, factor, fix_one, fix_two, weight, moment, second, average):
    grad = grad_raw * factor
    moment_new = beta_one * moment + (1.0 - beta_one) * grad
    second_new = beta_two * second + (1.0 - beta_two) * grad * grad
    weight_new = weight - learn_rate * (
        moment_new / fix_one / (jnp.sqrt(second_new / fix_two) + epsilon) + weight_decay * weight
    )
    average_new = average_decay * average + (1.0 - average_decay) * weight_new
    return [moment_new, second_new, weight_new, average_new, weight_new.astype(BF)]


def pack(encoder, up_proj, down_proj, readout):
    lines = up_proj.shape[0]
    spare = lines - encoder.shape[0] - readout.shape[0]
    side = jnp.concatenate(
        [
            encoder.astype(BF),
            jnp.pad(readout.astype(BF), ((0, 0), (0, 128 - readout.shape[1]))),
            jnp.zeros((spare, 128), BF),
        ],
        axis=0,
    )
    up = up_proj.astype(BF)
    early = jnp.concatenate([up[:, :384], side], axis=1)
    late = jnp.concatenate([up[:, 384:], down_proj.T.astype(BF)], axis=1)
    return early, late


def to_lines(array, wide):
    if wide == 8:
        return array
    lines, width = array.shape[2:]
    return jnp.moveaxis(jnp.moveaxis(array, 1, 0).reshape(GROUPS, 8, LINES, width), 0, 1)


def side_to_lines(side, wide):
    if wide == 8:
        return side
    enc_rows, read_rows = IN // wide, D // (GROUPS * wide)
    enc = to_rows(side[:, :, :enc_rows], 32)
    read = to_rows(side[:, :, enc_rows : enc_rows + read_rows], 16)
    return jnp.concatenate([enc, read, jnp.zeros((8, GROUPS, 16, 128), side.dtype)], axis=2)


def to_rows(array, rows):
    return jnp.moveaxis(jnp.moveaxis(array, 1, 0).reshape(GROUPS, 8, rows, array.shape[3]), 0, 1)


def from_rows(array, wide):
    rows, width = array.shape[2:]
    return jnp.moveaxis(jnp.moveaxis(array, 1, 0).reshape(GROUPS, wide, 8 * rows // wide, width), 0, 1)


def early_from_lines(array, wide):
    if wide == 8:
        return array
    main = from_rows(array[..., :384], wide)
    enc = from_rows(array[:, :, :32, 384:], wide)
    read = from_rows(array[:, :, 32:48, 384:], wide)
    spare = main.shape[2] - enc.shape[2] - read.shape[2]
    side = jnp.concatenate([enc, read, jnp.zeros((wide, GROUPS, spare, 128), array.dtype)], axis=2)
    return jnp.concatenate([main, side], axis=3)


def gather_weights(early, late, wide):
    both = jnp.concatenate([early, late], axis=1)
    full = lax.all_gather(both, ("wide", "narrow"), axis=0, tiled=False)
    full = full.reshape(wide, GROUPS, *both.shape)
    early_full, late_full = full[..., :EARLY], full[..., EARLY:]
    if wide != 8:
        early_full = jnp.concatenate(
            [to_lines(early_full[..., :384], wide), side_to_lines(early_full[..., 384:], wide)], axis=3
        )
        late_full = to_lines(late_full, wide)
    return early_full, late_full


def swap(array, bit):
    count = lax.axis_size("wide") * lax.axis_size("narrow")
    return lax.ppermute(array, ("wide", "narrow"), [(i, i ^ (1 << bit)) for i in range(count)])


def halve(parts, axis, bit):
    sent = sum(lax.index_in_dim(part, 1, axis, keepdims=False).astype(F32) for part in parts).astype(BF)
    return [lax.index_in_dim(part, 0, axis, keepdims=False) for part in parts] + [swap(sent, bit)]


def reduce_parts(parts, order):
    axes = [1, 4, 3, 2]
    for bit in order:
        axis = axes.index(bit)
        parts = halve(parts, axis, bit)
        axes.pop(axis)
    return sum(part.astype(F32) for part in parts)


def cube(array):
    return array.reshape(2, 2, 2, 2, *array.shape[2:])


ORDERS = ((1, 2, 3, 4), (2, 3, 1, 4), (3, 1, 2, 4))


def reduce_late(keep, send):
    got = swap(send, 0)
    return jnp.concatenate(
        [reduce_parts([cube(keep[i]), cube(got[i])], order) for i, order in enumerate(ORDERS)], axis=1
    )


def reduce_early(keep, send):
    got = swap(send, 0)
    cuts = ((0, 128), (128, 256), (256, 512))
    return jnp.concatenate(
        [
            reduce_parts([cube(keep[..., low:high]), cube(got[..., low:high])], order)
            for (low, high), order in zip(cuts, ORDERS)
        ],
        axis=1,
    )


def in_order(keep, send):
    both = jnp.stack([keep, send], axis=2)
    return jnp.moveaxis(both.reshape(both.shape[0], 4, *both.shape[3:]), 1, 2)


def scatter_sum(blocks):
    return lax.psum_scatter(
        blocks.astype(F32).reshape(-1, blocks.shape[3]), ("wide", "narrow"), scatter_dimension=0, tiled=True
    )


def sum_all(values):
    count = lax.axis_size("wide") * lax.axis_size("narrow")
    row = jnp.pad(jnp.stack(values)[None, :], ((0, 7), (0, 128 - len(values))))
    bit = 0
    while 1 << bit < count:
        row = row + swap(row, bit)
        bit += 1
    return [row[0, i] for i in range(len(values))]


def body(
    cond_fields,
    target,
    noise_draw,
    noise_sigma,
    grid_to_mesh,
    mesh_edges,
    mesh_to_grid,
    latitude_row,
    level_index,
    encoder,
    up_proj,
    down_proj,
    readout,
    encoder_moment,
    up_moment,
    down_moment,
    readout_moment,
    encoder_second,
    up_second,
    down_second,
    readout_second,
    encoder_average,
    up_average,
    down_average,
    readout_average,
):
    wide_index = lax.axis_index("wide")
    wide = lax.axis_size("wide")
    globe = lax.axis_index("narrow")
    nodes = mesh_edges.shape[0]
    pixels = cond_fields.shape[1]
    all_nodes = nodes * wide
    width = -(-pixels // 128) * 128

    early, late = pack(encoder, up_proj, down_proj, readout)
    early_full, late_full = gather_weights(early, late, wide)

    sigma = lax.dynamic_index_in_dim(noise_sigma, globe, 0, keepdims=False)
    square = sigma * sigma
    c_in = lax.rsqrt(square + 1.0)
    c_skip = 1.0 / (square + 1.0)
    c_out = sigma * c_in
    lam = (square + 1.0) / square
    cond = lax.dynamic_index_in_dim(cond_fields, globe, 0, keepdims=False)
    goal = lax.dynamic_index_in_dim(target, globe, 0, keepdims=False)
    noisy = goal + sigma * lax.dynamic_index_in_dim(noise_draw, globe, 0, keepdims=False)
    grid = jnp.concatenate([cond, (c_in * noisy).astype(BF)], axis=1)
    grid = jnp.pad(grid, ((0, width - pixels), (0, 0)))
    pixel_rows = grid_to_mesh - wide_index * pixels
    slot_rows = jnp.where(
        mesh_edges >= 0, (mesh_edges - wide_index * nodes + nodes + all_nodes) % all_nodes, -1
    )
    up_rows = jnp.pad(mesh_to_grid - wide_index * nodes, ((0, width - pixels), (0, 0)), constant_values=-1)
    sums, bias, pool, pull = prepare(grid, pixel_rows, slot_rows, up_rows, up_rows.T)
    before = lax.ppermute(sums, "wide", [(i, (i + 1) % wide) for i in range(wide)])
    after = lax.ppermute(sums, "wide", [((i + 1) % wide, i) for i in range(wide)])
    near = jnp.concatenate([before, sums, after], axis=0)

    lat_weight = jnp.cos((latitude_row.astype(F32) - 90.0) * (math.pi / 180.0))
    level_weight = (level_index.astype(F32) + 1.0) / LEVELS
    pix_total = jnp.sum(lat_weight) * jnp.sum(level_weight)

    state0, rows, normed, query, pair, mixed, probs = attend(early_full, near, bias)
    place = jnp.stack([wide_index, globe]) if wide == 8 else jnp.zeros((2,), jnp.int32)
    keep_late, send_late, grad_state, grad_mixed, grad_dec, loss_part = feed(
        place, jnp.stack([c_skip, c_out, lam]),
        late_full, early_full, state0, mixed, pool, pull, noisy, goal, lat_weight[:, None], level_weight[None, :],
    )
    keep_early, send_early = give_back(
        place, early_full, probs, query, pair, grad_mixed, grad_state, rows, normed, near, grad_dec
    )
    if wide == 8:
        share_late = reduce_late(keep_late, send_late)
        share_early = reduce_early(keep_early, send_early)
    else:
        late_lines = jnp.concatenate(list(in_order(keep_late, send_late)), axis=3)
        early_lines = in_order(keep_early[None], send_early[None])[0]
        share_late = scatter_sum(from_rows(late_lines, wide))
        share_early = scatter_sum(early_from_lines(early_lines, wide))
    share = jnp.concatenate([share_early, share_late], axis=1)
    share_up = jnp.concatenate([share[:, :384], share[:, 512:1024]], axis=1)
    share_down = share[:, 1024:].T
    enc_rows, read_rows = encoder.shape[0], readout.shape[0]
    share_enc = share[:enc_rows, 384:512]
    share_read = share[enc_rows : enc_rows + read_rows, 384 : 384 + OUT + 2]
    first = (globe == 0).astype(F32)
    square_all, loss_all, pixel_all = sum_all([jnp.sum(share * share), loss_part[0, 0], pix_total * first])
    total = pixel_all * MB
    norm_value = jnp.sqrt(square_all) / total
    factor = jnp.minimum(1.0, clip_norm / norm_value) / total
    step = jnp.asarray(STEPS_DONE, F32)
    fix_one = 1.0 - jnp.power(beta_one, step)
    fix_two = 1.0 - jnp.power(beta_two, step)
    states = [
        (share_enc, encoder, encoder_moment, encoder_second, encoder_average),
        (share_up, up_proj, up_moment, up_second, up_average),
        (share_down, down_proj, down_moment, down_second, down_average),
        (share_read, readout, readout_moment, readout_second, readout_average),
    ]
    outputs = [loss_all / total, norm_value]
    for part, weight, moment, second, average in states:
        outputs.extend(adam_update(part, factor, fix_one, fix_two, weight, moment, second, average))
    return tuple(outputs)


def solution(mesh):
    if mesh.shape["narrow"] != GROUPS or MB != GROUPS:
        raise ValueError("narrow size")
    by_pixel = P(None, "wide", None)
    pair = P("wide", "narrow")
    weights = (pair, pair, P("narrow", "wide"), P(("narrow", "wide"), None))
    placed = (by_pixel, by_pixel, by_pixel, P()) + (P("wide", None),) * 3 + (P("wide"), P()) + weights * 4
    given = (P(), P())
    for spec in weights:
        given = given + (spec,) * 5
    return jax.shard_map(body, mesh=mesh, in_specs=placed, out_specs=given, check_vma=False)
```

time: 1650 us -> 279 us (0.17); the launches traced: 1630 us -> 278 us
  other arithmetic: 475 us -> 19.7 us
  blocking collectives: 340 us -> 0 us
  local copies, waits for them, and re-layouts: 313 us -> 25.4 us
  waiting for transfers between devices: 304 us -> 85.8 us
  matrix products: 120 us -> 0 us
  Pallas kernels: 0 us -> 79.3 us
    scatter-add x12 -> x0, other arithmetic: 332 us -> none  [the longest x4 182 us: body(): grad_ext = jnp.zeros((3 * nodes, 2 * feat), jnp.float32).at[slot_rows.res...]
    all_gather x22 -> x0, blocking collectives: 253 us -> none  [the longest x8 57.9 us: branch_grad(): lax.all_gather(grad_state.astype(jnp.bfloat16), 'narrow', axis=1, tiled=T...]
    gather x16 -> x0, local copies, waits for them, and re-layouts: 224 us -> none  [the longest x4 132 us: body(): picked = extended[slot_rows]]
    unnamed x34 -> x1, waiting for transfers between devices: 183 us -> 0.02 us
    dot_general x84 -> x0, matrix products: 120 us -> none  [the longest x24 25.2 us: left_trans(): lax.dot_general(left, right, (((0,), (0,)), ((), ())), preferred_element_...]
    psum x2 -> x0, waiting for transfers between devices: 112 us -> none  [the longest x1 80.3 us: body(): summed = lax.psum((grad_enc, grad_up, grad_downs, grad_read), 'wide')]
    psum x2 -> x0, blocking collectives: 81.2 us -> none  [the longest x1 41.9 us: body(): summed = lax.psum((grad_enc, grad_up, grad_downs, grad_read), 'wide')]
    pallas_call x0 -> x4, Pallas kernels: none -> 79.3 us  [the longest x1 23.6 us: give_back(): pl.pallas_call(return_kernel, in_specs=[pl.BlockSpec(memory_space=pltpu.S...]
  transfers between devices with their start and end apart: 34 -> 34, of which waited for: 15 -> 23; matrix products, arithmetic and copies ran while one was open for 29% -> 6% of each run, Pallas kernels for 0% -> 5%
where the time goes in v1:
time: 279 us; the launch traced here: 278 us
  waiting for transfers between devices  85.8 us (31%)
  Pallas kernels  79.3 us (28%)
  starting transfers between devices  44.2 us (16%)
  local copies, waits for them, and re-layouts  25.4 us (9%)
  between operations  23.3 us (8%)
  other arithmetic  19.7 us (7%)
    ppermute x31, waiting for transfers between devices, swap(): lax.ppermute(array, ('wide', 'narrow'), [(i, i ^ 1 << bit) for i in range...  41.7 us
    ppermute x31, starting transfers between devices, swap(): lax.ppermute(array, ('wide', 'narrow'), [(i, i ^ 1 << bit) for i in range...  38.2 us
    all_gather x1, waiting for transfers between devices, gather_weights(): full = lax.all_gather(both, ('wide', 'narrow'), axis=0, tiled=False)  27.1 us
    pallas_call x1, Pallas kernels, give_back(): pl.pallas_call(return_kernel, in_specs=[pl.BlockSpec(memory_space=pltpu.S...  23.6 us
    pallas_call x1, Pallas kernels, feed(): pl.pallas_call(feed_kernel, in_specs=[pl.BlockSpec(memory_space=pltpu.SME...  23 us
    pallas_call x1, Pallas kernels, attend(): pl.pallas_call(attend_kernel, in_specs=[pl.BlockSpec(memory_space=pl.ANY)...  19.8 us
    ppermute x1, waiting for transfers between devices, body(): lax.ppermute(sums, 'wide', [(i, (i + 1) % wide) for i in range(wide)])  15.8 us
    pallas_call x1, Pallas kernels, prepare(): pl.pallas_call(prepare_kernel, out_shape=(jax.ShapeDtypeStruct((nodes, IN...  13 us
  transfers between devices with their start and end apart: 34, of which 23 were waited for; matrix products, arithmetic and copies ran while one was open for 6% of the time, Pallas kernels for 5%

profile of v1, /device:TPU:0, one launch (start us, length us, event | category | flops | bytes accessed | tf_op | source)
XLA Modules:
  0.0 277.8 jit_solution(1414251532617005772)
XLA Ops:
  11.5 1.2 dynamic_slice.16
  16.2 2.2 constant_dynamic-slice_fusion
  20.6 1.5 multiply_convert_fusion
  22.5 13.0 %prepare.1 = (f32[512,256]{1,0:T(8,128)S(1)}, f32[512,1280]{1,0:T(8,128)S(1)}, bf16[896,512]{1,0:T(8,128)(2,1)S(1)}, bf16[512,896]{1,0:T(8,128)(2,1)S(1)}) custom-call(bf16[896,256]{1,0:T(8,128)(2,1)S(1)} %fusion.2.grid_ref, s32[512,8]{1,0:T(8,128)S(1)} %broadcast_subtract_fusion.pixels_ref, s32[512,16]{1,0:T(8,128)S(1)} %fusion.12.slots_ref, ...), custom_call_target="tpu_custom_call" | custom-call | flops 400000000 | bytes 6000000 | tf_op jit(solution)/shard_map/prepare/pallas_call | solution.py:138
  35.5 1.5 copy-done.2
  38.9 6.0 %collective-permute-start.1 = (f32[512,256]{1,0:T(8,128)S(1)}, f32[512,256]{1,0:T(8,128)S(1)}, u32[]{:S(2)}, u32[]{:S(2)}) collective-permute-start(f32[512,256]{1,0:T(8,128)S(1)} %get-tuple-element.41), channel_id=1, source_target_pairs={{4,0},{8,4},{12,8},{16,12},{20,16},{24,20},{28,24},{0,28},{5,1},{9... | collective-permute-start | bytes 1572872 | tf_op jit(solution)/shard_map/ppermute | solution.py:698
  50.9 15.8 %collective-permute-done = f32[512,256]{1,0:T(8,128)S(1)} collective-permute-done((f32[512,256]{1,0:T(8,128)S(1)}, f32[512,256]{1,0:T(8,128)S(1)}, u32[]{:S(2)}, u32[]{:S(2)}) %collective-permute-start) | collective-permute-done | bytes 524320 | tf_op jit(solution)/shard_map/ppermute | solution.py:697
  66.8 1.1 collective-permute-done.1
  68.0 27.1 %all-gather.3.cloned.1.call-done = bf16[2048,1664]{1,0:T(8,128)(2,1)} async-done(((bf16[64,1664]{1,0:T(8,128)(2,1)}), bf16[2048,1664]{1,0:T(8,128)(2,1)}) %all-gather.3.cloned.1.call-update) | async-done | bytes 6815760 | tf_op jit(solution)/shard_map/all_gather | solution.py:565
  95.0 3.2 %slice.814.early_ref = bf16[8,4,64,512]{3,2,1,0:T(8,128)(2,1)} slice(bf16[8,4,64,1664]{3,2,1,0:T(8,128)(2,1)} %bitcast.341), slice={[0:8], [0:4], [0:64], [0:512]} | slice | bytes 4194304 | tf_op jit(solution)/shard_map/slice | solution.py:567
  98.2 4.9 %slice.815.late_ref = bf16[8,4,64,1152]{3,2,1,0:T(8,128)(2,1)} slice(bf16[8,4,64,1664]{3,2,1,0:T(8,128)(2,1)} %bitcast.342), slice={[0:8], [0:4], [0:64], [512:1664]} | slice | bytes 9437184 | tf_op jit(solution)/shard_map/slice | solution.py:567
  103.1 19.8 %attend.1 = (f32[512,512]{1,0:T(8,128)}, bf16[1536,512]{1,0:T(8,128)(2,1)}, bf16[1536,512]{1,0:T(8,128)(2,1)}, bf16[512,512]{1,0:T(8,128)(2,1)}, bf16[1536,1024]...) custom-call(bf16[8,4,64,512]{3,2,1,0:T(8,128)(2,1)} %slice.814.early_ref, ...), custom_call_target="tpu_custom_call" | custom-call | flops 5000000000 | bytes 18000000 | tf_op jit(solution)/shard_map/attend/pallas_call | solution.py:227
  122.9 23.0 %feed.1 = (bf16[3,2,8,64,384]{4,3,2,1,0:T(8,128)(2,1)}, bf16[3,2,8,64,384]{4,3,2,1,0:T(8,128)(2,1)}, f32[512,512]{1,0:T(8,128)}, f32[512,512]{1,0:T(8,128)}, f32[128,512]{1,0:T(8,128)}, /*index=5*/f32[8,128]{1,0:T(8,128)}) custom-call(s32[2]{0:T(128)} %pad_add_fusion.1.place_ref, f32[3]{0:T(128)} %pad_maximum_fusion.4.scalars_ref, ...), custom_call_target="tpu_custom_call" | custom-call | flops 8999999488 | bytes 20000000 | tf_op jit(solution)/shard_map/feed/pallas_call | solution.py:354
  145.9 23.6 %give_back.1 = (bf16[2,8,64,512]{3,2,1,0:T(8,128)(2,1)}, bf16[2,8,64,512]{3,2,1,0:T(8,128)(2,1)}) custom-call(s32[2]{0:T(128)} %pad_add_fusion.1.place_ref, bf16[8,4,64,512]{3,2,1,0:T(8,128)(2,1)} %slice.814.early_ref, bf16[4,512,1280]{2,1,0:T(8,128)(2,1)} %get-tuple-element.43.probs_ref, bf16[512,512]{1,0:T(8,128)(2,1)} %get-tuple-element.44.query_ref, ...), custom_call_target="tpu_custom_call" | custom-call | flops 8999999488 | bytes 20000000 | tf_op jit(solution)/shard_map/give_back/pallas_call | solution.py:474
  173.0 1.2 slice.803
  176.8 1.5 collective-permute-start.3
  178.9 1.5 collective-permute-start.11
  180.4 2.1 collective-permute-done.3
  182.6 1.5 collective-permute-start.4
  184.2 1.5 collective-permute-start.8
  185.7 1.2 collective-permute-done.4
  186.9 1.5 collective-permute-start.5
  188.9 1.1 collective-permute-start.9
  190.9 1.9 collective-permute-start.6
  192.9 1.8 collective-permute-start.10
  195.7 4.1 %collective-permute-done.12 = bf16[2,2,64,256]{3,2,1,0:T(8,128)(2,1)S(1)} collective-permute-done((bf16[2,2,64,256]{3,2,1,0:T(8,128)(2,1)S(1)}, bf16[2,2,64,256]{3,2,1,0:T(8,128)(2,1)S(1)}, u32[]{:S(2)}, u32[]{:S(2)}) %collective-permute-start.12) | collective-permute-done | bytes 131104 | tf_op jit(solution)/shard_map/ppermute | solution.py:578
  200.8 3.4 %collective-permute-done.13 = bf16[2,64,256]{2,1,0:T(8,128)(2,1)S(1)} collective-permute-done((bf16[2,64,256]{2,1,0:T(8,128)(2,1)S(1)}, bf16[2,64,256]{2,1,0:T(8,128)(2,1)S(1)}, u32[]{:S(2)}, u32[]{:S(2)}) %collective-permute-start.13) | collective-permute-done | bytes 65568 | tf_op jit(solution)/shard_map/ppermute | solution.py:578
  204.2 1.2 collective-permute-start.14
  205.4 3.8 %collective-permute-done.14 = bf16[64,256]{1,0:T(8,128)(2,1)S(1)} collective-permute-done((bf16[64,256]{1,0:T(8,128)(2,1)S(1)}, bf16[64,256]{1,0:T(8,128)(2,1)S(1)}, u32[]{:S(2)}, u32[]{:S(2)}) %collective-permute-start.14) | collective-permute-done | bytes 32800 | tf_op jit(solution)/shard_map/ppermute | solution.py:578
  209.9 1.1 collective-permute-start.24
  211.0 1.5 collective-permute-start.20
  213.1 6.7 %collective-permute-done.24 = bf16[2,2,2,64,384]{4,3,2,1,0:T(8,128)(2,1)S(1)} collective-permute-done((bf16[2,2,2,64,384]{4,3,2,1,0:T(8,128)(2,1)S(1)}, bf16[2,2,2,64,384]{4,3,2,1,0:T(8,128)(2,1)S(1)}, u32[]{:S(2)}, u32[]{:S(2)}) %collective-permute-start.24) | collective-permute-done | bytes 393248 | tf_op jit(solution)/shard_map/ppermute | solution.py:578
  223.8 1.8 collective-permute-done.25
  226.6 2.0 collective-permute-done.21
  228.7 1.6 collective-permute-start.22
  230.6 2.5 collective-permute-start.27
  233.1 2.0 collective-permute-done.18
  235.8 2.5 collective-permute-start.23
  238.3 2.0 collective-permute-done.19
  241.7 1.4 maximum_bitcast_fusion
  243.1 1.2 collective-permute-done.28
  244.2 1.9 collective-permute-start.29
  246.1 1.7 collective-permute-done.29
  248.9 2.6 collective-permute-done.30
  251.4 2.0 collective-permute-start.31
  253.5 1.6 collective-permute-done.31
  255.1 2.5 collective-permute-start.32
  257.5 2.0 collective-permute-done.32
  (206 shorter events, 40.6 us)
Async XLA Ops:
  7.2 87.8 %all-gather.3.cloned.1.call-start = ((), (), s32[]{:S(2)}) async-start(), calls=%async_computation | async-start | bytes 7028736 | tf_op jit(solution)/shard_map/all_gather | solution.py:565
  38.9 29.0 %collective-permute-start.1 = (f32[512,256]{1,0:T(8,128)S(1)}, f32[512,256]{1,0:T(8,128)S(1)}, u32[]{:S(2)}, u32[]{:S(2)}) collective-permute-start(f32[512,256]{1,0:T(8,128)S(1)} %get-tuple-element.41), channel_id=1, source_target_pairs={{4,0},{8,4},{12,8},{16,12},{20,16},{24,20},{28,24},{0,28},{5,1},{9... | collective-permute-start | bytes 1572872 | tf_op jit(solution)/shard_map/ppermute | solution.py:698
  44.9 21.8 %collective-permute-start = (f32[512,256]{1,0:T(8,128)S(1)}, f32[512,256]{1,0:T(8,128)S(1)}, u32[]{:S(2)}, u32[]{:S(2)}) collective-permute-start(f32[512,256]{1,0:T(8,128)S(1)} %get-tuple-element.41), channel_id=1, source_target_pairs={{0,4},{4,8},{8,12},{12,16},{16,20},{20,24},{24,28},{28,0},{1,5},{5... | collective-permute-start | bytes 1572872 | tf_op jit(solution)/shard_map/ppermute | solution.py:697
  67.9 30.2 %copy-start.15 = (f32[1536,256]{1,0:T(8,128)}, f32[1536,256]{1,0:T(8,128)S(1)}, u32[]{:S(2)}) copy-start(f32[1536,256]{1,0:T(8,128)S(1)} %constant_dynamic-update-slice_fusion.sums_ref) | copy-start | bytes 4718596
  172.6 2.9 %collective-permute-start.2 = (bf16[2,8,64,512]{3,2,1,0:T(8,128)(2,1)}, bf16[2,8,64,512]{3,2,1,0:T(8,128)(2,1)S(1)}, u32[]{:S(2)}, u32[]{:S(2)}) collective-permute-start(bf16[2,8,64,512]{3,2,1,0:T(8,128)(2,1)} %get-tuple-element.56), channel_id=1, source_target_pairs={{0,1},{1,0},{2,3},{3,2},{4,5},{5,4},{6,7},{7,6},{8,9},{9,8},{10,11... | collective-permute-start | bytes 3145736 | tf_op jit(solution)/shard_map/ppermute | solution.py:578
  174.2 35.0 %collective-permute-start.15 = (bf16[3,2,8,64,384]{4,3,2,1,0:T(8,128)(2,1)}, bf16[3,2,8,64,384]{4,3,2,1,0:T(8,128)(2,1)S(1)}, u32[]{:S(2)}, u32[]{:S(2)}) collective-permute-start(bf16[3,2,8,64,384]{4,3,2,1,0:T(8,128)(2,1)} %get-tuple-element.58), channel_id=1, source_target_pairs={{0,1},{1,0},{2,3},{3,2},{4,5},{5,4},{6,7},{7,6},{8,9},{9,8},{10,11... | collective-permute-start | bytes 7077896 | tf_op jit(solution)/shard_map/ppermute | solution.py:578
  176.8 5.8 %collective-permute-start.3 = (bf16[2,2,2,64,128]{4,3,1,0,2:T(8,128)(2,1)S(1)}, bf16[2,2,2,64,128]{4,3,1,0,2:T(8,128)(2,1)S(1)}, u32[]{:S(2)}, u32[]{:S(2)}) collective-permute-start(bf16[2,2,2,64,128]{4,3,1,0,2:T(8,128)(2,1)S(1)} %copy.138), channel_id=1, source_target_pairs={{0,2},{1,3},{2,0},{3,1},{4,6},{5,7},{6,4},{7,5},{8,10},{9,11},{10,... | collective-permute-start | bytes 393224 | tf_op jit(solution)/shard_map/ppermute | solution.py:578
  178.3 5.8 %collective-permute-start.7 = (bf16[2,2,2,64,128]{4,3,2,1,0:T(8,128)(2,1)S(1)}, bf16[2,2,2,64,128]{4,3,2,1,0:T(8,128)(2,1)S(1)}, u32[]{:S(2)}, u32[]{:S(2)}) collective-permute-start(bf16[2,2,2,64,128]{4,3,2,1,0:T(8,128)(2,1)S(1)} %fusion.26), channel_id=1, source_target_pairs={{0,4},{1,5},{2,6},{3,7},{4,0},{5,1},{6,2},{7,3},{8,12},{9,13},{10,... | collective-permute-start | bytes 393224 | tf_op jit(solution)/shard_map/ppermute | solution.py:578
  178.9 15.8 %collective-permute-start.11 = (bf16[2,2,2,64,256]{4,3,2,1,0:T(8,128)(2,1)S(1)}, bf16[2,2,2,64,256]{4,3,2,1,0:T(8,128)(2,1)S(1)}, u32[]{:S(2)}, u32[]{:S(2)}) collective-permute-start(bf16[2,2,2,64,256]{4,3,2,1,0:T(8,128)(2,1)S(1)} %fusion.13), channel_id=1, source_target_pairs={{0,8},{1,9},{2,10},{3,11},{4,12},{5,13},{6,14},{7,15},{8,0},{9,1},... | collective-permute-start | bytes 786440 | tf_op jit(solution)/shard_map/ppermute | solution.py:578
  182.6 4.3 %collective-permute-start.4 = (bf16[2,2,64,128]{3,2,1,0:T(8,128)(2,1)S(1)}, bf16[2,2,64,128]{3,2,1,0:T(8,128)(2,1)S(1)}, u32[]{:S(2)}, u32[]{:S(2)}) collective-permute-start(bf16[2,2,64,128]{3,2,1,0:T(8,128)(2,1)S(1)} %fusion.35), channel_id=1, source_target_pairs={{0,4},{1,5},{2,6},{3,7},{4,0},{5,1},{6,2},{7,3},{8,12},{9,13},{10,... | collective-permute-start | bytes 196616 | tf_op jit(solution)/shard_map/ppermute | solution.py:578
  184.2 4.7 %collective-permute-start.8 = (bf16[2,2,64,128]{3,2,1,0:T(8,128)(2,1)S(1)}, bf16[2,2,64,128]{3,2,1,0:T(8,128)(2,1)S(1)}, u32[]{:S(2)}, u32[]{:S(2)}) collective-permute-start(bf16[2,2,64,128]{3,2,1,0:T(8,128)(2,1)S(1)} %fusion.36), channel_id=1, source_target_pairs={{0,8},{1,9},{2,10},{3,11},{4,12},{5,13},{6,14},{7,15},{8,0},{9,1},... | collective-permute-start | bytes 196616 | tf_op jit(solution)/shard_map/ppermute | solution.py:578
  186.9 4.0 %collective-permute-start.5 = (bf16[2,64,128]{2,1,0:T(8,128)(2,1)S(1)}, bf16[2,64,128]{2,1,0:T(8,128)(2,1)S(1)}, u32[]{:S(2)}, u32[]{:S(2)}) collective-permute-start(bf16[2,64,128]{2,1,0:T(8,128)(2,1)S(1)} %fusion.41), channel_id=1, source_target_pairs={{0,8},{1,9},{2,10},{3,11},{4,12},{5,13},{6,14},{7,15},{8,0},{9,1},... | collective-permute-start | bytes 98312 | tf_op jit(solution)/shard_map/ppermute | solution.py:578
  188.9 4.0 %collective-permute-start.9 = (bf16[2,64,128]{2,1,0:T(8,128)(2,1)S(1)}, bf16[2,64,128]{2,1,0:T(8,128)(2,1)S(1)}, u32[]{:S(2)}, u32[]{:S(2)}) collective-permute-start(bf16[2,64,128]{2,1,0:T(8,128)(2,1)S(1)} %fusion.40), channel_id=1, source_target_pairs={{0,2},{1,3},{2,0},{3,1},{4,6},{5,7},{6,4},{7,5},{8,10},{9,11},{10,... | collective-permute-start | bytes 98312 | tf_op jit(solution)/shard_map/ppermute | solution.py:578
  190.9 9.8 %collective-permute-start.6 = (bf16[64,128]{1,0:T(8,128)(2,1)S(1)}, bf16[64,128]{1,0:T(8,128)(2,1)S(1)}, u32[]{:S(2)}, u32[]{:S(2)}) collective-permute-start(bf16[64,128]{1,0:T(8,128)(2,1)S(1)} %fusion.44), channel_id=1, source_target_pairs={{0,16},{1,17},{2,18},{3,19},{4,20},{5,21},{6,22},{7,23},{8,24},{9,... | collective-permute-start | bytes 49160 | tf_op jit(solution)/shard_map/ppermute | solution.py:578
  192.9 12.6 %collective-permute-start.10 = (bf16[64,128]{1,0:T(8,128)(2,1)S(1)}, bf16[64,128]{1,0:T(8,128)(2,1)S(1)}, u32[]{:S(2)}, u32[]{:S(2)}) collective-permute-start(bf16[64,128]{1,0:T(8,128)(2,1)S(1)} %fusion.42), channel_id=1, source_target_pairs={{0,16},{1,17},{2,18},{3,19},{4,20},{5,21},{6,22},{7,23},{8,24},{9,... | collective-permute-start | bytes 49160 | tf_op jit(solution)/shard_map/ppermute | solution.py:578
  194.8 5.0 %collective-permute-start.12 = (bf16[2,2,64,256]{3,2,1,0:T(8,128)(2,1)S(1)}, bf16[2,2,64,256]{3,2,1,0:T(8,128)(2,1)S(1)}, u32[]{:S(2)}, u32[]{:S(2)}) collective-permute-start(bf16[2,2,64,256]{3,2,1,0:T(8,128)(2,1)S(1)} %fusion.14), channel_id=1, source_target_pairs={{0,2},{1,3},{2,0},{3,1},{4,6},{5,7},{6,4},{7,5},{8,10},{9,11},{10,... | collective-permute-start | bytes 393224 | tf_op jit(solution)/shard_map/ppermute | solution.py:578
  199.9 4.3 %collective-permute-start.13 = (bf16[2,64,256]{2,1,0:T(8,128)(2,1)S(1)}, bf16[2,64,256]{2,1,0:T(8,128)(2,1)S(1)}, u32[]{:S(2)}, u32[]{:S(2)}) collective-permute-start(bf16[2,64,256]{2,1,0:T(8,128)(2,1)S(1)} %fusion.37), channel_id=1, source_target_pairs={{0,4},{1,5},{2,6},{3,7},{4,0},{5,1},{6,2},{7,3},{8,12},{9,13},{10,... | collective-permute-start | bytes 196616 | tf_op jit(solution)/shard_map/ppermute | solution.py:578
  204.2 5.0 %collective-permute-start.14 = (bf16[64,256]{1,0:T(8,128)(2,1)S(1)}, bf16[64,256]{1,0:T(8,128)(2,1)S(1)}, u32[]{:S(2)}, u32[]{:S(2)}) collective-permute-start(bf16[64,256]{1,0:T(8,128)(2,1)S(1)} %fusion.38), channel_id=1, source_target_pairs={{0,16},{1,17},{2,18},{3,19},{4,20},{5,21},{6,22},{7,23},{8,24},{9,... | collective-permute-start | bytes 98312 | tf_op jit(solution)/shard_map/ppermute | solution.py:578
  209.9 9.9 %collective-permute-start.24 = (bf16[2,2,2,64,384]{4,3,2,1,0:T(8,128)(2,1)S(1)}, bf16[2,2,2,64,384]{4,3,2,1,0:T(8,128)(2,1)S(1)}, u32[]{:S(2)}, u32[]{:S(2)}) collective-permute-start(bf16[2,2,2,64,384]{4,3,2,1,0:T(8,128)(2,1)S(1)} %fusion.8), channel_id=1, source_target_pairs={{0,8},{1,9},{2,10},{3,11},{4,12},{5,13},{6,14},{7,15},{8,0},{9,1},... | collective-permute-start | bytes 1179656 | tf_op jit(solution)/shard_map/ppermute | solution.py:578
  211.0 10.9 %collective-permute-start.20 = (bf16[2,2,2,64,384]{4,3,2,1,0:T(8,128)(2,1)S(1)}, bf16[2,2,2,64,384]{4,3,2,1,0:T(8,128)(2,1)S(1)}, u32[]{:S(2)}, u32[]{:S(2)}) collective-permute-start(bf16[2,2,2,64,384]{4,3,2,1,0:T(8,128)(2,1)S(1)} %fusion.7), channel_id=1, source_target_pairs={{0,4},{1,5},{2,6},{3,7},{4,0},{5,1},{6,2},{7,3},{8,12},{9,13},{10,... | collective-permute-start | bytes 1179656 | tf_op jit(solution)/shard_map/ppermute | solution.py:578
  212.5 10.1 %collective-permute-start.16 = (bf16[2,2,2,64,384]{4,3,1,0,2:T(8,128)(2,1)S(1)}, bf16[2,2,2,64,384]{4,3,1,0,2:T(8,128)(2,1)S(1)}, u32[]{:S(2)}, u32[]{:S(2)}) collective-permute-start(bf16[2,2,2,64,384]{4,3,1,0,2:T(8,128)(2,1)S(1)} %copy.153), channel_id=1, source_target_pairs={{0,2},{1,3},{2,0},{3,1},{4,6},{5,7},{6,4},{7,5},{8,10},{9,11},{10,... | collective-permute-start | bytes 1179656 | tf_op jit(solution)/shard_map/ppermute | solution.py:578
  219.9 5.7 %collective-permute-start.25 = (bf16[2,2,64,384]{3,2,1,0:T(8,128)(2,1)S(1)}, bf16[2,2,64,384]{3,2,1,0:T(8,128)(2,1)S(1)}, u32[]{:S(2)}, u32[]{:S(2)}) collective-permute-start(bf16[2,2,64,384]{3,2,1,0:T(8,128)(2,1)S(1)} %fusion.9), channel_id=1, source_target_pairs={{0,2},{1,3},{2,0},{3,1},{4,6},{5,7},{6,4},{7,5},{8,10},{9,11},{10,... | collective-permute-start | bytes 589832 | tf_op jit(solution)/shard_map/ppermute | solution.py:578
  222.0 6.6 %collective-permute-start.21 = (bf16[2,2,64,384]{3,2,1,0:T(8,128)(2,1)S(1)}, bf16[2,2,64,384]{3,2,1,0:T(8,128)(2,1)S(1)}, u32[]{:S(2)}, u32[]{:S(2)}) collective-permute-start(bf16[2,2,64,384]{3,2,1,0:T(8,128)(2,1)S(1)} %fusion.21), channel_id=1, source_target_pairs={{0,8},{1,9},{2,10},{3,11},{4,12},{5,13},{6,14},{7,15},{8,0},{9,1},... | collective-permute-start | bytes 589832 | tf_op jit(solution)/shard_map/ppermute | solution.py:578
  222.7 7.6 %collective-permute-start.17 = (bf16[2,2,64,384]{3,2,1,0:T(8,128)(2,1)S(1)}, bf16[2,2,64,384]{3,2,1,0:T(8,128)(2,1)S(1)}, u32[]{:S(2)}, u32[]{:S(2)}) collective-permute-start(bf16[2,2,64,384]{3,2,1,0:T(8,128)(2,1)S(1)} %fusion.20), channel_id=1, source_target_pairs={{0,4},{1,5},{2,6},{3,7},{4,0},{5,1},{6,2},{7,3},{8,12},{9,13},{10,... | collective-permute-start | bytes 589832 | tf_op jit(solution)/shard_map/ppermute | solution.py:578
  225.7 4.9 %collective-permute-start.26 = (bf16[2,64,384]{2,1,0:T(8,128)(2,1)S(1)}, bf16[2,64,384]{2,1,0:T(8,128)(2,1)S(1)}, u32[]{:S(2)}, u32[]{:S(2)}) collective-permute-start(bf16[2,64,384]{2,1,0:T(8,128)(2,1)S(1)} %fusion.28), channel_id=1, source_target_pairs={{0,4},{1,5},{2,6},{3,7},{4,0},{5,1},{6,2},{7,3},{8,12},{9,13},{10,... | collective-permute-start | bytes 294920 | tf_op jit(solution)/shard_map/ppermute | solution.py:578
  228.6 34.3 %copy-start.23 = (f32[16,86]{1,0:T(8,128)S(1)}, f32[16,86]{1,0:T(8,128)}, u32[]{:S(2)}) copy-start(f32[16,86]{1,0:T(8,128)} %param.37) | copy-start | bytes 16516
  228.6 34.3 %copy-start.29 = (f32[16,86]{1,0:T(8,128)S(1)}, f32[16,86]{1,0:T(8,128)}, u32[]{:S(2)}) copy-start(f32[16,86]{1,0:T(8,128)} %param.45) | copy-start | bytes 16516
  228.6 34.3 %copy-start.30 = (f32[16,86]{1,0:T(8,128)S(1)}, f32[16,86]{1,0:T(8,128)}, u32[]{:S(2)}) copy-start(f32[16,86]{1,0:T(8,128)} %param.41) | copy-start | bytes 16516
  228.7 7.1 %collective-permute-start.22 = (bf16[2,64,384]{2,1,0:T(8,128)(2,1)S(1)}, bf16[2,64,384]{2,1,0:T(8,128)(2,1)S(1)}, u32[]{:S(2)}, u32[]{:S(2)}) collective-permute-start(bf16[2,64,384]{2,1,0:T(8,128)(2,1)S(1)} %fusion.22), channel_id=1, source_target_pairs={{0,2},{1,3},{2,0},{3,1},{4,6},{5,7},{6,4},{7,5},{8,10},{9,11},{10,... | collective-permute-start | bytes 294920 | tf_op jit(solution)/shard_map/ppermute | solution.py:578
  230.4 33.2 %copy-start.31 = (f32[16,86]{1,0:T(8,128)S(1)}, f32[16,86]{1,0:T(8,128)}, u32[]{:S(2)}) copy-start(f32[16,86]{1,0:T(8,128)} %param.49) | copy-start | bytes 16516
  230.4 33.8 %copy-start.21 = (f32[32,128]{1,0:T(8,128)S(1)}, f32[32,128]{1,0:T(8,128)}, u32[]{:S(2)}) copy-start(f32[32,128]{1,0:T(8,128)} %param.34) | copy-start | bytes 49156
  230.4 33.8 %copy-start.25 = (f32[32,128]{1,0:T(8,128)S(1)}, f32[32,128]{1,0:T(8,128)}, u32[]{:S(2)}) copy-start(f32[32,128]{1,0:T(8,128)} %param.42) | copy-start | bytes 49156
  230.4 33.8 %copy-start.26 = (f32[32,128]{1,0:T(8,128)S(1)}, f32[32,128]{1,0:T(8,128)}, u32[]{:S(2)}) copy-start(f32[32,128]{1,0:T(8,128)} %param.38) | copy-start | bytes 49156
  230.4 34.4 %copy-start.27 = (f32[32,128]{1,0:T(8,128)S(1)}, f32[32,128]{1,0:T(8,128)}, u32[]{:S(2)}) copy-start(f32[32,128]{1,0:T(8,128)} %param.46) | copy-start | bytes 49156
  230.4 35.0 %copy-start.10 = (f32[640,64]{0,1:T(8,128)S(1)}, f32[640,64]{0,1:T(8,128)}, u32[]{:S(2)}) copy-start(f32[640,64]{0,1:T(8,128)} %param.36) | copy-start | bytes 491524
  230.4 35.0 %copy-start.16 = (f32[640,64]{0,1:T(8,128)S(1)}, f32[640,64]{0,1:T(8,128)}, u32[]{:S(2)}) copy-start(f32[640,64]{0,1:T(8,128)} %param.44) | copy-start | bytes 491524
  230.4 35.0 %copy-start.17 = (f32[640,64]{0,1:T(8,128)S(1)}, f32[640,64]{0,1:T(8,128)}, u32[]{:S(2)}) copy-start(f32[640,64]{0,1:T(8,128)} %param.40) | copy-start | bytes 491524
  230.5 4.7 %collective-permute-start.18 = (bf16[2,64,384]{2,1,0:T(8,128)(2,1)S(1)}, bf16[2,64,384]{2,1,0:T(8,128)(2,1)S(1)}, u32[]{:S(2)}, u32[]{:S(2)}) collective-permute-start(bf16[2,64,384]{2,1,0:T(8,128)(2,1)S(1)} %fusion.27), channel_id=1, source_target_pairs={{0,8},{1,9},{2,10},{3,11},{4,12},{5,13},{6,14},{7,15},{8,0},{9,1},... | collective-permute-start | bytes 294920 | tf_op jit(solution)/shard_map/ppermute | solution.py:578
  230.6 10.3 %collective-permute-start.27 = (bf16[64,384]{1,0:T(8,128)(2,1)S(1)}, bf16[64,384]{1,0:T(8,128)(2,1)S(1)}, u32[]{:S(2)}, u32[]{:S(2)}) collective-permute-start(bf16[64,384]{1,0:T(8,128)(2,1)S(1)} %fusion.29), channel_id=1, source_target_pairs={{0,16},{1,17},{2,18},{3,19},{4,20},{5,21},{6,22},{7,23},{8,24},{9,... | collective-permute-start | bytes 147464 | tf_op jit(solution)/shard_map/ppermute | solution.py:578
  235.2 5.1 %collective-permute-start.19 = (bf16[64,384]{1,0:T(8,128)(2,1)S(1)}, bf16[64,384]{1,0:T(8,128)(2,1)S(1)}, u32[]{:S(2)}, u32[]{:S(2)}) collective-permute-start(bf16[64,384]{1,0:T(8,128)(2,1)S(1)} %fusion.33), channel_id=1, source_target_pairs={{0,16},{1,17},{2,18},{3,19},{4,20},{5,21},{6,22},{7,23},{8,24},{9,... | collective-permute-start | bytes 147464 | tf_op jit(solution)/shard_map/ppermute | solution.py:578
  235.8 5.1 %collective-permute-start.23 = (bf16[64,384]{1,0:T(8,128)(2,1)S(1)}, bf16[64,384]{1,0:T(8,128)(2,1)S(1)}, u32[]{:S(2)}, u32[]{:S(2)}) collective-permute-start(bf16[64,384]{1,0:T(8,128)(2,1)S(1)} %fusion.31), channel_id=1, source_target_pairs={{0,16},{1,17},{2,18},{3,19},{4,20},{5,21},{6,22},{7,23},{8,24},{9,... | collective-permute-start | bytes 147464 | tf_op jit(solution)/shard_map/ppermute | solution.py:578
  240.9 26.2 %copy-start.8 = (f32[64,896]{1,0:T(8,128)S(1)}, f32[64,896]{1,0:T(8,128)}, u32[]{:S(2)}) copy-start(f32[64,896]{1,0:T(8,128)} %param.35) | copy-start | bytes 688132
  240.9 26.1 %copy-start.12 = (f32[64,896]{1,0:T(8,128)S(1)}, f32[64,896]{1,0:T(8,128)}, u32[]{:S(2)}) copy-start(f32[64,896]{1,0:T(8,128)} %param.43) | copy-start | bytes 688132
  243.0 1.2 collective-permute-start.28
  244.2 3.6 %collective-permute-start.29 = (f32[8,128]{1,0:T(8,128)S(1)}, f32[8,128]{1,0:T(8,128)S(1)}, u32[]{:S(2)}, u32[]{:S(2)}) collective-permute-start(f32[8,128]{1,0:T(8,128)S(1)} %pad_add_fusion), channel_id=1, source_target_pairs={{0,2},{1,3},{2,0},{3,1},{4,6},{5,7},{6,4},{7,5},{8,10},{9,11},{10,... | collective-permute-start | bytes 12296 | tf_op jit(solution)/shard_map/ppermute | solution.py:578
  247.8 3.6 %collective-permute-start.30 = (f32[8,128]{1,0:T(8,128)S(1)}, f32[8,128]{1,0:T(8,128)S(1)}, u32[]{:S(2)}, u32[]{:S(2)}) collective-permute-start(f32[8,128]{1,0:T(8,128)S(1)} %fusion.68), channel_id=1, source_target_pairs={{0,4},{1,5},{2,6},{3,7},{4,0},{5,1},{6,2},{7,3},{8,12},{9,13},{10,... | collective-permute-start | bytes 12296 | tf_op jit(solution)/shard_map/ppermute | solution.py:578
  251.4 3.6 %collective-permute-start.31 = (f32[8,128]{1,0:T(8,128)S(1)}, f32[8,128]{1,0:T(8,128)S(1)}, u32[]{:S(2)}, u32[]{:S(2)}) collective-permute-start(f32[8,128]{1,0:T(8,128)S(1)} %add.629), channel_id=1, source_target_pairs={{0,8},{1,9},{2,10},{3,11},{4,12},{5,13},{6,14},{7,15},{8,0},{9,1},... | collective-permute-start | bytes 12296 | tf_op jit(solution)/shard_map/ppermute | solution.py:578
  255.1 4.5 %collective-permute-start.32 = (f32[8,128]{1,0:T(8,128)S(1)}, f32[8,128]{1,0:T(8,128)S(1)}, u32[]{:S(2)}, u32[]{:S(2)}) collective-permute-start(f32[8,128]{1,0:T(8,128)S(1)} %add.630), channel_id=1, source_target_pairs={{0,16},{1,17},{2,18},{3,19},{4,20},{5,21},{6,22},{7,23},{8,24},{9,... | collective-permute-start | bytes 12296 | tf_op jit(solution)/shard_map/ppermute | solution.py:578
  (20 other events, 163.0 us)
Sparse Core Ops, SparseCore 0:
  11.6 83.3 all-gather.2

commit v2 on v1

v2 whole, which is shorter than its diff:
```python
import functools
import math

import jax
import jax.numpy as jnp
from jax import lax
from jax.experimental import pallas as pl
from jax.experimental.pallas import tpu as pltpu
from jax.sharding import PartitionSpec as P

D = 512
HEADS = 4
HEAD_DIM = 128
OUT = 84
IN = 256
LEVELS = 13
KM = 16
KG = 8
KD = 3
STEPS_DONE = 7
MB = 4
GROUPS = 4
HID = 512
ROWS = 8
LINES = 64
EARLY = 512
LATE = 1152
BAND = 256
WINDOW = 1280
NEAR = 1536

clip_norm = 0.001
beta_one = 0.9
beta_two = 0.999
epsilon = 1e-08
learn_rate = 0.04
weight_decay = 0.1
average_decay = 0.9

BF = jnp.bfloat16
F32 = jnp.float32
MIB = 1024 * 1024
BIG = 60 * MIB


def mm(left, right):
    return jnp.dot(left, right, preferred_element_type=F32)


def mm_nt(left, right):
    return lax.dot_general(left, right, (((1,), (1,)), ((), ())), preferred_element_type=F32)


def mm_tn(left, right):
    return lax.dot_general(left, right, (((0,), (0,)), ((), ())), preferred_element_type=F32)


def split_two(value):
    high = value.astype(BF)
    return high, (value - high.astype(F32)).astype(BF)


def norm_parts(rows_low):
    values = rows_low.astype(F32)
    center = values - jnp.mean(values, axis=-1, keepdims=True)
    inverse = lax.rsqrt(jnp.mean(center * center, axis=-1, keepdims=True) + 1e-05)
    return center * inverse, inverse


def norm_pull(grad_out, normal, inverse, gain):
    scaled = grad_out * gain
    inner = (
        scaled
        - jnp.mean(scaled, axis=-1, keepdims=True)
        - normal * jnp.mean(scaled * normal, axis=-1, keepdims=True)
    )
    return inner * inverse, jnp.sum(grad_out * normal, axis=0, keepdims=True)


def sums_kernel(grid_ref, pixels_ref, sums_ref, count_ref):
    width, nodes = count_ref.shape
    step = 32
    picks = [jnp.broadcast_to(pixels_ref[k : k + 1, :], (step, nodes)) for k in range(KG)]
    rows = lax.broadcasted_iota(jnp.int32, (step, nodes), 0)

    def count(i, _):
        at = pl.multiple_of(i * step, step)
        total = jnp.zeros((step, nodes), F32)
        for pick in picks:
            total = total + jnp.where(pick - at == rows, 1.0, 0.0)
        count_ref[pl.ds(at, step), :] = total.astype(BF)
        return 0

    lax.fori_loop(0, width // step, count, 0)
    sums_ref[...] = mm(grid_ref[...], count_ref[...])


def grid_sums(grid, pixel_rows):
    nodes, width = pixel_rows.shape[1], grid.shape[1]
    return pl.pallas_call(
        sums_kernel,
        out_shape=jax.ShapeDtypeStruct((IN, nodes), F32),
        scratch_shapes=[pltpu.VMEM((width, nodes), BF)],
        compiler_params=pltpu.CompilerParams(vmem_limit_bytes=16 * 1024 * 1024),
        cost_estimate=pl.CostEstimate(flops=240_000_000, bytes_accessed=1_000_000, transcendentals=0),
        name="grid_sums",
    )(grid, pixel_rows)


def counts_kernel(slots_ref, across_ref, bias_ref, pool_ref, pull_ref):
    nodes, width = pull_ref.shape
    step = 64
    for band in range(nodes // BAND):
        low = band * BAND
        picks = slots_ref[:, low : low + BAND] - low
        rows = lax.broadcasted_iota(jnp.int32, (step, BAND), 0)

        def count_slots(i, _):
            at = pl.multiple_of(i * step, step)
            total = jnp.zeros((step, BAND), F32)
            for k in range(KM):
                total = total + jnp.where(picks[k : k + 1, :] - at == rows, 1.0, 0.0)
            bias_ref[band, pl.ds(at, step), :] = jnp.where(total > 0.0, jnp.log2(jnp.maximum(total, 1.0)), -1e30)
            return 0

        lax.fori_loop(0, WINDOW // step, count_slots, 0)

    def count_across(i, _):
        at = pl.multiple_of(i * 128, 128)
        rows = lax.broadcasted_iota(jnp.int32, (128, width), 0) + at
        total = jnp.zeros((128, width), F32)
        for k in range(KD):
            total = total + jnp.where(across_ref[k : k + 1, :] == rows, 1.0, 0.0)
        pull_ref[pl.ds(at, 128), :] = total.astype(BF)
        pool_ref[:, pl.ds(at, 128)] = total.T.astype(BF)
        return 0

    lax.fori_loop(0, nodes // 128, count_across, 0)


def counts(slot_rows, across_rows):
    nodes, width = slot_rows.shape[1], across_rows.shape[1]
    return pl.pallas_call(
        counts_kernel,
        out_shape=(
            jax.ShapeDtypeStruct((nodes // BAND, WINDOW, BAND), F32),
            jax.ShapeDtypeStruct((width, nodes), BF),
            jax.ShapeDtypeStruct((nodes, width), BF),
        ),
        compiler_params=pltpu.CompilerParams(vmem_limit_bytes=16 * 1024 * 1024),
        cost_estimate=pl.CostEstimate(flops=60_000_000, bytes_accessed=5_000_000, transcendentals=700_000),
        name="counts",
    )(slot_rows, across_rows)


def blocks_of(place_ref, dims, refs):
    own_wide, own_narrow = place_ref[0], place_ref[1]
    found = []
    for side in range(2):
        for j in range(16):
            bits = dict(zip(dims, ((j >> 3) & 1, (j >> 2) & 1, (j >> 1) & 1, j & 1)))
            wide = own_wide ^ (bits[4] * 4 + bits[3] * 2 + bits[2])
            narrow = own_narrow ^ (bits[1] * 2 + side)
            found.append((wide, narrow, refs[2 * side + (j >> 3)].at[j & 7]))
    return found


def fetch_early(place_ref, refs, early, sems):
    copies = []
    for colour in range(2):
        for wide, narrow, source in blocks_of(place_ref, DIMS[colour], refs[4 * colour : 4 * colour + 4]):
            copies.append(
                pltpu.make_async_copy(
                    source, early.at[wide, narrow, :, colour * 256 : colour * 256 + 256], sems.at[len(copies)]
                )
            )
    return copies


def enc_of(early):
    return jnp.concatenate([early[:, n, 0:32, 384:512].reshape(IN, 128) for n in range(GROUPS)], axis=1)


def dec_of(early):
    return jnp.concatenate([early[:, n, 32:48, 384:512].reshape(128, 128) for n in range(GROUPS)], axis=0)


def query_of(early):
    return jnp.concatenate([early[:, n, :, 0:128].reshape(D, 128) for n in range(GROUPS)], axis=1)


def pair_of(early):
    return jnp.concatenate([early[:, n, :, 128:384].reshape(D, 256) for n in range(GROUPS)], axis=1)


class Leaving:
    def __init__(self, sems):
        self.sems, self.copies = sems, []

    def __call__(self, source, there):
        self.copies.append(pltpu.make_async_copy(source, there, self.sems.at[len(self.copies)]))
        self.copies[-1].start()

    def wait(self):
        for copy in self.copies:
            copy.wait()


def encode_kernel(
    place_ref, a_0, a_1, a_2, a_3, b_0, b_1, b_2, b_3, before_ref, sums_ref, after_ref,
    state_ref, rows_ref, normed_ref, query_ref, pair_ref, early_ref,
    early, state, rows_all, normed_all, query_all, pair_all, sems, out_sems,
):
    copies = fetch_early(place_ref, (a_0, a_1, a_2, a_3, b_0, b_1, b_2, b_3), early, sems)
    for copy in copies:
        copy.start()
    for copy in copies:
        copy.wait()
    leave = Leaving(out_sems)
    leave(early, early_ref)
    gain = dec_of(early).astype(F32).T[OUT : OUT + 1, :]
    enc = enc_of(early)
    weights = pair_of(early)
    for block, ref in enumerate((before_ref, sums_ref, after_ref)):
        here = slice(block * 512, block * 512 + 512)
        if block == 1:
            high, low = split_two(ref[...])
            embedded = (mm_tn(high, enc) + mm_tn(low, enc)) * (1.0 / KG)
            state[...] = embedded
            leave(state, state_ref)
        else:
            embedded = mm_tn(ref[...], enc) * (1.0 / KG)
        rows = embedded.astype(BF)
        rows_all[here, :] = rows
        leave(rows_all.at[here], rows_ref.at[here])
        normal, _inverse = norm_parts(rows)
        normed = (normal * gain).astype(BF)
        normed_all[here, :] = normed
        leave(normed_all.at[here], normed_ref.at[here])
        if block == 1:
            query_all[...] = mm(normed, query_of(early)).astype(BF)
            leave(query_all, query_ref)
        pair_all[here, :] = mm(normed, weights).astype(BF)
        leave(pair_all.at[here], pair_ref.at[here])
    leave.wait()


def encode(place, gathered, before, sums, after):
    nodes = sums.shape[1]
    vmem = pl.BlockSpec(memory_space=pltpu.VMEM)
    outside = pl.BlockSpec(memory_space=pltpu.HBM)
    shapes = (
        jax.ShapeDtypeStruct((nodes, D), F32),
        jax.ShapeDtypeStruct((NEAR, D), BF),
        jax.ShapeDtypeStruct((NEAR, D), BF),
        jax.ShapeDtypeStruct((nodes, D), BF),
        jax.ShapeDtypeStruct((NEAR, 2 * D), BF),
        jax.ShapeDtypeStruct((8, GROUPS, LINES, EARLY), BF),
    )
    return pl.pallas_call(
        encode_kernel,
        in_specs=[pl.BlockSpec(memory_space=pltpu.SMEM)] + [outside] * 8 + [vmem] * 3,
        out_specs=[outside] * 6,
        out_shape=shapes,
        scratch_shapes=[pltpu.VMEM((8, GROUPS, LINES, EARLY), BF)]
        + [pltpu.VMEM(shape.shape, shape.dtype) for shape in shapes[:5]]
        + [pltpu.SemaphoreType.DMA((64,)), pltpu.SemaphoreType.DMA((12,))],
        compiler_params=pltpu.CompilerParams(vmem_limit_bytes=BIG),
        cost_estimate=pl.CostEstimate(flops=5_000_000_000, bytes_accessed=12_000_000, transcendentals=0),
        name="encode",
    )(place, *gathered, before, sums, after)


def attend_kernel(
    query_in, pair_in, bias_in, mixed_ref, probs_ref,
    query_all, pair_all, bias, mixed_all, probs, scores, value_turned, sems, out_sems,
):
    def pair_copy(h):
        return pltpu.make_async_copy(pair_in.at[:, pl.ds(pl.multiple_of(h * 256, 256), 256)], pair_all.at[h], sems.at[h])

    query_copy = pltpu.make_async_copy(query_in, query_all, sems.at[4])
    bias_copies = [pltpu.make_async_copy(bias_in.at[i], bias.at[i], sems.at[5 + i]) for i in range(2)]
    pair_copy(0).start()
    query_copy.start()
    bias_copies[0].start()
    bias_copies[1].start()
    for h in range(1, HEADS):
        pair_copy(h).start()
    query_copy.wait()
    bias_copies[0].wait()
    bias_copies[1].wait()
    factor = HEAD_DIM ** (-0.5) * math.log2(math.e)
    chunk = 128

    def head(h, _):
        lane = pl.multiple_of(h * HEAD_DIM, HEAD_DIM)
        pair_copy(h).wait()
        value_turned[...] = pair_all[h, :, HEAD_DIM:].astype(F32).T.astype(BF)
        for band in range(2):
            at = band * BAND
            query = query_all[at : at + BAND, pl.ds(lane, HEAD_DIM)]
            top = jnp.full((1, BAND), -3e38, F32)
            for i in range(WINDOW // chunk):
                row = i * chunk
                part = mm_nt(pair_all[h, at + row : at + row + chunk, :HEAD_DIM], query)
                part = part * factor + bias[band, row : row + chunk, :]
                scores[row : row + chunk, :] = part
                top = jnp.maximum(top, jnp.max(part, axis=0, keepdims=True))
            total = jnp.zeros((1, BAND), F32)
            mixed = jnp.zeros((HEAD_DIM, BAND), F32)
            for i in range(WINDOW // chunk):
                row = i * chunk
                expo = jnp.exp2(scores[row : row + chunk, :] - top)
                scores[row : row + chunk, :] = expo
                total = total + jnp.sum(expo, axis=0, keepdims=True)
                mixed = mixed + mm(value_turned[:, at + row : at + row + chunk], expo.astype(BF))
            inverse = 1.0 / total
            mixed_all[at : at + BAND, pl.ds(lane, HEAD_DIM)] = (mixed * inverse).T.astype(BF)
            for i in range(WINDOW // chunk):
                row = i * chunk
                probs[h, band, row : row + chunk, :] = (scores[row : row + chunk, :] * inverse).astype(BF)
            pltpu.make_async_copy(probs.at[h, band], probs_ref.at[h, band], out_sems.at[1 + 2 * h + band]).start()
        return 0

    lax.fori_loop(0, HEADS, head, 0)
    leave = pltpu.make_async_copy(mixed_all, mixed_ref, out_sems.at[0])
    leave.start()
    leave.wait()
    for h in range(HEADS):
        for band in range(2):
            pltpu.make_async_copy(probs.at[h, band], probs_ref.at[h, band], out_sems.at[1 + 2 * h + band]).wait()


def attend(query, pair, bias):
    nodes = query.shape[0]
    outside = pl.BlockSpec(memory_space=pltpu.HBM)
    return pl.pallas_call(
        attend_kernel,
        in_specs=[outside] * 3,
        out_specs=[outside] * 2,
        out_shape=(
            jax.ShapeDtypeStruct((nodes, D), BF),
            jax.ShapeDtypeStruct((HEADS, 2, WINDOW, BAND), BF),
        ),
        scratch_shapes=[
            pltpu.VMEM((nodes, D), BF),
            pltpu.VMEM((HEADS, NEAR, 2 * HEAD_DIM), BF),
            pltpu.VMEM((2, WINDOW, BAND), F32),
            pltpu.VMEM((nodes, D), BF),
            pltpu.VMEM((HEADS, 2, WINDOW, BAND), BF),
            pltpu.VMEM((WINDOW, BAND), F32),
            pltpu.VMEM((HEAD_DIM, NEAR), BF),
            pltpu.SemaphoreType.DMA((7,)),
            pltpu.SemaphoreType.DMA((9,)),
        ],
        compiler_params=pltpu.CompilerParams(vmem_limit_bytes=BIG),
        cost_estimate=pl.CostEstimate(flops=3_000_000_000, bytes_accessed=12_000_000, transcendentals=3_000_000),
        name="attend",
    )(query, pair, bias)


def feed_kernel(
    place_ref, scalars_ref, a_0, a_1, a_2, a_3, b_0, b_1, b_2, b_3, early_ref, state_in, mixed_in, pool_in, pull_in, noisy_ref, target_ref, lat_ref, level_ref,
    keep_out, send_out, grad_state_out, grad_mixed_out, grad_dec_ref, loss_ref,
    late, dec, pre_ref, act_ref, grad_pred_ref,
    state_ref, mixed_ref, pool_ref, pull_ref, keep_ref, send_ref, grad_state_ref, grad_mixed_ref, sems, group_sems, out_sems,
):
    own_wide, own_narrow = place_ref[0], place_ref[1]

    refs = (a_0, a_1, a_2, a_3), (b_0, b_1, b_2, b_3)

    def fetch(colour, columns, first, sem):
        there = slice(first, first + columns.stop - columns.start)
        return [
            pltpu.make_async_copy(source.at[:, columns], late.at[wide, narrow, :, there], sem(narrow, i))
            for i, (wide, narrow, source) in enumerate(blocks_of(place_ref, DIMS[colour], refs[colour]))
        ]

    def group(n, columns, row):
        return pltpu.make_async_copy(late.at[:, n, :, columns], late.at[:, n, :, columns], group_sems.at[row, n])

    hidden, outer, lower = slice(0, 512), slice(512, 640), slice(640, 1152)
    pairs = [(state_in, state_ref), (mixed_in, mixed_ref), (early_ref.at[:, :, 32:48, 384:512], dec)]
    small = [pltpu.make_async_copy(source, there, sems.at[32 + i]) for i, (source, there) in enumerate(pairs)]
    small += fetch(0, outer, 512, lambda n, i: sems.at[i])
    pool_copy = pltpu.make_async_copy(pool_in, pool_ref, sems.at[35])
    pull_copy = pltpu.make_async_copy(pull_in, pull_ref, sems.at[36])
    first = fetch(0, hidden, 0, lambda n, i: group_sems.at[0, n])
    second = fetch(1, slice(0, 512), 640, lambda n, i: group_sems.at[1, n])
    for copy in (*small, *first, *second, pool_copy, pull_copy):
        copy.start()
    for copy in small:
        copy.wait()
    dec_turned = jnp.concatenate([dec[:, n].reshape(128, 128) for n in range(GROUPS)], axis=0).astype(F32).T
    gain = dec_turned[OUT + 1 : OUT + 2, :]
    rows = lax.broadcasted_iota(jnp.int32, (128, 1), 0)
    dec_only = jnp.where(rows < OUT, dec_turned, 0.0).astype(BF)
    out_full = jnp.concatenate([late[:, n, :, 512:640].reshape(D, 128) for n in range(GROUPS)], axis=1)
    mixed = mixed_ref[...]
    state1 = state_ref[...] + mm_nt(mixed, out_full)
    normal, inverse = norm_parts(state1.astype(BF))
    normed = (normal * gain).astype(BF)

    def forward(i, state):
        n = i ^ own_narrow
        group(n, hidden, 0).wait()
        pre = mm(normed, late[:, n, :, 0:512].reshape(D, HID))
        pre_ref[n] = pre
        act = (pre / (1.0 + jnp.exp(-pre))).astype(BF)
        act_ref[n] = act
        group(n, lower, 1).wait()
        return state + mm_nt(act, late[:, n, :, 640:1152].reshape(D, HID))

    state2 = lax.fori_loop(0, GROUPS, forward, state1)
    high, low = split_two(state2)
    pool_copy.wait()
    pull_copy.wait()
    pool = pool_ref[...]
    pooled = ((mm(pool, high) + mm(pool, low)) / KD).astype(BF)
    pixels = noisy_ref.shape[1]
    pred = mm_nt(dec_only, pooled)[:OUT, :pixels]
    c_skip, c_out, lam = scalars_ref[0], scalars_ref[1], scalars_ref[2]
    error = c_skip * noisy_ref[...] + c_out * pred - target_ref[...]
    weighted = lam * (lat_ref[...] * level_ref[...])
    loss_ref[...] = jnp.broadcast_to(jnp.sum(weighted * error * error), loss_ref.shape)
    grad_pred_ref[...] = jnp.zeros_like(grad_pred_ref)
    grad_pred_ref[:OUT, :pixels] = 2.0 * c_out * weighted * error
    grad_pred = grad_pred_ref[...].astype(BF)
    grad_dec_ref[...] = mm(grad_pred, pooled)
    up_high, up_low = split_two(mm_nt(pull_ref[...], grad_pred))
    grad_state2 = (mm(up_high, dec_only) + mm(up_low, dec_only)) / KD
    grad_low = grad_state2.astype(BF)
    grad_turned = grad_state2.T.astype(BF)
    normed_turned = normed.astype(F32).T.astype(BF)

    def put(out_ref, side, part, first, value):
        done = 0
        while done < value.shape[1]:
            colour, column = divmod(first + done, 384)
            count = min(384 - column, value.shape[1] - done)
            for w in range(8):
                out_ref[colour, part, w ^ own_wide, :, column : column + count] = value[
                    w * LINES : (w + 1) * LINES, done : done + count
                ]
            done += count

    def backward(part, grad_n, out_ref, side):
        n = (part * 2 + side) ^ own_narrow
        act = act_ref[n]
        pre = pre_ref[n]
        put(out_ref, side, part, 640, mm(grad_turned, act).astype(BF))
        grad_act = mm(grad_low, late[:, n, :, 640:1152].reshape(D, HID))
        logistic = 1.0 / (1.0 + jnp.exp(-pre))
        grad_pre = (grad_act * logistic * (1.0 + pre * (1.0 - logistic))).astype(BF)
        put(out_ref, side, part, 0, mm(normed_turned, grad_pre).astype(BF))
        return grad_n + mm_nt(grad_pre, late[:, n, :, 0:512].reshape(D, HID))

    grad_n = jnp.zeros((D, D), F32)
    leaving = []

    def leave(source, there):
        leaving.append(pltpu.make_async_copy(source, there, out_sems.at[len(leaving)]))
        leaving[-1].start()

    for side, out_ref, there in ((1, send_ref, send_out), (0, keep_ref, keep_out)):
        grad_n = lax.fori_loop(0, 2, functools.partial(backward, out_ref=out_ref, side=side), grad_n)
        leave(out_ref.at[0], there.at[0])
        leave(out_ref.at[2], there.at[2])
    back, gain_grad = norm_pull(grad_n, normal, inverse, gain)
    grad_dec_ref[OUT + 1 : OUT + 2, :] = gain_grad
    grad_state1 = grad_state2 + back
    grad_state_ref[...] = grad_state1
    leave(grad_state_ref, grad_state_out)
    grad_low1 = grad_state1.astype(BF)
    grad_turned1 = grad_state1.T.astype(BF)
    for side, out_ref, there in ((1, send_ref, send_out), (0, keep_ref, keep_out)):
        for part in range(2):
            lane = pl.multiple_of(((part * 2 + side) ^ own_narrow) * 128, 128)
            put(out_ref, side, part, 512, mm(grad_turned1, mixed_ref[:, pl.ds(lane, 128)]).astype(BF))
        leave(out_ref.at[1], there.at[1])
    grad_mixed_ref[...] = mm(grad_low1, out_full).astype(BF)
    leave(grad_mixed_ref, grad_mixed_out)
    for copy in leaving:
        copy.wait()


def feed(place, scalars, late, early, state0, mixed, pool, pull, noisy, target, lat, level):
    nodes = state0.shape[0]
    width = pool.shape[0]
    vmem = pl.BlockSpec(memory_space=pltpu.VMEM)
    outside = pl.BlockSpec(memory_space=pltpu.HBM)
    return pl.pallas_call(
        feed_kernel,
        in_specs=[pl.BlockSpec(memory_space=pltpu.SMEM)] * 2 + [outside] * 13 + [vmem] * 4,
        out_specs=[outside] * 4 + [vmem] * 2,
        out_shape=(
            jax.ShapeDtypeStruct((3, 2, 8, LINES, 384), BF),
            jax.ShapeDtypeStruct((3, 2, 8, LINES, 384), BF),
            jax.ShapeDtypeStruct((nodes, D), F32),
            jax.ShapeDtypeStruct((nodes, D), BF),
            jax.ShapeDtypeStruct((128, D), F32),
            jax.ShapeDtypeStruct((8, 128), F32),
        ),
        scratch_shapes=[
            pltpu.VMEM((8, GROUPS, LINES, LATE), BF),
            pltpu.VMEM((8, GROUPS, 16, 128), BF),
            pltpu.VMEM((GROUPS, nodes, HID), F32),
            pltpu.VMEM((GROUPS, nodes, HID), BF),
            pltpu.VMEM((128, width), F32),
            pltpu.VMEM((nodes, D), F32),
            pltpu.VMEM((nodes, D), BF),
            pltpu.VMEM((width, nodes), BF),
            pltpu.VMEM((nodes, width), BF),
            pltpu.VMEM((3, 2, 8, LINES, 384), BF),
            pltpu.VMEM((3, 2, 8, LINES, 384), BF),
            pltpu.VMEM((nodes, D), F32),
            pltpu.VMEM((nodes, D), BF),
            pltpu.SemaphoreType.DMA((37,)),
            pltpu.SemaphoreType.DMA((2, GROUPS)),
            pltpu.SemaphoreType.DMA((8,)),
        ],
        compiler_params=pltpu.CompilerParams(vmem_limit_bytes=BIG),
        cost_estimate=pl.CostEstimate(flops=9_000_000_000, bytes_accessed=20_000_000, transcendentals=3_000_000),
        name="feed",
    )(place, scalars, *late, early, state0, mixed, pool, pull, noisy, target, lat, level)


def unmix_kernel(probs_ref, query_ref, keys_ref, values_ref, grad_mixed_ref, grad_query_ref, grad_pair_ref,
                 keys_sum, values_sum, grad_scores, grad_probs, key_turned):
    scale = HEAD_DIM ** (-0.5)
    chunk = 128

    def head(h, lane):
        keys_sum[...] = jnp.zeros_like(keys_sum)
        values_sum[...] = jnp.zeros_like(values_sum)
        key_turned[...] = keys_ref[:, pl.ds(lane, HEAD_DIM)].astype(F32).T.astype(BF)
        for band in range(2):
            at = band * BAND
            grad = grad_mixed_ref[at : at + BAND, pl.ds(lane, HEAD_DIM)]
            query = query_ref[at : at + BAND, pl.ds(lane, HEAD_DIM)]
            inner = jnp.zeros((1, BAND), F32)
            for i in range(WINDOW // chunk):
                row = i * chunk
                part = mm_nt(values_ref[at + row : at + row + chunk, pl.ds(lane, HEAD_DIM)], grad)
                grad_probs[row : row + chunk, :] = part
                inner = inner + jnp.sum(part * probs_ref[h, band, row : row + chunk, :].astype(F32), axis=0, keepdims=True)
            for i in range(WINDOW // chunk):
                row = i * chunk
                probs = probs_ref[h, band, row : row + chunk, :]
                low = (probs.astype(F32) * (grad_probs[row : row + chunk, :] - inner) * scale).astype(BF)
                grad_scores[row : row + chunk, :] = low
                keys_sum[at + row : at + row + chunk, :] += mm(low, query)
                values_sum[at + row : at + row + chunk, :] += mm(probs, grad)
            turned = mm(key_turned[:, at : at + WINDOW], grad_scores[...])
            grad_query_ref[at : at + BAND, pl.ds(lane, HEAD_DIM)] = turned.T.astype(BF)
        grad_pair_ref[:, 0:HEAD_DIM] = keys_sum[...].astype(BF)
        grad_pair_ref[:, HEAD_DIM : 2 * HEAD_DIM] = values_sum[...].astype(BF)

    head(0, 0)


def unmix(first, heads, probs, query, pair, grad_mixed):
    nodes = query.shape[0]
    part = pl.BlockSpec((nodes, HEAD_DIM), lambda i: (0, first + i))
    return pl.pallas_call(
        unmix_kernel,
        grid=(heads,),
        in_specs=[
            pl.BlockSpec((1, 2, WINDOW, BAND), lambda i: (first + i, 0, 0, 0)),
            part,
            pl.BlockSpec((NEAR, HEAD_DIM), lambda i: (0, 2 * (first + i))),
            pl.BlockSpec((NEAR, HEAD_DIM), lambda i: (0, 2 * (first + i) + 1)),
            part,
        ],
        out_specs=(
            pl.BlockSpec((nodes, HEAD_DIM), lambda i: (0, i)),
            pl.BlockSpec((NEAR, 2 * HEAD_DIM), lambda i: (0, i)),
        ),
        out_shape=(
            jax.ShapeDtypeStruct((nodes, heads * HEAD_DIM), BF),
            jax.ShapeDtypeStruct((NEAR, heads * 2 * HEAD_DIM), BF),
        ),
        scratch_shapes=[
            pltpu.VMEM((NEAR, HEAD_DIM), F32),
            pltpu.VMEM((NEAR, HEAD_DIM), F32),
            pltpu.VMEM((WINDOW, BAND), BF),
            pltpu.VMEM((WINDOW, BAND), F32),
            pltpu.VMEM((HEAD_DIM, NEAR), BF),
        ],
        compiler_params=pltpu.CompilerParams(vmem_limit_bytes=BIG),
        cost_estimate=pl.CostEstimate(
            flops=1_000_000_000 * heads, bytes_accessed=3_000_000 * heads, transcendentals=0
        ),
        name="unmix",
    )(probs, query, pair, pair, grad_mixed)


def return_kernel(
    place_ref, early_ref, query_in_a, query_in_b, pair_in_a, pair_in_b,
    grad_state_in, rows_in, normed_in, before_ref, sums_ref, after_ref, grad_dec_ref,
    keep_out, send_out,
    early, normed_ref, rows_ref, grad_state_ref, query_g, pair_g, keep_ref, send_ref, sems,
):
    pairs = (
        (normed_in, normed_ref),
        (query_in_a, query_g.at[:, 0:128]), (query_in_b, query_g.at[:, 128:512]),
        (pair_in_a, pair_g.at[:, 0:256]), (pair_in_b, pair_g.at[:, 256:1024]),
        (early_ref, early), (rows_in, rows_ref), (grad_state_in, grad_state_ref),
    )
    copies = [pltpu.make_async_copy(source, there, sems.at[i]) for i, (source, there) in enumerate(pairs)]
    for copy in copies:
        copy.start()
    own_wide, own_narrow = place_ref[0], place_ref[1]
    def put(n, colour, column, value, low):
        lines = value.shape[0] // 8
        for side, out_ref in ((1, send_ref), (0, keep_ref)):

            @pl.when(((n ^ own_narrow) & 1) == side)
            def _():
                part = (n ^ own_narrow) >> 1
                for w in range(8):
                    out_ref[colour, part, w ^ own_wide, low : low + lines, column : column + 128] = value[
                        w * lines : (w + 1) * lines, :
                    ]

    copies[0].wait()
    turned = normed_ref[...].astype(F32).T.astype(BF)
    for copy in copies[1:5]:
        copy.wait()
    weight_query = mm(turned[:, 512:1024], query_g[...]).astype(BF)
    weight_pair = mm(turned, pair_g[...]).astype(BF)
    for n in range(GROUPS):
        put(n, 0, 0, weight_query[:, n * 128 : n * 128 + 128], 0)
        put(n, 0, 128, weight_pair[:, n * 256 : n * 256 + 128], 0)
        put(n, 1, 0, weight_pair[:, n * 256 + 128 : n * 256 + 256], 0)
    leaving = [
        pltpu.make_async_copy(send_ref.at[0], send_out.at[0], sems.at[10]),
        pltpu.make_async_copy(keep_ref.at[0], keep_out.at[0], sems.at[11]),
        pltpu.make_async_copy(send_ref.at[1], send_out.at[1], sems.at[12]),
        pltpu.make_async_copy(keep_ref.at[1], keep_out.at[1], sems.at[13]),
    ]
    leaving[0].start()
    leaving[1].start()
    for copy in copies[5:]:
        copy.wait()
    gain = dec_of(early).astype(F32).T[OUT : OUT + 1, :]
    pair_weights = pair_of(early)
    grad_enc = jnp.zeros((IN, D), F32)
    gain_grad = jnp.zeros((1, D), F32)
    for block, sums in enumerate((before_ref, sums_ref, after_ref)):
        at = block * 512
        grad_block = mm_nt(pair_g[at : at + 512, :], pair_weights)
        if block == 1:
            grad_block = grad_block + mm_nt(query_g[...], query_of(early))
        normal, inverse = norm_parts(rows_ref[at : at + 512, :])
        back, gain_part = norm_pull(grad_block, normal, inverse, gain)
        gain_grad = gain_grad + gain_part
        if block == 1:
            back = back + grad_state_ref[...]
        back_low = (back * (1.0 / KG)).astype(BF)
        grad_enc = grad_enc + mm(sums[...].astype(BF), back_low)
    grad_enc = grad_enc.astype(BF)
    rows = lax.broadcasted_iota(jnp.int32, (128, 1), 0)
    grad_dec = jnp.where(rows == OUT, gain_grad, grad_dec_ref[...]).T.astype(BF)
    for n in range(GROUPS):
        put(n, 1, 128, grad_enc[:, n * 128 : n * 128 + 128], 0)
        put(n, 1, 128, grad_dec[n * 128 : n * 128 + 128, :], 32)
        put(n, 1, 128, jnp.zeros((128, 128), BF), 48)
    leaving[2].start()
    leaving[3].start()
    for copy in leaving:
        copy.wait()


def give_back(place, early, first, second, grad_state, rows, normed, before, sums, after, grad_dec):
    vmem = pl.BlockSpec(memory_space=pltpu.VMEM)
    outside = pl.BlockSpec(memory_space=pltpu.HBM)
    return pl.pallas_call(
        return_kernel,
        in_specs=[pl.BlockSpec(memory_space=pltpu.SMEM), outside] + [outside] * 7 + [vmem] * 4,
        out_specs=[outside] * 2,
        out_shape=(
            jax.ShapeDtypeStruct((2, 2, 8, LINES, 256), BF),
            jax.ShapeDtypeStruct((2, 2, 8, LINES, 256), BF),
        ),
        scratch_shapes=[
            pltpu.VMEM((8, GROUPS, LINES, EARLY), BF),
            pltpu.VMEM((NEAR, D), BF),
            pltpu.VMEM((NEAR, D), BF),
            pltpu.VMEM((512, D), F32),
            pltpu.VMEM((512, D), BF),
            pltpu.VMEM((NEAR, 2 * D), BF),
            pltpu.VMEM((2, 2, 8, LINES, 256), BF),
            pltpu.VMEM((2, 2, 8, LINES, 256), BF),
            pltpu.SemaphoreType.DMA((14,)),
        ],
        compiler_params=pltpu.CompilerParams(vmem_limit_bytes=BIG),
        cost_estimate=pl.CostEstimate(flops=5_000_000_000, bytes_accessed=12_000_000, transcendentals=0),
        name="give_back",
    )(
        place, early, first[0], second[0], first[1], second[1],
        grad_state, rows, normed, before, sums, after, grad_dec,
    )


def adam_kernel(row_ref, early_ref, late_ref, *refs):
    total = row_ref[0:1, 2:3] * MB
    norm_value = jnp.sqrt(row_ref[0:1, 0:1]) / total
    factor = jnp.minimum(1.0, clip_norm / norm_value) / total
    lanes = lax.broadcasted_iota(jnp.int32, (8, 128), 1)
    refs[36][...] = jnp.where(lanes == 0, row_ref[0:1, 1:2] / total, norm_value)
    fix_one = 1.0 - beta_one**STEPS_DONE
    fix_two = 1.0 - beta_two**STEPS_DONE
    enc_rows, read_rows = refs[0].shape[0], refs[12].shape[0]
    shares = (
        ((early_ref, slice(0, enc_rows), slice(384, 512), slice(None)),),
        ((early_ref, slice(None), slice(0, 384), slice(0, 384)), (late_ref, slice(None), slice(0, 512), slice(384, 896))),
        ((late_ref, slice(None), slice(512, 1152), slice(None)),),
        ((early_ref, slice(enc_rows, enc_rows + read_rows), slice(384, 384 + OUT + 2), slice(None)),),
    )
    for i, pieces in enumerate(shares):
        weight_ref, moment_ref, second_ref, average_ref = refs[4 * i : 4 * i + 4]
        outs = refs[16 + 5 * i : 21 + 5 * i]
        for share_ref, rows, columns, there in pieces:
            grad = share_ref[rows, columns] * factor
            weight = weight_ref[:, there]
            moment = beta_one * moment_ref[:, there] + (1.0 - beta_one) * grad
            second = beta_two * second_ref[:, there] + (1.0 - beta_two) * grad * grad
            weight = weight - learn_rate * (
                moment / fix_one / (jnp.sqrt(second / fix_two) + epsilon) + weight_decay * weight
            )
            outs[0][:, there] = moment
            outs[1][:, there] = second
            outs[2][:, there] = weight
            outs[3][:, there] = average_decay * average_ref[:, there] + (1.0 - average_decay) * weight
            outs[4][:, there] = weight.astype(BF)


def adam(row, early, late, states):
    arrays = [array for state in states for array in state]
    shapes = []
    for state in states:
        shapes += [jax.ShapeDtypeStruct(state[0].shape, F32)] * 4 + [jax.ShapeDtypeStruct(state[0].shape, BF)]
    shapes.append(jax.ShapeDtypeStruct((8, 128), F32))
    vmem = pl.BlockSpec(memory_space=pltpu.VMEM)
    return pl.pallas_call(
        adam_kernel,
        in_specs=[vmem] * 19,
        out_specs=[vmem] * 21,
        out_shape=shapes,
        compiler_params=pltpu.CompilerParams(vmem_limit_bytes=16 * MIB),
        cost_estimate=pl.CostEstimate(flops=3_000_000, bytes_accessed=4_000_000, transcendentals=200_000),
        name="adam",
    )(row, early, late, *arrays)


def pack_kernel(encoder_ref, up_ref, down_ref, readout_ref, early_ref, late_ref):
    enc_rows, read_rows = encoder_ref.shape[0], readout_ref.shape[0]
    early_ref[:, 0:384] = up_ref[:, 0:384].astype(BF)
    side = jnp.zeros((early_ref.shape[0] - enc_rows, 128), F32)
    early_ref[enc_rows:, 384:512] = side.astype(BF)
    early_ref[0:enc_rows, 384:512] = encoder_ref[...].astype(BF)
    early_ref[enc_rows : enc_rows + read_rows, 384 : 384 + OUT + 2] = readout_ref[...].astype(BF)
    late_ref[:, 0:512] = up_ref[:, 384:896].astype(BF)
    late_ref[:, 512:1152] = down_ref[...].astype(BF)


def pack(encoder, up_proj, down_turned, readout):
    lines = up_proj.shape[0]
    vmem = pl.BlockSpec(memory_space=pltpu.VMEM)
    return pl.pallas_call(
        pack_kernel,
        in_specs=[vmem] * 4,
        out_specs=[vmem] * 2,
        out_shape=(jax.ShapeDtypeStruct((lines, EARLY), BF), jax.ShapeDtypeStruct((lines, LATE), BF)),
        compiler_params=pltpu.CompilerParams(vmem_limit_bytes=8 * MIB),
        cost_estimate=pl.CostEstimate(flops=100_000, bytes_accessed=600_000, transcendentals=0),
        name="pack",
    )(encoder, up_proj, down_turned, readout)


def to_lines(array, wide):
    if wide == 8:
        return array
    lines, width = array.shape[2:]
    return jnp.moveaxis(jnp.moveaxis(array, 1, 0).reshape(GROUPS, 8, LINES, width), 0, 1)


def side_to_lines(side, wide):
    if wide == 8:
        return side
    enc_rows, read_rows = IN // wide, D // (GROUPS * wide)
    enc = to_rows(side[:, :, :enc_rows], 32)
    read = to_rows(side[:, :, enc_rows : enc_rows + read_rows], 16)
    return jnp.concatenate([enc, read, jnp.zeros((8, GROUPS, 16, 128), side.dtype)], axis=2)


def to_rows(array, rows):
    return jnp.moveaxis(jnp.moveaxis(array, 1, 0).reshape(GROUPS, 8, rows, array.shape[3]), 0, 1)


def from_rows(array, wide):
    rows, width = array.shape[2:]
    return jnp.moveaxis(jnp.moveaxis(array, 1, 0).reshape(GROUPS, wide, 8 * rows // wide, width), 0, 1)


def early_from_lines(array, wide):
    if wide == 8:
        return array
    main = from_rows(array[..., :384], wide)
    enc = from_rows(array[:, :, :32, 384:], wide)
    read = from_rows(array[:, :, 32:48, 384:], wide)
    spare = main.shape[2] - enc.shape[2] - read.shape[2]
    side = jnp.concatenate([enc, read, jnp.zeros((wide, GROUPS, spare, 128), array.dtype)], axis=2)
    return jnp.concatenate([main, side], axis=3)


ORDERS = ((1, 2, 3, 4), (2, 3, 1, 4), (3, 1, 2, 4))
DIMS = ((1, 2, 3, 4), (2, 1, 3, 4))
CUTS = (640, 512)


def by_relative(array, dims):
    array = array.reshape(2, 2, 2, 2, 2, *array.shape[2:])
    axes = {4: 0, 3: 1, 2: 2, 1: 3}
    turned = jnp.transpose(array, (4, *(axes[bit] for bit in dims), 5, 6))
    turned = turned.reshape(4, 8, *turned.shape[5:])
    return [turned[i] for i in range(4)]


def gather_plain(early, late, wide):
    def gathered(array):
        full = lax.all_gather(array, ("wide", "narrow"), axis=0, tiled=False)
        return full.reshape(wide, GROUPS, *array.shape)

    full = gathered(early)
    full = jnp.concatenate([to_lines(full[..., :384], wide), side_to_lines(full[..., 384:], wide)], axis=3)
    first = [by_relative(full[..., 256 * i : 256 * i + 256], DIMS[i]) for i in range(2)]
    full = to_lines(gathered(late), wide)
    second = [by_relative(part, DIMS[i]) for i, part in enumerate(jnp.split(full, [CUTS[0]], axis=3))]
    return sum(first, []), sum(second, [])


def joined(array, other):
    return jnp.concatenate([array[None], other[None]], axis=0)


def swap(array, bit):
    count = lax.axis_size("wide") * lax.axis_size("narrow")
    return lax.ppermute(array, ("wide", "narrow"), [(i, i ^ (1 << bit)) for i in range(count)])


def half_sum(parts, axis):
    return sum(lax.index_in_dim(part, 1, axis, keepdims=False).astype(F32) for part in parts).astype(BF)


def half_left(parts, axis):
    return [lax.index_in_dim(part, 0, axis, keepdims=False) for part in parts]


def halve(parts, axis, bit):
    return half_left(parts, axis) + [swap(half_sum(parts, axis), bit)]


def cube(array):
    return array.reshape(2, 2, 2, 2, *array.shape[2:])


def flat(array):
    return array.reshape(8, *array.shape[3:])


class Late:
    def __init__(self, keep, send):
        got = swap(send, 0)
        self.parts = [[cube(keep[i]), cube(got[i])] for i in range(3)]
        self.axes = [[1, 4, 3, 2] for _ in range(3)]

    def step(self, phase, values=()):
        at = [self.axes[i].index(order[phase]) for i, order in enumerate(ORDERS)]
        sent = [half_sum(self.parts[i], at[i]) for i in range(3)]
        sent, values = lax.optimization_barrier((sent, values))
        for i, order in enumerate(ORDERS):
            self.parts[i] = half_left(self.parts[i], at[i]) + [swap(sent[i], order[phase])]
            self.axes[i].pop(at[i])
        return values

    def last(self):
        sent = jnp.concatenate([half_sum(parts, 0) for parts in self.parts], axis=1)
        self.got = swap(sent, 4)
        self.parts = [half_left(parts, 0) for parts in self.parts]

    def total(self):
        kept = [sum(part.astype(F32) for part in parts) for parts in self.parts]
        return jnp.concatenate(kept, axis=1) + self.got.astype(F32)


class Early:
    def __init__(self, keep, send):
        got = swap(send, 0)
        self.first = [cube(keep[0]), cube(got[0])]
        self.second = [cube(keep[1]), cube(got[1])]

    def step(self, phase, late=None):
        if phase < 2:
            (at, bit), (at_other, bit_other) = (((0, 1), (3, 2)), ((2, 2), (0, 1)))[phase]
            sent = [half_sum(self.first, at), half_sum(self.second, at_other)]
            sent, late.parts = lax.optimization_barrier((sent, late.parts))
            self.first = half_left(self.first, at) + [swap(sent[0], bit)]
            self.second = half_left(self.second, at_other) + [swap(sent[1], bit_other)]
        else:
            if phase == 2:
                self.parts = [jnp.concatenate(pair, axis=3) for pair in zip(self.first, self.second)]
            self.parts = halve(self.parts, 3 - phase, phase + 1)

    def total(self):
        return sum(part.astype(F32) for part in self.parts)


def in_order(keep, send):
    both = jnp.stack([keep, send], axis=2)
    return jnp.moveaxis(both.reshape(both.shape[0], 4, *both.shape[3:]), 1, 2)


def scatter_sum(blocks):
    return lax.psum_scatter(
        blocks.astype(F32).reshape(-1, blocks.shape[3]), ("wide", "narrow"), scatter_dimension=0, tiled=True
    )


def sum_all(values):
    row = jnp.pad(jnp.stack(values)[None, :], ((0, 7), (0, 128 - len(values))))
    count = lax.axis_size("wide") * lax.axis_size("narrow")
    bit = 0
    while 1 << bit < count:
        masks = (1,) if bit == 0 or 2 << bit == count else (1, 2, 3)
        others = [lax.ppermute(row, ("wide", "narrow"), [(i, i ^ (mask << bit)) for i in range(count)]) for mask in masks]
        row = sum(others, row)
        bit += 1 if len(masks) == 1 else 2
    return row


def body(
    cond_fields,
    target,
    noise_draw,
    noise_sigma,
    grid_to_mesh,
    mesh_edges,
    mesh_to_grid,
    latitude_row,
    level_index,
    encoder,
    up_proj,
    down_proj,
    readout,
    encoder_moment,
    up_moment,
    down_moment,
    readout_moment,
    encoder_second,
    up_second,
    down_second,
    readout_second,
    encoder_average,
    up_average,
    down_average,
    readout_average,
):
    wide_index = lax.axis_index("wide")
    wide = lax.axis_size("wide")
    globe = lax.axis_index("narrow")
    nodes = mesh_edges.shape[0]
    pixels = cond_fields.shape[1]
    all_nodes = nodes * wide
    width = -(-pixels // 128) * 128

    place = jnp.stack([wide_index, globe]) if wide == 8 else jnp.zeros((2,), jnp.int32)
    early, late = pack(encoder, up_proj, down_proj.T, readout)
    moving = wide == 8
    tie = lax.optimization_barrier
    if moving:
        early_4 = swap(early, 4)

    if moving:
        early_1 = joined(early, early_4)
        late, early_1 = tie((late, early_1))
        late_4 = swap(late, 4)
        early_3 = swap(early_1, 3)
        early_1, target, noise_draw, noise_sigma = tie((early_1, target, noise_draw, noise_sigma))

    def own(array):
        return lax.dynamic_index_in_dim(jnp.transpose(array, (2, 0, 1)), globe, 1, keepdims=False)

    goal, noise = own(target), own(noise_draw)
    sigma = lax.dynamic_index_in_dim(noise_sigma, globe, 0, keepdims=False)
    square = sigma * sigma
    c_in = lax.rsqrt(square + 1.0)
    c_skip = 1.0 / (square + 1.0)
    c_out = sigma * c_in
    lam = (square + 1.0) / square
    if moving:
        early_3, late_4, goal, noise = tie((early_3, late_4, goal, noise))
        both, late_1 = joined(early_1, early_3), joined(late, late_4)
        first, second = both[..., :256], both[..., 256:]
        first, second, late_1, goal, noise = tie((first, second, late_1, goal, noise))
        first_2, second_2 = swap(first, 2), swap(second, 1)
        late_3 = swap(late_1, 3)
    noisy = goal + sigma * noise
    grid = jnp.concatenate([own(cond_fields), (c_in * noisy).astype(BF)], axis=0)
    grid = jnp.pad(grid, ((0, 0), (0, width - pixels)))
    edges = mesh_edges.T
    slot_rows = jnp.where(edges >= 0, (edges - wide_index * nodes + nodes + all_nodes) % all_nodes, -1)
    across = jnp.pad(mesh_to_grid.T - wide_index * nodes, ((0, 0), (0, width - pixels)), constant_values=-1)

    def halo(sums):
        low = sums.astype(BF)
        ring = [(i, (i + 1) % wide) for i in range(wide)]
        return lax.ppermute(low, "wide", ring), lax.ppermute(low, "wide", [(j, i) for i, j in ring])

    if moving:
        sums = grid_sums(grid, grid_to_mesh.T - wide_index * pixels)
        before, after = halo(sums)
        first_2, second_2, sums = tie((first_2, second_2, sums))
        first, second = joined(first, first_2), joined(second, second_2)
        first, second, late_3 = tie((first, second, late_3))
        first_1, second_1 = swap(first, 1), swap(second, 2)
        both = joined(late_1, late_3)
        parts = [both[..., : CUTS[0]], both[..., CUTS[0] :]]
        parts, slot_rows = tie((parts, slot_rows))
        got = [swap(parts[0], 2), swap(parts[1], 1)]
        bias, pool, pull = counts(slot_rows, across)
        bias, first_1, second_1, before, after, got = tie((bias, first_1, second_1, before, after, got))
        halves = [flat(first), first_1.reshape(8, LINES, 256), flat(second), second_1.reshape(8, LINES, 256)]
        others = [swap(half, 0) for half in halves]
        gathered = halves[:2] + others[:2] + halves[2:] + others[2:]
        parts = [joined(part, one) for part, one in zip(parts, got)]
        parts, sums = tie((parts, sums))
        got = [swap(parts[0], 1), swap(parts[1], 2)]
    else:
        gathered, late_full = gather_plain(early, late, wide)
        sums = grid_sums(grid, grid_to_mesh.T - wide_index * pixels)
        bias, pool, pull = counts(slot_rows, across)
        before, after = halo(sums)

    lat_weight = jnp.cos((latitude_row.astype(F32) - 90.0) * (math.pi / 180.0))
    level_weight = (level_index.astype(F32) + 1.0) / LEVELS
    pix_total = jnp.sum(lat_weight) * jnp.sum(level_weight)

    state0, rows, normed, query, pair, early_full = encode(place, gathered, before, sums, after)
    if moving:
        got, query = tie((got, query))
        late_full = []
        for part, one, cut in zip(parts, got, CUTS):
            halves = [flat(part), one.reshape(8, LINES, cut)]
            late_full += halves + [swap(half, 0) for half in halves]
    mixed, probs = attend(query, pair, bias)
    if moving:
        mixed, late_full = tie((mixed, late_full))
    keep_late, send_late, grad_state, grad_mixed, grad_dec, loss_part = feed(
        place, jnp.stack([c_skip, c_out, lam]),
        late_full, early_full, state0, mixed, pool, pull, noisy, goal, lat_weight[None, :], level_weight[:, None],
    )
    if moving:
        late_sum = Late(keep_late, send_late)
    first_heads = unmix(0, 1, probs, query, pair, grad_mixed)
    if moving:
        query, first_heads = late_sum.step(0, (query, first_heads))
    last_heads = unmix(1, 3, probs, query, pair, grad_mixed)
    if moving:
        grad_state, last_heads = late_sum.step(1, (grad_state, last_heads))
    keep_early, send_early = give_back(
        place, early_full, first_heads, last_heads, grad_state, rows, normed, before, sums, after, grad_dec
    )
    if moving:
        early_sum = Early(keep_early, send_early)
        early_sum.step(0, late_sum)
        late_sum.step(2)
        early_sum.step(1, late_sum)
        late_sum.last()
        early_sum.step(2)
        early_sum.step(3)
        share_late, share_early = late_sum.total(), early_sum.total()
    else:
        late_lines = jnp.concatenate(list(in_order(keep_late, send_late)), axis=3)
        early_lines = jnp.concatenate(list(in_order(keep_early, send_early)), axis=3)
        share_late = scatter_sum(from_rows(late_lines, wide))
        share_early = scatter_sum(early_from_lines(early_lines, wide))
    first_globe = (globe == 0).astype(F32)
    row = sum_all(
        [jnp.sum(share_early * share_early) + jnp.sum(share_late * share_late), loss_part[0, 0], pix_total * first_globe]
    )
    states = [
        (encoder, encoder_moment, encoder_second, encoder_average),
        (up_proj, up_moment, up_second, up_average),
        (down_proj.T, down_moment.T, down_second.T, down_average.T),
        (readout, readout_moment, readout_second, readout_average),
    ]
    news = list(adam(row, share_early, share_late, states))
    news[10:15] = [array.T for array in news[10:15]]
    return (news[20][0, 0], news[20][0, 1], *news[:20])


def solution(mesh):
    if mesh.shape["narrow"] != GROUPS or MB != GROUPS:
        raise ValueError("narrow size")
    by_pixel = P(None, "wide", None)
    pair = P("wide", "narrow")
    weights = (pair, pair, P("narrow", "wide"), P(("narrow", "wide"), None))
    placed = (by_pixel, by_pixel, by_pixel, P()) + (P("wide", None),) * 3 + (P("wide"), P()) + weights * 4
    given = (P(), P())
    for spec in weights:
        given = given + (spec,) * 5
    return jax.shard_map(body, mesh=mesh, in_specs=placed, out_specs=given, check_vma=False)
```

time: 279 us -> 216 us (0.77)
  waiting for transfers between devices: 85.8 us -> 39.3 us
  between operations: 23.3 us -> 6.6 us
  starting transfers between devices: 44.2 us -> 53.5 us
  other arithmetic: 19.7 us -> 12.6 us
    all_gather x1 -> x0, waiting for transfers between devices: 27.1 us -> none  [gather_weights(): full = lax.all_gather(both, ('wide', 'narrow'), axis=0, tiled=False)]
    ppermute x31 -> x38, waiting for transfers between devices: 41.7 us -> 27.9 us  [swap(): lax.ppermute(array, ('wide', 'narrow'), [(i, i ^ 1 << bit) for i in range...]
    pallas_call x1, Pallas kernels: 23.6 us -> 11.6 us  [give_back(): pl.pallas_call(return_kernel, in_specs=[pl.BlockSpec(memory_space=pltpu.S...]
    pallas_call x2 -> x8, Pallas kernels: 32.8 us -> 43.4 us  [the longest x2 14.2 us: unmix(): pl.pallas_call(unmix_kernel, grid=(heads,), in_specs=[pl.BlockSpec((1, 2,...]
    unnamed x73 -> x116, local copies, waits for them, and re-layouts: 4.2 us -> 11.7 us
    ppermute x2 -> x9, starting transfers between devices: 6.01 us -> 13 us  [the longest x7 8.55 us: sum_all(): lax.ppermute(row, ('wide', 'narrow'), [(i, i ^ mask << bit) for i in rang...]
    ppermute x2 -> x9, waiting for transfers between devices: 16.9 us -> 11.4 us  [the longest x7 8.16 us: sum_all(): lax.ppermute(row, ('wide', 'narrow'), [(i, i ^ mask << bit) for i in rang...]
    convert_element_type x29 -> x13, other arithmetic: 9.88 us -> 5.71 us  [the longest x11 4.28 us: half_sum(): sum((lax.index_in_dim(part, 1, axis, keepdims=False).astype(F32) for part...]
  transfers between devices with their start and end apart: 34 -> 47, of which waited for: 23 -> 23; matrix products, arithmetic and copies ran while one was open for 6% -> 9% of each run, Pallas kernels for 5% -> 19%
where the time goes in v2:
time: 216 us; the launch traced here: 215 us
  Pallas kernels  76.9 us (36%)
  starting transfers between devices  53.5 us (25%)
  waiting for transfers between devices  39.3 us (18%)
  local copies, waits for them, and re-layouts  26.5 us (12%)
  other arithmetic  12.6 us (6%)
  between operations  6.6 us (3%)
    ppermute x38, starting transfers between devices, swap(): lax.ppermute(array, ('wide', 'narrow'), [(i, i ^ 1 << bit) for i in range...  40.6 us
    ppermute x38, waiting for transfers between devices, swap(): lax.ppermute(array, ('wide', 'narrow'), [(i, i ^ 1 << bit) for i in range...  27.9 us
    pallas_call x1, Pallas kernels, feed(): pl.pallas_call(feed_kernel, in_specs=[pl.BlockSpec(memory_space=pltpu.SME...  21.8 us
    pallas_call x2, Pallas kernels, unmix(): pl.pallas_call(unmix_kernel, grid=(heads,), in_specs=[pl.BlockSpec((1, 2,...  14.2 us
    unnamed x116, local copies, waits for them, and re-layouts  11.7 us
    pallas_call x1, Pallas kernels, give_back(): pl.pallas_call(return_kernel, in_specs=[pl.BlockSpec(memory_space=pltpu.S...  11.6 us
    pallas_call x1, Pallas kernels, attend(): pl.pallas_call(attend_kernel, in_specs=[outside] * 3, out_specs=[outside]...  11.1 us
    ppermute x7, starting transfers between devices, sum_all(): lax.ppermute(row, ('wide', 'narrow'), [(i, i ^ mask << bit) for i in rang...  8.55 us
  transfers between devices with their start and end apart: 47, of which 23 were waited for; matrix products, arithmetic and copies ran while one was open for 9% of the time, Pallas kernels for 19%

profile of v2, /device:TPU:0, one launch (start us, length us, event | category | flops | bytes accessed | tf_op | source)
XLA Modules:
  0.0 215.5 jit_solution(13111633029021785748)
XLA Ops:
  4.1 4.1 %collective-permute-start = (bf16[64,512]{1,0:T(8,128)(2,1)S(1)}, bf16[64,512]{1,0:T(8,128)(2,1)S(1)}, u32[]{:S(2)}, u32[]{:S(2)}) collective-permute-start(bf16[64,512]{1,0:T(8,128)(2,1)S(1)} %get-tuple-element.161), channel_id=1, source_target_pairs={{0,16},{1,17},{2,18},{3,19},{4,20},{5,21},{6,22},{7,23},{8,24},{9,... | collective-permute-start | bytes 196616 | tf_op jit(solution)/shard_map/ppermute | solution.py:850
  9.7 2.1 collective-permute-done
  12.5 3.4 %collective-permute-start.2 = (bf16[64,1152]{1,0:T(8,128)(2,1)S(1)}, bf16[64,1152]{1,0:T(8,128)(2,1)S(1)}, u32[]{:S(2)}, u32[]{:S(2)}) collective-permute-start(bf16[64,1152]{1,0:T(8,128)(2,1)S(1)} %get-tuple-element.164), channel_id=1, source_target_pairs={{0,16},{1,17},{2,18},{3,19},{4,20},{5,21},{6,22},{7,23},{8,24},{9,... | collective-permute-start | bytes 442376 | tf_op jit(solution)/shard_map/ppermute | solution.py:850
  18.6 1.4 copy.54
  20.1 2.4 %collective-permute-done.2 = bf16[64,1152]{1,0:T(8,128)(2,1)S(1)} collective-permute-done((bf16[64,1152]{1,0:T(8,128)(2,1)S(1)}, bf16[64,1152]{1,0:T(8,128)(2,1)S(1)}, u32[]{:S(2)}, u32[]{:S(2)}) %collective-permute-start.2) | collective-permute-done | bytes 147488 | tf_op jit(solution)/shard_map/ppermute | solution.py:850
  22.5 1.6 collective-permute-start.3
  24.1 1.5 collective-permute-start.4
  25.6 1.4 multiply_convert_fusion
  27.1 2.4 %grid_sums.1.sums_ref = f32[256,512]{1,0:T(8,128)S(1)} custom-call(bf16[256,896]{1,0:T(8,128)(2,1)S(1)} %fusion.2.grid_ref, s32[8,512]{1,0:T(8,128)S(1)} %subtract_bitcast_fusion.pixels_ref), custom_call_target="tpu_custom_call" | custom-call | flops 240000000 | bytes 1000000 | tf_op jit(solution)/shard_map/grid_sums/pallas_call | solution.py:100
  29.6 2.4 %collective-permute-start.9 = (bf16[256,512]{1,0:T(8,128)(2,1)S(1)}, bf16[256,512]{1,0:T(8,128)(2,1)S(1)}, u32[]{:S(2)}, u32[]{:S(2)}) collective-permute-start(bf16[256,512]{1,0:T(8,128)(2,1)S(1)} %convert_element_type.438), channel_id=1, source_target_pairs={{4,0},{8,4},{12,8},{16,12},{20,16},{24,20},{28,24},{0,28},{5,1},{9... | collective-permute-start | bytes 786440 | tf_op jit(solution)/shard_map/ppermute | solution.py:1019
  32.1 2.2 %collective-permute-done.5 = bf16[2,64,1152]{2,1,0:T(8,128)(2,1)S(1)} collective-permute-done((bf16[2,64,1152]{2,1,0:T(8,128)(2,1)S(1)}, bf16[2,64,1152]{2,1,0:T(8,128)(2,1)S(1)}, u32[]{:S(2)}, u32[]{:S(2)}) %collective-permute-start.5) | collective-permute-done | bytes 294944 | tf_op jit(solution)/shard_map/ppermute | solution.py:850
  34.4 2.0 collective-permute-start.8
  37.0 1.5 collective-permute-start.6
  38.5 3.2 %collective-permute-done.9.after_ref = bf16[256,512]{1,0:T(8,128)(2,1)S(1)} collective-permute-done((bf16[256,512]{1,0:T(8,128)(2,1)S(1)}, bf16[256,512]{1,0:T(8,128)(2,1)S(1)}, u32[]{:S(2)}, u32[]{:S(2)}) %collective-permute-start.9) | collective-permute-done | bytes 262176 | tf_op jit(solution)/shard_map/ppermute | solution.py:1019
  42.4 6.0 %counts.1 = (f32[2,1280,256]{2,1,0:T(8,128)S(1)}, bf16[896,512]{1,0:T(8,128)(2,1)S(1)}, bf16[512,896]{1,0:T(8,128)(2,1)S(1)}) custom-call(s32[16,512]{1,0:T(8,128)S(1)} %fusion.26.slots_ref, s32[3,896]{1,0:T(4,128)S(1)} %pad.13.across_ref), custom_call_target="tpu_custom_call" | custom-call | flops 60000000 | bytes 5000000 | tf_op jit(solution)/shard_map/counts/pallas_call | solution.py:143
  48.5 1.5 copy-done.23
  51.4 2.9 %collective-permute-done.7 = bf16[2,2,2,64,256]{4,3,2,1,0:T(8,128)(2,1)S(1)} collective-permute-done((bf16[2,2,2,64,256]{4,3,2,1,0:T(8,128)(2,1)S(1)}, bf16[2,2,2,64,256]{4,3,2,1,0:T(8,128)(2,1)S(1)}, u32[]{:S(2)}, u32[]{:S(2)}) %collective-permute-start.7) | collective-permute-done | bytes 262176 | tf_op jit(solution)/shard_map/ppermute | solution.py:850
  55.6 2.1 collective-permute-start.17
  59.8 8.0 %encode.1 = (f32[512,512]{1,0:T(8,128)}, bf16[1536,512]{1,0:T(8,128)(2,1)}, bf16[1536,512]{1,0:T(8,128)(2,1)}, bf16[512,512]{1,0:T(8,128)(2,1)}, bf16[1536,1024]...) custom-call(s32[2]{0:T(128)} %pad_add_fusion.1.place_ref, bf16[8,64,256]{2,1,0:T(8,128)(2,1)} %bitcast.296, ...), custom_call_target="tpu_custom_call" | custom-call | flops 5000000000 | bytes 12000000 | tf_op jit(solution)/shard_map/encode/pallas_call | solution.py:260
  67.8 1.9 collective-permute-done.17
  69.7 2.1 collective-permute-done.16
  76.2 11.1 %attend.1 = (bf16[512,512]{1,0:T(8,128)(2,1)}, bf16[4,2,1280,256]{3,2,1,0:T(8,128)(2,1)}) custom-call(bf16[512,512]{1,0:T(8,128)(2,1)} %get-tuple-element.227.query_in.query_ref, bf16[1536,1024]{1,0:T(8,128)(2,1)} %get-tuple-element.199.pair_in.keys_ref.values_ref, f32[2,1280,256]{2,1,0:T(8,128)} %copy-done.23), custom_call_target="tpu_custom_call" | custom-call | flops 3000000000 | bytes 12000000 | tf_op jit(solution)/shard_map/attend/pallas_call | solution.py:337
  88.5 21.8 %feed.1 = (bf16[3,2,8,64,384]{4,3,2,1,0:T(8,128)(2,1)}, bf16[3,2,8,64,384]{4,3,2,1,0:T(8,128)(2,1)}, f32[512,512]{1,0:T(8,128)}, bf16[512,512]{1,0:T(8,128)(2,1)}, f32[128,512]{1,0:T(8,128)}, /*index=5*/f32[8,128]{1,0:T(8,128)}) custom-call(s32[2]{0:T(128)} %pad_add_fusion.1.place_ref, f32[3]{0:T(128)} %pad_maximum_fusion.12.scalars_ref, ...), custom_call_target="tpu_custom_call" | custom-call | flops 8999999488 | bytes 20000000 | tf_op jit(solution)/shard_map/feed/pallas_call | solution.py:492
  112.1 1.2 slice.565
  115.7 1.5 fusion.31
  118.2 4.7 %unmix.2 = (bf16[512,128]{1,0:T(8,128)(2,1)}, bf16[1536,256]{1,0:T(8,128)(2,1)}) custom-call(bf16[4,2,1280,256]{3,2,1,0:T(8,128)(2,1)} %get-tuple-element.218.probs_ref, bf16[512,512]{1,0:T(8,128)(2,1)} %get-tuple-element.227.query_in.query_ref, bf16[1536,1024]{1,0:T(8,128)(2,1)} %get-tuple-element.199.pair_in.keys_ref.values_ref, ...), custom_call_target="tpu_custom_call" | custom-call | flops 1000000000 | bytes 3000000 | tf_op jit(solution)/shard_map/unmix/pallas_call | solution.py:565
  130.3 2.1 collective-permute-start.24
  133.5 9.4 %unmix.3 = (bf16[512,384]{1,0:T(8,128)(2,1)}, bf16[1536,768]{1,0:T(8,128)(2,1)}) custom-call(bf16[4,2,1280,256]{3,2,1,0:T(8,128)(2,1)} %get-tuple-element.218.probs_ref, bf16[512,512]{1,0:T(8,128)(2,1)} %get-tuple-element.227.query_in.query_ref, bf16[1536,1024]{1,0:T(8,128)(2,1)} %get-tuple-element.199.pair_in.keys_ref.values_ref, ...), custom_call_target="tpu_custom_call" | custom-call | flops 3000000000 | bytes 9000000 | tf_op jit(solution)/shard_map/unmix/pallas_call | solution.py:565
  143.3 11.6 %give_back.1 = (bf16[2,2,8,64,256]{4,3,2,1,0:T(8,128)(2,1)}, bf16[2,2,8,64,256]{4,3,2,1,0:T(8,128)(2,1)}) custom-call(s32[2]{0:T(128)} %pad_add_fusion.1.place_ref, bf16[8,4,64,512]{3,2,1,0:T(8,128)(2,1)} %get-tuple-element.194.early_ref, bf16[512,128]{1,0:T(8,128)(2,1)} %get-tuple-element.222.query_in_a, bf16[512,384]{1,0:T(8,128)(2,1)} %get-tuple-element.230.query_in_b, ...), custom_call_target="tpu_custom_call" | custom-call | flops 5000000000 | bytes 12000000 | tf_op jit(solution)/shard_map/give_back/pallas_call | solution.py:678
  158.6 1.5 collective-permute-start.29
  160.2 2.7 %collective-permute-done.26 = bf16[2,2,8,64,256]{4,3,2,1,0:T(8,128)(2,1)S(1)} collective-permute-done((bf16[2,2,8,64,256]{4,3,2,1,0:T(8,128)(2,1)}, bf16[2,2,8,64,256]{4,3,2,1,0:T(8,128)(2,1)S(1)}, u32[]{:S(2)}, u32[]{:S(2)}) %collective-permute-start.26) | collective-permute-done | bytes 1048608 | tf_op jit(solution)/shard_map/ppermute | solution.py:850
  165.1 1.2 collective-permute-start.30
  166.3 1.6 collective-permute-start.31
  170.4 3.9 %collective-permute-done.30 = bf16[2,2,2,64,256]{4,3,1,0,2:T(8,128)(2,1)S(1)} collective-permute-done((bf16[2,2,2,64,256]{4,3,1,0,2:T(8,128)(2,1)S(1)}, bf16[2,2,2,64,256]{4,3,1,0,2:T(8,128)(2,1)S(1)}, u32[]{:S(2)}, u32[]{:S(2)}) %collective-permute-start.30) | collective-permute-done | bytes 262176 | tf_op jit(solution)/shard_map/ppermute | solution.py:850
  176.0 1.5 collective-permute-start.35
  177.5 1.5 collective-permute-start.36
  179.4 1.5 collective-permute-done.35
  181.0 1.5 collective-permute-done.36
  183.6 3.0 %collective-permute-start.39 = (bf16[64,1152]{1,0:T(8,128)(2,1)S(1)}, bf16[64,1152]{1,0:T(8,128)(2,1)S(1)}, u32[]{:S(2)}, u32[]{:S(2)}) collective-permute-start(bf16[64,1152]{1,0:T(8,128)(2,1)S(1)} %pad_maximum_fusion.6), channel_id=1, source_target_pairs={{0,16},{1,17},{2,18},{3,19},{4,20},{5,21},{6,22},{7,23},{8,24},{9,... | collective-permute-start | bytes 442376 | tf_op jit(solution)/shard_map/ppermute | solution.py:850
  186.6 1.4 collective-permute-done.37
  188.1 3.3 %collective-permute-start.38 = (bf16[64,512]{1,0:T(8,128)(2,1)S(1)}, bf16[64,512]{1,0:T(8,128)(2,1)S(1)}, u32[]{:S(2)}, u32[]{:S(2)}) collective-permute-start(bf16[64,512]{1,0:T(8,128)(2,1)S(1)} %fusion.17), channel_id=1, source_target_pairs={{0,16},{1,17},{2,18},{3,19},{4,20},{5,21},{6,22},{7,23},{8,24},{9,... | collective-permute-start | bytes 196616 | tf_op jit(solution)/shard_map/ppermute | solution.py:850
  191.4 1.6 collective-permute-done.39
  196.3 1.2 collective-permute-done.40
  197.7 2.8 %collective-permute-start.43 = (f32[8,128]{1,0:T(8,128)S(1)}, f32[8,128]{1,0:T(8,128)S(1)}, u32[]{:S(2)}, u32[]{:S(2)}) collective-permute-start(f32[8,128]{1,0:T(8,128)S(1)} %pad_add_fusion), channel_id=1, source_target_pairs={{0,6},{1,7},{2,4},{3,5},{4,2},{5,3},{6,0},{7,1},{8,14},{9,15},{10,... | collective-permute-start | bytes 12296 | tf_op jit(solution)/shard_map/ppermute | solution.py:937
  202.2 1.9 collective-permute-done.41
  204.1 4.4 %collective-permute-start.46 = (f32[8,128]{1,0:T(8,128)S(1)}, f32[8,128]{1,0:T(8,128)S(1)}, u32[]{:S(2)}, u32[]{:S(2)}) collective-permute-start(f32[8,128]{1,0:T(8,128)S(1)} %add_add_fusion.1), channel_id=1, source_target_pairs={{0,24},{1,25},{2,26},{3,27},{4,28},{5,29},{6,30},{7,31},{8,16},{9,... | collective-permute-start | bytes 12296 | tf_op jit(solution)/shard_map/ppermute | solution.py:937
  210.1 2.9 %collective-permute-done.45 = f32[8,128]{1,0:T(8,128)S(1)} collective-permute-done((f32[8,128]{1,0:T(8,128)S(1)}, f32[8,128]{1,0:T(8,128)S(1)}, u32[]{:S(2)}, u32[]{:S(2)}) %collective-permute-start.45) | collective-permute-done | bytes 4128 | tf_op jit(solution)/shard_map/ppermute | solution.py:937
  213.2 1.6 adam.1
  (267 shorter events, 48.3 us)
Async XLA Ops:
  4.1 7.8 %collective-permute-start = (bf16[64,512]{1,0:T(8,128)(2,1)S(1)}, bf16[64,512]{1,0:T(8,128)(2,1)S(1)}, u32[]{:S(2)}, u32[]{:S(2)}) collective-permute-start(bf16[64,512]{1,0:T(8,128)(2,1)S(1)} %get-tuple-element.161), channel_id=1, source_target_pairs={{0,16},{1,17},{2,18},{3,19},{4,20},{5,21},{6,22},{7,23},{8,24},{9,... | collective-permute-start | bytes 196616 | tf_op jit(solution)/shard_map/ppermute | solution.py:850
  11.9 8.2 %collective-permute-start.1 = (bf16[2,64,512]{2,1,0:T(8,128)(2,1)S(1)}, bf16[2,64,512]{2,1,0:T(8,128)(2,1)S(1)}, u32[]{:S(2)}, u32[]{:S(2)}) collective-permute-start(bf16[2,64,512]{2,1,0:T(8,128)(2,1)S(1)} %pad_maximum_fusion.8), channel_id=1, source_target_pairs={{0,8},{1,9},{2,10},{3,11},{4,12},{5,13},{6,14},{7,15},{8,0},{9,1},... | collective-permute-start | bytes 393224 | tf_op jit(solution)/shard_map/ppermute | solution.py:850
  12.5 10.0 %collective-permute-start.2 = (bf16[64,1152]{1,0:T(8,128)(2,1)S(1)}, bf16[64,1152]{1,0:T(8,128)(2,1)S(1)}, u32[]{:S(2)}, u32[]{:S(2)}) collective-permute-start(bf16[64,1152]{1,0:T(8,128)(2,1)S(1)} %get-tuple-element.164), channel_id=1, source_target_pairs={{0,16},{1,17},{2,18},{3,19},{4,20},{5,21},{6,22},{7,23},{8,24},{9,... | collective-permute-start | bytes 442376 | tf_op jit(solution)/shard_map/ppermute | solution.py:850
  22.5 9.5 %collective-permute-start.3 = (bf16[2,2,64,256]{3,2,1,0:T(8,128)(2,1)S(1)}, bf16[2,2,64,256]{3,2,1,0:T(8,128)(2,1)S(1)}, u32[]{:S(2)}, u32[]{:S(2)}) collective-permute-start(bf16[2,2,64,256]{3,2,1,0:T(8,128)(2,1)S(1)} %get-tuple-element.171), channel_id=1, source_target_pairs={{0,4},{1,5},{2,6},{3,7},{4,0},{5,1},{6,2},{7,3},{8,12},{9,13},{10,... | collective-permute-start | bytes 393224 | tf_op jit(solution)/shard_map/ppermute | solution.py:850
  24.1 7.9 %collective-permute-start.4 = (bf16[2,2,64,256]{3,2,1,0:T(8,128)(2,1)S(1)}, bf16[2,2,64,256]{3,2,1,0:T(8,128)(2,1)S(1)}, u32[]{:S(2)}, u32[]{:S(2)}) collective-permute-start(bf16[2,2,64,256]{3,2,1,0:T(8,128)(2,1)S(1)} %get-tuple-element.172), channel_id=1, source_target_pairs={{0,2},{1,3},{2,0},{3,1},{4,6},{5,7},{6,4},{7,5},{8,10},{9,11},{10,... | collective-permute-start | bytes 393224 | tf_op jit(solution)/shard_map/ppermute | solution.py:850
  25.6 8.7 %collective-permute-start.5 = (bf16[2,64,1152]{2,1,0:T(8,128)(2,1)S(1)}, bf16[2,64,1152]{2,1,0:T(8,128)(2,1)S(1)}, u32[]{:S(2)}, u32[]{:S(2)}) collective-permute-start(bf16[2,64,1152]{2,1,0:T(8,128)(2,1)S(1)} %pad_maximum_fusion.2), channel_id=1, source_target_pairs={{0,8},{1,9},{2,10},{3,11},{4,12},{5,13},{6,14},{7,15},{8,0},{9,1},... | collective-permute-start | bytes 884744 | tf_op jit(solution)/shard_map/ppermute | solution.py:850
  29.6 12.1 %collective-permute-start.9 = (bf16[256,512]{1,0:T(8,128)(2,1)S(1)}, bf16[256,512]{1,0:T(8,128)(2,1)S(1)}, u32[]{:S(2)}, u32[]{:S(2)}) collective-permute-start(bf16[256,512]{1,0:T(8,128)(2,1)S(1)} %convert_element_type.438), channel_id=1, source_target_pairs={{4,0},{8,4},{12,8},{16,12},{20,16},{24,20},{28,24},{0,28},{5,1},{9... | collective-permute-start | bytes 786440 | tf_op jit(solution)/shard_map/ppermute | solution.py:1019
  34.4 19.9 %collective-permute-start.10 = (bf16[2,2,64,640]{3,2,1,0:T(8,128)(2,1)S(1)}, bf16[2,2,64,640]{3,2,1,0:T(8,128)(2,1)S(1)}, u32[]{:S(2)}, u32[]{:S(2)}) collective-permute-start(bf16[2,2,64,640]{3,2,1,0:T(8,128)(2,1)S(1)} %fusion.6), channel_id=1, source_target_pairs={{0,4},{1,5},{2,6},{3,7},{4,0},{5,1},{6,2},{7,3},{8,12},{9,13},{10,... | collective-permute-start | bytes 983048 | tf_op jit(solution)/shard_map/ppermute | solution.py:850
  34.4 16.5 %collective-permute-start.8 = (bf16[256,512]{1,0:T(8,128)(2,1)S(1)}, bf16[256,512]{1,0:T(8,128)(2,1)S(1)}, u32[]{:S(2)}, u32[]{:S(2)}) collective-permute-start(bf16[256,512]{1,0:T(8,128)(2,1)S(1)} %convert_element_type.438), channel_id=1, source_target_pairs={{0,4},{4,8},{8,12},{12,16},{16,20},{20,24},{24,28},{28,0},{1,5},{5... | collective-permute-start | bytes 786440 | tf_op jit(solution)/shard_map/ppermute | solution.py:1019
  36.4 14.5 %collective-permute-start.11 = (bf16[2,2,64,512]{3,2,1,0:T(8,128)(2,1)S(1)}, bf16[2,2,64,512]{3,2,1,0:T(8,128)(2,1)S(1)}, u32[]{:S(2)}, u32[]{:S(2)}) collective-permute-start(bf16[2,2,64,512]{3,2,1,0:T(8,128)(2,1)S(1)} %pad_maximum_fusion.3), channel_id=1, source_target_pairs={{0,2},{1,3},{2,0},{3,1},{4,6},{5,7},{6,4},{7,5},{8,10},{9,11},{10,... | collective-permute-start | bytes 786440 | tf_op jit(solution)/shard_map/ppermute | solution.py:850
  37.0 14.4 %collective-permute-start.6 = (bf16[2,2,2,64,256]{4,3,2,1,0:T(8,128)(2,1)S(1)}, bf16[2,2,2,64,256]{4,3,2,1,0:T(8,128)(2,1)S(1)}, u32[]{:S(2)}, u32[]{:S(2)}) collective-permute-start(bf16[2,2,2,64,256]{4,3,2,1,0:T(8,128)(2,1)S(1)} %pad_maximum_fusion.4), channel_id=1, source_target_pairs={{0,2},{1,3},{2,0},{3,1},{4,6},{5,7},{6,4},{7,5},{8,10},{9,11},{10,... | collective-permute-start | bytes 786440 | tf_op jit(solution)/shard_map/ppermute | solution.py:850
  41.7 12.6 %collective-permute-start.7 = (bf16[2,2,2,64,256]{4,3,2,1,0:T(8,128)(2,1)S(1)}, bf16[2,2,2,64,256]{4,3,2,1,0:T(8,128)(2,1)S(1)}, u32[]{:S(2)}, u32[]{:S(2)}) collective-permute-start(bf16[2,2,2,64,256]{4,3,2,1,0:T(8,128)(2,1)S(1)} %pad_maximum_fusion.5), channel_id=1, source_target_pairs={{0,4},{1,5},{2,6},{3,7},{4,0},{5,1},{6,2},{7,3},{8,12},{9,13},{10,... | collective-permute-start | bytes 786440 | tf_op jit(solution)/shard_map/ppermute | solution.py:850
  50.9 4.7 %collective-permute-start.12 = (bf16[8,64,256]{2,1,0:T(8,128)(2,1)S(1)}, bf16[8,64,256]{2,1,0:T(8,128)(2,1)S(1)}, u32[]{:S(2)}, u32[]{:S(2)}) collective-permute-start(bf16[8,64,256]{2,1,0:T(8,128)(2,1)S(1)} %bitcast.295), channel_id=1, source_target_pairs={{0,1},{1,0},{2,3},{3,2},{4,5},{5,4},{6,7},{7,6},{8,9},{9,8},{10,11... | collective-permute-start | bytes 786440 | tf_op jit(solution)/shard_map/ppermute | solution.py:850
  50.9 7.4 %collective-permute-start.14 = (bf16[8,64,256]{2,1,0:T(8,128)(2,1)S(1)}, bf16[8,64,256]{2,1,0:T(8,128)(2,1)S(1)}, u32[]{:S(2)}, u32[]{:S(2)}) collective-permute-start(bf16[8,64,256]{2,1,0:T(8,128)(2,1)S(1)} %bitcast.297), channel_id=1, source_target_pairs={{0,1},{1,0},{2,3},{3,2},{4,5},{5,4},{6,7},{7,6},{8,9},{9,8},{10,11... | collective-permute-start | bytes 786440 | tf_op jit(solution)/shard_map/ppermute | solution.py:850
  54.3 4.1 %collective-permute-start.15 = (bf16[8,64,256]{2,1,0:T(8,128)(2,1)S(1)}, bf16[8,64,256]{2,1,0:T(8,128)(2,1)S(1)}, u32[]{:S(2)}, u32[]{:S(2)}) collective-permute-start(bf16[8,64,256]{2,1,0:T(8,128)(2,1)S(1)} %bitcast.309), channel_id=1, source_target_pairs={{0,1},{1,0},{2,3},{3,2},{4,5},{5,4},{6,7},{7,6},{8,9},{9,8},{10,11... | collective-permute-start | bytes 786440 | tf_op jit(solution)/shard_map/ppermute | solution.py:850
  54.3 5.5 %collective-permute-start.13 = (bf16[8,64,256]{2,1,0:T(8,128)(2,1)S(1)}, bf16[8,64,256]{2,1,0:T(8,128)(2,1)}, u32[]{:S(2)}, u32[]{:S(2)}) collective-permute-start(bf16[8,64,256]{2,1,0:T(8,128)(2,1)S(1)} %bitcast.307), channel_id=1, source_target_pairs={{0,1},{1,0},{2,3},{3,2},{4,5},{5,4},{6,7},{7,6},{8,9},{9,8},{10,11... | collective-permute-start | bytes 786440 | tf_op jit(solution)/shard_map/ppermute | solution.py:850
  55.0 16.8 %collective-permute-start.16 = (bf16[2,2,2,64,640]{4,3,2,1,0:T(8,128)(2,1)S(1)}, bf16[2,2,2,64,640]{4,3,2,1,0:T(8,128)(2,1)S(1)}, u32[]{:S(2)}, u32[]{:S(2)}) collective-permute-start(bf16[2,2,2,64,640]{4,3,2,1,0:T(8,128)(2,1)S(1)} %pad_maximum_fusion), channel_id=1, source_target_pairs={{0,2},{1,3},{2,0},{3,1},{4,6},{5,7},{6,4},{7,5},{8,10},{9,11},{10,... | collective-permute-start | bytes 1966088 | tf_op jit(solution)/shard_map/ppermute | solution.py:850
  55.6 14.1 %collective-permute-start.17 = (bf16[2,2,2,64,512]{4,3,2,1,0:T(8,128)(2,1)S(1)}, bf16[2,2,2,64,512]{4,3,2,1,0:T(8,128)(2,1)}, u32[]{:S(2)}, u32[]{:S(2)}) collective-permute-start(bf16[2,2,2,64,512]{4,3,2,1,0:T(8,128)(2,1)S(1)} %pad_maximum_fusion.1), channel_id=1, source_target_pairs={{0,4},{1,5},{2,6},{3,7},{4,0},{5,1},{6,2},{7,3},{8,12},{9,13},{10,... | collective-permute-start | bytes 1572872 | tf_op jit(solution)/shard_map/ppermute | solution.py:850
  58.3 29.0 %collective-permute-start.18 = (bf16[8,64,640]{2,1,0:T(8,128)(2,1)S(1)}, bf16[8,64,640]{2,1,0:T(8,128)(2,1)S(1)}, u32[]{:S(2)}, u32[]{:S(2)}) collective-permute-start(bf16[8,64,640]{2,1,0:T(8,128)(2,1)S(1)} %bitcast.287), channel_id=1, source_target_pairs={{0,1},{1,0},{2,3},{3,2},{4,5},{5,4},{6,7},{7,6},{8,9},{9,8},{10,11... | collective-permute-start | bytes 1966088 | tf_op jit(solution)/shard_map/ppermute | solution.py:850
  71.8 15.6 %collective-permute-start.19 = (bf16[8,64,640]{2,1,0:T(8,128)(2,1)S(1)}, bf16[8,64,640]{2,1,0:T(8,128)(2,1)S(1)}, u32[]{:S(2)}, u32[]{:S(2)}) collective-permute-start(bf16[8,64,640]{2,1,0:T(8,128)(2,1)S(1)} %bitcast.305), channel_id=1, source_target_pairs={{0,1},{1,0},{2,3},{3,2},{4,5},{5,4},{6,7},{7,6},{8,9},{9,8},{10,11... | collective-permute-start | bytes 1966088 | tf_op jit(solution)/shard_map/ppermute | solution.py:850
  73.1 14.3 %collective-permute-start.20 = (bf16[8,64,512]{2,1,0:T(8,128)(2,1)S(1)}, bf16[8,64,512]{2,1,0:T(8,128)(2,1)}, u32[]{:S(2)}, u32[]{:S(2)}) collective-permute-start(bf16[8,64,512]{2,1,0:T(8,128)(2,1)S(1)} %bitcast.289), channel_id=1, source_target_pairs={{0,1},{1,0},{2,3},{3,2},{4,5},{5,4},{6,7},{7,6},{8,9},{9,8},{10,11... | collective-permute-start | bytes 1572872 | tf_op jit(solution)/shard_map/ppermute | solution.py:850
  73.5 13.9 %collective-permute-start.21 = (bf16[8,64,512]{2,1,0:T(8,128)(2,1)}, bf16[8,64,512]{2,1,0:T(8,128)(2,1)}, u32[]{:S(2)}, u32[]{:S(2)}) collective-permute-start(bf16[8,64,512]{2,1,0:T(8,128)(2,1)} %bitcast.40.b_1), channel_id=1, source_target_pairs={{0,1},{1,0},{2,3},{3,2},{4,5},{5,4},{6,7},{7,6},{8,9},{9,8},{10,11... | collective-permute-start | bytes 1572872 | tf_op jit(solution)/shard_map/ppermute | solution.py:850
  110.3 13.3 %collective-permute-start.22 = (bf16[3,2,8,64,384]{4,3,2,1,0:T(8,128)(2,1)}, bf16[3,2,8,64,384]{4,3,2,1,0:T(8,128)(2,1)S(1)}, u32[]{:S(2)}, u32[]{:S(2)}) collective-permute-start(bf16[3,2,8,64,384]{4,3,2,1,0:T(8,128)(2,1)} %get-tuple-element.217), channel_id=1, source_target_pairs={{0,1},{1,0},{2,3},{3,2},{4,5},{5,4},{6,7},{7,6},{8,9},{9,8},{10,11... | collective-permute-start | bytes 7077896 | tf_op jit(solution)/shard_map/ppermute | solution.py:850
  129.7 13.4 %collective-permute-start.23 = (bf16[2,2,2,64,384]{4,3,0,1,2:T(8,128)(2,1)S(1)}, bf16[2,2,2,64,384]{4,3,0,1,2:T(8,128)(2,1)S(1)}, u32[]{:S(2)}, u32[]{:S(2)}) collective-permute-start(bf16[2,2,2,64,384]{4,3,0,1,2:T(8,128)(2,1)S(1)} %copy.63), channel_id=1, source_target_pairs={{0,2},{1,3},{2,0},{3,1},{4,6},{5,7},{6,4},{7,5},{8,10},{9,11},{10,... | collective-permute-start | bytes 1179656 | tf_op jit(solution)/shard_map/ppermute | solution.py:850
  130.3 12.7 %collective-permute-start.24 = (bf16[2,2,2,64,384]{4,3,1,0,2:T(8,128)(2,1)}, bf16[2,2,2,64,384]{4,3,1,0,2:T(8,128)(2,1)S(1)}, u32[]{:S(2)}, u32[]{:S(2)}) collective-permute-start(bf16[2,2,2,64,384]{4,3,1,0,2:T(8,128)(2,1)} %fusion.3), channel_id=1, source_target_pairs={{0,4},{1,5},{2,6},{3,7},{4,0},{5,1},{6,2},{7,3},{8,12},{9,13},{10,... | collective-permute-start | bytes 1179656 | tf_op jit(solution)/shard_map/ppermute | solution.py:850
  132.4 10.7 %collective-permute-start.25 = (bf16[2,2,2,64,384]{4,3,1,2,0:T(8,128)(2,1)}, bf16[2,2,2,64,384]{4,3,1,2,0:T(8,128)(2,1)S(1)}, u32[]{:S(2)}, u32[]{:S(2)}) collective-permute-start(bf16[2,2,2,64,384]{4,3,1,2,0:T(8,128)(2,1)} %fusion.4), channel_id=1, source_target_pairs={{0,8},{1,9},{2,10},{3,11},{4,12},{5,13},{6,14},{7,15},{8,0},{9,1},... | collective-permute-start | bytes 1179656 | tf_op jit(solution)/shard_map/ppermute | solution.py:850
  157.0 7.1 %collective-permute-start.27 = (bf16[2,2,64,384]{3,2,0,1:T(8,128)(2,1)S(1)}, bf16[2,2,64,384]{3,2,0,1:T(8,128)(2,1)S(1)}, u32[]{:S(2)}, u32[]{:S(2)}) collective-permute-start(bf16[2,2,64,384]{3,2,0,1:T(8,128)(2,1)S(1)} %fusion.9), channel_id=1, source_target_pairs={{0,4},{1,5},{2,6},{3,7},{4,0},{5,1},{6,2},{7,3},{8,12},{9,13},{10,... | collective-permute-start | bytes 589832 | tf_op jit(solution)/shard_map/ppermute | solution.py:850
  157.6 6.6 %collective-permute-start.28 = (bf16[2,2,64,384]{3,2,1,0:T(8,128)(2,1)S(1)}, bf16[2,2,64,384]{3,2,1,0:T(8,128)(2,1)S(1)}, u32[]{:S(2)}, u32[]{:S(2)}) collective-permute-start(bf16[2,2,64,384]{3,2,1,0:T(8,128)(2,1)S(1)} %fusion.10), channel_id=1, source_target_pairs={{0,8},{1,9},{2,10},{3,11},{4,12},{5,13},{6,14},{7,15},{8,0},{9,1},... | collective-permute-start | bytes 589832 | tf_op jit(solution)/shard_map/ppermute | solution.py:850
  158.6 5.7 %collective-permute-start.29 = (bf16[2,2,64,384]{3,2,0,1:T(8,128)(2,1)S(1)}, bf16[2,2,64,384]{3,2,0,1:T(8,128)(2,1)S(1)}, u32[]{:S(2)}, u32[]{:S(2)}) collective-permute-start(bf16[2,2,64,384]{3,2,0,1:T(8,128)(2,1)S(1)} %fusion.5), channel_id=1, source_target_pairs={{0,2},{1,3},{2,0},{3,1},{4,6},{5,7},{6,4},{7,5},{8,10},{9,11},{10,... | collective-permute-start | bytes 589832 | tf_op jit(solution)/shard_map/ppermute | solution.py:850
  160.1 2.9 %collective-permute-start.26 = (bf16[2,2,8,64,256]{4,3,2,1,0:T(8,128)(2,1)}, bf16[2,2,8,64,256]{4,3,2,1,0:T(8,128)(2,1)S(1)}, u32[]{:S(2)}, u32[]{:S(2)}) collective-permute-start(bf16[2,2,8,64,256]{4,3,2,1,0:T(8,128)(2,1)} %get-tuple-element.238), channel_id=1, source_target_pairs={{0,1},{1,0},{2,3},{3,2},{4,5},{5,4},{6,7},{7,6},{8,9},{9,8},{10,11... | collective-permute-start | bytes 3145736 | tf_op jit(solution)/shard_map/ppermute | solution.py:850
  165.1 9.2 %collective-permute-start.30 = (bf16[2,2,2,64,256]{4,3,1,0,2:T(8,128)(2,1)S(1)}, bf16[2,2,2,64,256]{4,3,1,0,2:T(8,128)(2,1)S(1)}, u32[]{:S(2)}, u32[]{:S(2)}) collective-permute-start(bf16[2,2,2,64,256]{4,3,1,0,2:T(8,128)(2,1)S(1)} %copy.78), channel_id=1, source_target_pairs={{0,2},{1,3},{2,0},{3,1},{4,6},{5,7},{6,4},{7,5},{8,10},{9,11},{10,... | collective-permute-start | bytes 786440 | tf_op jit(solution)/shard_map/ppermute | solution.py:850
  166.3 8.6 %collective-permute-start.31 = (bf16[2,2,2,64,256]{4,3,2,1,0:T(8,128)(2,1)S(1)}, bf16[2,2,2,64,256]{4,3,2,1,0:T(8,128)(2,1)S(1)}, u32[]{:S(2)}, u32[]{:S(2)}) collective-permute-start(bf16[2,2,2,64,256]{4,3,2,1,0:T(8,128)(2,1)S(1)} %fusion.7), channel_id=1, source_target_pairs={{0,4},{1,5},{2,6},{3,7},{4,0},{5,1},{6,2},{7,3},{8,12},{9,13},{10,... | collective-permute-start | bytes 786440 | tf_op jit(solution)/shard_map/ppermute | solution.py:850
  167.9 7.1 %collective-permute-start.32 = (bf16[2,64,384]{2,1,0:T(8,128)(2,1)S(1)}, bf16[2,64,384]{2,1,0:T(8,128)(2,1)S(1)}, u32[]{:S(2)}, u32[]{:S(2)}) collective-permute-start(bf16[2,64,384]{2,1,0:T(8,128)(2,1)S(1)} %fusion.19), channel_id=1, source_target_pairs={{0,8},{1,9},{2,10},{3,11},{4,12},{5,13},{6,14},{7,15},{8,0},{9,1},... | collective-permute-start | bytes 294920 | tf_op jit(solution)/shard_map/ppermute | solution.py:850
  169.0 6.6 %collective-permute-start.33 = (bf16[2,64,384]{2,1,0:T(8,128)(2,1)S(1)}, bf16[2,64,384]{2,1,0:T(8,128)(2,1)S(1)}, u32[]{:S(2)}, u32[]{:S(2)}) collective-permute-start(bf16[2,64,384]{2,1,0:T(8,128)(2,1)S(1)} %fusion.20), channel_id=1, source_target_pairs={{0,2},{1,3},{2,0},{3,1},{4,6},{5,7},{6,4},{7,5},{8,10},{9,11},{10,... | collective-permute-start | bytes 294920 | tf_op jit(solution)/shard_map/ppermute | solution.py:850
  169.9 6.1 %collective-permute-start.34 = (bf16[2,64,384]{2,1,0:T(8,128)(2,1)S(1)}, bf16[2,64,384]{2,1,0:T(8,128)(2,1)S(1)}, u32[]{:S(2)}, u32[]{:S(2)}) collective-permute-start(bf16[2,64,384]{2,1,0:T(8,128)(2,1)S(1)} %fusion.21), channel_id=1, source_target_pairs={{0,4},{1,5},{2,6},{3,7},{4,0},{5,1},{6,2},{7,3},{8,12},{9,13},{10,... | collective-permute-start | bytes 294920 | tf_op jit(solution)/shard_map/ppermute | solution.py:850
  176.0 5.0 %collective-permute-start.35 = (bf16[2,2,64,256]{3,2,1,0:T(8,128)(2,1)S(1)}, bf16[2,2,64,256]{3,2,1,0:T(8,128)(2,1)S(1)}, u32[]{:S(2)}, u32[]{:S(2)}) collective-permute-start(bf16[2,2,64,256]{3,2,1,0:T(8,128)(2,1)S(1)} %fusion.11), channel_id=1, source_target_pairs={{0,4},{1,5},{2,6},{3,7},{4,0},{5,1},{6,2},{7,3},{8,12},{9,13},{10,... | collective-permute-start | bytes 393224 | tf_op jit(solution)/shard_map/ppermute | solution.py:850
  177.5 5.0 %collective-permute-start.36 = (bf16[2,2,64,256]{3,2,1,0:T(8,128)(2,1)S(1)}, bf16[2,2,64,256]{3,2,1,0:T(8,128)(2,1)S(1)}, u32[]{:S(2)}, u32[]{:S(2)}) collective-permute-start(bf16[2,2,64,256]{3,2,1,0:T(8,128)(2,1)S(1)} %fusion.8), channel_id=1, source_target_pairs={{0,2},{1,3},{2,0},{3,1},{4,6},{5,7},{6,4},{7,5},{8,10},{9,11},{10,... | collective-permute-start | bytes 393224 | tf_op jit(solution)/shard_map/ppermute | solution.py:850
  179.2 33.8 %copy-start.4 = (f32[64,896]{1,0:T(8,128)S(1)}, f32[64,896]{1,0:T(8,128)}, u32[]{:S(2)}) copy-start(f32[64,896]{1,0:T(8,128)} %refs_4_.1) | copy-start | bytes 688132
  182.6 5.4 %collective-permute-start.37 = (bf16[2,64,512]{2,1,0:T(8,128)(2,1)S(1)}, bf16[2,64,512]{2,1,0:T(8,128)(2,1)S(1)}, u32[]{:S(2)}, u32[]{:S(2)}) collective-permute-start(bf16[2,64,512]{2,1,0:T(8,128)(2,1)S(1)} %fusion.12), channel_id=1, source_target_pairs={{0,8},{1,9},{2,10},{3,11},{4,12},{5,13},{6,14},{7,15},{8,0},{9,1},... | collective-permute-start | bytes 393224 | tf_op jit(solution)/shard_map/ppermute | solution.py:850
  183.6 9.3 %collective-permute-start.39 = (bf16[64,1152]{1,0:T(8,128)(2,1)S(1)}, bf16[64,1152]{1,0:T(8,128)(2,1)S(1)}, u32[]{:S(2)}, u32[]{:S(2)}) collective-permute-start(bf16[64,1152]{1,0:T(8,128)(2,1)S(1)} %pad_maximum_fusion.6), channel_id=1, source_target_pairs={{0,16},{1,17},{2,18},{3,19},{4,20},{5,21},{6,22},{7,23},{8,24},{9,... | collective-permute-start | bytes 442376 | tf_op jit(solution)/shard_map/ppermute | solution.py:850
  188.1 5.6 %collective-permute-start.38 = (bf16[64,512]{1,0:T(8,128)(2,1)S(1)}, bf16[64,512]{1,0:T(8,128)(2,1)S(1)}, u32[]{:S(2)}, u32[]{:S(2)}) collective-permute-start(bf16[64,512]{1,0:T(8,128)(2,1)S(1)} %fusion.17), channel_id=1, source_target_pairs={{0,16},{1,17},{2,18},{3,19},{4,20},{5,21},{6,22},{7,23},{8,24},{9,... | collective-permute-start | bytes 196616 | tf_op jit(solution)/shard_map/ppermute | solution.py:850
  196.3 1.2 collective-permute-start.40
  197.5 3.6 %collective-permute-start.42 = (f32[8,128]{1,0:T(8,128)S(1)}, f32[8,128]{1,0:T(8,128)S(1)}, u32[]{:S(2)}, u32[]{:S(2)}) collective-permute-start(f32[8,128]{1,0:T(8,128)S(1)} %pad_add_fusion), channel_id=1, source_target_pairs={{0,4},{1,5},{2,6},{3,7},{4,0},{5,1},{6,2},{7,3},{8,12},{9,13},{10,... | collective-permute-start | bytes 12296 | tf_op jit(solution)/shard_map/ppermute | solution.py:937
  197.7 4.5 %collective-permute-start.43 = (f32[8,128]{1,0:T(8,128)S(1)}, f32[8,128]{1,0:T(8,128)S(1)}, u32[]{:S(2)}, u32[]{:S(2)}) collective-permute-start(f32[8,128]{1,0:T(8,128)S(1)} %pad_add_fusion), channel_id=1, source_target_pairs={{0,6},{1,7},{2,4},{3,5},{4,2},{5,3},{6,0},{7,1},{8,14},{9,15},{10,... | collective-permute-start | bytes 12296 | tf_op jit(solution)/shard_map/ppermute | solution.py:937
  200.5 3.6 %collective-permute-start.41 = (f32[8,128]{1,0:T(8,128)S(1)}, f32[8,128]{1,0:T(8,128)S(1)}, u32[]{:S(2)}, u32[]{:S(2)}) collective-permute-start(f32[8,128]{1,0:T(8,128)S(1)} %pad_add_fusion), channel_id=1, source_target_pairs={{0,2},{1,3},{2,0},{3,1},{4,6},{5,7},{6,4},{7,5},{8,10},{9,11},{10,... | collective-permute-start | bytes 12296 | tf_op jit(solution)/shard_map/ppermute | solution.py:937
  204.1 6.0 %collective-permute-start.46 = (f32[8,128]{1,0:T(8,128)S(1)}, f32[8,128]{1,0:T(8,128)S(1)}, u32[]{:S(2)}, u32[]{:S(2)}) collective-permute-start(f32[8,128]{1,0:T(8,128)S(1)} %add_add_fusion.1), channel_id=1, source_target_pairs={{0,24},{1,25},{2,26},{3,27},{4,28},{5,29},{6,30},{7,31},{8,16},{9,... | collective-permute-start | bytes 12296 | tf_op jit(solution)/shard_map/ppermute | solution.py:937
  208.5 4.5 %collective-permute-start.45 = (f32[8,128]{1,0:T(8,128)S(1)}, f32[8,128]{1,0:T(8,128)S(1)}, u32[]{:S(2)}, u32[]{:S(2)}) collective-permute-start(f32[8,128]{1,0:T(8,128)S(1)} %add_add_fusion.1), channel_id=1, source_target_pairs={{0,16},{1,17},{2,18},{3,19},{4,20},{5,21},{6,22},{7,23},{8,24},{9,... | collective-permute-start | bytes 12296 | tf_op jit(solution)/shard_map/ppermute | solution.py:937
  208.5 4.5 %collective-permute-start.44 = (f32[8,128]{1,0:T(8,128)S(1)}, f32[8,128]{1,0:T(8,128)S(1)}, u32[]{:S(2)}, u32[]{:S(2)}) collective-permute-start(f32[8,128]{1,0:T(8,128)S(1)} %add_add_fusion.1), channel_id=1, source_target_pairs={{0,8},{1,9},{2,10},{3,11},{4,12},{5,13},{6,14},{7,15},{8,0},{9,1},... | collective-permute-start | bytes 12296 | tf_op jit(solution)/shard_map/ppermute | solution.py:937
  (53 other events, 867.3 us)

commit v3 on v2

v3 whole, which is shorter than its diff:
```python
import functools
import math

import jax
import jax.numpy as jnp
from jax import lax
from jax.experimental import pallas as pl
from jax.experimental.pallas import tpu as pltpu
from jax.sharding import PartitionSpec as P

D = 512
HEADS = 4
HEAD_DIM = 128
OUT = 84
IN = 256
LEVELS = 13
KM = 16
KG = 8
KD = 3
STEPS_DONE = 7
MB = 4
GROUPS = 4
HID = 512
ROWS = 8
LINES = 64
EARLY = 512
LATE = 1152
BAND = 256
WINDOW = 1280
NEAR = 1536

clip_norm = 0.001
beta_one = 0.9
beta_two = 0.999
epsilon = 1e-08
learn_rate = 0.04
weight_decay = 0.1
average_decay = 0.9

BF = jnp.bfloat16
F32 = jnp.float32
MIB = 1024 * 1024
QUICK = pl.CostEstimate(flops=1000, bytes_accessed=1000, transcendentals=0)
BIG = 60 * MIB


def mm(left, right):
    return jnp.dot(left, right, preferred_element_type=F32)


def mm_nt(left, right):
    return lax.dot_general(left, right, (((1,), (1,)), ((), ())), preferred_element_type=F32)


def mm_tn(left, right):
    return lax.dot_general(left, right, (((0,), (0,)), ((), ())), preferred_element_type=F32)


def split_two(value):
    high = value.astype(BF)
    return high, (value - high.astype(F32)).astype(BF)


def norm_parts(rows_low):
    values = rows_low.astype(F32)
    center = values - jnp.mean(values, axis=-1, keepdims=True)
    inverse = lax.rsqrt(jnp.mean(center * center, axis=-1, keepdims=True) + 1e-05)
    return center * inverse, inverse


def norm_pull(grad_out, normal, inverse, gain):
    scaled = grad_out * gain
    inner = (
        scaled
        - jnp.mean(scaled, axis=-1, keepdims=True)
        - normal * jnp.mean(scaled * normal, axis=-1, keepdims=True)
    )
    return inner * inverse, jnp.sum(grad_out * normal, axis=0, keepdims=True)


class Leaving:
    def __init__(self, sems):
        self.sems, self.copies = sems, []

    def __call__(self, source, there):
        self.copies.append(pltpu.make_async_copy(source, there, self.sems.at[len(self.copies)]))
        self.copies[-1].start()

    def wait(self):
        for copy in self.copies:
            copy.wait()


def sums_kernel(grid_ref, pixels_ref, sums_ref, count_ref):
    width, nodes = count_ref.shape
    step = 32
    picks = [jnp.broadcast_to(pixels_ref[k : k + 1, :], (step, nodes)) for k in range(KG)]
    rows = lax.broadcasted_iota(jnp.int32, (step, nodes), 0)

    def count(i, _):
        at = pl.multiple_of(i * step, step)
        total = jnp.zeros((step, nodes), F32)
        for pick in picks:
            total = total + jnp.where(pick - at == rows, 1.0, 0.0)
        count_ref[pl.ds(at, step), :] = total.astype(BF)
        return 0

    lax.fori_loop(0, width // step, count, 0)
    sums_ref[...] = mm(grid_ref[...], count_ref[...])


def grid_sums(grid, pixel_rows):
    nodes, width = pixel_rows.shape[1], grid.shape[1]
    return pl.pallas_call(
        sums_kernel,
        out_shape=jax.ShapeDtypeStruct((IN, nodes), F32),
        scratch_shapes=[pltpu.VMEM((width, nodes), BF)],
        compiler_params=pltpu.CompilerParams(vmem_limit_bytes=16 * 1024 * 1024),
        cost_estimate=QUICK,
        name="grid_sums",
    )(grid, pixel_rows)


def counts_kernel(slots_ref, across_ref, bias_out, pool_out, pull_out, bias_ref, pool_ref, pull_ref, sems):
    nodes, width = pull_ref.shape
    step = 64
    leave = Leaving(sems)

    def count_across(i, _):
        at = pl.multiple_of(i * 128, 128)
        rows = lax.broadcasted_iota(jnp.int32, (128, width), 0) + at
        total = jnp.zeros((128, width), F32)
        for k in range(KD):
            total = total + jnp.where(across_ref[k : k + 1, :] == rows, 1.0, 0.0)
        pull_ref[pl.ds(at, 128), :] = total.astype(BF)
        pool_ref[:, pl.ds(at, 128)] = total.T.astype(BF)
        return 0

    lax.fori_loop(0, nodes // 128, count_across, 0)
    leave(pool_ref, pool_out)
    leave(pull_ref, pull_out)
    for band in range(nodes // BAND):
        low = band * BAND
        picks = slots_ref[:, low : low + BAND] - low
        rows = lax.broadcasted_iota(jnp.int32, (step, BAND), 0)
        alike = jnp.zeros((KM, BAND), F32)
        for k in range(KM):
            alike = alike + jnp.where(picks == picks[k : k + 1, :], 1.0, 0.0)
        weight = jnp.log2(alike)

        def count_slots(i, _):
            at = pl.multiple_of(i * step, step)
            value = jnp.full((step, BAND), -1e30, F32)
            for k in range(KM):
                value = jnp.where(picks[k : k + 1, :] - at == rows, weight[k : k + 1, :], value)
            bias_ref[band, pl.ds(at, step), :] = value
            return 0

        for part in range(2):
            half = WINDOW // step // 2
            lax.fori_loop(part * half, (part + 1) * half, count_slots, 0)
            here = slice(part * half * step, (part + 1) * half * step)
            leave(bias_ref.at[band, here], bias_out.at[band, here])
    leave.wait()


def counts(slot_rows, across_rows):
    nodes, width = slot_rows.shape[1], across_rows.shape[1]
    shapes = (
        jax.ShapeDtypeStruct((nodes // BAND, WINDOW, BAND), F32),
        jax.ShapeDtypeStruct((width, nodes), BF),
        jax.ShapeDtypeStruct((nodes, width), BF),
    )
    return pl.pallas_call(
        counts_kernel,
        out_specs=[pl.BlockSpec(memory_space=pltpu.HBM)] * 3,
        out_shape=shapes,
        scratch_shapes=[pltpu.VMEM(shape.shape, shape.dtype) for shape in shapes] + [pltpu.SemaphoreType.DMA((6,))],
        compiler_params=pltpu.CompilerParams(vmem_limit_bytes=BIG),
        cost_estimate=QUICK,
        name="counts",
    )(slot_rows, across_rows)


def blocks_of(place_ref, dims, refs):
    own_wide, own_narrow = place_ref[0], place_ref[1]
    found = []
    for side in range(2):
        for j in range(16):
            bits = dict(zip(dims, ((j >> 3) & 1, (j >> 2) & 1, (j >> 1) & 1, j & 1)))
            wide = own_wide ^ (bits[4] * 4 + bits[3] * 2 + bits[2])
            narrow = own_narrow ^ (bits[1] * 2 + side)
            found.append((wide, narrow, refs[2 * side + (j >> 3)].at[j & 7]))
    return found


def block_at(dims, part, wide):
    bits = {1: part, 2: wide & 1, 3: (wide >> 1) & 1, 4: wide >> 2}
    return ((bits[dims[0]] * 2 + bits[dims[1]]) * 2 + bits[dims[2]]) * 2 + bits[dims[3]]


def fetch_early(place_ref, refs, early, sems):
    return [
        pltpu.make_async_copy(source, early.at[wide, narrow], sems.at[i])
        for i, (wide, narrow, source) in enumerate(blocks_of(place_ref, DIMS[0], refs))
    ]


def enc_of(early):
    return jnp.concatenate([early[:, n, 0:32, 384:512].reshape(IN, 128) for n in range(GROUPS)], axis=1)


def dec_of(early):
    return jnp.concatenate([early[:, n, 32:48, 384:512].reshape(128, 128) for n in range(GROUPS)], axis=0)


def query_of(early):
    return jnp.concatenate([early[:, n, :, 0:128].reshape(D, 128) for n in range(GROUPS)], axis=1)


def pair_of(early):
    return jnp.concatenate([early[:, n, :, 128:384].reshape(D, 256) for n in range(GROUPS)], axis=1)


def encode_kernel(
    place_ref, a_0, a_1, a_2, a_3, before_ref, sums_ref, after_ref,
    state_ref, rows_ref, normed_ref, early_ref,
    early, state, rows_all, normed_all, sems, out_sems,
):
    copies = fetch_early(place_ref, (a_0, a_1, a_2, a_3), early, sems)
    for copy in copies:
        copy.start()
    for copy in copies:
        copy.wait()
    leave = Leaving(out_sems)
    leave(early, early_ref)
    gain = dec_of(early).astype(F32).T[OUT : OUT + 1, :]
    enc = enc_of(early)
    for block, ref in enumerate((before_ref, sums_ref, after_ref)):
        here = slice(block * 512, block * 512 + 512)
        if block == 1:
            high, low = split_two(ref[...])
            embedded = (mm_tn(high, enc) + mm_tn(low, enc)) * (1.0 / KG)
            state[...] = embedded
            leave(state, state_ref)
        else:
            embedded = mm_tn(ref[...], enc) * (1.0 / KG)
        rows = embedded.astype(BF)
        rows_all[here, :] = rows
        leave(rows_all.at[here], rows_ref.at[here])
        normal, _inverse = norm_parts(rows)
        normed_all[here, :] = (normal * gain).astype(BF)
        leave(normed_all.at[here], normed_ref.at[here])
    leave.wait()


def encode(place, gathered, before, sums, after):
    nodes = sums.shape[1]
    vmem = pl.BlockSpec(memory_space=pltpu.VMEM)
    outside = pl.BlockSpec(memory_space=pltpu.HBM)
    shapes = (
        jax.ShapeDtypeStruct((nodes, D), F32),
        jax.ShapeDtypeStruct((NEAR, D), BF),
        jax.ShapeDtypeStruct((NEAR, D), BF),
        jax.ShapeDtypeStruct((8, GROUPS, LINES, EARLY), BF),
    )
    return pl.pallas_call(
        encode_kernel,
        in_specs=[pl.BlockSpec(memory_space=pltpu.SMEM)] + [outside] * 4 + [vmem] * 3,
        out_specs=[outside] * 4,
        out_shape=shapes,
        scratch_shapes=[pltpu.VMEM((8, GROUPS, LINES, EARLY), BF)]
        + [pltpu.VMEM(shape.shape, shape.dtype) for shape in shapes[:3]]
        + [pltpu.SemaphoreType.DMA((32,)), pltpu.SemaphoreType.DMA((8,))],
        compiler_params=pltpu.CompilerParams(vmem_limit_bytes=BIG),
        cost_estimate=QUICK,
        name="encode",
    )(place, *gathered, before, sums, after)


def attend_kernel(
    normed_in, early_in, bias_in, mixed_ref, probs_ref, query_ref, pair_ref, inverse_ref,
    normed, early, bias, query_all, pair_all, mixed_all, probs, inverse_all, sems, out_sems,
):
    def weight_copy(h):
        return pltpu.make_async_copy(early_in.at[:, h, :, 0:384], early.at[h], sems.at[h])

    normed_copy = pltpu.make_async_copy(normed_in, normed, sems.at[4])
    bias_copies = [pltpu.make_async_copy(bias_in.at[i], bias.at[i], sems.at[5 + i]) for i in range(2)]
    weight_copy(0).start()
    normed_copy.start()
    bias_copies[0].start()
    bias_copies[1].start()
    for h in range(1, HEADS):
        weight_copy(h).start()
    normed_copy.wait()
    factor = HEAD_DIM ** (-0.5) * math.log2(math.e)

    def pair_leave(h):
        return pltpu.make_async_copy(pair_all.at[h], pair_ref.at[h], out_sems.at[8 + h])

    def probs_leave(h):
        return pltpu.make_async_copy(probs.at[h], probs_ref.at[h], out_sems.at[4 + h])

    for h in range(HEADS):
        lanes = slice(h * HEAD_DIM, h * HEAD_DIM + HEAD_DIM)
        weight_copy(h).wait()
        weights = early[h].reshape(D, 384)
        pair_all[h] = mm(normed[...], weights[:, 128:384]).astype(BF)
        query_all[:, lanes] = mm(normed[512:1024, :], weights[:, 0:128]).astype(BF)
        if h == 0:
            bias_copies[0].wait()
            bias_copies[1].wait()
        for band in range(2):
            at = band * BAND
            near, here = slice(at, at + WINDOW), slice(at, at + BAND)
            part = mm_nt(pair_all[h, near, :HEAD_DIM], query_all[here, lanes]) * factor + bias[band]
            expo = jnp.exp2(part - jnp.max(part, axis=0, keepdims=True))
            inverse = 1.0 / jnp.sum(expo, axis=0, keepdims=True)
            low = expo.astype(BF)
            probs[h, near, here] = low
            inverse_all[h : h + 1, here] = inverse
            column = jnp.broadcast_to(inverse, (8, BAND)).T[:, 0:1]
            mixed_all[here, lanes] = mm_tn(low, pair_all[h, near, HEAD_DIM:]) * column
        probs_leave(h).start()
        pair_leave(h).start()
    inverse_all[HEADS:8, :] = jnp.zeros((8 - HEADS, inverse_all.shape[1]), F32)
    leave = Leaving(out_sems)
    leave(mixed_all, mixed_ref)
    leave(query_all, query_ref)
    leave(inverse_all, inverse_ref)
    leave.wait()
    for h in range(HEADS):
        pair_leave(h).wait()
        probs_leave(h).wait()


def attend(normed, early, bias):
    nodes = normed.shape[0] // 3
    outside = pl.BlockSpec(memory_space=pltpu.HBM)
    return pl.pallas_call(
        attend_kernel,
        in_specs=[outside] * 3,
        out_specs=[outside] * 5,
        out_shape=(
            jax.ShapeDtypeStruct((nodes, D), F32),
            jax.ShapeDtypeStruct((HEADS, NEAR, nodes), BF),
            jax.ShapeDtypeStruct((nodes, D), BF),
            jax.ShapeDtypeStruct((HEADS, NEAR, 2 * HEAD_DIM), BF),
            jax.ShapeDtypeStruct((8, nodes), F32),
        ),
        scratch_shapes=[
            pltpu.VMEM((NEAR, D), BF),
            pltpu.VMEM((GROUPS, 8, LINES, 384), BF),
            pltpu.VMEM((2, WINDOW, BAND), F32),
            pltpu.VMEM((nodes, D), BF),
            pltpu.VMEM((HEADS, NEAR, 2 * HEAD_DIM), BF),
            pltpu.VMEM((nodes, D), F32),
            pltpu.VMEM((HEADS, NEAR, nodes), BF),
            pltpu.VMEM((8, nodes), F32),
            pltpu.SemaphoreType.DMA((7,)),
            pltpu.SemaphoreType.DMA((12,)),
        ],
        compiler_params=pltpu.CompilerParams(vmem_limit_bytes=BIG),
        cost_estimate=QUICK,
        name="attend",
    )(normed, early, bias)


def feed_kernel(
    place_ref, sigma_ref, a_0, a_1, a_2, a_3, b_0, b_1, b_2, b_3, early_ref, state_in, mixed_in, pool_in, pull_in, inverse_ref, noisy_ref, target_ref, lat_ref, level_ref,
    keep_0, keep_1, keep_2, send_0, send_1, send_2, grad_state_out, grad_mixed_out, grad_scaled_out, inner_ref, grad_dec_ref, loss_ref,
    late, dec, pre_ref, act_ref, grad_pred_ref,
    state_ref, mixed_ref, pool_ref, pull_ref, keep_ref, send_ref, grad_state_ref, grad_mixed_ref, grad_scaled_ref, sems, group_sems, out_sems,
):
    own_wide, own_narrow = place_ref[0], place_ref[1]

    refs = (a_0, a_1, a_2, a_3), (b_0, b_1, b_2, b_3)

    def fetch(colour, columns, first, sem):
        there = slice(first, first + columns.stop - columns.start)
        return [
            pltpu.make_async_copy(source.at[:, columns], late.at[wide, narrow, :, there], sem(narrow, i))
            for i, (wide, narrow, source) in enumerate(blocks_of(place_ref, DIMS[colour], refs[colour]))
        ]

    def group(n, columns, row):
        return pltpu.make_async_copy(late.at[:, n, :, columns], late.at[:, n, :, columns], group_sems.at[row, n])

    hidden, outer, lower = slice(0, 512), slice(512, 640), slice(640, 1152)
    pairs = [(state_in, state_ref), (mixed_in, mixed_ref), (early_ref.at[:, :, 32:48, 384:512], dec)]
    small = [pltpu.make_async_copy(source, there, sems.at[32 + i]) for i, (source, there) in enumerate(pairs)]
    small += fetch(0, outer, 512, lambda n, i: sems.at[i])
    pool_copy = pltpu.make_async_copy(pool_in, pool_ref, sems.at[35])
    pull_copy = pltpu.make_async_copy(pull_in, pull_ref, sems.at[36])
    first = fetch(0, hidden, 0, lambda n, i: group_sems.at[0, n])
    second = fetch(1, slice(0, 512), 640, lambda n, i: group_sems.at[1, n])
    for copy in (*small, *first, *second, pool_copy, pull_copy):
        copy.start()
    for copy in small:
        copy.wait()
    dec_turned = jnp.concatenate([dec[:, n].reshape(128, 128) for n in range(GROUPS)], axis=0).astype(F32).T
    gain = dec_turned[OUT + 1 : OUT + 2, :]
    rows = lax.broadcasted_iota(jnp.int32, (128, 1), 0)
    dec_only = jnp.where(rows < OUT, dec_turned, 0.0).astype(BF)
    out_full = jnp.concatenate([late[:, n, :, 512:640].reshape(D, 128) for n in range(GROUPS)], axis=1)
    mixed = mixed_ref[...].astype(BF)
    state1 = state_ref[...] + mm_nt(mixed, out_full)
    normal, inverse = norm_parts(state1.astype(BF))
    normed = (normal * gain).astype(BF)

    def forward(i, state):
        n = i ^ own_narrow
        group(n, hidden, 0).wait()
        pre = mm(normed, late[:, n, :, 0:512].reshape(D, HID))
        pre_ref[n] = pre
        act = (pre / (1.0 + jnp.exp(-pre))).astype(BF)
        act_ref[n] = act
        group(n, lower, 1).wait()
        return state + mm_nt(act, late[:, n, :, 640:1152].reshape(D, HID))

    state2 = state1
    for i in range(GROUPS):
        state2 = forward(i, state2)
    high, low = split_two(state2)
    pool_copy.wait()
    pull_copy.wait()
    pool = pool_ref[...]
    pooled = ((mm(pool, high) + mm(pool, low)) / KD).astype(BF)
    pixels = noisy_ref.shape[1]
    pred = mm_nt(dec_only, pooled)[:OUT, :pixels]
    sigma = jnp.full((1, 1), sigma_ref[place_ref[2]], F32)
    square = sigma * sigma
    c_skip = 1.0 / (square + 1.0)
    c_out = sigma * lax.rsqrt(square + 1.0)
    lam = (square + 1.0) / square
    error = c_skip * noisy_ref[...] + c_out * pred - target_ref[...]
    weight = jnp.cos((lat_ref[...].astype(F32) - 90.0) * (math.pi / 180.0)) * ((level_ref[...].astype(F32) + 1.0) / LEVELS)
    weighted = lam * weight
    first_globe = (jnp.full((1, 1), place_ref[2], jnp.int32) == 0).astype(F32)
    lanes = lax.broadcasted_iota(jnp.int32, (1, 128), 1)
    loss_ref[...] = jnp.where(lanes == 1, jnp.sum(weighted * error * error), 0.0) + jnp.where(
        lanes == 2, jnp.sum(weight) * first_globe, 0.0
    )
    grad_pred_ref[...] = jnp.zeros_like(grad_pred_ref)
    grad_pred_ref[:OUT, :pixels] = 2.0 * c_out * weighted * error
    grad_pred = grad_pred_ref[...].astype(BF)
    grad_dec_ref[...] = mm(grad_pred, pooled)
    up_high, up_low = split_two(mm_nt(pull_ref[...], grad_pred))
    grad_state2 = (mm(up_high, dec_only) + mm(up_low, dec_only)) / KD
    grad_low = grad_state2.astype(BF)
    grad_turned = grad_state2.T.astype(BF)
    normed_turned = normed.astype(F32).T.astype(BF)

    def put(out_ref, side, part, first, value):
        done = 0
        while done < value.shape[1]:
            colour, column = divmod(first + done, 384)
            count = min(384 - column, value.shape[1] - done)
            for w in range(8):
                out_ref[colour, block_at(ORDERS[colour], part, w ^ own_wide), :, column : column + count] = value[
                    w * LINES : (w + 1) * LINES, done : done + count
                ]
            done += count

    def backward(part, grad_n, out_ref, side):
        n = (part * 2 + side) ^ own_narrow
        act = act_ref[n]
        pre = pre_ref[n]
        put(out_ref, side, part, 640, mm(grad_turned, act).astype(BF))
        grad_act = mm(grad_low, late[:, n, :, 640:1152].reshape(D, HID))
        logistic = 1.0 / (1.0 + jnp.exp(-pre))
        grad_pre = (grad_act * logistic * (1.0 + pre * (1.0 - logistic))).astype(BF)
        put(out_ref, side, part, 0, mm(normed_turned, grad_pre).astype(BF))
        return grad_n + mm_nt(grad_pre, late[:, n, :, 0:512].reshape(D, HID))

    grad_n = jnp.zeros((D, D), F32)
    leaving = []

    def leave(source, there):
        leaving.append(pltpu.make_async_copy(source, there, out_sems.at[len(leaving)]))
        leaving[-1].start()

    sides = ((1, send_ref, (send_0, send_1, send_2)), (0, keep_ref, (keep_0, keep_1, keep_2)))
    for side, out_ref, there in sides:
        for part in range(2):
            grad_n = backward(part, grad_n, out_ref, side)
        leave(out_ref.at[0], there[0])
        leave(out_ref.at[2], there[2])
    back, gain_grad = norm_pull(grad_n, normal, inverse, gain)
    grad_dec_ref[OUT + 1 : OUT + 2, :] = gain_grad
    grad_state1 = grad_state2 + back
    grad_state_ref[...] = grad_state1
    leave(grad_state_ref, grad_state_out)
    grad_low1 = grad_state1.astype(BF)
    act_ref[0] = mixed
    grad_turned1 = grad_state1.T.astype(BF)
    for side, out_ref, there in sides:
        for part in range(2):
            lane = pl.multiple_of(((part * 2 + side) ^ own_narrow) * 128, 128)
            put(out_ref, side, part, 512, mm(grad_turned1, act_ref[0, :, pl.ds(lane, 128)]).astype(BF))
        leave(out_ref.at[1], there[1])
    grad_mixed = mm(grad_low1, out_full)
    grad_mixed_ref[...] = grad_mixed.astype(BF)
    leave(grad_mixed_ref, grad_mixed_out)
    columns = inverse_ref[...].T
    lanes = lax.broadcasted_iota(jnp.int32, (1, 128), 1)
    inner = jnp.zeros((grad_mixed.shape[0], 128), F32)
    for h in range(HEADS):
        here = slice(h * HEAD_DIM, h * HEAD_DIM + HEAD_DIM)
        grad = grad_mixed[:, here]
        grad_scaled_ref[:, here] = (grad * columns[:, h : h + 1]).astype(BF)
        inner = jnp.where(lanes == h, jnp.sum(grad * mixed_ref[:, here], axis=1, keepdims=True), inner)
    leave(grad_scaled_ref, grad_scaled_out)
    inner_ref[...] = inner.T[0:8, :]
    for copy in leaving:
        copy.wait()


def feed(place, sigma, late, early, state0, mixed, pool, pull, inverse, noisy, target, lat, level):
    nodes = state0.shape[0]
    width = pool.shape[0]
    vmem = pl.BlockSpec(memory_space=pltpu.VMEM)
    outside = pl.BlockSpec(memory_space=pltpu.HBM)
    return pl.pallas_call(
        feed_kernel,
        in_specs=[pl.BlockSpec(memory_space=pltpu.SMEM)] * 2 + [outside] * 13 + [vmem] * 5,
        out_specs=[outside] * 9 + [vmem] * 3,
        out_shape=(
            *([jax.ShapeDtypeStruct((16, LINES, 384), BF)] * 6),
            jax.ShapeDtypeStruct((nodes, D), F32),
            jax.ShapeDtypeStruct((nodes, D), BF),
            jax.ShapeDtypeStruct((nodes, D), BF),
            jax.ShapeDtypeStruct((8, nodes), F32),
            jax.ShapeDtypeStruct((128, D), F32),
            jax.ShapeDtypeStruct((1, 128), F32),
        ),
        scratch_shapes=[
            pltpu.VMEM((8, GROUPS, LINES, LATE), BF),
            pltpu.VMEM((8, GROUPS, 16, 128), BF),
            pltpu.VMEM((GROUPS, nodes, HID), F32),
            pltpu.VMEM((GROUPS, nodes, HID), BF),
            pltpu.VMEM((128, width), F32),
            pltpu.VMEM((nodes, D), F32),
            pltpu.VMEM((nodes, D), F32),
            pltpu.VMEM((width, nodes), BF),
            pltpu.VMEM((nodes, width), BF),
            pltpu.VMEM((3, 16, LINES, 384), BF),
            pltpu.VMEM((3, 16, LINES, 384), BF),
            pltpu.VMEM((nodes, D), F32),
            pltpu.VMEM((nodes, D), BF),
            pltpu.VMEM((nodes, D), BF),
            pltpu.SemaphoreType.DMA((37,)),
            pltpu.SemaphoreType.DMA((2, GROUPS)),
            pltpu.SemaphoreType.DMA((9,)),
        ],
        compiler_params=pltpu.CompilerParams(vmem_limit_bytes=BIG),
        cost_estimate=QUICK,
        name="feed",
    )(place, sigma, *late, early, state0, mixed, pool, pull, inverse, noisy, target, lat, level)


def unmix_kernel(first, probs_ref, query_ref, keys_ref, values_ref, grad_mixed_ref, grad_scaled_ref, inner_ref, inverse_ref,
                 grad_query_ref, grad_pair_ref, grad_scores):
    scale = HEAD_DIM ** (-0.5)
    row = pl.ds(first + pl.program_id(0), 1)
    inner = inner_ref[row, :]
    factor = inverse_ref[row, :] * scale
    pieces = ((0, 256, 0, 256), (256, 768, 0, 512), (768, 1280, 0, 512), (1280, 1536, 256, 512))
    for low_row, high_row, low_column, high_column in pieces:
        rows, columns = slice(low_row, high_row), slice(low_column, high_column)
        probs = probs_ref[0, rows, columns]
        grad_probs = mm_nt(values_ref[0, rows, :], grad_mixed_ref[columns, :])
        low = (probs.astype(F32) * ((grad_probs - inner[:, columns]) * factor[:, columns])).astype(BF)
        grad_scores[rows, columns] = low
        grad_pair_ref[rows, 0:HEAD_DIM] = mm(low, query_ref[columns, :]).astype(BF)
        grad_pair_ref[rows, HEAD_DIM : 2 * HEAD_DIM] = mm(probs, grad_scaled_ref[columns, :]).astype(BF)
    for at in (0, BAND):
        grad_query_ref[at : at + BAND, :] = mm_tn(
            grad_scores[at : at + WINDOW, at : at + BAND], keys_ref[0, at : at + WINDOW, :]
        ).astype(BF)


def unmix(first, heads, probs, query, pair, grad_mixed, grad_scaled, inner, inverse):
    nodes = query.shape[0]
    part = pl.BlockSpec((nodes, HEAD_DIM), lambda i: (0, first + i))
    whole = pl.BlockSpec((8, nodes), lambda i: (0, 0))
    return pl.pallas_call(
        functools.partial(unmix_kernel, first),
        grid=(heads,),
        in_specs=[
            pl.BlockSpec((1, NEAR, nodes), lambda i: (first + i, 0, 0)),
            part,
            pl.BlockSpec((1, NEAR, HEAD_DIM), lambda i: (first + i, 0, 0)),
            pl.BlockSpec((1, NEAR, HEAD_DIM), lambda i: (first + i, 0, 1)),
            part,
            part,
            whole,
            whole,
        ],
        out_specs=(
            pl.BlockSpec((nodes, HEAD_DIM), lambda i: (0, i)),
            pl.BlockSpec((NEAR, 2 * HEAD_DIM), lambda i: (0, i)),
        ),
        out_shape=(
            jax.ShapeDtypeStruct((nodes, heads * HEAD_DIM), BF),
            jax.ShapeDtypeStruct((NEAR, heads * 2 * HEAD_DIM), BF),
        ),
        scratch_shapes=[pltpu.VMEM((NEAR, nodes), BF)],
        compiler_params=pltpu.CompilerParams(vmem_limit_bytes=BIG),
        cost_estimate=QUICK,
        name="unmix",
    )(probs, query, pair, pair, grad_mixed, grad_scaled, inner, inverse)


def return_kernel(
    place_ref, early_ref, query_in_a, query_in_b, pair_in_a, pair_in_b,
    grad_state_in, rows_in, normed_in, before_ref, sums_ref, after_ref, grad_dec_ref,
    keep_0, keep_1, send_0, send_1,
    early, normed_ref, rows_ref, grad_state_ref, query_g, pair_g, keep_ref, send_ref, sems,
):
    pairs = (
        (normed_in, normed_ref),
        (query_in_a, query_g.at[:, 0:128]), (query_in_b, query_g.at[:, 128:512]),
        (pair_in_a, pair_g.at[:, 0:256]), (pair_in_b, pair_g.at[:, 256:1024]),
        (early_ref, early), (rows_in, rows_ref), (grad_state_in, grad_state_ref),
    )
    copies = [pltpu.make_async_copy(source, there, sems.at[i]) for i, (source, there) in enumerate(pairs)]
    for copy in copies:
        copy.start()
    own_wide, own_narrow = place_ref[0], place_ref[1]
    def put(n, colour, column, value, low):
        lines = value.shape[0] // 8
        for side, out_ref in ((1, send_ref), (0, keep_ref)):

            @pl.when(((n ^ own_narrow) & 1) == side)
            def _():
                part = (n ^ own_narrow) >> 1
                for w in range(8):
                    out_ref[colour, block_at(DIMS[colour], part, w ^ own_wide), low : low + lines, column : column + 128] = value[
                        w * lines : (w + 1) * lines, :
                    ]

    copies[0].wait()
    turned = normed_ref[...].astype(F32).T.astype(BF)
    for copy in copies[1:5]:
        copy.wait()
    weight_query = mm(turned[:, 512:1024], query_g[...]).astype(BF)
    weight_pair = mm(turned, pair_g[...]).astype(BF)
    for n in range(GROUPS):
        put(n, 0, 0, weight_query[:, n * 128 : n * 128 + 128], 0)
        put(n, 0, 128, weight_pair[:, n * 256 : n * 256 + 128], 0)
        put(n, 1, 0, weight_pair[:, n * 256 + 128 : n * 256 + 256], 0)
    leaving = [
        pltpu.make_async_copy(send_ref.at[0], send_0, sems.at[10]),
        pltpu.make_async_copy(keep_ref.at[0], keep_0, sems.at[11]),
        pltpu.make_async_copy(send_ref.at[1], send_1, sems.at[12]),
        pltpu.make_async_copy(keep_ref.at[1], keep_1, sems.at[13]),
    ]
    leaving[0].start()
    leaving[1].start()
    for copy in copies[5:]:
        copy.wait()
    gain = dec_of(early).astype(F32).T[OUT : OUT + 1, :]
    pair_weights = pair_of(early)
    grad_enc = jnp.zeros((IN, D), F32)
    gain_grad = jnp.zeros((1, D), F32)
    for block, sums in enumerate((before_ref, sums_ref, after_ref)):
        at = block * 512
        grad_block = mm_nt(pair_g[at : at + 512, :], pair_weights)
        if block == 1:
            grad_block = grad_block + mm_nt(query_g[...], query_of(early))
        normal, inverse = norm_parts(rows_ref[at : at + 512, :])
        back, gain_part = norm_pull(grad_block, normal, inverse, gain)
        gain_grad = gain_grad + gain_part
        if block == 1:
            back = back + grad_state_ref[...]
        back_low = (back * (1.0 / KG)).astype(BF)
        grad_enc = grad_enc + mm(sums[...].astype(BF), back_low)
    grad_enc = grad_enc.astype(BF)
    rows = lax.broadcasted_iota(jnp.int32, (128, 1), 0)
    grad_dec = jnp.where(rows == OUT, gain_grad, grad_dec_ref[...]).T.astype(BF)
    for n in range(GROUPS):
        put(n, 1, 128, grad_enc[:, n * 128 : n * 128 + 128], 0)
        put(n, 1, 128, grad_dec[n * 128 : n * 128 + 128, :], 32)
        put(n, 1, 128, jnp.zeros((128, 128), BF), 48)
    leaving[2].start()
    leaving[3].start()
    for copy in leaving:
        copy.wait()


def give_back(place, early, first, second, grad_state, rows, normed, before, sums, after, grad_dec):
    vmem = pl.BlockSpec(memory_space=pltpu.VMEM)
    outside = pl.BlockSpec(memory_space=pltpu.HBM)
    return pl.pallas_call(
        return_kernel,
        in_specs=[pl.BlockSpec(memory_space=pltpu.SMEM), outside] + [outside] * 7 + [vmem] * 4,
        out_specs=[outside] * 4,
        out_shape=[jax.ShapeDtypeStruct((16, LINES, 256), BF)] * 4,
        scratch_shapes=[
            pltpu.VMEM((8, GROUPS, LINES, EARLY), BF),
            pltpu.VMEM((NEAR, D), BF),
            pltpu.VMEM((NEAR, D), BF),
            pltpu.VMEM((512, D), F32),
            pltpu.VMEM((512, D), BF),
            pltpu.VMEM((NEAR, 2 * D), BF),
            pltpu.VMEM((2, 16, LINES, 256), BF),
            pltpu.VMEM((2, 16, LINES, 256), BF),
            pltpu.SemaphoreType.DMA((14,)),
        ],
        compiler_params=pltpu.CompilerParams(vmem_limit_bytes=BIG),
        cost_estimate=QUICK,
        name="give_back",
    )(
        place, early, first[0], second[0], first[1], second[1],
        grad_state, rows, normed, before, sums, after, grad_dec,
    )


def adam_kernel(row_ref, early_ref, late_ref, *refs):
    total = row_ref[0:1, 2:3] * MB
    norm_value = jnp.sqrt(row_ref[0:1, 0:1]) / total
    factor = jnp.minimum(1.0, clip_norm / norm_value) / total
    lanes = lax.broadcasted_iota(jnp.int32, (8, 128), 1)
    refs[36][...] = jnp.where(lanes == 0, row_ref[0:1, 1:2] / total, norm_value)
    fix_one = 1.0 - beta_one**STEPS_DONE
    fix_two = 1.0 - beta_two**STEPS_DONE
    enc_rows, read_rows = refs[0].shape[0], refs[12].shape[0]
    shares = (
        ((early_ref, slice(0, enc_rows), slice(384, 512), slice(None)),),
        ((early_ref, slice(None), slice(0, 384), slice(0, 384)), (late_ref, slice(None), slice(0, 512), slice(384, 896))),
        ((late_ref, slice(None), slice(512, 1152), slice(None)),),
        ((early_ref, slice(enc_rows, enc_rows + read_rows), slice(384, 384 + OUT + 2), slice(None)),),
    )
    for i, pieces in enumerate(shares):
        weight_ref, moment_ref, second_ref, average_ref = refs[4 * i : 4 * i + 4]
        outs = refs[16 + 5 * i : 21 + 5 * i]
        for share_ref, rows, columns, there in pieces:
            grad = share_ref[rows, columns] * factor
            weight = weight_ref[:, there]
            moment = beta_one * moment_ref[:, there] + (1.0 - beta_one) * grad
            second = beta_two * second_ref[:, there] + (1.0 - beta_two) * grad * grad
            weight = weight - learn_rate * (
                moment / fix_one / (jnp.sqrt(second / fix_two) + epsilon) + weight_decay * weight
            )
            outs[0][:, there] = moment
            outs[1][:, there] = second
            outs[2][:, there] = weight
            outs[3][:, there] = average_decay * average_ref[:, there] + (1.0 - average_decay) * weight
            outs[4][:, there] = weight.astype(BF)


def adam(row, early, late, states):
    arrays = [array for state in states for array in state]
    shapes = []
    for state in states:
        shapes += [jax.ShapeDtypeStruct(state[0].shape, F32)] * 4 + [jax.ShapeDtypeStruct(state[0].shape, BF)]
    shapes.append(jax.ShapeDtypeStruct((8, 128), F32))
    vmem = pl.BlockSpec(memory_space=pltpu.VMEM)
    return pl.pallas_call(
        adam_kernel,
        in_specs=[vmem] * 19,
        out_specs=[vmem] * 21,
        out_shape=shapes,
        compiler_params=pltpu.CompilerParams(vmem_limit_bytes=16 * MIB),
        cost_estimate=QUICK,
        name="adam",
    )(row, early, late, *arrays)


def pack_kernel(encoder_in, up_in, down_in, readout_in, early_ref, late_ref, encoder_ref, up_ref, down_ref, readout_ref, sems):
    pairs = ((up_in, up_ref), (encoder_in, encoder_ref), (readout_in, readout_ref), (down_in, down_ref))
    copies = [pltpu.make_async_copy(source, there, sems.at[i]) for i, (source, there) in enumerate(pairs)]
    for copy in copies:
        copy.start()
    for copy in copies:
        copy.wait()
    enc_rows, read_rows = encoder_ref.shape[0], readout_ref.shape[0]
    early_ref[:, 0:384] = up_ref[:, 0:384].astype(BF)
    side = jnp.zeros((early_ref.shape[0] - enc_rows, 128), F32)
    early_ref[enc_rows:, 384:512] = side.astype(BF)
    early_ref[0:enc_rows, 384:512] = encoder_ref[...].astype(BF)
    early_ref[enc_rows : enc_rows + read_rows, 384 : 384 + OUT + 2] = readout_ref[...].astype(BF)
    late_ref[:, 0:512] = up_ref[:, 384:896].astype(BF)
    late_ref[:, 512:1152] = down_ref[...].astype(BF)


def pack(encoder, up_proj, down_turned, readout):
    lines = up_proj.shape[0]
    vmem = pl.BlockSpec(memory_space=pltpu.VMEM)
    outside = pl.BlockSpec(memory_space=pltpu.HBM)
    return pl.pallas_call(
        pack_kernel,
        in_specs=[outside] * 4,
        out_specs=[vmem] * 2,
        out_shape=(jax.ShapeDtypeStruct((lines, EARLY), BF), jax.ShapeDtypeStruct((lines, LATE), BF)),
        scratch_shapes=[pltpu.VMEM(array.shape, F32) for array in (encoder, up_proj, down_turned, readout)]
        + [pltpu.SemaphoreType.DMA((4,))],
        compiler_params=pltpu.CompilerParams(vmem_limit_bytes=BIG),
        cost_estimate=QUICK,
        name="pack",
    )(encoder, up_proj, down_turned, readout)


def to_lines(array, wide):
    if wide == 8:
        return array
    lines, width = array.shape[2:]
    return jnp.moveaxis(jnp.moveaxis(array, 1, 0).reshape(GROUPS, 8, LINES, width), 0, 1)


def side_to_lines(side, wide):
    if wide == 8:
        return side
    enc_rows, read_rows = IN // wide, D // (GROUPS * wide)
    enc = to_rows(side[:, :, :enc_rows], 32)
    read = to_rows(side[:, :, enc_rows : enc_rows + read_rows], 16)
    return jnp.concatenate([enc, read, jnp.zeros((8, GROUPS, 16, 128), side.dtype)], axis=2)


def to_rows(array, rows):
    return jnp.moveaxis(jnp.moveaxis(array, 1, 0).reshape(GROUPS, 8, rows, array.shape[3]), 0, 1)


def from_rows(array, wide):
    rows, width = array.shape[2:]
    return jnp.moveaxis(jnp.moveaxis(array, 1, 0).reshape(GROUPS, wide, 8 * rows // wide, width), 0, 1)


def early_from_lines(array, wide):
    if wide == 8:
        return array
    main = from_rows(array[..., :384], wide)
    enc = from_rows(array[:, :, :32, 384:], wide)
    read = from_rows(array[:, :, 32:48, 384:], wide)
    spare = main.shape[2] - enc.shape[2] - read.shape[2]
    side = jnp.concatenate([enc, read, jnp.zeros((wide, GROUPS, spare, 128), array.dtype)], axis=2)
    return jnp.concatenate([main, side], axis=3)


ORDERS = ((1, 2, 3, 4), (2, 3, 1, 4), (3, 1, 2, 4))
DIMS = ((1, 2, 3, 4), (2, 1, 3, 4))
CUTS = (640, 512)


def by_relative(array, dims):
    array = array.reshape(2, 2, 2, 2, 2, *array.shape[2:])
    axes = {4: 0, 3: 1, 2: 2, 1: 3}
    turned = jnp.transpose(array, (4, *(axes[bit] for bit in dims), 5, 6))
    turned = turned.reshape(4, 8, *turned.shape[5:])
    return [turned[i] for i in range(4)]


def gather_plain(early, late, wide):
    def gathered(array):
        full = lax.all_gather(array, ("wide", "narrow"), axis=0, tiled=False)
        return full.reshape(wide, GROUPS, *array.shape)

    full = gathered(early)
    full = jnp.concatenate([to_lines(full[..., :384], wide), side_to_lines(full[..., 384:], wide)], axis=3)
    first = by_relative(full, DIMS[0])
    full = to_lines(gathered(late), wide)
    second = [by_relative(part, DIMS[i]) for i, part in enumerate(jnp.split(full, [CUTS[0]], axis=3))]
    return first, sum(second, [])


def joined(array, other):
    return jnp.concatenate([array[None], other[None]], axis=0)


def swap(array, bit):
    count = lax.axis_size("wide") * lax.axis_size("narrow")
    return lax.ppermute(array, ("wide", "narrow"), [(i, i ^ (1 << bit)) for i in range(count)])


def cube(array):
    return array.reshape(2, 2, 2, 2, *array.shape[1:])


def flat(array):
    return array.reshape(8, *array.shape[3:])


def halve_kernel(groups, keep, *refs):
    count = len(groups)
    total = sum(groups)
    flat_refs, refs = refs[:total], refs[total:]
    outs, refs = refs[: count * (1 + keep)], refs[count * (1 + keep) :]
    flat_there, refs = refs[:total], refs[total:]
    held, (in_sems, out_sems) = refs[:-2], refs[-2:]
    starts = [sum(groups[:i]) for i in range(count)]
    order = [(i, side) for side in ((1, 0) if keep else (1,)) for i in range(count)]

    def fetch(i, side):
        half = held[i].shape[0]
        here = pl.ds(side * half, half)
        return [
            pltpu.make_async_copy(
                flat_refs[starts[i] + k].at[here],
                flat_there[starts[i] + k].at[here if keep else pl.ds(0, half)],
                in_sems.at[starts[i] + k, side],
            )
            for k in range(groups[i])
        ]

    def leave(i, side):
        at = i if side else count + i
        return pltpu.make_async_copy(held[at], outs[at], out_sems.at[at])

    fetches = {at: fetch(*at) for at in order}
    for at in order:
        for copy in fetches[at]:
            copy.start()
    for i, side in order:
        for copy in fetches[i, side]:
            copy.wait()
        half = held[i].shape[0]
        here = pl.ds(side * half if keep else 0, half)
        added = sum(ref[here].astype(F32) for ref in flat_there[starts[i] : starts[i] + groups[i]])
        at = i if side else count + i
        held[at][...] = added.astype(held[at].dtype)
        leave(i, side).start()
    for i, side in order:
        leave(i, side).wait()


def halve_far(lists, keep):
    groups = [len(arrays) for arrays in lists]
    sizes = [min(array.shape[0] for array in arrays) for arrays in lists]
    halves = [(size // 2, *arrays[0].shape[1:]) for size, arrays in zip(sizes, lists)]
    kinds = (BF, F32)[: 1 + keep]
    outside = pl.BlockSpec(memory_space=pltpu.HBM)
    there = [
        pltpu.VMEM((size if keep else size // 2, *array.shape[1:]), array.dtype)
        for size, arrays in zip(sizes, lists)
        for array in arrays
    ]
    outs = pl.pallas_call(
        functools.partial(halve_kernel, groups, keep),
        in_specs=[outside] * sum(groups),
        out_specs=[outside] * (len(kinds) * len(lists)),
        out_shape=[jax.ShapeDtypeStruct(shape, kind) for kind in kinds for shape in halves],
        scratch_shapes=there
        + [pltpu.VMEM(shape, kind) for kind in kinds for shape in halves]
        + [pltpu.SemaphoreType.DMA((sum(groups), 2)), pltpu.SemaphoreType.DMA((len(kinds) * len(lists),))],
        compiler_params=pltpu.CompilerParams(vmem_limit_bytes=BIG),
        cost_estimate=QUICK,
        name="halve_far",
    )(*(array for arrays in lists for array in arrays))
    return outs[: len(lists)], outs[len(lists) :]


def halve_near_kernel(joint, count, *refs):
    column = 0
    for i in range(count):
        first, second = refs[2 * i], refs[2 * i + 1]
        half, width = first.shape[0] // 2, first.shape[2]
        sent, kept = (refs[2 * count], refs[2 * count + 1]) if joint else refs[2 * count + 2 * i : 2 * count + 2 * i + 2]
        there = slice(column, column + width) if joint else slice(None)
        sent[:, :, there] = (first[half:].astype(F32) + second[half:].astype(F32)).astype(BF)
        kept[:, :, there] = first[:half].astype(F32) + second[:half].astype(F32)
        column += width


def halve_near(pairs, joint=False):
    count = len(pairs)
    vmem = pl.BlockSpec(memory_space=pltpu.VMEM)
    halves = [(pair[0].shape[0] // 2, *pair[0].shape[1:]) for pair in pairs]
    if joint:
        halves = [(*halves[0][:2], sum(shape[2] for shape in halves))]
    outs = pl.pallas_call(
        functools.partial(halve_near_kernel, joint, count),
        in_specs=[vmem] * (2 * count),
        out_specs=[vmem] * (2 * len(halves)),
        out_shape=[jax.ShapeDtypeStruct(shape, kind) for shape in halves for kind in (BF, F32)],
        compiler_params=pltpu.CompilerParams(vmem_limit_bytes=12 * MIB),
        cost_estimate=QUICK,
        name="halve_near",
    )(*(array for pair in pairs for array in pair))
    return outs[0::2], outs[1::2]


class Sums:
    def __init__(self, keep, send, orders):
        self.pairs = [(mine, swap(other, 0)) for mine, other in zip(keep, send)]
        self.orders = orders

    def far_step(self, phase, values):
        sent, kept = halve_far(self.pairs, keep=phase > 0)
        sent, values = lax.optimization_barrier((sent, values))
        came = [swap(out, order[phase]) for out, order in zip(sent, self.orders)]
        self.pairs = [(*(pair if phase == 0 else (kept[i],)), came[i]) for i, pair in enumerate(self.pairs)]
        return values

    def step(self, phase, values=(), **how):
        sent, kept = halve_near(self.pairs, **how)
        sent, values = lax.optimization_barrier((sent, values))
        self.pairs = [(mine, swap(out, order[phase])) for mine, out, order in zip(kept, sent, self.orders)]
        return values

    def came(self, values):
        others, values = lax.optimization_barrier(([other for _, other in self.pairs], values))
        self.pairs = [(mine, other) for (mine, _), other in zip(self.pairs, others)]
        return values


def shares_kernel(loss_ref, early_a, early_b, late_a, late_b, early_ref, late_ref, row_ref):
    early = early_a[0] + early_b[0].astype(F32)
    early_ref[...] = early
    late = late_a[0] + late_b[0].astype(F32)
    late_ref[...] = late
    total = jnp.sum(early * early) + jnp.sum(late * late)
    lanes = lax.broadcasted_iota(jnp.int32, (1, 128), 1)
    row_ref[...] = loss_ref[...] + jnp.where(lanes == 0, total, 0.0)


def shares(loss_part, early, late):
    lines = early[0].shape[1]
    vmem = pl.BlockSpec(memory_space=pltpu.VMEM)
    return pl.pallas_call(
        shares_kernel,
        in_specs=[vmem] * 5,
        out_specs=[vmem] * 3,
        out_shape=(
            jax.ShapeDtypeStruct((lines, EARLY), F32),
            jax.ShapeDtypeStruct((lines, LATE), F32),
            jax.ShapeDtypeStruct((1, 128), F32),
        ),
        compiler_params=pltpu.CompilerParams(vmem_limit_bytes=8 * MIB),
        cost_estimate=QUICK,
        name="shares",
    )(loss_part, *early, *late)


def in_order(keep, send, dims):
    both = jnp.stack([keep, send]).reshape(2, 2, 2, 2, 2, *keep.shape[1:])
    turned = jnp.transpose(both, (*(1 + dims.index(bit) for bit in (4, 3, 2, 1)), 0, 5, 6))
    return turned.reshape(8, 4, *keep.shape[1:])


def scatter_sum(blocks):
    return lax.psum_scatter(
        blocks.astype(F32).reshape(-1, blocks.shape[3]), ("wide", "narrow"), scatter_dimension=0, tiled=True
    )


def sum_all(row):
    count = lax.axis_size("wide") * lax.axis_size("narrow")
    bit = 0
    while 1 << bit < count:
        masks = (1, 2, 3) if bit == 1 else (1,)
        others = [lax.ppermute(row, ("wide", "narrow"), [(i, i ^ (mask << bit)) for i in range(count)]) for mask in masks]
        row = sum(others, row)
        bit += len(masks) // 2 + 1
    return row


def body(
    cond_fields,
    target,
    noise_draw,
    noise_sigma,
    grid_to_mesh,
    mesh_edges,
    mesh_to_grid,
    latitude_row,
    level_index,
    encoder,
    up_proj,
    down_proj,
    readout,
    encoder_moment,
    up_moment,
    down_moment,
    readout_moment,
    encoder_second,
    up_second,
    down_second,
    readout_second,
    encoder_average,
    up_average,
    down_average,
    readout_average,
):
    wide_index = lax.axis_index("wide")
    wide = lax.axis_size("wide")
    globe = lax.axis_index("narrow")
    nodes = mesh_edges.shape[0]
    pixels = cond_fields.shape[1]
    all_nodes = nodes * wide
    width = -(-pixels // 128) * 128

    own_place = [wide_index, globe] if wide == 8 else [0, 0]
    place = jnp.stack([*own_place, globe]).astype(jnp.int32)
    early, late = pack(encoder, up_proj, down_proj.T, readout)
    moving = wide == 8
    tie = lax.optimization_barrier
    if moving:
        early_4 = swap(early, 4)

    if moving:
        early_1 = joined(early, early_4)
        early_3 = swap(early_1, 3)
        early_1, target, noise_draw, noise_sigma = tie((early_1, target, noise_draw, noise_sigma))

    def own(array):
        return lax.dynamic_index_in_dim(jnp.transpose(array, (2, 0, 1)), globe, 1, keepdims=False)

    goal, noise = own(target), own(noise_draw)
    sigma = lax.dynamic_index_in_dim(noise_sigma, globe, 0, keepdims=False)
    square = sigma * sigma
    c_in = lax.rsqrt(square + 1.0)
    if moving:
        early_3, goal, noise = tie((early_3, goal, noise))
        both = joined(early_1, early_3)
        both, goal, noise = tie((both, goal, noise))
        early_2 = swap(both, 2)
    noisy = goal + sigma * noise
    if moving:
        noisy, late = tie((noisy, late))
        late_4 = swap(late, 4)
    grid = jnp.concatenate([own(cond_fields), (c_in * noisy).astype(BF)], axis=0)
    grid = jnp.pad(grid, ((0, 0), (0, width - pixels)))
    edges = mesh_edges.T
    slot_rows = jnp.where(edges >= 0, (edges - wide_index * nodes + nodes + all_nodes) % all_nodes, -1)
    across = jnp.pad(mesh_to_grid.T - wide_index * nodes, ((0, 0), (0, width - pixels)), constant_values=-1)

    def halo(sums):
        low = sums.astype(BF)
        ring = [(i, (i + 1) % wide) for i in range(wide)]
        return lax.ppermute(low, "wide", ring), lax.ppermute(low, "wide", [(j, i) for i, j in ring])

    if moving:
        sums = grid_sums(grid, grid_to_mesh.T - wide_index * pixels)
        before, after = halo(sums)
        early_2, sums = tie((early_2, sums))
        quad, late_1 = joined(both, early_2), joined(late, late_4)
        quad, late_1, slot_rows = tie((quad, late_1, slot_rows))
        early_0 = swap(quad, 1)
        late_3 = swap(late_1, 3)
        bias, pool, pull = counts(slot_rows, across)
        bias, late_3 = tie((bias, late_3))
        both = joined(late_1, late_3)
        parts = [both[..., : CUTS[0]], both[..., CUTS[0] :]]
        parts, early_0, before, after = tie((parts, early_0, before, after))
        got = [swap(parts[0], 2), swap(parts[1], 1)]
        halves = [flat(quad), flat(early_0)]
        gathered = halves + [swap(half, 0) for half in halves]
    else:
        gathered, late_full = gather_plain(early, late, wide)
        sums = grid_sums(grid, grid_to_mesh.T - wide_index * pixels)
        bias, pool, pull = counts(slot_rows, across)
        before, after = halo(sums)

    state0, rows, normed, early_full = encode(place, gathered, before, sums, after)
    if moving:
        got, normed = tie((got, normed))
        parts = [joined(part, one) for part, one in zip(parts, got)]
        parts, normed = tie((parts, normed))
        got = [swap(parts[0], 1), swap(parts[1], 2)]
        halves = [flat(part) for part in parts]
        others = [swap(half, 0) for half in halves]
    mixed, probs, query, pair, inverse = attend(normed, early_full, bias)
    if moving:
        mixed, got, others = tie((mixed, got, others))
        late_full = []
        for half, one, other in zip(halves, got, others):
            late_full += [half, flat(one), other, swap(flat(one), 0)]
    *blocks, grad_state, grad_mixed, grad_scaled, inner, grad_dec, loss_part = feed(
        place, noise_sigma,
        late_full, early_full, state0, mixed, pool, pull, inverse, noisy, goal, latitude_row[None, :], level_index[:, None],
    )
    keep_late, send_late = blocks[:3], blocks[3:]
    if moving:
        late_sum = Sums(keep_late, send_late, ORDERS)
    first_heads = unmix(0, 1, probs, query, pair, grad_mixed, grad_scaled, inner, inverse)
    if moving:
        query, first_heads = late_sum.far_step(0, (query, first_heads))
    last_heads = unmix(1, 3, probs, query, pair, grad_mixed, grad_scaled, inner, inverse)
    if moving:
        grad_state, last_heads = late_sum.far_step(1, (grad_state, last_heads))
    *blocks, = give_back(
        place, early_full, first_heads, last_heads, grad_state, rows, normed, before, sums, after, grad_dec
    )
    keep_early, send_early = blocks[:2], blocks[2:]
    if moving:
        keep_early, send_early = late_sum.came((keep_early, send_early))
        early_sum = Sums(keep_early, send_early, DIMS)
        late_sum.pairs = early_sum.step(0, late_sum.pairs)
        late_sum.step(2)
        late_sum.pairs = early_sum.step(1, late_sum.pairs)
        late_sum.step(3, joint=True)
        early_sum.step(2, joint=True)
        early_sum.step(3)
        share_early, share_late, row = shares(loss_part, early_sum.pairs[0], late_sum.pairs[0])
    else:
        late_lines = jnp.concatenate([in_order(keep_late[i], send_late[i], ORDERS[i]) for i in range(3)], axis=3)
        early_lines = jnp.concatenate([in_order(keep_early[i], send_early[i], DIMS[i]) for i in range(2)], axis=3)
        share_late = scatter_sum(from_rows(late_lines, wide))
        share_early = scatter_sum(early_from_lines(early_lines, wide))
        squares = jnp.sum(share_early * share_early) + jnp.sum(share_late * share_late)
        row = loss_part + jnp.where(lax.broadcasted_iota(jnp.int32, (1, 128), 1) == 0, squares, 0.0)
    row = sum_all(row)
    states = [
        (encoder, encoder_moment, encoder_second, encoder_average),
        (up_proj, up_moment, up_second, up_average),
        (down_proj.T, down_moment.T, down_second.T, down_average.T),
        (readout, readout_moment, readout_second, readout_average),
    ]
    news = list(adam(row, share_early, share_late, states))
    news[10:15] = [array.T for array in news[10:15]]
    return (news[20][0, 0], news[20][0, 1], *news[:20])


def solution(mesh):
    if mesh.shape["narrow"] != GROUPS or MB != GROUPS:
        raise ValueError("narrow size")
    by_pixel = P(None, "wide", None)
    pair = P("wide", "narrow")
    weights = (pair, pair, P("narrow", "wide"), P(("narrow", "wide"), None))
    placed = (by_pixel, by_pixel, by_pixel, P()) + (P("wide", None),) * 3 + (P("wide"), P()) + weights * 4
    given = (P(), P())
    for spec in weights:
        given = given + (spec,) * 5
    return jax.shard_map(body, mesh=mesh, in_specs=placed, out_specs=given, check_vma=False)
```

time: 216 us -> 194 us (0.90); the launches traced: 215 us -> 190 us
  local copies, waits for them, and re-layouts: 26.5 us -> 12.5 us
  starting transfers between devices: 53.5 us -> 42.2 us
  other arithmetic: 12.6 us -> 4.91 us
  Pallas kernels: 76.9 us -> 83.5 us
  waiting for transfers between devices: 39.3 us -> 44.2 us
  between operations: 6.6 us -> 3.06 us
    slice x15 -> x0, local copies, waits for them, and re-layouts: 9.12 us -> none  [the longest x10 5.11 us: half_left(): return [lax.index_in_dim(part, 0, axis, keepdims=False) for part in parts]]
    pallas_call x4 -> x13, Pallas kernels: 20.2 us -> 27.8 us  [the longest x2 12.3 us: unmix(): pl.pallas_call(functools.partial(unmix_kernel, first), grid=(heads,), in_...]
    ppermute x7 -> x6, starting transfers between devices: 8.55 us -> 3.65 us  [sum_all(): lax.ppermute(row, ('wide', 'narrow'), [(i, i ^ mask << bit) for i in rang...]
    ppermute x38 -> x37, starting transfers between devices: 40.6 us -> 36.1 us  [swap(): lax.ppermute(array, ('wide', 'narrow'), [(i, i ^ 1 << bit) for i in range...]
    unnamed x116 -> x107, local copies, waits for them, and re-layouts: 11.7 us -> 7.26 us
    convert_element_type x11 -> x0, other arithmetic: 4.28 us -> none  [half_sum(): sum((lax.index_in_dim(part, 1, axis, keepdims=False).astype(F32) for part...]
    ppermute x7 -> x6, waiting for transfers between devices: 8.16 us -> 11.7 us  [sum_all(): lax.ppermute(row, ('wide', 'narrow'), [(i, i ^ mask << bit) for i in rang...]
    ppermute x1, waiting for transfers between devices: 3.22 us -> 0.01 us  [halo(): lax.ppermute(low, 'wide', [(j, i) for i, j in ring])]
  transfers between devices with their start and end apart: 47 -> 45, of which waited for: 23 -> 27; matrix products, arithmetic and copies ran while one was open for 9% -> 4% of each run, Pallas kernels for 19% -> 28%
where the time goes in v3:
time: 194 us; the launch traced here: 190 us
  Pallas kernels  83.5 us (43%)
  waiting for transfers between devices  44.2 us (23%)
  starting transfers between devices  42.2 us (22%)
  local copies, waits for them, and re-layouts  12.5 us (6%)
  other arithmetic  4.91 us (3%)
  between operations  3.06 us (2%)
    ppermute x37, starting transfers between devices, swap(): lax.ppermute(array, ('wide', 'narrow'), [(i, i ^ 1 << bit) for i in range...  36.1 us
    ppermute x37, waiting for transfers between devices, swap(): lax.ppermute(array, ('wide', 'narrow'), [(i, i ^ 1 << bit) for i in range...  30.4 us
    pallas_call x1, Pallas kernels, feed(): pl.pallas_call(feed_kernel, in_specs=[pl.BlockSpec(memory_space=pltpu.SME...  20.1 us
    pallas_call x1, Pallas kernels, attend(): pl.pallas_call(attend_kernel, in_specs=[outside] * 3, out_specs=[outside]...  13.9 us
    pallas_call x2, Pallas kernels, unmix(): pl.pallas_call(functools.partial(unmix_kernel, first), grid=(heads,), in_...  12.3 us
    pallas_call x1, Pallas kernels, give_back(): pl.pallas_call(return_kernel, in_specs=[pl.BlockSpec(memory_space=pltpu.S...  11.9 us
    ppermute x6, waiting for transfers between devices, sum_all(): lax.ppermute(row, ('wide', 'narrow'), [(i, i ^ mask << bit) for i in rang...  11.7 us
    unnamed x107, local copies, waits for them, and re-layouts  7.26 us
  transfers between devices with their start and end apart: 45, of which 27 were waited for; matrix products, arithmetic and copies ran while one was open for 4% of the time, Pallas kernels for 28%

profile of v3, /device:TPU:0, one launch (start us, length us, event | category | flops | bytes accessed | tf_op | source)
XLA Modules:
  0.0 190.4 jit_solution(18283903789672469163)
XLA Ops:
  0.7 1.9 pack.1
  2.6 4.1 %collective-permute-start = (bf16[64,512]{1,0:T(8,128)(2,1)}, bf16[64,512]{1,0:T(8,128)(2,1)S(1)}, u32[]{:S(2)}, u32[]{:S(2)}) collective-permute-start(bf16[64,512]{1,0:T(8,128)(2,1)} %get-tuple-element.182), channel_id=1, source_target_pairs={{0,16},{1,17},{2,18},{3,19},{4,20},{5,21},{6,22},{7,23},{8,24},{9,... | collective-permute-start | bytes 196616 | tf_op jit(solution)/shard_map/ppermute | solution.py:874
  7.4 3.1 %collective-permute-done = bf16[64,512]{1,0:T(8,128)(2,1)S(1)} collective-permute-done((bf16[64,512]{1,0:T(8,128)(2,1)}, bf16[64,512]{1,0:T(8,128)(2,1)S(1)}, u32[]{:S(2)}, u32[]{:S(2)}) %collective-permute-start) | collective-permute-done | bytes 65568 | tf_op jit(solution)/shard_map/ppermute | solution.py:874
  14.9 1.4 copy.48
  17.2 3.3 %collective-permute-start.3 = (bf16[64,1152]{1,0:T(8,128)(2,1)S(1)}, bf16[64,1152]{1,0:T(8,128)(2,1)S(1)}, u32[]{:S(2)}, u32[]{:S(2)}) collective-permute-start(bf16[64,1152]{1,0:T(8,128)(2,1)S(1)} %copy-done.47), channel_id=1, source_target_pairs={{0,16},{1,17},{2,18},{3,19},{4,20},{5,21},{6,22},{7,23},{8,24},{9,... | collective-permute-start | bytes 442376 | tf_op jit(solution)/shard_map/ppermute | solution.py:874
  20.5 1.5 collective-permute-start.2
  22.8 2.4 %grid_sums.1.sums_ref = f32[256,512]{1,0:T(8,128)S(1)} custom-call(bf16[256,896]{1,0:T(8,128)(2,1)S(1)} %fusion.2.grid_ref, s32[8,512]{1,0:T(8,128)S(1)} %subtract_bitcast_fusion.pixels_ref), custom_call_target="tpu_custom_call" | custom-call | flops 1000 | bytes 1000 | tf_op jit(solution)/shard_map/grid_sums/pallas_call | solution.py:114
  25.3 1.6 collective-permute-done.3
  28.3 1.5 collective-permute-start.5
  29.8 2.5 %collective-permute-start.7 = (bf16[256,512]{1,0:T(8,128)(2,1)S(1)}, bf16[256,512]{1,0:T(8,128)(2,1)S(1)}, u32[]{:S(2)}, u32[]{:S(2)}) collective-permute-start(bf16[256,512]{1,0:T(8,128)(2,1)S(1)} %convert_element_type.9), channel_id=1, source_target_pairs={{4,0},{8,4},{12,8},{16,12},{20,16},{24,20},{28,24},{0,28},{5,1},{9... | collective-permute-start | bytes 786440 | tf_op jit(solution)/shard_map/ppermute | solution.py:1132
  33.0 7.2 %counts.1 = (f32[2,1280,256]{2,1,0:T(8,128)}, bf16[896,512]{1,0:T(8,128)(2,1)}, bf16[512,896]{1,0:T(8,128)(2,1)}) custom-call(s32[16,512]{1,0:T(8,128)} %fusion.5.slots_ref, s32[3,896]{1,0:T(4,128)} %pad.9.across_ref), custom_call_target="tpu_custom_call" | custom-call | flops 1000 | bytes 1000 | tf_op jit(solution)/shard_map/counts/pallas_call | solution.py:174
  40.3 2.0 %collective-permute-done.6.before_ref = bf16[256,512]{1,0:T(8,128)(2,1)S(1)} collective-permute-done((bf16[256,512]{1,0:T(8,128)(2,1)S(1)}, bf16[256,512]{1,0:T(8,128)(2,1)S(1)}, u32[]{:S(2)}, u32[]{:S(2)}) %collective-permute-start.6) | collective-permute-done | bytes 262176 | tf_op jit(solution)/shard_map/ppermute | solution.py:1132
  42.4 2.4 %collective-permute-start.8 = (bf16[2,2,64,640]{3,2,1,0:T(8,128)(2,1)S(1)}, bf16[2,2,64,640]{3,2,1,0:T(8,128)(2,1)}, u32[]{:S(2)}, u32[]{:S(2)}) collective-permute-start(bf16[2,2,64,640]{3,2,1,0:T(8,128)(2,1)S(1)} %fusion.3), channel_id=1, source_target_pairs={{0,4},{1,5},{2,6},{3,7},{4,0},{5,1},{6,2},{7,3},{8,12},{9,13},{10,... | collective-permute-start | bytes 983048 | tf_op jit(solution)/shard_map/ppermute | solution.py:874
  47.5 5.7 %encode.1 = (f32[512,512]{1,0:T(8,128)}, bf16[1536,512]{1,0:T(8,128)(2,1)}, bf16[1536,512]{1,0:T(8,128)(2,1)}, bf16[8,4,64,512]{3,2,1,0:T(8,128)(2,1)}) custom-call(s32[3]{0:T(128)} %pad_add_fusion.place_ref, bf16[8,64,512]{2,1,0:T(8,128)(2,1)} %bitcast.70, bf16[8,64,512]{2,1,0:T(8,128)(2,1)} %bitcast.81, bf16[8,64,512]{2,1,0:T(8,128)(2,1)} %copy-done.42, ...), custom_call_target="tpu_custom_call" | custom-call | flops 1000 | bytes 1000 | tf_op jit(solution)/shard_map/encode/pallas_call | solution.py:267
  53.2 1.0 pad_maximum_fusion
  54.4 1.6 collective-permute-start.12
  56.9 13.9 %attend.1 = (f32[512,512]{1,0:T(8,128)}, bf16[4,1536,512]{2,1,0:T(8,128)(2,1)}, bf16[512,512]{1,0:T(8,128)(2,1)}, bf16[4,1536,256]{2,1,0:T(8,128)(2,1)}, f32[8,512]{1,0:T(8,128)}) custom-call(bf16[1536,512]{1,0:T(8,128)(2,1)} %get-tuple-element.213.normed_in, bf16[8,4,64,512]{3,2,1,0:T(8,128)(2,1)} %get-tuple-element.214.early_in.early_ref, ...), custom_call_target="tpu_custom_call" | custom-call | flops 1000 | bytes 1000 | tf_op jit(solution)/shard_map/attend/pallas_call | solution.py:341
  75.6 20.1 %feed.1 = (bf16[16,64,384]{2,1,0:T(8,128)(2,1)}, bf16[16,64,384]{2,1,0:T(8,128)(2,1)}, bf16[16,64,384]{2,1,0:T(8,128)(2,1)}, bf16[16,64,384]{2,1,0:T(8,128)(2,1)...) custom-call(s32[3]{0:T(128)} %pad_add_fusion.place_ref, ...), custom_call_target="tpu_custom_call" | custom-call | flops 1000 | bytes 1000 | tf_op jit(solution)/shard_map/feed/pallas_call | solution.py:525
  96.4 4.5 %unmix.2 = (bf16[512,128]{1,0:T(8,128)(2,1)}, bf16[1536,256]{1,0:T(8,128)(2,1)}) custom-call(bf16[4,1536,512]{2,1,0:T(8,128)(2,1)} %get-tuple-element.238.probs_ref, bf16[512,512]{1,0:T(8,128)(2,1)} %get-tuple-element.252.query_ref, bf16[4,1536,256]{2,1,0:T(8,128)(2,1)} %get-tuple-element.239.keys_ref.values_ref, ...), custom_call_target="tpu_custom_call" | custom-call | flops 1000 | bytes 1000 | tf_op jit(solution)/shard_map/unmix/pallas_call | solution.py:588
  102.3 2.6 %halve_far.2 = (bf16[8,64,384]{2,1,0:T(8,128)(2,1)}, bf16[8,64,384]{2,1,0:T(8,128)(2,1)}, bf16[8,64,384]{2,1,0:T(8,128)(2,1)}) custom-call(bf16[16,64,384]{2,1,0:T(8,128)(2,1)} %get-tuple-element.228.refs_0_, bf16[16,64,384]{2,1,0:T(8,128)(2,1)} %copy-done.25, bf16[16,64,384]{2,1,0:T(8,128)(2,1)} %get-tuple-element.230.refs_2_.refs_3_, ...), custom_call_target="tpu_custom_call" | custom-call | flops 1000 | bytes 1000 | tf_op jit(solution)/shard_map/halve_far/pallas_call | solution.py:939
  104.9 1.6 collective-permute-start.21
  107.2 1.0 collective-permute-start.23
  108.3 7.8 %unmix.3 = (bf16[512,384]{1,0:T(8,128)(2,1)}, bf16[1536,768]{1,0:T(8,128)(2,1)}) custom-call(bf16[4,1536,512]{2,1,0:T(8,128)(2,1)} %get-tuple-element.238.probs_ref, bf16[512,512]{1,0:T(8,128)(2,1)} %get-tuple-element.252.query_ref, bf16[4,1536,256]{2,1,0:T(8,128)(2,1)} %get-tuple-element.239.keys_ref.values_ref, ...), custom_call_target="tpu_custom_call" | custom-call | flops 1000 | bytes 1000 | tf_op jit(solution)/shard_map/unmix/pallas_call | solution.py:588
  116.6 1.2 collective-permute-done.22.refs_5_
  119.3 3.1 %halve_far.3 = (bf16[4,64,384]{2,1,0:T(8,128)(2,1)}, bf16[4,64,384]{2,1,0:T(8,128)(2,1)}, bf16[4,64,384]{2,1,0:T(8,128)(2,1)}, f32[4,64,384]{2,1,0:T(8,128)}, f3...) custom-call(bf16[16,64,384]{2,1,0:T(8,128)(2,1)} %get-tuple-element.228.refs_0_, bf16[16,64,384]{2,1,0:T(8,128)(2,1)} %copy-done.25, ...), custom_call_target="tpu_custom_call" | custom-call | flops 1000 | bytes 1000 | tf_op jit(solution)/shard_map/halve_far/pallas_call | solution.py:939
  122.4 1.1 collective-permute-start.24
  123.4 1.0 collective-permute-start.25
  124.5 1.2 collective-permute-start.26
  125.7 11.9 %give_back.1 = (bf16[16,64,256]{2,1,0:T(8,128)(2,1)}, bf16[16,64,256]{2,1,0:T(8,128)(2,1)}, bf16[16,64,256]{2,1,0:T(8,128)(2,1)}, bf16[16,64,256]{2,1,0:T(8,128)(2,1)}) custom-call(s32[3]{0:T(128)} %pad_add_fusion.place_ref, bf16[8,4,64,512]{3,2,1,0:T(8,128)(2,1)} %get-tuple-element.214.early_in.early_ref, bf16[512,128]{1,0:T(8,128)(2,1)} %get-tuple-element.258.query_in_a, ...), custom_call_target="tpu_custom_call" | custom-call | flops 1000 | bytes 1000 | tf_op jit(solution)/shard_map/give_back/pallas_call | solution.py:696
  138.3 1.6 collective-permute-done.27.refs_1_
  140.6 1.0 copy-done.5
  141.7 1.0 copy-done.6
  145.0 1.0 collective-permute-start.31
  146.0 1.2 collective-permute-start.32
  147.2 1.0 collective-permute-start.33
  148.3 3.9 %collective-permute-done.29.refs_1_ = bf16[8,64,256]{2,1,0:T(8,128)(2,1)S(1)} collective-permute-done((bf16[8,64,256]{2,1,0:T(8,128)(2,1)S(1)}, bf16[8,64,256]{2,1,0:T(8,128)(2,1)S(1)}, u32[]{:S(2)}, u32[]{:S(2)}) %collective-permute-start.29) | collective-permute-done | bytes 262176 | tf_op jit(solution)/shard_map/ppermute | solution.py:874
  155.0 1.2 collective-permute-start.35
  156.2 2.8 %collective-permute-done.34.refs_1_ = bf16[4,64,256]{2,1,0:T(8,128)(2,1)S(1)} collective-permute-done((bf16[4,64,256]{2,1,0:T(8,128)(2,1)S(1)}, bf16[4,64,256]{2,1,0:T(8,128)(2,1)S(1)}, u32[]{:S(2)}, u32[]{:S(2)}) %collective-permute-start.34) | collective-permute-done | bytes 131104 | tf_op jit(solution)/shard_map/ppermute | solution.py:874
  160.2 1.0 collective-permute-start.36
  161.3 1.8 collective-permute-start.38
  163.1 3.7 %collective-permute-done.36.refs_1_ = bf16[2,64,512]{2,1,0:T(8,128)(2,1)S(1)} collective-permute-done((bf16[2,64,512]{2,1,0:T(8,128)(2,1)S(1)}, bf16[2,64,512]{2,1,0:T(8,128)(2,1)S(1)}, u32[]{:S(2)}, u32[]{:S(2)}) %collective-permute-start.36) | collective-permute-done | bytes 131104 | tf_op jit(solution)/shard_map/ppermute | solution.py:874
  166.9 3.3 %collective-permute-done.38.late_b = bf16[1,64,1152]{2,1,0:T(8,128)(2,1)S(1)} collective-permute-done((bf16[1,64,1152]{2,1,0:T(8,128)(2,1)S(1)}, bf16[1,64,1152]{2,1,0:T(8,128)(2,1)S(1)}, u32[]{:S(2)}, u32[]{:S(2)}) %collective-permute-start.38) | collective-permute-done | bytes 147488 | tf_op jit(solution)/shard_map/ppermute | solution.py:874
  170.2 1.9 %collective-permute-done.37.early_b = bf16[1,64,512]{2,1,0:T(8,128)(2,1)S(1)} collective-permute-done((bf16[1,64,512]{2,1,0:T(8,128)(2,1)S(1)}, bf16[1,64,512]{2,1,0:T(8,128)(2,1)S(1)}, u32[]{:S(2)}, u32[]{:S(2)}) %collective-permute-start.37) | collective-permute-done | bytes 65568 | tf_op jit(solution)/shard_map/ppermute | solution.py:874
  172.5 1.1 collective-permute-done.39
  173.6 1.7 collective-permute-start.42
  179.8 3.5 %collective-permute-done.43 = f32[1,128]{1,0:T(1,128)S(1)} collective-permute-done((f32[1,128]{1,0:T(1,128)S(1)}, f32[1,128]{1,0:T(1,128)S(1)}, u32[]{:S(2)}, u32[]{:S(2)}) %collective-permute-start.43) | collective-permute-done | bytes 544 | tf_op jit(solution)/shard_map/ppermute | solution.py:1053
  183.4 4.3 %collective-permute-done.44 = f32[1,128]{1,0:T(1,128)S(1)} collective-permute-done((f32[1,128]{1,0:T(1,128)S(1)}, f32[1,128]{1,0:T(1,128)S(1)}, u32[]{:S(2)}, u32[]{:S(2)}) %collective-permute-start.44) | collective-permute-done | bytes 544 | tf_op jit(solution)/shard_map/ppermute | solution.py:1053
  187.9 1.7 adam.1
  (197 shorter events, 34.2 us)
Async XLA Ops:
  2.6 8.0 %collective-permute-start = (bf16[64,512]{1,0:T(8,128)(2,1)}, bf16[64,512]{1,0:T(8,128)(2,1)S(1)}, u32[]{:S(2)}, u32[]{:S(2)}) collective-permute-start(bf16[64,512]{1,0:T(8,128)(2,1)} %get-tuple-element.182), channel_id=1, source_target_pairs={{0,16},{1,17},{2,18},{3,19},{4,20},{5,21},{6,22},{7,23},{8,24},{9,... | collective-permute-start | bytes 196616 | tf_op jit(solution)/shard_map/ppermute | solution.py:874
  11.4 5.0 %collective-permute-start.1 = (bf16[2,64,512]{2,1,0:T(8,128)(2,1)S(1)}, bf16[2,64,512]{2,1,0:T(8,128)(2,1)S(1)}, u32[]{:S(2)}, u32[]{:S(2)}) collective-permute-start(bf16[2,64,512]{2,1,0:T(8,128)(2,1)S(1)} %pad_maximum_fusion.6), channel_id=1, source_target_pairs={{0,8},{1,9},{2,10},{3,11},{4,12},{5,13},{6,14},{7,15},{8,0},{9,1},... | collective-permute-start | bytes 393224 | tf_op jit(solution)/shard_map/ppermute | solution.py:874
  17.2 9.6 %collective-permute-start.3 = (bf16[64,1152]{1,0:T(8,128)(2,1)S(1)}, bf16[64,1152]{1,0:T(8,128)(2,1)S(1)}, u32[]{:S(2)}, u32[]{:S(2)}) collective-permute-start(bf16[64,1152]{1,0:T(8,128)(2,1)S(1)} %copy-done.47), channel_id=1, source_target_pairs={{0,16},{1,17},{2,18},{3,19},{4,20},{5,21},{6,22},{7,23},{8,24},{9,... | collective-permute-start | bytes 442376 | tf_op jit(solution)/shard_map/ppermute | solution.py:874
  20.5 7.3 %collective-permute-start.2 = (bf16[2,2,64,512]{3,2,1,0:T(8,128)(2,1)S(1)}, bf16[2,2,64,512]{3,2,1,0:T(8,128)(2,1)S(1)}, u32[]{:S(2)}, u32[]{:S(2)}) collective-permute-start(bf16[2,2,64,512]{3,2,1,0:T(8,128)(2,1)S(1)} %pad_maximum_fusion.5), channel_id=1, source_target_pairs={{0,4},{1,5},{2,6},{3,7},{4,0},{5,1},{6,2},{7,3},{8,12},{9,13},{10,... | collective-permute-start | bytes 786440 | tf_op jit(solution)/shard_map/ppermute | solution.py:874
  27.9 12.2 %collective-permute-start.4 = (bf16[2,64,1152]{2,1,0:T(8,128)(2,1)S(1)}, bf16[2,64,1152]{2,1,0:T(8,128)(2,1)S(1)}, u32[]{:S(2)}, u32[]{:S(2)}) collective-permute-start(bf16[2,64,1152]{2,1,0:T(8,128)(2,1)S(1)} %pad_maximum_fusion.3), channel_id=1, source_target_pairs={{0,8},{1,9},{2,10},{3,11},{4,12},{5,13},{6,14},{7,15},{8,0},{9,1},... | collective-permute-start | bytes 884744 | tf_op jit(solution)/shard_map/ppermute | solution.py:874
  28.3 14.0 %collective-permute-start.5 = (bf16[2,2,2,64,512]{4,3,2,1,0:T(8,128)(2,1)S(1)}, bf16[2,2,2,64,512]{4,3,2,1,0:T(8,128)(2,1)S(1)}, u32[]{:S(2)}, u32[]{:S(2)}) collective-permute-start(bf16[2,2,2,64,512]{4,3,2,1,0:T(8,128)(2,1)S(1)} %pad_maximum_fusion.1), channel_id=1, source_target_pairs={{0,2},{1,3},{2,0},{3,1},{4,6},{5,7},{6,4},{7,5},{8,10},{9,11},{10,... | collective-permute-start | bytes 1572872 | tf_op jit(solution)/shard_map/ppermute | solution.py:874
  29.8 10.4 %collective-permute-start.7 = (bf16[256,512]{1,0:T(8,128)(2,1)S(1)}, bf16[256,512]{1,0:T(8,128)(2,1)S(1)}, u32[]{:S(2)}, u32[]{:S(2)}) collective-permute-start(bf16[256,512]{1,0:T(8,128)(2,1)S(1)} %convert_element_type.9), channel_id=1, source_target_pairs={{4,0},{8,4},{12,8},{16,12},{20,16},{24,20},{28,24},{0,28},{5,1},{9... | collective-permute-start | bytes 786440 | tf_op jit(solution)/shard_map/ppermute | solution.py:1132
  32.3 10.0 %collective-permute-start.6 = (bf16[256,512]{1,0:T(8,128)(2,1)S(1)}, bf16[256,512]{1,0:T(8,128)(2,1)S(1)}, u32[]{:S(2)}, u32[]{:S(2)}) collective-permute-start(bf16[256,512]{1,0:T(8,128)(2,1)S(1)} %convert_element_type.9), channel_id=1, source_target_pairs={{0,4},{4,8},{8,12},{12,16},{16,20},{20,24},{24,28},{28,0},{1,5},{5... | collective-permute-start | bytes 786440 | tf_op jit(solution)/shard_map/ppermute | solution.py:1132
  33.0 12.9 %collective-permute-start.10 = (bf16[8,64,512]{2,1,0:T(8,128)(2,1)S(1)}, bf16[8,64,512]{2,1,0:T(8,128)(2,1)S(1)}, u32[]{:S(2)}, u32[]{:S(2)}) collective-permute-start(bf16[8,64,512]{2,1,0:T(8,128)(2,1)S(1)} %bitcast.69), channel_id=1, source_target_pairs={{0,1},{1,0},{2,3},{3,2},{4,5},{5,4},{6,7},{7,6},{8,9},{9,8},{10,11... | collective-permute-start | bytes 1572872 | tf_op jit(solution)/shard_map/ppermute | solution.py:874
  42.3 3.6 %collective-permute-start.11 = (bf16[8,64,512]{2,1,0:T(8,128)(2,1)S(1)}, bf16[8,64,512]{2,1,0:T(8,128)(2,1)S(1)}, u32[]{:S(2)}, u32[]{:S(2)}) collective-permute-start(bf16[8,64,512]{2,1,0:T(8,128)(2,1)S(1)} %bitcast.80), channel_id=1, source_target_pairs={{0,1},{1,0},{2,3},{3,2},{4,5},{5,4},{6,7},{7,6},{8,9},{9,8},{10,11... | collective-permute-start | bytes 1572872 | tf_op jit(solution)/shard_map/ppermute | solution.py:874
  42.4 10.8 %collective-permute-start.8 = (bf16[2,2,64,640]{3,2,1,0:T(8,128)(2,1)S(1)}, bf16[2,2,64,640]{3,2,1,0:T(8,128)(2,1)}, u32[]{:S(2)}, u32[]{:S(2)}) collective-permute-start(bf16[2,2,64,640]{3,2,1,0:T(8,128)(2,1)S(1)} %fusion.3), channel_id=1, source_target_pairs={{0,4},{1,5},{2,6},{3,7},{4,0},{5,1},{6,2},{7,3},{8,12},{9,13},{10,... | collective-permute-start | bytes 983048 | tf_op jit(solution)/shard_map/ppermute | solution.py:874
  44.8 8.5 %collective-permute-start.9 = (bf16[2,2,64,512]{3,2,1,0:T(8,128)(2,1)S(1)}, bf16[2,2,64,512]{3,2,1,0:T(8,128)(2,1)S(1)}, u32[]{:S(2)}, u32[]{:S(2)}) collective-permute-start(bf16[2,2,64,512]{3,2,1,0:T(8,128)(2,1)S(1)} %pad_maximum_fusion.4), channel_id=1, source_target_pairs={{0,2},{1,3},{2,0},{3,1},{4,6},{5,7},{6,4},{7,5},{8,10},{9,11},{10,... | collective-permute-start | bytes 786440 | tf_op jit(solution)/shard_map/ppermute | solution.py:874
  54.4 16.5 %collective-permute-start.14 = (bf16[8,64,640]{2,1,0:T(8,128)(2,1)S(1)}, bf16[8,64,640]{2,1,0:T(8,128)(2,1)S(1)}, u32[]{:S(2)}, u32[]{:S(2)}) collective-permute-start(bf16[8,64,640]{2,1,0:T(8,128)(2,1)S(1)} %bitcast.65), channel_id=1, source_target_pairs={{0,1},{1,0},{2,3},{3,2},{4,5},{5,4},{6,7},{7,6},{8,9},{9,8},{10,11... | collective-permute-start | bytes 1966088 | tf_op jit(solution)/shard_map/ppermute | solution.py:874
  54.4 17.1 %collective-permute-start.12 = (bf16[2,2,2,64,640]{4,3,2,1,0:T(8,128)(2,1)S(1)}, bf16[2,2,2,64,640]{4,3,2,1,0:T(8,128)(2,1)S(1)}, u32[]{:S(2)}, u32[]{:S(2)}) collective-permute-start(bf16[2,2,2,64,640]{4,3,2,1,0:T(8,128)(2,1)S(1)} %pad_maximum_fusion), channel_id=1, source_target_pairs={{0,2},{1,3},{2,0},{3,1},{4,6},{5,7},{6,4},{7,5},{8,10},{9,11},{10,... | collective-permute-start | bytes 1966088 | tf_op jit(solution)/shard_map/ppermute | solution.py:874
  56.0 14.8 %collective-permute-start.15 = (bf16[8,64,512]{2,1,0:T(8,128)(2,1)S(1)}, bf16[8,64,512]{2,1,0:T(8,128)(2,1)S(1)}, u32[]{:S(2)}, u32[]{:S(2)}) collective-permute-start(bf16[8,64,512]{2,1,0:T(8,128)(2,1)S(1)} %bitcast.67), channel_id=1, source_target_pairs={{0,1},{1,0},{2,3},{3,2},{4,5},{5,4},{6,7},{7,6},{8,9},{9,8},{10,11... | collective-permute-start | bytes 1572872 | tf_op jit(solution)/shard_map/ppermute | solution.py:874
  56.2 14.6 %collective-permute-start.13 = (bf16[2,2,2,64,512]{4,3,2,1,0:T(8,128)(2,1)S(1)}, bf16[2,2,2,64,512]{4,3,2,1,0:T(8,128)(2,1)}, u32[]{:S(2)}, u32[]{:S(2)}) collective-permute-start(bf16[2,2,2,64,512]{4,3,2,1,0:T(8,128)(2,1)S(1)} %pad_maximum_fusion.2), channel_id=1, source_target_pairs={{0,4},{1,5},{2,6},{3,7},{4,0},{5,1},{6,2},{7,3},{8,12},{9,13},{10,... | collective-permute-start | bytes 1572872 | tf_op jit(solution)/shard_map/ppermute | solution.py:874
  71.6 3.1 %collective-permute-start.16 = (bf16[8,64,640]{2,1,0:T(8,128)(2,1)S(1)}, bf16[8,64,640]{2,1,0:T(8,128)(2,1)S(1)}, u32[]{:S(2)}, u32[]{:S(2)}) collective-permute-start(bf16[8,64,640]{2,1,0:T(8,128)(2,1)S(1)} %bitcast.77), channel_id=1, source_target_pairs={{0,1},{1,0},{2,3},{3,2},{4,5},{5,4},{6,7},{7,6},{8,9},{9,8},{10,11... | collective-permute-start | bytes 1966088 | tf_op jit(solution)/shard_map/ppermute | solution.py:874
  71.6 3.1 %collective-permute-start.17 = (bf16[8,64,512]{2,1,0:T(8,128)(2,1)}, bf16[8,64,512]{2,1,0:T(8,128)(2,1)S(1)}, u32[]{:S(2)}, u32[]{:S(2)}) collective-permute-start(bf16[8,64,512]{2,1,0:T(8,128)(2,1)} %bitcast.33.b_1), channel_id=1, source_target_pairs={{0,1},{1,0},{2,3},{3,2},{4,5},{5,4},{6,7},{7,6},{8,9},{9,8},{10,11... | collective-permute-start | bytes 1572872 | tf_op jit(solution)/shard_map/ppermute | solution.py:874
  95.7 5.2 %collective-permute-start.18 = (bf16[16,64,384]{2,1,0:T(8,128)(2,1)}, bf16[16,64,384]{2,1,0:T(8,128)(2,1)S(1)}, u32[]{:S(2)}, u32[]{:S(2)}) collective-permute-start(bf16[16,64,384]{2,1,0:T(8,128)(2,1)} %get-tuple-element.229), channel_id=1, source_target_pairs={{0,1},{1,0},{2,3},{3,2},{4,5},{5,4},{6,7},{7,6},{8,9},{9,8},{10,11... | collective-permute-start | bytes 2359304 | tf_op jit(solution)/shard_map/ppermute | solution.py:874
  95.9 5.0 %collective-permute-start.19 = (bf16[16,64,384]{2,1,0:T(8,128)(2,1)}, bf16[16,64,384]{2,1,0:T(8,128)(2,1)S(1)}, u32[]{:S(2)}, u32[]{:S(2)}) collective-permute-start(bf16[16,64,384]{2,1,0:T(8,128)(2,1)} %get-tuple-element.231), channel_id=1, source_target_pairs={{0,1},{1,0},{2,3},{3,2},{4,5},{5,4},{6,7},{7,6},{8,9},{9,8},{10,11... | collective-permute-start | bytes 2359304 | tf_op jit(solution)/shard_map/ppermute | solution.py:874
  96.3 4.6 %collective-permute-start.20 = (bf16[16,64,384]{2,1,0:T(8,128)(2,1)}, bf16[16,64,384]{2,1,0:T(8,128)(2,1)S(1)}, u32[]{:S(2)}, u32[]{:S(2)}) collective-permute-start(bf16[16,64,384]{2,1,0:T(8,128)(2,1)} %get-tuple-element.233), channel_id=1, source_target_pairs={{0,1},{1,0},{2,3},{3,2},{4,5},{5,4},{6,7},{7,6},{8,9},{9,8},{10,11... | collective-permute-start | bytes 2359304 | tf_op jit(solution)/shard_map/ppermute | solution.py:874
  104.9 11.7 %collective-permute-start.21 = (bf16[8,64,384]{2,1,0:T(8,128)(2,1)}, bf16[8,64,384]{2,1,0:T(8,128)(2,1)S(1)}, u32[]{:S(2)}, u32[]{:S(2)}) collective-permute-start(bf16[8,64,384]{2,1,0:T(8,128)(2,1)} %get-tuple-element.245), channel_id=1, source_target_pairs={{0,2},{1,3},{2,0},{3,1},{4,6},{5,7},{6,4},{7,5},{8,10},{9,11},{10,... | collective-permute-start | bytes 1179656 | tf_op jit(solution)/shard_map/ppermute | solution.py:874
  106.5 11.3 %collective-permute-start.22 = (bf16[8,64,384]{2,1,0:T(8,128)(2,1)}, bf16[8,64,384]{2,1,0:T(8,128)(2,1)S(1)}, u32[]{:S(2)}, u32[]{:S(2)}) collective-permute-start(bf16[8,64,384]{2,1,0:T(8,128)(2,1)} %get-tuple-element.246), channel_id=1, source_target_pairs={{0,4},{1,5},{2,6},{3,7},{4,0},{5,1},{6,2},{7,3},{8,12},{9,13},{10,... | collective-permute-start | bytes 1179656 | tf_op jit(solution)/shard_map/ppermute | solution.py:874
  107.2 11.0 %collective-permute-start.23 = (bf16[8,64,384]{2,1,0:T(8,128)(2,1)}, bf16[8,64,384]{2,1,0:T(8,128)(2,1)S(1)}, u32[]{:S(2)}, u32[]{:S(2)}) collective-permute-start(bf16[8,64,384]{2,1,0:T(8,128)(2,1)} %get-tuple-element.247), channel_id=1, source_target_pairs={{0,8},{1,9},{2,10},{3,11},{4,12},{5,13},{6,14},{7,15},{8,0},{9,1},... | collective-permute-start | bytes 1179656 | tf_op jit(solution)/shard_map/ppermute | solution.py:874
  122.4 15.3 %collective-permute-start.24 = (bf16[4,64,384]{2,1,0:T(8,128)(2,1)}, bf16[4,64,384]{2,1,0:T(8,128)(2,1)S(1)}, u32[]{:S(2)}, u32[]{:S(2)}) collective-permute-start(bf16[4,64,384]{2,1,0:T(8,128)(2,1)} %get-tuple-element.255), channel_id=1, source_target_pairs={{0,4},{1,5},{2,6},{3,7},{4,0},{5,1},{6,2},{7,3},{8,12},{9,13},{10,... | collective-permute-start | bytes 589832 | tf_op jit(solution)/shard_map/ppermute | solution.py:874
  123.4 14.3 %collective-permute-start.25 = (bf16[4,64,384]{2,1,0:T(8,128)(2,1)}, bf16[4,64,384]{2,1,0:T(8,128)(2,1)S(1)}, u32[]{:S(2)}, u32[]{:S(2)}) collective-permute-start(bf16[4,64,384]{2,1,0:T(8,128)(2,1)} %get-tuple-element.256), channel_id=1, source_target_pairs={{0,8},{1,9},{2,10},{3,11},{4,12},{5,13},{6,14},{7,15},{8,0},{9,1},... | collective-permute-start | bytes 589832 | tf_op jit(solution)/shard_map/ppermute | solution.py:874
  124.5 13.2 %collective-permute-start.26 = (bf16[4,64,384]{2,1,0:T(8,128)(2,1)}, bf16[4,64,384]{2,1,0:T(8,128)(2,1)S(1)}, u32[]{:S(2)}, u32[]{:S(2)}) collective-permute-start(bf16[4,64,384]{2,1,0:T(8,128)(2,1)} %get-tuple-element.257), channel_id=1, source_target_pairs={{0,2},{1,3},{2,0},{3,1},{4,6},{5,7},{6,4},{7,5},{8,10},{9,11},{10,... | collective-permute-start | bytes 589832 | tf_op jit(solution)/shard_map/ppermute | solution.py:874
  137.7 2.2 %collective-permute-start.27 = (bf16[16,64,256]{2,1,0:T(8,128)(2,1)}, bf16[16,64,256]{2,1,0:T(8,128)(2,1)S(1)}, u32[]{:S(2)}, u32[]{:S(2)}) collective-permute-start(bf16[16,64,256]{2,1,0:T(8,128)(2,1)} %get-tuple-element.270), channel_id=1, source_target_pairs={{0,1},{1,0},{2,3},{3,2},{4,5},{5,4},{6,7},{7,6},{8,9},{9,8},{10,11... | collective-permute-start | bytes 1572872 | tf_op jit(solution)/shard_map/ppermute | solution.py:874
  137.8 2.9 %collective-permute-start.28 = (bf16[16,64,256]{2,1,0:T(8,128)(2,1)}, bf16[16,64,256]{2,1,0:T(8,128)(2,1)S(1)}, u32[]{:S(2)}, u32[]{:S(2)}) collective-permute-start(bf16[16,64,256]{2,1,0:T(8,128)(2,1)} %get-tuple-element.272), channel_id=1, source_target_pairs={{0,1},{1,0},{2,3},{3,2},{4,5},{5,4},{6,7},{7,6},{8,9},{9,8},{10,11... | collective-permute-start | bytes 1572872 | tf_op jit(solution)/shard_map/ppermute | solution.py:874
  142.9 9.2 %collective-permute-start.29 = (bf16[8,64,256]{2,1,0:T(8,128)(2,1)S(1)}, bf16[8,64,256]{2,1,0:T(8,128)(2,1)S(1)}, u32[]{:S(2)}, u32[]{:S(2)}) collective-permute-start(bf16[8,64,256]{2,1,0:T(8,128)(2,1)S(1)} %get-tuple-element.282), channel_id=1, source_target_pairs={{0,2},{1,3},{2,0},{3,1},{4,6},{5,7},{6,4},{7,5},{8,10},{9,11},{10,... | collective-permute-start | bytes 786440 | tf_op jit(solution)/shard_map/ppermute | solution.py:874
  143.8 9.1 %collective-permute-start.30 = (bf16[8,64,256]{2,1,0:T(8,128)(2,1)S(1)}, bf16[8,64,256]{2,1,0:T(8,128)(2,1)S(1)}, u32[]{:S(2)}, u32[]{:S(2)}) collective-permute-start(bf16[8,64,256]{2,1,0:T(8,128)(2,1)S(1)} %get-tuple-element.284), channel_id=1, source_target_pairs={{0,4},{1,5},{2,6},{3,7},{4,0},{5,1},{6,2},{7,3},{8,12},{9,13},{10,... | collective-permute-start | bytes 786440 | tf_op jit(solution)/shard_map/ppermute | solution.py:874
  145.0 8.1 %collective-permute-start.31 = (bf16[2,64,384]{2,1,0:T(8,128)(2,1)S(1)}, bf16[2,64,384]{2,1,0:T(8,128)(2,1)S(1)}, u32[]{:S(2)}, u32[]{:S(2)}) collective-permute-start(bf16[2,64,384]{2,1,0:T(8,128)(2,1)S(1)} %get-tuple-element.298), channel_id=1, source_target_pairs={{0,8},{1,9},{2,10},{3,11},{4,12},{5,13},{6,14},{7,15},{8,0},{9,1},... | collective-permute-start | bytes 294920 | tf_op jit(solution)/shard_map/ppermute | solution.py:874
  146.0 7.4 %collective-permute-start.32 = (bf16[2,64,384]{2,1,0:T(8,128)(2,1)S(1)}, bf16[2,64,384]{2,1,0:T(8,128)(2,1)S(1)}, u32[]{:S(2)}, u32[]{:S(2)}) collective-permute-start(bf16[2,64,384]{2,1,0:T(8,128)(2,1)S(1)} %get-tuple-element.300), channel_id=1, source_target_pairs={{0,2},{1,3},{2,0},{3,1},{4,6},{5,7},{6,4},{7,5},{8,10},{9,11},{10,... | collective-permute-start | bytes 294920 | tf_op jit(solution)/shard_map/ppermute | solution.py:874
  147.2 6.8 %collective-permute-start.33 = (bf16[2,64,384]{2,1,0:T(8,128)(2,1)S(1)}, bf16[2,64,384]{2,1,0:T(8,128)(2,1)S(1)}, u32[]{:S(2)}, u32[]{:S(2)}) collective-permute-start(bf16[2,64,384]{2,1,0:T(8,128)(2,1)S(1)} %get-tuple-element.302), channel_id=1, source_target_pairs={{0,4},{1,5},{2,6},{3,7},{4,0},{5,1},{6,2},{7,3},{8,12},{9,13},{10,... | collective-permute-start | bytes 294920 | tf_op jit(solution)/shard_map/ppermute | solution.py:874
  154.0 5.0 %collective-permute-start.34 = (bf16[4,64,256]{2,1,0:T(8,128)(2,1)S(1)}, bf16[4,64,256]{2,1,0:T(8,128)(2,1)S(1)}, u32[]{:S(2)}, u32[]{:S(2)}) collective-permute-start(bf16[4,64,256]{2,1,0:T(8,128)(2,1)S(1)} %get-tuple-element.303), channel_id=1, source_target_pairs={{0,4},{1,5},{2,6},{3,7},{4,0},{5,1},{6,2},{7,3},{8,12},{9,13},{10,... | collective-permute-start | bytes 393224 | tf_op jit(solution)/shard_map/ppermute | solution.py:874
  155.0 5.0 %collective-permute-start.35 = (bf16[4,64,256]{2,1,0:T(8,128)(2,1)S(1)}, bf16[4,64,256]{2,1,0:T(8,128)(2,1)S(1)}, u32[]{:S(2)}, u32[]{:S(2)}) collective-permute-start(bf16[4,64,256]{2,1,0:T(8,128)(2,1)S(1)} %get-tuple-element.305), channel_id=1, source_target_pairs={{0,2},{1,3},{2,0},{3,1},{4,6},{5,7},{6,4},{7,5},{8,10},{9,11},{10,... | collective-permute-start | bytes 393224 | tf_op jit(solution)/shard_map/ppermute | solution.py:874
  160.0 27.8 %copy-start.12 = (f32[64,896]{1,0:T(8,128)S(1)}, f32[64,896]{1,0:T(8,128)}, u32[]{:S(2)}) copy-start(f32[64,896]{1,0:T(8,128)} %refs_7_.1) | copy-start | bytes 688132
  160.0 27.8 %copy-start.13 = (f32[640,64]{0,1:T(8,128)S(1)}, f32[640,64]{0,1:T(8,128)}, u32[]{:S(2)}) copy-start(f32[640,64]{0,1:T(8,128)} %param.40) | copy-start | bytes 491524
  160.0 27.8 %copy-start.14 = (f32[640,64]{0,1:T(8,128)S(1)}, f32[640,64]{0,1:T(8,128)}, u32[]{:S(2)}) copy-start(f32[640,64]{0,1:T(8,128)} %param.44) | copy-start | bytes 491524
  160.2 6.6 %collective-permute-start.36 = (bf16[2,64,512]{2,1,0:T(8,128)(2,1)S(1)}, bf16[2,64,512]{2,1,0:T(8,128)(2,1)S(1)}, u32[]{:S(2)}, u32[]{:S(2)}) collective-permute-start(bf16[2,64,512]{2,1,0:T(8,128)(2,1)S(1)} %get-tuple-element.307), channel_id=1, source_target_pairs={{0,8},{1,9},{2,10},{3,11},{4,12},{5,13},{6,14},{7,15},{8,0},{9,1},... | collective-permute-start | bytes 393224 | tf_op jit(solution)/shard_map/ppermute | solution.py:874
  161.3 8.9 %collective-permute-start.38 = (bf16[1,64,1152]{2,1,0:T(8,128)(2,1)S(1)}, bf16[1,64,1152]{2,1,0:T(8,128)(2,1)S(1)}, u32[]{:S(2)}, u32[]{:S(2)}) collective-permute-start(bf16[1,64,1152]{2,1,0:T(8,128)(2,1)S(1)} %get-tuple-element.317), channel_id=1, source_target_pairs={{0,16},{1,17},{2,18},{3,19},{4,20},{5,21},{6,22},{7,23},{8,24},{9,... | collective-permute-start | bytes 442376 | tf_op jit(solution)/shard_map/ppermute | solution.py:874
  166.8 5.3 %collective-permute-start.37 = (bf16[1,64,512]{2,1,0:T(8,128)(2,1)S(1)}, bf16[1,64,512]{2,1,0:T(8,128)(2,1)S(1)}, u32[]{:S(2)}, u32[]{:S(2)}) collective-permute-start(bf16[1,64,512]{2,1,0:T(8,128)(2,1)S(1)} %get-tuple-element.309), channel_id=1, source_target_pairs={{0,16},{1,17},{2,18},{3,19},{4,20},{5,21},{6,22},{7,23},{8,24},{9,... | collective-permute-start | bytes 196616 | tf_op jit(solution)/shard_map/ppermute | solution.py:874
  172.4 1.2 collective-permute-start.39
  173.6 4.4 %collective-permute-start.42 = (f32[1,128]{1,0:T(1,128)S(1)}, f32[1,128]{1,0:T(1,128)S(1)}, u32[]{:S(2)}, u32[]{:S(2)}) collective-permute-start(f32[1,128]{1,0:T(1,128)S(1)} %add.63), channel_id=1, source_target_pairs={{0,6},{1,7},{2,4},{3,5},{4,2},{5,3},{6,0},{7,1},{8,14},{9,15},{10,... | collective-permute-start | bytes 1544 | tf_op jit(solution)/shard_map/ppermute | solution.py:1053
  175.2 3.5 %collective-permute-start.41 = (f32[1,128]{1,0:T(1,128)S(1)}, f32[1,128]{1,0:T(1,128)S(1)}, u32[]{:S(2)}, u32[]{:S(2)}) collective-permute-start(f32[1,128]{1,0:T(1,128)S(1)} %add.63), channel_id=1, source_target_pairs={{0,4},{1,5},{2,6},{3,7},{4,0},{5,1},{6,2},{7,3},{8,12},{9,13},{10,... | collective-permute-start | bytes 1544 | tf_op jit(solution)/shard_map/ppermute | solution.py:1053
  176.2 3.5 %collective-permute-start.40 = (f32[1,128]{1,0:T(1,128)S(1)}, f32[1,128]{1,0:T(1,128)S(1)}, u32[]{:S(2)}, u32[]{:S(2)}) collective-permute-start(f32[1,128]{1,0:T(1,128)S(1)} %add.63), channel_id=1, source_target_pairs={{0,2},{1,3},{2,0},{3,1},{4,6},{5,7},{6,4},{7,5},{8,10},{9,11},{10,... | collective-permute-start | bytes 1544 | tf_op jit(solution)/shard_map/ppermute | solution.py:1053
  179.8 3.5 %collective-permute-start.43 = (f32[1,128]{1,0:T(1,128)S(1)}, f32[1,128]{1,0:T(1,128)S(1)}, u32[]{:S(2)}, u32[]{:S(2)}) collective-permute-start(f32[1,128]{1,0:T(1,128)S(1)} %add_add_fusion), channel_id=1, source_target_pairs={{0,8},{1,9},{2,10},{3,11},{4,12},{5,13},{6,14},{7,15},{8,0},{9,1},... | collective-permute-start | bytes 1544 | tf_op jit(solution)/shard_map/ppermute | solution.py:1053
  183.3 4.4 %collective-permute-start.44 = (f32[1,128]{1,0:T(1,128)S(1)}, f32[1,128]{1,0:T(1,128)S(1)}, u32[]{:S(2)}, u32[]{:S(2)}) collective-permute-start(f32[1,128]{1,0:T(1,128)S(1)} %add.67), channel_id=1, source_target_pairs={{0,16},{1,17},{2,18},{3,19},{4,20},{5,21},{6,22},{7,23},{8,24},{9,... | collective-permute-start | bytes 1544 | tf_op jit(solution)/shard_map/ppermute | solution.py:1053
  (50 other events, 646.3 us)

commit v4 on v3

--- a/solution.py
+++ b/solution.py
@@ -125,13 +125,14 @@
     nodes, width = pull_ref.shape
     step = 64
     leave = Leaving(sems)
+    across = across_ref[...]
 
     def count_across(i, _):
         at = pl.multiple_of(i * 128, 128)
         rows = lax.broadcasted_iota(jnp.int32, (128, width), 0) + at
         total = jnp.zeros((128, width), F32)
         for k in range(KD):
-            total = total + jnp.where(across_ref[k : k + 1, :] == rows, 1.0, 0.0)
+            total = total + jnp.where(across[k : k + 1, :] == rows, 1.0, 0.0)
         pull_ref[pl.ds(at, 128), :] = total.astype(BF)
         pool_ref[:, pl.ds(at, 128)] = total.T.astype(BF)
         return 0

time: 194 us -> 194 us (level)
  no operation moved by 1% of the time
where the time goes in v4:
time: 194 us; the launch traced here: 190 us
  Pallas kernels  83.5 us (43%)
  waiting for transfers between devices  44.2 us (23%)
  starting transfers between devices  42.2 us (22%)
  local copies, waits for them, and re-layouts  12.5 us (6%)
  other arithmetic  4.91 us (3%)
  between operations  3.06 us (2%)
    ppermute x37, starting transfers between devices, swap(): lax.ppermute(array, ('wide', 'narrow'), [(i, i ^ 1 << bit) for i in range...  36.1 us
    ppermute x37, waiting for transfers between devices, swap(): lax.ppermute(array, ('wide', 'narrow'), [(i, i ^ 1 << bit) for i in range...  30.4 us
    pallas_call x1, Pallas kernels, feed(): pl.pallas_call(feed_kernel, in_specs=[pl.BlockSpec(memory_space=pltpu.SME...  20.1 us
    pallas_call x1, Pallas kernels, attend(): pl.pallas_call(attend_kernel, in_specs=[outside] * 3, out_specs=[outside]...  13.9 us
    pallas_call x2, Pallas kernels, unmix(): pl.pallas_call(functools.partial(unmix_kernel, first), grid=(heads,), in_...  12.3 us
    pallas_call x1, Pallas kernels, give_back(): pl.pallas_call(return_kernel, in_specs=[pl.BlockSpec(memory_space=pltpu.S...  11.9 us
    ppermute x6, waiting for transfers between devices, sum_all(): lax.ppermute(row, ('wide', 'narrow'), [(i, i ^ mask << bit) for i in rang...  11.7 us
    unnamed x107, local copies, waits for them, and re-layouts  7.26 us
  transfers between devices with their start and end apart: 45, of which 27 were waited for; matrix products, arithmetic and copies ran while one was open for 4% of the time, Pallas kernels for 28%

profile of v4, /device:TPU:0, one launch (start us, length us, event | category | flops | bytes accessed | tf_op | source)
XLA Modules:
  0.0 190.4 jit_solution(14985888898881111933)
XLA Ops:
  0.7 1.9 pack.1
  2.6 4.1 %collective-permute-start = (bf16[64,512]{1,0:T(8,128)(2,1)}, bf16[64,512]{1,0:T(8,128)(2,1)S(1)}, u32[]{:S(2)}, u32[]{:S(2)}) collective-permute-start(bf16[64,512]{1,0:T(8,128)(2,1)} %get-tuple-element.182), channel_id=1, source_target_pairs={{0,16},{1,17},{2,18},{3,19},{4,20},{5,21},{6,22},{7,23},{8,24},{9,... | collective-permute-start | bytes 196616 | tf_op jit(solution)/shard_map/ppermute | solution.py:875
  7.4 3.1 %collective-permute-done = bf16[64,512]{1,0:T(8,128)(2,1)S(1)} collective-permute-done((bf16[64,512]{1,0:T(8,128)(2,1)}, bf16[64,512]{1,0:T(8,128)(2,1)S(1)}, u32[]{:S(2)}, u32[]{:S(2)}) %collective-permute-start) | collective-permute-done | bytes 65568 | tf_op jit(solution)/shard_map/ppermute | solution.py:875
  14.9 1.4 copy.48
  17.2 3.3 %collective-permute-start.3 = (bf16[64,1152]{1,0:T(8,128)(2,1)S(1)}, bf16[64,1152]{1,0:T(8,128)(2,1)S(1)}, u32[]{:S(2)}, u32[]{:S(2)}) collective-permute-start(bf16[64,1152]{1,0:T(8,128)(2,1)S(1)} %copy-done.47), channel_id=1, source_target_pairs={{0,16},{1,17},{2,18},{3,19},{4,20},{5,21},{6,22},{7,23},{8,24},{9,... | collective-permute-start | bytes 442376 | tf_op jit(solution)/shard_map/ppermute | solution.py:875
  20.5 1.5 collective-permute-start.2
  22.8 2.4 %grid_sums.1.sums_ref = f32[256,512]{1,0:T(8,128)S(1)} custom-call(bf16[256,896]{1,0:T(8,128)(2,1)S(1)} %fusion.2.grid_ref, s32[8,512]{1,0:T(8,128)S(1)} %subtract_bitcast_fusion.pixels_ref), custom_call_target="tpu_custom_call" | custom-call | flops 1000 | bytes 1000 | tf_op jit(solution)/shard_map/grid_sums/pallas_call | solution.py:114
  25.3 1.6 collective-permute-done.3
  28.3 1.5 collective-permute-start.5
  29.8 2.5 %collective-permute-start.7 = (bf16[256,512]{1,0:T(8,128)(2,1)S(1)}, bf16[256,512]{1,0:T(8,128)(2,1)S(1)}, u32[]{:S(2)}, u32[]{:S(2)}) collective-permute-start(bf16[256,512]{1,0:T(8,128)(2,1)S(1)} %convert_element_type.9), channel_id=1, source_target_pairs={{4,0},{8,4},{12,8},{16,12},{20,16},{24,20},{28,24},{0,28},{5,1},{9... | collective-permute-start | bytes 786440 | tf_op jit(solution)/shard_map/ppermute | solution.py:1133
  33.0 7.2 %counts.1 = (f32[2,1280,256]{2,1,0:T(8,128)}, bf16[896,512]{1,0:T(8,128)(2,1)}, bf16[512,896]{1,0:T(8,128)(2,1)}) custom-call(s32[16,512]{1,0:T(8,128)} %fusion.5.slots_ref, s32[3,896]{1,0:T(4,128)} %pad.9.across_ref), custom_call_target="tpu_custom_call" | custom-call | flops 1000 | bytes 1000 | tf_op jit(solution)/shard_map/counts/pallas_call | solution.py:175
  40.3 2.0 %collective-permute-done.6.before_ref = bf16[256,512]{1,0:T(8,128)(2,1)S(1)} collective-permute-done((bf16[256,512]{1,0:T(8,128)(2,1)S(1)}, bf16[256,512]{1,0:T(8,128)(2,1)S(1)}, u32[]{:S(2)}, u32[]{:S(2)}) %collective-permute-start.6) | collective-permute-done | bytes 262176 | tf_op jit(solution)/shard_map/ppermute | solution.py:1133
  42.4 2.4 %collective-permute-start.8 = (bf16[2,2,64,640]{3,2,1,0:T(8,128)(2,1)S(1)}, bf16[2,2,64,640]{3,2,1,0:T(8,128)(2,1)}, u32[]{:S(2)}, u32[]{:S(2)}) collective-permute-start(bf16[2,2,64,640]{3,2,1,0:T(8,128)(2,1)S(1)} %fusion.3), channel_id=1, source_target_pairs={{0,4},{1,5},{2,6},{3,7},{4,0},{5,1},{6,2},{7,3},{8,12},{9,13},{10,... | collective-permute-start | bytes 983048 | tf_op jit(solution)/shard_map/ppermute | solution.py:875
  47.5 5.7 %encode.1 = (f32[512,512]{1,0:T(8,128)}, bf16[1536,512]{1,0:T(8,128)(2,1)}, bf16[1536,512]{1,0:T(8,128)(2,1)}, bf16[8,4,64,512]{3,2,1,0:T(8,128)(2,1)}) custom-call(s32[3]{0:T(128)} %pad_add_fusion.place_ref, bf16[8,64,512]{2,1,0:T(8,128)(2,1)} %bitcast.70, bf16[8,64,512]{2,1,0:T(8,128)(2,1)} %bitcast.81, bf16[8,64,512]{2,1,0:T(8,128)(2,1)} %copy-done.42, ...), custom_call_target="tpu_custom_call" | custom-call | flops 1000 | bytes 1000 | tf_op jit(solution)/shard_map/encode/pallas_call | solution.py:268
  53.2 1.0 pad_maximum_fusion
  54.4 1.6 collective-permute-start.12
  56.9 13.9 %attend.1 = (f32[512,512]{1,0:T(8,128)}, bf16[4,1536,512]{2,1,0:T(8,128)(2,1)}, bf16[512,512]{1,0:T(8,128)(2,1)}, bf16[4,1536,256]{2,1,0:T(8,128)(2,1)}, f32[8,512]{1,0:T(8,128)}) custom-call(bf16[1536,512]{1,0:T(8,128)(2,1)} %get-tuple-element.213.normed_in, bf16[8,4,64,512]{3,2,1,0:T(8,128)(2,1)} %get-tuple-element.214.early_in.early_ref, ...), custom_call_target="tpu_custom_call" | custom-call | flops 1000 | bytes 1000 | tf_op jit(solution)/shard_map/attend/pallas_call | solution.py:342
  75.6 20.1 %feed.1 = (bf16[16,64,384]{2,1,0:T(8,128)(2,1)}, bf16[16,64,384]{2,1,0:T(8,128)(2,1)}, bf16[16,64,384]{2,1,0:T(8,128)(2,1)}, bf16[16,64,384]{2,1,0:T(8,128)(2,1)...) custom-call(s32[3]{0:T(128)} %pad_add_fusion.place_ref, ...), custom_call_target="tpu_custom_call" | custom-call | flops 1000 | bytes 1000 | tf_op jit(solution)/shard_map/feed/pallas_call | solution.py:526
  96.4 4.5 %unmix.2 = (bf16[512,128]{1,0:T(8,128)(2,1)}, bf16[1536,256]{1,0:T(8,128)(2,1)}) custom-call(bf16[4,1536,512]{2,1,0:T(8,128)(2,1)} %get-tuple-element.238.probs_ref, bf16[512,512]{1,0:T(8,128)(2,1)} %get-tuple-element.252.query_ref, bf16[4,1536,256]{2,1,0:T(8,128)(2,1)} %get-tuple-element.239.keys_ref.values_ref, ...), custom_call_target="tpu_custom_call" | custom-call | flops 1000 | bytes 1000 | tf_op jit(solution)/shard_map/unmix/pallas_call | solution.py:589
  102.3 2.6 %halve_far.2 = (bf16[8,64,384]{2,1,0:T(8,128)(2,1)}, bf16[8,64,384]{2,1,0:T(8,128)(2,1)}, bf16[8,64,384]{2,1,0:T(8,128)(2,1)}) custom-call(bf16[16,64,384]{2,1,0:T(8,128)(2,1)} %get-tuple-element.228.refs_0_, bf16[16,64,384]{2,1,0:T(8,128)(2,1)} %copy-done.25, bf16[16,64,384]{2,1,0:T(8,128)(2,1)} %get-tuple-element.230.refs_2_.refs_3_, ...), custom_call_target="tpu_custom_call" | custom-call | flops 1000 | bytes 1000 | tf_op jit(solution)/shard_map/halve_far/pallas_call | solution.py:940
  104.9 1.6 collective-permute-start.21
  107.2 1.0 collective-permute-start.23
  108.3 7.8 %unmix.3 = (bf16[512,384]{1,0:T(8,128)(2,1)}, bf16[1536,768]{1,0:T(8,128)(2,1)}) custom-call(bf16[4,1536,512]{2,1,0:T(8,128)(2,1)} %get-tuple-element.238.probs_ref, bf16[512,512]{1,0:T(8,128)(2,1)} %get-tuple-element.252.query_ref, bf16[4,1536,256]{2,1,0:T(8,128)(2,1)} %get-tuple-element.239.keys_ref.values_ref, ...), custom_call_target="tpu_custom_call" | custom-call | flops 1000 | bytes 1000 | tf_op jit(solution)/shard_map/unmix/pallas_call | solution.py:589
  116.6 1.2 collective-permute-done.22.refs_5_
  119.3 3.1 %halve_far.3 = (bf16[4,64,384]{2,1,0:T(8,128)(2,1)}, bf16[4,64,384]{2,1,0:T(8,128)(2,1)}, bf16[4,64,384]{2,1,0:T(8,128)(2,1)}, f32[4,64,384]{2,1,0:T(8,128)}, f3...) custom-call(bf16[16,64,384]{2,1,0:T(8,128)(2,1)} %get-tuple-element.228.refs_0_, bf16[16,64,384]{2,1,0:T(8,128)(2,1)} %copy-done.25, ...), custom_call_target="tpu_custom_call" | custom-call | flops 1000 | bytes 1000 | tf_op jit(solution)/shard_map/halve_far/pallas_call | solution.py:940
  122.4 1.1 collective-permute-start.24
  123.4 1.0 collective-permute-start.25
  124.5 1.2 collective-permute-start.26
  125.7 11.9 %give_back.1 = (bf16[16,64,256]{2,1,0:T(8,128)(2,1)}, bf16[16,64,256]{2,1,0:T(8,128)(2,1)}, bf16[16,64,256]{2,1,0:T(8,128)(2,1)}, bf16[16,64,256]{2,1,0:T(8,128)(2,1)}) custom-call(s32[3]{0:T(128)} %pad_add_fusion.place_ref, bf16[8,4,64,512]{3,2,1,0:T(8,128)(2,1)} %get-tuple-element.214.early_in.early_ref, bf16[512,128]{1,0:T(8,128)(2,1)} %get-tuple-element.258.query_in_a, ...), custom_call_target="tpu_custom_call" | custom-call | flops 1000 | bytes 1000 | tf_op jit(solution)/shard_map/give_back/pallas_call | solution.py:697
  138.3 1.6 collective-permute-done.27.refs_1_
  140.6 1.0 copy-done.5
  141.7 1.0 copy-done.6
  145.0 1.0 collective-permute-start.31
  146.0 1.2 collective-permute-start.32
  147.2 1.0 collective-permute-start.33
  148.3 3.9 %collective-permute-done.29.refs_1_ = bf16[8,64,256]{2,1,0:T(8,128)(2,1)S(1)} collective-permute-done((bf16[8,64,256]{2,1,0:T(8,128)(2,1)S(1)}, bf16[8,64,256]{2,1,0:T(8,128)(2,1)S(1)}, u32[]{:S(2)}, u32[]{:S(2)}) %collective-permute-start.29) | collective-permute-done | bytes 262176 | tf_op jit(solution)/shard_map/ppermute | solution.py:875
  155.0 1.2 collective-permute-start.35
  156.2 2.8 %collective-permute-done.34.refs_1_ = bf16[4,64,256]{2,1,0:T(8,128)(2,1)S(1)} collective-permute-done((bf16[4,64,256]{2,1,0:T(8,128)(2,1)S(1)}, bf16[4,64,256]{2,1,0:T(8,128)(2,1)S(1)}, u32[]{:S(2)}, u32[]{:S(2)}) %collective-permute-start.34) | collective-permute-done | bytes 131104 | tf_op jit(solution)/shard_map/ppermute | solution.py:875
  160.2 1.0 collective-permute-start.36
  161.3 1.8 collective-permute-start.38
  163.1 3.7 %collective-permute-done.36.refs_1_ = bf16[2,64,512]{2,1,0:T(8,128)(2,1)S(1)} collective-permute-done((bf16[2,64,512]{2,1,0:T(8,128)(2,1)S(1)}, bf16[2,64,512]{2,1,0:T(8,128)(2,1)S(1)}, u32[]{:S(2)}, u32[]{:S(2)}) %collective-permute-start.36) | collective-permute-done | bytes 131104 | tf_op jit(solution)/shard_map/ppermute | solution.py:875
  166.9 3.3 %collective-permute-done.38.late_b = bf16[1,64,1152]{2,1,0:T(8,128)(2,1)S(1)} collective-permute-done((bf16[1,64,1152]{2,1,0:T(8,128)(2,1)S(1)}, bf16[1,64,1152]{2,1,0:T(8,128)(2,1)S(1)}, u32[]{:S(2)}, u32[]{:S(2)}) %collective-permute-start.38) | collective-permute-done | bytes 147488 | tf_op jit(solution)/shard_map/ppermute | solution.py:875
  170.2 1.9 %collective-permute-done.37.early_b = bf16[1,64,512]{2,1,0:T(8,128)(2,1)S(1)} collective-permute-done((bf16[1,64,512]{2,1,0:T(8,128)(2,1)S(1)}, bf16[1,64,512]{2,1,0:T(8,128)(2,1)S(1)}, u32[]{:S(2)}, u32[]{:S(2)}) %collective-permute-start.37) | collective-permute-done | bytes 65568 | tf_op jit(solution)/shard_map/ppermute | solution.py:875
  172.5 1.1 collective-permute-done.39
  173.6 1.7 collective-permute-start.42
  179.8 3.5 %collective-permute-done.43 = f32[1,128]{1,0:T(1,128)S(1)} collective-permute-done((f32[1,128]{1,0:T(1,128)S(1)}, f32[1,128]{1,0:T(1,128)S(1)}, u32[]{:S(2)}, u32[]{:S(2)}) %collective-permute-start.43) | collective-permute-done | bytes 544 | tf_op jit(solution)/shard_map/ppermute | solution.py:1054
  183.4 4.3 %collective-permute-done.44 = f32[1,128]{1,0:T(1,128)S(1)} collective-permute-done((f32[1,128]{1,0:T(1,128)S(1)}, f32[1,128]{1,0:T(1,128)S(1)}, u32[]{:S(2)}, u32[]{:S(2)}) %collective-permute-start.44) | collective-permute-done | bytes 544 | tf_op jit(solution)/shard_map/ppermute | solution.py:1054
  187.9 1.7 adam.1
  (197 shorter events, 34.2 us)
Async XLA Ops:
  2.6 8.0 %collective-permute-start = (bf16[64,512]{1,0:T(8,128)(2,1)}, bf16[64,512]{1,0:T(8,128)(2,1)S(1)}, u32[]{:S(2)}, u32[]{:S(2)}) collective-permute-start(bf16[64,512]{1,0:T(8,128)(2,1)} %get-tuple-element.182), channel_id=1, source_target_pairs={{0,16},{1,17},{2,18},{3,19},{4,20},{5,21},{6,22},{7,23},{8,24},{9,... | collective-permute-start | bytes 196616 | tf_op jit(solution)/shard_map/ppermute | solution.py:875
  11.4 5.0 %collective-permute-start.1 = (bf16[2,64,512]{2,1,0:T(8,128)(2,1)S(1)}, bf16[2,64,512]{2,1,0:T(8,128)(2,1)S(1)}, u32[]{:S(2)}, u32[]{:S(2)}) collective-permute-start(bf16[2,64,512]{2,1,0:T(8,128)(2,1)S(1)} %pad_maximum_fusion.6), channel_id=1, source_target_pairs={{0,8},{1,9},{2,10},{3,11},{4,12},{5,13},{6,14},{7,15},{8,0},{9,1},... | collective-permute-start | bytes 393224 | tf_op jit(solution)/shard_map/ppermute | solution.py:875
  17.2 9.6 %collective-permute-start.3 = (bf16[64,1152]{1,0:T(8,128)(2,1)S(1)}, bf16[64,1152]{1,0:T(8,128)(2,1)S(1)}, u32[]{:S(2)}, u32[]{:S(2)}) collective-permute-start(bf16[64,1152]{1,0:T(8,128)(2,1)S(1)} %copy-done.47), channel_id=1, source_target_pairs={{0,16},{1,17},{2,18},{3,19},{4,20},{5,21},{6,22},{7,23},{8,24},{9,... | collective-permute-start | bytes 442376 | tf_op jit(solution)/shard_map/ppermute | solution.py:875
  20.5 7.3 %collective-permute-start.2 = (bf16[2,2,64,512]{3,2,1,0:T(8,128)(2,1)S(1)}, bf16[2,2,64,512]{3,2,1,0:T(8,128)(2,1)S(1)}, u32[]{:S(2)}, u32[]{:S(2)}) collective-permute-start(bf16[2,2,64,512]{3,2,1,0:T(8,128)(2,1)S(1)} %pad_maximum_fusion.5), channel_id=1, source_target_pairs={{0,4},{1,5},{2,6},{3,7},{4,0},{5,1},{6,2},{7,3},{8,12},{9,13},{10,... | collective-permute-start | bytes 786440 | tf_op jit(solution)/shard_map/ppermute | solution.py:875
  27.9 12.2 %collective-permute-start.4 = (bf16[2,64,1152]{2,1,0:T(8,128)(2,1)S(1)}, bf16[2,64,1152]{2,1,0:T(8,128)(2,1)S(1)}, u32[]{:S(2)}, u32[]{:S(2)}) collective-permute-start(bf16[2,64,1152]{2,1,0:T(8,128)(2,1)S(1)} %pad_maximum_fusion.3), channel_id=1, source_target_pairs={{0,8},{1,9},{2,10},{3,11},{4,12},{5,13},{6,14},{7,15},{8,0},{9,1},... | collective-permute-start | bytes 884744 | tf_op jit(solution)/shard_map/ppermute | solution.py:875
  28.3 14.0 %collective-permute-start.5 = (bf16[2,2,2,64,512]{4,3,2,1,0:T(8,128)(2,1)S(1)}, bf16[2,2,2,64,512]{4,3,2,1,0:T(8,128)(2,1)S(1)}, u32[]{:S(2)}, u32[]{:S(2)}) collective-permute-start(bf16[2,2,2,64,512]{4,3,2,1,0:T(8,128)(2,1)S(1)} %pad_maximum_fusion.1), channel_id=1, source_target_pairs={{0,2},{1,3},{2,0},{3,1},{4,6},{5,7},{6,4},{7,5},{8,10},{9,11},{10,... | collective-permute-start | bytes 1572872 | tf_op jit(solution)/shard_map/ppermute | solution.py:875
  29.8 10.4 %collective-permute-start.7 = (bf16[256,512]{1,0:T(8,128)(2,1)S(1)}, bf16[256,512]{1,0:T(8,128)(2,1)S(1)}, u32[]{:S(2)}, u32[]{:S(2)}) collective-permute-start(bf16[256,512]{1,0:T(8,128)(2,1)S(1)} %convert_element_type.9), channel_id=1, source_target_pairs={{4,0},{8,4},{12,8},{16,12},{20,16},{24,20},{28,24},{0,28},{5,1},{9... | collective-permute-start | bytes 786440 | tf_op jit(solution)/shard_map/ppermute | solution.py:1133
  32.3 10.0 %collective-permute-start.6 = (bf16[256,512]{1,0:T(8,128)(2,1)S(1)}, bf16[256,512]{1,0:T(8,128)(2,1)S(1)}, u32[]{:S(2)}, u32[]{:S(2)}) collective-permute-start(bf16[256,512]{1,0:T(8,128)(2,1)S(1)} %convert_element_type.9), channel_id=1, source_target_pairs={{0,4},{4,8},{8,12},{12,16},{16,20},{20,24},{24,28},{28,0},{1,5},{5... | collective-permute-start | bytes 786440 | tf_op jit(solution)/shard_map/ppermute | solution.py:1133
  33.0 12.9 %collective-permute-start.10 = (bf16[8,64,512]{2,1,0:T(8,128)(2,1)S(1)}, bf16[8,64,512]{2,1,0:T(8,128)(2,1)S(1)}, u32[]{:S(2)}, u32[]{:S(2)}) collective-permute-start(bf16[8,64,512]{2,1,0:T(8,128)(2,1)S(1)} %bitcast.69), channel_id=1, source_target_pairs={{0,1},{1,0},{2,3},{3,2},{4,5},{5,4},{6,7},{7,6},{8,9},{9,8},{10,11... | collective-permute-start | bytes 1572872 | tf_op jit(solution)/shard_map/ppermute | solution.py:875
  42.3 3.6 %collective-permute-start.11 = (bf16[8,64,512]{2,1,0:T(8,128)(2,1)S(1)}, bf16[8,64,512]{2,1,0:T(8,128)(2,1)S(1)}, u32[]{:S(2)}, u32[]{:S(2)}) collective-permute-start(bf16[8,64,512]{2,1,0:T(8,128)(2,1)S(1)} %bitcast.80), channel_id=1, source_target_pairs={{0,1},{1,0},{2,3},{3,2},{4,5},{5,4},{6,7},{7,6},{8,9},{9,8},{10,11... | collective-permute-start | bytes 1572872 | tf_op jit(solution)/shard_map/ppermute | solution.py:875
  42.4 10.8 %collective-permute-start.8 = (bf16[2,2,64,640]{3,2,1,0:T(8,128)(2,1)S(1)}, bf16[2,2,64,640]{3,2,1,0:T(8,128)(2,1)}, u32[]{:S(2)}, u32[]{:S(2)}) collective-permute-start(bf16[2,2,64,640]{3,2,1,0:T(8,128)(2,1)S(1)} %fusion.3), channel_id=1, source_target_pairs={{0,4},{1,5},{2,6},{3,7},{4,0},{5,1},{6,2},{7,3},{8,12},{9,13},{10,... | collective-permute-start | bytes 983048 | tf_op jit(solution)/shard_map/ppermute | solution.py:875
  44.8 8.5 %collective-permute-start.9 = (bf16[2,2,64,512]{3,2,1,0:T(8,128)(2,1)S(1)}, bf16[2,2,64,512]{3,2,1,0:T(8,128)(2,1)S(1)}, u32[]{:S(2)}, u32[]{:S(2)}) collective-permute-start(bf16[2,2,64,512]{3,2,1,0:T(8,128)(2,1)S(1)} %pad_maximum_fusion.4), channel_id=1, source_target_pairs={{0,2},{1,3},{2,0},{3,1},{4,6},{5,7},{6,4},{7,5},{8,10},{9,11},{10,... | collective-permute-start | bytes 786440 | tf_op jit(solution)/shard_map/ppermute | solution.py:875
  54.4 16.5 %collective-permute-start.14 = (bf16[8,64,640]{2,1,0:T(8,128)(2,1)S(1)}, bf16[8,64,640]{2,1,0:T(8,128)(2,1)S(1)}, u32[]{:S(2)}, u32[]{:S(2)}) collective-permute-start(bf16[8,64,640]{2,1,0:T(8,128)(2,1)S(1)} %bitcast.65), channel_id=1, source_target_pairs={{0,1},{1,0},{2,3},{3,2},{4,5},{5,4},{6,7},{7,6},{8,9},{9,8},{10,11... | collective-permute-start | bytes 1966088 | tf_op jit(solution)/shard_map/ppermute | solution.py:875
  54.4 17.1 %collective-permute-start.12 = (bf16[2,2,2,64,640]{4,3,2,1,0:T(8,128)(2,1)S(1)}, bf16[2,2,2,64,640]{4,3,2,1,0:T(8,128)(2,1)S(1)}, u32[]{:S(2)}, u32[]{:S(2)}) collective-permute-start(bf16[2,2,2,64,640]{4,3,2,1,0:T(8,128)(2,1)S(1)} %pad_maximum_fusion), channel_id=1, source_target_pairs={{0,2},{1,3},{2,0},{3,1},{4,6},{5,7},{6,4},{7,5},{8,10},{9,11},{10,... | collective-permute-start | bytes 1966088 | tf_op jit(solution)/shard_map/ppermute | solution.py:875
  56.0 14.8 %collective-permute-start.15 = (bf16[8,64,512]{2,1,0:T(8,128)(2,1)S(1)}, bf16[8,64,512]{2,1,0:T(8,128)(2,1)S(1)}, u32[]{:S(2)}, u32[]{:S(2)}) collective-permute-start(bf16[8,64,512]{2,1,0:T(8,128)(2,1)S(1)} %bitcast.67), channel_id=1, source_target_pairs={{0,1},{1,0},{2,3},{3,2},{4,5},{5,4},{6,7},{7,6},{8,9},{9,8},{10,11... | collective-permute-start | bytes 1572872 | tf_op jit(solution)/shard_map/ppermute | solution.py:875
  56.2 14.6 %collective-permute-start.13 = (bf16[2,2,2,64,512]{4,3,2,1,0:T(8,128)(2,1)S(1)}, bf16[2,2,2,64,512]{4,3,2,1,0:T(8,128)(2,1)}, u32[]{:S(2)}, u32[]{:S(2)}) collective-permute-start(bf16[2,2,2,64,512]{4,3,2,1,0:T(8,128)(2,1)S(1)} %pad_maximum_fusion.2), channel_id=1, source_target_pairs={{0,4},{1,5},{2,6},{3,7},{4,0},{5,1},{6,2},{7,3},{8,12},{9,13},{10,... | collective-permute-start | bytes 1572872 | tf_op jit(solution)/shard_map/ppermute | solution.py:875
  71.6 3.1 %collective-permute-start.16 = (bf16[8,64,640]{2,1,0:T(8,128)(2,1)S(1)}, bf16[8,64,640]{2,1,0:T(8,128)(2,1)S(1)}, u32[]{:S(2)}, u32[]{:S(2)}) collective-permute-start(bf16[8,64,640]{2,1,0:T(8,128)(2,1)S(1)} %bitcast.77), channel_id=1, source_target_pairs={{0,1},{1,0},{2,3},{3,2},{4,5},{5,4},{6,7},{7,6},{8,9},{9,8},{10,11... | collective-permute-start | bytes 1966088 | tf_op jit(solution)/shard_map/ppermute | solution.py:875
  71.6 3.1 %collective-permute-start.17 = (bf16[8,64,512]{2,1,0:T(8,128)(2,1)}, bf16[8,64,512]{2,1,0:T(8,128)(2,1)S(1)}, u32[]{:S(2)}, u32[]{:S(2)}) collective-permute-start(bf16[8,64,512]{2,1,0:T(8,128)(2,1)} %bitcast.33.b_1), channel_id=1, source_target_pairs={{0,1},{1,0},{2,3},{3,2},{4,5},{5,4},{6,7},{7,6},{8,9},{9,8},{10,11... | collective-permute-start | bytes 1572872 | tf_op jit(solution)/shard_map/ppermute | solution.py:875
  95.7 5.2 %collective-permute-start.18 = (bf16[16,64,384]{2,1,0:T(8,128)(2,1)}, bf16[16,64,384]{2,1,0:T(8,128)(2,1)S(1)}, u32[]{:S(2)}, u32[]{:S(2)}) collective-permute-start(bf16[16,64,384]{2,1,0:T(8,128)(2,1)} %get-tuple-element.229), channel_id=1, source_target_pairs={{0,1},{1,0},{2,3},{3,2},{4,5},{5,4},{6,7},{7,6},{8,9},{9,8},{10,11... | collective-permute-start | bytes 2359304 | tf_op jit(solution)/shard_map/ppermute | solution.py:875
  95.9 5.0 %collective-permute-start.19 = (bf16[16,64,384]{2,1,0:T(8,128)(2,1)}, bf16[16,64,384]{2,1,0:T(8,128)(2,1)S(1)}, u32[]{:S(2)}, u32[]{:S(2)}) collective-permute-start(bf16[16,64,384]{2,1,0:T(8,128)(2,1)} %get-tuple-element.231), channel_id=1, source_target_pairs={{0,1},{1,0},{2,3},{3,2},{4,5},{5,4},{6,7},{7,6},{8,9},{9,8},{10,11... | collective-permute-start | bytes 2359304 | tf_op jit(solution)/shard_map/ppermute | solution.py:875
  96.3 4.6 %collective-permute-start.20 = (bf16[16,64,384]{2,1,0:T(8,128)(2,1)}, bf16[16,64,384]{2,1,0:T(8,128)(2,1)S(1)}, u32[]{:S(2)}, u32[]{:S(2)}) collective-permute-start(bf16[16,64,384]{2,1,0:T(8,128)(2,1)} %get-tuple-element.233), channel_id=1, source_target_pairs={{0,1},{1,0},{2,3},{3,2},{4,5},{5,4},{6,7},{7,6},{8,9},{9,8},{10,11... | collective-permute-start | bytes 2359304 | tf_op jit(solution)/shard_map/ppermute | solution.py:875
  104.9 11.7 %collective-permute-start.21 = (bf16[8,64,384]{2,1,0:T(8,128)(2,1)}, bf16[8,64,384]{2,1,0:T(8,128)(2,1)S(1)}, u32[]{:S(2)}, u32[]{:S(2)}) collective-permute-start(bf16[8,64,384]{2,1,0:T(8,128)(2,1)} %get-tuple-element.245), channel_id=1, source_target_pairs={{0,2},{1,3},{2,0},{3,1},{4,6},{5,7},{6,4},{7,5},{8,10},{9,11},{10,... | collective-permute-start | bytes 1179656 | tf_op jit(solution)/shard_map/ppermute | solution.py:875
  106.5 11.3 %collective-permute-start.22 = (bf16[8,64,384]{2,1,0:T(8,128)(2,1)}, bf16[8,64,384]{2,1,0:T(8,128)(2,1)S(1)}, u32[]{:S(2)}, u32[]{:S(2)}) collective-permute-start(bf16[8,64,384]{2,1,0:T(8,128)(2,1)} %get-tuple-element.246), channel_id=1, source_target_pairs={{0,4},{1,5},{2,6},{3,7},{4,0},{5,1},{6,2},{7,3},{8,12},{9,13},{10,... | collective-permute-start | bytes 1179656 | tf_op jit(solution)/shard_map/ppermute | solution.py:875
  107.2 11.0 %collective-permute-start.23 = (bf16[8,64,384]{2,1,0:T(8,128)(2,1)}, bf16[8,64,384]{2,1,0:T(8,128)(2,1)S(1)}, u32[]{:S(2)}, u32[]{:S(2)}) collective-permute-start(bf16[8,64,384]{2,1,0:T(8,128)(2,1)} %get-tuple-element.247), channel_id=1, source_target_pairs={{0,8},{1,9},{2,10},{3,11},{4,12},{5,13},{6,14},{7,15},{8,0},{9,1},... | collective-permute-start | bytes 1179656 | tf_op jit(solution)/shard_map/ppermute | solution.py:875
  122.4 15.3 %collective-permute-start.24 = (bf16[4,64,384]{2,1,0:T(8,128)(2,1)}, bf16[4,64,384]{2,1,0:T(8,128)(2,1)S(1)}, u32[]{:S(2)}, u32[]{:S(2)}) collective-permute-start(bf16[4,64,384]{2,1,0:T(8,128)(2,1)} %get-tuple-element.255), channel_id=1, source_target_pairs={{0,4},{1,5},{2,6},{3,7},{4,0},{5,1},{6,2},{7,3},{8,12},{9,13},{10,... | collective-permute-start | bytes 589832 | tf_op jit(solution)/shard_map/ppermute | solution.py:875
  123.4 14.3 %collective-permute-start.25 = (bf16[4,64,384]{2,1,0:T(8,128)(2,1)}, bf16[4,64,384]{2,1,0:T(8,128)(2,1)S(1)}, u32[]{:S(2)}, u32[]{:S(2)}) collective-permute-start(bf16[4,64,384]{2,1,0:T(8,128)(2,1)} %get-tuple-element.256), channel_id=1, source_target_pairs={{0,8},{1,9},{2,10},{3,11},{4,12},{5,13},{6,14},{7,15},{8,0},{9,1},... | collective-permute-start | bytes 589832 | tf_op jit(solution)/shard_map/ppermute | solution.py:875
  124.5 13.2 %collective-permute-start.26 = (bf16[4,64,384]{2,1,0:T(8,128)(2,1)}, bf16[4,64,384]{2,1,0:T(8,128)(2,1)S(1)}, u32[]{:S(2)}, u32[]{:S(2)}) collective-permute-start(bf16[4,64,384]{2,1,0:T(8,128)(2,1)} %get-tuple-element.257), channel_id=1, source_target_pairs={{0,2},{1,3},{2,0},{3,1},{4,6},{5,7},{6,4},{7,5},{8,10},{9,11},{10,... | collective-permute-start | bytes 589832 | tf_op jit(solution)/shard_map/ppermute | solution.py:875
  137.7 2.2 %collective-permute-start.27 = (bf16[16,64,256]{2,1,0:T(8,128)(2,1)}, bf16[16,64,256]{2,1,0:T(8,128)(2,1)S(1)}, u32[]{:S(2)}, u32[]{:S(2)}) collective-permute-start(bf16[16,64,256]{2,1,0:T(8,128)(2,1)} %get-tuple-element.270), channel_id=1, source_target_pairs={{0,1},{1,0},{2,3},{3,2},{4,5},{5,4},{6,7},{7,6},{8,9},{9,8},{10,11... | collective-permute-start | bytes 1572872 | tf_op jit(solution)/shard_map/ppermute | solution.py:875
  137.8 2.9 %collective-permute-start.28 = (bf16[16,64,256]{2,1,0:T(8,128)(2,1)}, bf16[16,64,256]{2,1,0:T(8,128)(2,1)S(1)}, u32[]{:S(2)}, u32[]{:S(2)}) collective-permute-start(bf16[16,64,256]{2,1,0:T(8,128)(2,1)} %get-tuple-element.272), channel_id=1, source_target_pairs={{0,1},{1,0},{2,3},{3,2},{4,5},{5,4},{6,7},{7,6},{8,9},{9,8},{10,11... | collective-permute-start | bytes 1572872 | tf_op jit(solution)/shard_map/ppermute | solution.py:875
  142.9 9.2 %collective-permute-start.29 = (bf16[8,64,256]{2,1,0:T(8,128)(2,1)S(1)}, bf16[8,64,256]{2,1,0:T(8,128)(2,1)S(1)}, u32[]{:S(2)}, u32[]{:S(2)}) collective-permute-start(bf16[8,64,256]{2,1,0:T(8,128)(2,1)S(1)} %get-tuple-element.282), channel_id=1, source_target_pairs={{0,2},{1,3},{2,0},{3,1},{4,6},{5,7},{6,4},{7,5},{8,10},{9,11},{10,... | collective-permute-start | bytes 786440 | tf_op jit(solution)/shard_map/ppermute | solution.py:875
  143.8 9.1 %collective-permute-start.30 = (bf16[8,64,256]{2,1,0:T(8,128)(2,1)S(1)}, bf16[8,64,256]{2,1,0:T(8,128)(2,1)S(1)}, u32[]{:S(2)}, u32[]{:S(2)}) collective-permute-start(bf16[8,64,256]{2,1,0:T(8,128)(2,1)S(1)} %get-tuple-element.284), channel_id=1, source_target_pairs={{0,4},{1,5},{2,6},{3,7},{4,0},{5,1},{6,2},{7,3},{8,12},{9,13},{10,... | collective-permute-start | bytes 786440 | tf_op jit(solution)/shard_map/ppermute | solution.py:875
  145.0 8.1 %collective-permute-start.31 = (bf16[2,64,384]{2,1,0:T(8,128)(2,1)S(1)}, bf16[2,64,384]{2,1,0:T(8,128)(2,1)S(1)}, u32[]{:S(2)}, u32[]{:S(2)}) collective-permute-start(bf16[2,64,384]{2,1,0:T(8,128)(2,1)S(1)} %get-tuple-element.298), channel_id=1, source_target_pairs={{0,8},{1,9},{2,10},{3,11},{4,12},{5,13},{6,14},{7,15},{8,0},{9,1},... | collective-permute-start | bytes 294920 | tf_op jit(solution)/shard_map/ppermute | solution.py:875
  146.0 7.4 %collective-permute-start.32 = (bf16[2,64,384]{2,1,0:T(8,128)(2,1)S(1)}, bf16[2,64,384]{2,1,0:T(8,128)(2,1)S(1)}, u32[]{:S(2)}, u32[]{:S(2)}) collective-permute-start(bf16[2,64,384]{2,1,0:T(8,128)(2,1)S(1)} %get-tuple-element.300), channel_id=1, source_target_pairs={{0,2},{1,3},{2,0},{3,1},{4,6},{5,7},{6,4},{7,5},{8,10},{9,11},{10,... | collective-permute-start | bytes 294920 | tf_op jit(solution)/shard_map/ppermute | solution.py:875
  147.2 6.8 %collective-permute-start.33 = (bf16[2,64,384]{2,1,0:T(8,128)(2,1)S(1)}, bf16[2,64,384]{2,1,0:T(8,128)(2,1)S(1)}, u32[]{:S(2)}, u32[]{:S(2)}) collective-permute-start(bf16[2,64,384]{2,1,0:T(8,128)(2,1)S(1)} %get-tuple-element.302), channel_id=1, source_target_pairs={{0,4},{1,5},{2,6},{3,7},{4,0},{5,1},{6,2},{7,3},{8,12},{9,13},{10,... | collective-permute-start | bytes 294920 | tf_op jit(solution)/shard_map/ppermute | solution.py:875
  154.0 5.0 %collective-permute-start.34 = (bf16[4,64,256]{2,1,0:T(8,128)(2,1)S(1)}, bf16[4,64,256]{2,1,0:T(8,128)(2,1)S(1)}, u32[]{:S(2)}, u32[]{:S(2)}) collective-permute-start(bf16[4,64,256]{2,1,0:T(8,128)(2,1)S(1)} %get-tuple-element.303), channel_id=1, source_target_pairs={{0,4},{1,5},{2,6},{3,7},{4,0},{5,1},{6,2},{7,3},{8,12},{9,13},{10,... | collective-permute-start | bytes 393224 | tf_op jit(solution)/shard_map/ppermute | solution.py:875
  155.0 5.0 %collective-permute-start.35 = (bf16[4,64,256]{2,1,0:T(8,128)(2,1)S(1)}, bf16[4,64,256]{2,1,0:T(8,128)(2,1)S(1)}, u32[]{:S(2)}, u32[]{:S(2)}) collective-permute-start(bf16[4,64,256]{2,1,0:T(8,128)(2,1)S(1)} %get-tuple-element.305), channel_id=1, source_target_pairs={{0,2},{1,3},{2,0},{3,1},{4,6},{5,7},{6,4},{7,5},{8,10},{9,11},{10,... | collective-permute-start | bytes 393224 | tf_op jit(solution)/shard_map/ppermute | solution.py:875
  160.0 27.8 %copy-start.12 = (f32[64,896]{1,0:T(8,128)S(1)}, f32[64,896]{1,0:T(8,128)}, u32[]{:S(2)}) copy-start(f32[64,896]{1,0:T(8,128)} %refs_7_.1) | copy-start | bytes 688132
  160.0 27.8 %copy-start.13 = (f32[640,64]{0,1:T(8,128)S(1)}, f32[640,64]{0,1:T(8,128)}, u32[]{:S(2)}) copy-start(f32[640,64]{0,1:T(8,128)} %param.40) | copy-start | bytes 491524
  160.0 27.8 %copy-start.14 = (f32[640,64]{0,1:T(8,128)S(1)}, f32[640,64]{0,1:T(8,128)}, u32[]{:S(2)}) copy-start(f32[640,64]{0,1:T(8,128)} %param.44) | copy-start | bytes 491524
  160.2 6.6 %collective-permute-start.36 = (bf16[2,64,512]{2,1,0:T(8,128)(2,1)S(1)}, bf16[2,64,512]{2,1,0:T(8,128)(2,1)S(1)}, u32[]{:S(2)}, u32[]{:S(2)}) collective-permute-start(bf16[2,64,512]{2,1,0:T(8,128)(2,1)S(1)} %get-tuple-element.307), channel_id=1, source_target_pairs={{0,8},{1,9},{2,10},{3,11},{4,12},{5,13},{6,14},{7,15},{8,0},{9,1},... | collective-permute-start | bytes 393224 | tf_op jit(solution)/shard_map/ppermute | solution.py:875
  161.3 8.9 %collective-permute-start.38 = (bf16[1,64,1152]{2,1,0:T(8,128)(2,1)S(1)}, bf16[1,64,1152]{2,1,0:T(8,128)(2,1)S(1)}, u32[]{:S(2)}, u32[]{:S(2)}) collective-permute-start(bf16[1,64,1152]{2,1,0:T(8,128)(2,1)S(1)} %get-tuple-element.317), channel_id=1, source_target_pairs={{0,16},{1,17},{2,18},{3,19},{4,20},{5,21},{6,22},{7,23},{8,24},{9,... | collective-permute-start | bytes 442376 | tf_op jit(solution)/shard_map/ppermute | solution.py:875
  166.8 5.3 %collective-permute-start.37 = (bf16[1,64,512]{2,1,0:T(8,128)(2,1)S(1)}, bf16[1,64,512]{2,1,0:T(8,128)(2,1)S(1)}, u32[]{:S(2)}, u32[]{:S(2)}) collective-permute-start(bf16[1,64,512]{2,1,0:T(8,128)(2,1)S(1)} %get-tuple-element.309), channel_id=1, source_target_pairs={{0,16},{1,17},{2,18},{3,19},{4,20},{5,21},{6,22},{7,23},{8,24},{9,... | collective-permute-start | bytes 196616 | tf_op jit(solution)/shard_map/ppermute | solution.py:875
  172.4 1.2 collective-permute-start.39
  173.6 4.4 %collective-permute-start.42 = (f32[1,128]{1,0:T(1,128)S(1)}, f32[1,128]{1,0:T(1,128)S(1)}, u32[]{:S(2)}, u32[]{:S(2)}) collective-permute-start(f32[1,128]{1,0:T(1,128)S(1)} %add.63), channel_id=1, source_target_pairs={{0,6},{1,7},{2,4},{3,5},{4,2},{5,3},{6,0},{7,1},{8,14},{9,15},{10,... | collective-permute-start | bytes 1544 | tf_op jit(solution)/shard_map/ppermute | solution.py:1054
  175.2 3.5 %collective-permute-start.41 = (f32[1,128]{1,0:T(1,128)S(1)}, f32[1,128]{1,0:T(1,128)S(1)}, u32[]{:S(2)}, u32[]{:S(2)}) collective-permute-start(f32[1,128]{1,0:T(1,128)S(1)} %add.63), channel_id=1, source_target_pairs={{0,4},{1,5},{2,6},{3,7},{4,0},{5,1},{6,2},{7,3},{8,12},{9,13},{10,... | collective-permute-start | bytes 1544 | tf_op jit(solution)/shard_map/ppermute | solution.py:1054
  176.2 3.5 %collective-permute-start.40 = (f32[1,128]{1,0:T(1,128)S(1)}, f32[1,128]{1,0:T(1,128)S(1)}, u32[]{:S(2)}, u32[]{:S(2)}) collective-permute-start(f32[1,128]{1,0:T(1,128)S(1)} %add.63), channel_id=1, source_target_pairs={{0,2},{1,3},{2,0},{3,1},{4,6},{5,7},{6,4},{7,5},{8,10},{9,11},{10,... | collective-permute-start | bytes 1544 | tf_op jit(solution)/shard_map/ppermute | solution.py:1054
  179.8 3.5 %collective-permute-start.43 = (f32[1,128]{1,0:T(1,128)S(1)}, f32[1,128]{1,0:T(1,128)S(1)}, u32[]{:S(2)}, u32[]{:S(2)}) collective-permute-start(f32[1,128]{1,0:T(1,128)S(1)} %add_add_fusion), channel_id=1, source_target_pairs={{0,8},{1,9},{2,10},{3,11},{4,12},{5,13},{6,14},{7,15},{8,0},{9,1},... | collective-permute-start | bytes 1544 | tf_op jit(solution)/shard_map/ppermute | solution.py:1054
  183.3 4.4 %collective-permute-start.44 = (f32[1,128]{1,0:T(1,128)S(1)}, f32[1,128]{1,0:T(1,128)S(1)}, u32[]{:S(2)}, u32[]{:S(2)}) collective-permute-start(f32[1,128]{1,0:T(1,128)S(1)} %add.67), channel_id=1, source_target_pairs={{0,16},{1,17},{2,18},{3,19},{4,20},{5,21},{6,22},{7,23},{8,24},{9,... | collective-permute-start | bytes 1544 | tf_op jit(solution)/shard_map/ppermute | solution.py:1054
  (50 other events, 646.3 us)

commit v5 on v4

--- a/solution.py
+++ b/solution.py
@@ -121,10 +121,8 @@
     )(grid, pixel_rows)
 
 
-def counts_kernel(slots_ref, across_ref, bias_out, pool_out, pull_out, bias_ref, pool_ref, pull_ref, sems):
+def pull_kernel(across_ref, pool_ref, pull_ref):
     nodes, width = pull_ref.shape
-    step = 64
-    leave = Leaving(sems)
     across = across_ref[...]
 
     def count_across(i, _):
@@ -138,8 +136,23 @@
         return 0
 
     lax.fori_loop(0, nodes // 128, count_across, 0)
-    leave(pool_ref, pool_out)
-    leave(pull_ref, pull_out)
+
+
+def pull_counts(across_rows, nodes):
+    width = across_rows.shape[1]
+    return pl.pallas_call(
+        pull_kernel,
+        out_shape=(jax.ShapeDtypeStruct((width, nodes), BF), jax.ShapeDtypeStruct((nodes, width), BF)),
+        compiler_params=pltpu.CompilerParams(vmem_limit_bytes=BIG),
+        cost_estimate=QUICK,
+        name="pull_counts",
+    )(across_rows)
+
+
+def counts_kernel(slots_ref, bias_out, bias_ref, sems):
+    nodes = slots_ref.shape[1]
+    step = 64
+    leave = Leaving(sems)
     for band in range(nodes // BAND):
         low = band * BAND
         picks = slots_ref[:, low : low + BAND] - low
@@ -165,22 +178,18 @@
     leave.wait()
 
 
-def counts(slot_rows, across_rows):
-    nodes, width = slot_rows.shape[1], across_rows.shape[1]
-    shapes = (
-        jax.ShapeDtypeStruct((nodes // BAND, WINDOW, BAND), F32),
-        jax.ShapeDtypeStruct((width, nodes), BF),
-        jax.ShapeDtypeStruct((nodes, width), BF),
-    )
+def counts(slot_rows):
+    nodes = slot_rows.shape[1]
+    shape = jax.ShapeDtypeStruct((nodes // BAND, WINDOW, BAND), F32)
     return pl.pallas_call(
         counts_kernel,
-        out_specs=[pl.BlockSpec(memory_space=pltpu.HBM)] * 3,
-        out_shape=shapes,
-        scratch_shapes=[pltpu.VMEM(shape.shape, shape.dtype) for shape in shapes] + [pltpu.SemaphoreType.DMA((6,))],
+        out_specs=pl.BlockSpec(memory_space=pltpu.HBM),
+        out_shape=shape,
+        scratch_shapes=[pltpu.VMEM(shape.shape, shape.dtype), pltpu.SemaphoreType.DMA((4,))],
         compiler_params=pltpu.CompilerParams(vmem_limit_bytes=BIG),
         cost_estimate=QUICK,
         name="counts",
-    )(slot_rows, across_rows)
+    )(slot_rows)
 
 
 def blocks_of(place_ref, dims, refs):
@@ -618,7 +627,7 @@
     place_ref, early_ref, query_in_a, query_in_b, pair_in_a, pair_in_b,
     grad_state_in, rows_in, normed_in, before_ref, sums_ref, after_ref, grad_dec_ref,
     keep_0, keep_1, send_0, send_1,
-    early, normed_ref, rows_ref, grad_state_ref, query_g, pair_g, keep_ref, send_ref, sems,
+    early, normed_ref, rows_ref, grad_state_ref, query_g, pair_g, sems,
 ):
     pairs = (
         (normed_in, normed_ref),
@@ -632,13 +641,13 @@
     own_wide, own_narrow = place_ref[0], place_ref[1]
     def put(n, colour, column, value, low):
         lines = value.shape[0] // 8
-        for side, out_ref in ((1, send_ref), (0, keep_ref)):
+        for side, out_refs in ((1, (send_0, send_1)), (0, (keep_0, keep_1))):
 
             @pl.when(((n ^ own_narrow) & 1) == side)
             def _():
                 part = (n ^ own_narrow) >> 1
                 for w in range(8):
-                    out_ref[colour, block_at(DIMS[colour], part, w ^ own_wide), low : low + lines, column : column + 128] = value[
+                    out_refs[colour][block_at(DIMS[colour], part, w ^ own_wide), low : low + lines, column : column + 128] = value[
                         w * lines : (w + 1) * lines, :
                     ]
 
@@ -652,14 +661,6 @@
         put(n, 0, 0, weight_query[:, n * 128 : n * 128 + 128], 0)
         put(n, 0, 128, weight_pair[:, n * 256 : n * 256 + 128], 0)
         put(n, 1, 0, weight_pair[:, n * 256 + 128 : n * 256 + 256], 0)
-    leaving = [
-        pltpu.make_async_copy(send_ref.at[0], send_0, sems.at[10]),
-        pltpu.make_async_copy(keep_ref.at[0], keep_0, sems.at[11]),
-        pltpu.make_async_copy(send_ref.at[1], send_1, sems.at[12]),
-        pltpu.make_async_copy(keep_ref.at[1], keep_1, sems.at[13]),
-    ]
-    leaving[0].start()
-    leaving[1].start()
     for copy in copies[5:]:
         copy.wait()
     gain = dec_of(early).astype(F32).T[OUT : OUT + 1, :]
@@ -685,10 +686,6 @@
         put(n, 1, 128, grad_enc[:, n * 128 : n * 128 + 128], 0)
         put(n, 1, 128, grad_dec[n * 128 : n * 128 + 128, :], 32)
         put(n, 1, 128, jnp.zeros((128, 128), BF), 48)
-    leaving[2].start()
-    leaving[3].start()
-    for copy in leaving:
-        copy.wait()
 
 
 def give_back(place, early, first, second, grad_state, rows, normed, before, sums, after, grad_dec):
@@ -697,7 +694,7 @@
     return pl.pallas_call(
         return_kernel,
         in_specs=[pl.BlockSpec(memory_space=pltpu.SMEM), outside] + [outside] * 7 + [vmem] * 4,
-        out_specs=[outside] * 4,
+        out_specs=[vmem] * 4,
         out_shape=[jax.ShapeDtypeStruct((16, LINES, 256), BF)] * 4,
         scratch_shapes=[
             pltpu.VMEM((8, GROUPS, LINES, EARLY), BF),
@@ -706,16 +703,18 @@
             pltpu.VMEM((512, D), F32),
             pltpu.VMEM((512, D), BF),
             pltpu.VMEM((NEAR, 2 * D), BF),
-            pltpu.VMEM((2, 16, LINES, 256), BF),
-            pltpu.VMEM((2, 16, LINES, 256), BF),
             pltpu.SemaphoreType.DMA((14,)),
         ],
-        compiler_params=pltpu.CompilerParams(vmem_limit_bytes=BIG),
+        compiler_params=pltpu.CompilerParams(vmem_limit_bytes=36 * MIB),
         cost_estimate=QUICK,
         name="give_back",
     )(
-        place, early, first[0], second[0], first[1], second[1],
-        grad_state, rows, normed, before, sums, after, grad_dec,
+        place,
+        *(
+            pltpu.with_memory_space_constraint(array, pltpu.HBM)
+            for array in (early, first[0], second[0], first[1], second[1], grad_state, rows, normed)
+        ),
+        before, sums, after, grad_dec,
     )
 
 
@@ -931,7 +930,7 @@
     sizes = [min(array.shape[0] for array in arrays) for arrays in lists]
     halves = [(size // 2, *arrays[0].shape[1:]) for size, arrays in zip(sizes, lists)]
     kinds = (BF, F32)[: 1 + keep]
-    outside = pl.BlockSpec(memory_space=pltpu.HBM)
+    outside = pl.BlockSpec(memory_space=pl.ANY)
     there = [
         pltpu.VMEM((size if keep else size // 2, *array.shape[1:]), array.dtype)
         for size, arrays in zip(sizes, lists)
@@ -945,7 +944,7 @@
         scratch_shapes=there
         + [pltpu.VMEM(shape, kind) for kind in kinds for shape in halves]
         + [pltpu.SemaphoreType.DMA((sum(groups), 2)), pltpu.SemaphoreType.DMA((len(kinds) * len(lists),))],
-        compiler_params=pltpu.CompilerParams(vmem_limit_bytes=BIG),
+        compiler_params=pltpu.CompilerParams(vmem_limit_bytes=20 * MIB),
         cost_estimate=QUICK,
         name="halve_far",
     )(*(array for arrays in lists for array in arrays))
@@ -1100,10 +1099,12 @@
     if moving:
         early_4 = swap(early, 4)
 
+    across = jnp.pad(mesh_to_grid.T - wide_index * nodes, ((0, 0), (0, width - pixels)), constant_values=-1)
+    pool, pull = pull_counts(across, nodes)
     if moving:
+        early_4, pull = tie((early_4, pull))
         early_1 = joined(early, early_4)
         early_3 = swap(early_1, 3)
-        early_1, target, noise_draw, noise_sigma = tie((early_1, target, noise_draw, noise_sigma))
 
     def own(array):
         return lax.dynamic_index_in_dim(jnp.transpose(array, (2, 0, 1)), globe, 1, keepdims=False)
@@ -1125,7 +1126,6 @@
     grid = jnp.pad(grid, ((0, 0), (0, width - pixels)))
     edges = mesh_edges.T
     slot_rows = jnp.where(edges >= 0, (edges - wide_index * nodes + nodes + all_nodes) % all_nodes, -1)
-    across = jnp.pad(mesh_to_grid.T - wide_index * nodes, ((0, 0), (0, width - pixels)), constant_values=-1)
 
     def halo(sums):
         low = sums.astype(BF)
@@ -1140,7 +1140,7 @@
         quad, late_1, slot_rows = tie((quad, late_1, slot_rows))
         early_0 = swap(quad, 1)
         late_3 = swap(late_1, 3)
-        bias, pool, pull = counts(slot_rows, across)
+        bias = counts(slot_rows)
         bias, late_3 = tie((bias, late_3))
         both = joined(late_1, late_3)
         parts = [both[..., : CUTS[0]], both[..., CUTS[0] :]]
@@ -1151,7 +1151,7 @@
     else:
         gathered, late_full = gather_plain(early, late, wide)
         sums = grid_sums(grid, grid_to_mesh.T - wide_index * pixels)
-        bias, pool, pull = counts(slot_rows, across)
+        bias = counts(slot_rows)
         before, after = halo(sums)
 
     state0, rows, normed, early_full = encode(place, gathered, before, sums, after)

time: 194 us -> 189 us (0.974)
  local copies, waits for them, and re-layouts: 12.5 us -> 8.61 us
  other arithmetic: 4.91 us -> 2.37 us
  waiting for transfers between devices: 44.2 us -> 41.8 us
    unnamed x107 -> x103, local copies, waits for them, and re-layouts: 7.26 us -> 2.07 us
    another operation x1 -> x2, local copies, waits for them, and re-layouts: 0.64 us -> 2.81 us
    pallas_call x1 -> x2, Pallas kernels: 7.18 us -> 9.11 us  [the longest x1 6.29 us: counts(): pl.pallas_call(counts_kernel, out_specs=pl.BlockSpec(memory_space=pltpu.H...]
  transfers between devices with their start and end apart: 45 -> 45, of which waited for: 27 -> 24; matrix products, arithmetic and copies ran while one was open for 4% -> 4% of each run, Pallas kernels for 28% -> 29%
where the time goes in v5:
time: 189 us; the launch traced here: 185 us
  Pallas kernels  85.4 us (45%)
  starting transfers between devices  44 us (23%)
  waiting for transfers between devices  41.8 us (22%)
  local copies, waits for them, and re-layouts  8.61 us (5%)
  between operations  3.15 us (2%)
  other arithmetic  2.37 us (1%)
    ppermute x37, starting transfers between devices, swap(): lax.ppermute(array, ('wide', 'narrow'), [(i, i ^ 1 << bit) for i in range...  35.4 us
    ppermute x37, waiting for transfers between devices, swap(): lax.ppermute(array, ('wide', 'narrow'), [(i, i ^ 1 << bit) for i in range...  29.1 us
    pallas_call x1, Pallas kernels, feed(): pl.pallas_call(feed_kernel, in_specs=[pl.BlockSpec(memory_space=pltpu.SME...  20 us
    pallas_call x1, Pallas kernels, attend(): pl.pallas_call(attend_kernel, in_specs=[outside] * 3, out_specs=[outside]...  13.9 us
    pallas_call x2, Pallas kernels, unmix(): pl.pallas_call(functools.partial(unmix_kernel, first), grid=(heads,), in_...  12.4 us
    pallas_call x1, Pallas kernels, give_back(): pl.pallas_call(return_kernel, in_specs=[pl.BlockSpec(memory_space=pltpu.S...  10.2 us
    ppermute x6, waiting for transfers between devices, sum_all(): lax.ppermute(row, ('wide', 'narrow'), [(i, i ^ mask << bit) for i in rang...  10 us
    pallas_call x2, Pallas kernels, halve_far(): pl.pallas_call(functools.partial(halve_kernel, groups, keep), in_specs=[o...  7.38 us
  transfers between devices with their start and end apart: 45, of which 24 were waited for; matrix products, arithmetic and copies ran while one was open for 4% of the time, Pallas kernels for 29%

profile of v5, /device:TPU:0, one launch (start us, length us, event | category | flops | bytes accessed | tf_op | source)
XLA Modules:
  0.0 185.2 jit_solution(7593935685839002219)
XLA Ops:
  0.7 1.9 %pack.1 = (bf16[64,512]{1,0:T(8,128)(2,1)}, bf16[64,1152]{1,0:T(8,128)(2,1)}) custom-call(f32[32,128]{1,0:T(8,128)} %refs_0_.1, f32[64,896]{1,0:T(8,128)} %refs_4_.1, f32[64,640]{1,0:T(8,128)} %bitcast.61, f32[16,86]{1,0:T(8,128)} %refs_12_.1), custom_call_target="tpu_custom_call" | custom-call | flops 1000 | bytes 1000 | tf_op jit(solution)/shard_map/pack/pallas_call | solution.py:793
  2.6 4.1 %collective-permute-start = (bf16[64,512]{1,0:T(8,128)(2,1)}, bf16[64,512]{1,0:T(8,128)(2,1)S(1)}, u32[]{:S(2)}, u32[]{:S(2)}) collective-permute-start(bf16[64,512]{1,0:T(8,128)(2,1)} %get-tuple-element.179), channel_id=1, source_target_pairs={{0,16},{1,17},{2,18},{3,19},{4,20},{5,21},{6,22},{7,23},{8,24},{9,... | collective-permute-start | bytes 196616 | tf_op jit(solution)/shard_map/ppermute | solution.py:874
  6.7 1.2 dynamic_slice.18
  9.3 2.2 %constant_dynamic-slice_fusion.1 = (f32[1,853,84]{1,0,2:T(1,128)S(1)}, f32[1,853,84]{1,0,2:T(1,128)S(1)}) fusion(f32[4,853,84]{1,0,2:T(4,128)} %param.27, s32[]{:T(128)S(6)} %select_n.20, f32[4,853,84]{1,0,2:T(4,128)} %param.26), kind=kLoop, calls=%fused_computation.27 | loop fusion | bytes 1146436 | tf_op jit(solution)/shard_map/dynamic-slice.1
  12.1 2.8 %pull_counts.1 = (bf16[896,512]{1,0:T(8,128)(2,1)}, bf16[512,896]{1,0:T(8,128)(2,1)}) custom-call(s32[3,896]{1,0:T(4,128)} %pad.8.across_ref), custom_call_target="tpu_custom_call" | custom-call | flops 1000 | bytes 1000 | tf_op jit(solution)/shard_map/pull_counts/pallas_call | solution.py:143
  15.7 1.6 collective-permute-start.1
  17.4 3.4 %collective-permute-done.1 = bf16[2,64,512]{2,1,0:T(8,128)(2,1)S(1)} collective-permute-done((bf16[2,64,512]{2,1,0:T(8,128)(2,1)S(1)}, bf16[2,64,512]{2,1,0:T(8,128)(2,1)S(1)}, u32[]{:S(2)}, u32[]{:S(2)}) %collective-permute-start.1) | collective-permute-done | bytes 131104 | tf_op jit(solution)/shard_map/ppermute | solution.py:874
  21.9 1.6 collective-permute-start.2
  24.2 2.4 %grid_sums.1.sums_ref = f32[256,512]{1,0:T(8,128)S(1)} custom-call(bf16[256,896]{1,0:T(8,128)(2,1)S(1)} %fusion.2.grid_ref, s32[8,512]{1,0:T(8,128)S(1)} %subtract_bitcast_fusion.pixels_ref), custom_call_target="tpu_custom_call" | custom-call | flops 1000 | bytes 1000 | tf_op jit(solution)/shard_map/grid_sums/pallas_call | solution.py:114
  26.6 3.2 %collective-permute-done.3 = bf16[64,1152]{1,0:T(8,128)(2,1)S(1)} collective-permute-done((bf16[64,1152]{1,0:T(8,128)(2,1)S(1)}, bf16[64,1152]{1,0:T(8,128)(2,1)S(1)}, u32[]{:S(2)}, u32[]{:S(2)}) %collective-permute-start.3) | collective-permute-done | bytes 147488 | tf_op jit(solution)/shard_map/ppermute | solution.py:874
  30.0 1.6 collective-permute-start.5
  31.6 3.4 %collective-permute-start.7 = (bf16[256,512]{1,0:T(8,128)(2,1)S(1)}, bf16[256,512]{1,0:T(8,128)(2,1)S(1)}, u32[]{:S(2)}, u32[]{:S(2)}) collective-permute-start(bf16[256,512]{1,0:T(8,128)(2,1)S(1)} %convert_element_type.9), channel_id=1, source_target_pairs={{4,0},{8,4},{12,8},{16,12},{20,16},{24,20},{28,24},{0,28},{5,1},{9... | collective-permute-start | bytes 786440 | tf_op jit(solution)/shard_map/ppermute | solution.py:1133
  35.0 6.3 %counts.1.bias_in = f32[2,1280,256]{2,1,0:T(8,128)} custom-call(s32[16,512]{1,0:T(8,128)} %fusion.5.slots_ref), custom_call_target="tpu_custom_call" | custom-call | flops 1000 | bytes 1000 | tf_op jit(solution)/shard_map/counts/pallas_call | solution.py:184
  41.4 2.6 %collective-permute-done.6.before_ref = bf16[256,512]{1,0:T(8,128)(2,1)S(1)} collective-permute-done((bf16[256,512]{1,0:T(8,128)(2,1)S(1)}, bf16[256,512]{1,0:T(8,128)(2,1)S(1)}, u32[]{:S(2)}, u32[]{:S(2)}) %collective-permute-start.6) | collective-permute-done | bytes 262176 | tf_op jit(solution)/shard_map/ppermute | solution.py:1133
  44.2 1.8 collective-permute-start.8
  48.4 5.8 %encode.1 = (f32[512,512]{1,0:T(8,128)}, bf16[1536,512]{1,0:T(8,128)(2,1)}, bf16[1536,512]{1,0:T(8,128)(2,1)}, bf16[8,4,64,512]{3,2,1,0:T(8,128)(2,1)}) custom-call(s32[3]{0:T(128)} %pad_add_fusion.place_ref, bf16[8,64,512]{2,1,0:T(8,128)(2,1)} %bitcast.75, bf16[8,64,512]{2,1,0:T(8,128)(2,1)} %bitcast.88, bf16[8,64,512]{2,1,0:T(8,128)(2,1)} %collective-permute-done.10.a_2, ...), custom_call_target="tpu_custom_call" | custom-call | flops 1000 | bytes 1000 | tf_op jit(solution)/shard_map/encode/pallas_call | solution.py:277
  54.6 1.4 collective-permute-start.12
  56.1 1.5 collective-permute-start.13
  57.6 13.9 %attend.1 = (f32[512,512]{1,0:T(8,128)}, bf16[4,1536,512]{2,1,0:T(8,128)(2,1)}, bf16[512,512]{1,0:T(8,128)(2,1)}, bf16[4,1536,256]{2,1,0:T(8,128)(2,1)}, f32[8,512]{1,0:T(8,128)}) custom-call(bf16[1536,512]{1,0:T(8,128)(2,1)} %get-tuple-element.207.normed_in, bf16[8,4,64,512]{3,2,1,0:T(8,128)(2,1)} %get-tuple-element.208.early_in.early_ref, ...), custom_call_target="tpu_custom_call" | custom-call | flops 1000 | bytes 1000 | tf_op jit(solution)/shard_map/attend/pallas_call | solution.py:351
  75.6 20.0 %feed.1 = (bf16[16,64,384]{2,1,0:T(8,128)(2,1)}, bf16[16,64,384]{2,1,0:T(8,128)(2,1)}, bf16[16,64,384]{2,1,0:T(8,128)(2,1)}, bf16[16,64,384]{2,1,0:T(8,128)(2,1)...) custom-call(s32[3]{0:T(128)} %pad_add_fusion.place_ref, ...), custom_call_target="tpu_custom_call" | custom-call | flops 1000 | bytes 1000 | tf_op jit(solution)/shard_map/feed/pallas_call | solution.py:535
  96.3 4.6 %unmix.2 = (bf16[512,128]{1,0:T(8,128)(2,1)}, bf16[1536,256]{1,0:T(8,128)(2,1)}) custom-call(bf16[4,1536,512]{2,1,0:T(8,128)(2,1)} %get-tuple-element.232.probs_ref, bf16[512,512]{1,0:T(8,128)(2,1)} %get-tuple-element.246.query_ref, bf16[4,1536,256]{2,1,0:T(8,128)(2,1)} %get-tuple-element.233.keys_ref.values_ref, ...), custom_call_target="tpu_custom_call" | custom-call | flops 1000 | bytes 1000 | tf_op jit(solution)/shard_map/unmix/pallas_call | solution.py:598
  100.9 2.9 %halve_far.2 = (bf16[8,64,384]{2,1,0:T(8,128)(2,1)}, bf16[8,64,384]{2,1,0:T(8,128)(2,1)}, bf16[8,64,384]{2,1,0:T(8,128)(2,1)}) custom-call(bf16[16,64,384]{2,1,0:T(8,128)(2,1)S(1)} %copy-done.4, bf16[16,64,384]{2,1,0:T(8,128)(2,1)S(1)} %collective-permute-done.18.refs_1_, bf16[16,64,384]{2,1,0:T(8,128)(2,1)S(1)} %copy-done.5, ...), custom_call_target="tpu_custom_call" | custom-call | flops 1000 | bytes 1000 | tf_op jit(solution)/shard_map/halve_far/pallas_call | solution.py:939
  103.8 1.4 collective-permute-start.21
  105.2 1.5 collective-permute-start.22
  106.6 7.8 %unmix.3 = (bf16[512,384]{1,0:T(8,128)(2,1)}, bf16[1536,768]{1,0:T(8,128)(2,1)}) custom-call(bf16[4,1536,512]{2,1,0:T(8,128)(2,1)} %get-tuple-element.232.probs_ref, bf16[512,512]{1,0:T(8,128)(2,1)} %get-tuple-element.246.query_ref, bf16[4,1536,256]{2,1,0:T(8,128)(2,1)} %get-tuple-element.233.keys_ref.values_ref, ...), custom_call_target="tpu_custom_call" | custom-call | flops 1000 | bytes 1000 | tf_op jit(solution)/shard_map/unmix/pallas_call | solution.py:598
  117.8 4.5 %halve_far.3 = (bf16[4,64,384]{2,1,0:T(8,128)(2,1)S(1)}, bf16[4,64,384]{2,1,0:T(8,128)(2,1)S(1)}, bf16[4,64,384]{2,1,0:T(8,128)(2,1)S(1)}, f32[4,64,384]{2,1,0:T...) custom-call(bf16[16,64,384]{2,1,0:T(8,128)(2,1)S(1)} %copy-done.4, ...), custom_call_target="tpu_custom_call" | custom-call | flops 1000 | bytes 1000 | tf_op jit(solution)/shard_map/halve_far/pallas_call | solution.py:939
  124.0 10.2 %give_back.1 = (bf16[16,64,256]{2,1,0:T(8,128)(2,1)S(1)}, bf16[16,64,256]{2,1,0:T(8,128)(2,1)S(1)}, bf16[16,64,256]{2,1,0:T(8,128)(2,1)S(1)}, bf16[16,64,256]{2,1,0:T(8,128)(2,1)S(1)}) custom-call(s32[3]{0:T(128)S(1)} %copy-done.28, bf16[8,4,64,512]{3,2,1,0:T(8,128)(2,1)} %get-tuple-element.208.early_in.early_ref, ...), custom_call_target="tpu_custom_call" | custom-call | flops 1000 | bytes 1000 | tf_op jit(solution)/shard_map/give_back/pallas_call | solution.py:694
  134.8 1.4 collective-permute-done.27.refs_1_
  137.2 1.3 collective-permute-start.29
  138.5 1.5 collective-permute-start.30
  140.0 1.8 collective-permute-start.31
  143.2 3.2 %collective-permute-done.29.refs_1_ = bf16[8,64,256]{2,1,0:T(8,128)(2,1)S(1)} collective-permute-done((bf16[8,64,256]{2,1,0:T(8,128)(2,1)S(1)}, bf16[8,64,256]{2,1,0:T(8,128)(2,1)S(1)}, u32[]{:S(2)}, u32[]{:S(2)}) %collective-permute-start.29) | collective-permute-done | bytes 262176 | tf_op jit(solution)/shard_map/ppermute | solution.py:874
  146.4 1.2 collective-permute-done.30.refs_3_
  148.7 1.5 collective-permute-start.34
  151.1 2.5 %collective-permute-done.34.refs_1_ = bf16[4,64,256]{2,1,0:T(8,128)(2,1)S(1)} collective-permute-done((bf16[4,64,256]{2,1,0:T(8,128)(2,1)S(1)}, bf16[4,64,256]{2,1,0:T(8,128)(2,1)S(1)}, u32[]{:S(2)}, u32[]{:S(2)}) %collective-permute-start.34) | collective-permute-done | bytes 131104 | tf_op jit(solution)/shard_map/ppermute | solution.py:874
  153.6 1.5 collective-permute-done.35.refs_3_
  155.1 1.8 collective-permute-start.36
  157.0 1.4 collective-permute-start.38
  158.4 1.7 collective-permute-done.36.refs_1_
  160.2 2.1 %collective-permute-start.37 = (bf16[1,64,512]{2,1,0:T(8,128)(2,1)S(1)}, bf16[1,64,512]{2,1,0:T(8,128)(2,1)S(1)}, u32[]{:S(2)}, u32[]{:S(2)}) collective-permute-start(bf16[1,64,512]{2,1,0:T(8,128)(2,1)S(1)} %get-tuple-element.303), channel_id=1, source_target_pairs={{0,16},{1,17},{2,18},{3,19},{4,20},{5,21},{6,22},{7,23},{8,24},{9,... | collective-permute-start | bytes 196616 | tf_op jit(solution)/shard_map/ppermute | solution.py:874
  162.3 3.6 %collective-permute-done.38.late_b = bf16[1,64,1152]{2,1,0:T(8,128)(2,1)S(1)} collective-permute-done((bf16[1,64,1152]{2,1,0:T(8,128)(2,1)S(1)}, bf16[1,64,1152]{2,1,0:T(8,128)(2,1)S(1)}, u32[]{:S(2)}, u32[]{:S(2)}) %collective-permute-start.38) | collective-permute-done | bytes 147488 | tf_op jit(solution)/shard_map/ppermute | solution.py:874
  165.8 1.4 collective-permute-done.37.early_b
  168.7 2.4 %collective-permute-start.41 = (f32[1,128]{1,0:T(1,128)S(1)}, f32[1,128]{1,0:T(1,128)S(1)}, u32[]{:S(2)}, u32[]{:S(2)}) collective-permute-start(f32[1,128]{1,0:T(1,128)S(1)} %add.63), channel_id=1, source_target_pairs={{0,4},{1,5},{2,6},{3,7},{4,0},{5,1},{6,2},{7,3},{8,12},{9,13},{10,... | collective-permute-start | bytes 1544 | tf_op jit(solution)/shard_map/ppermute | solution.py:1053
  173.1 1.5 collective-permute-done.40
  174.9 3.3 %collective-permute-done.43 = f32[1,128]{1,0:T(1,128)S(1)} collective-permute-done((f32[1,128]{1,0:T(1,128)S(1)}, f32[1,128]{1,0:T(1,128)S(1)}, u32[]{:S(2)}, u32[]{:S(2)}) %collective-permute-start.43) | collective-permute-done | bytes 544 | tf_op jit(solution)/shard_map/ppermute | solution.py:1053
  178.2 1.3 collective-permute-start.44
  179.5 3.2 %collective-permute-done.44 = f32[1,128]{1,0:T(1,128)S(1)} collective-permute-done((f32[1,128]{1,0:T(1,128)S(1)}, f32[1,128]{1,0:T(1,128)S(1)}, u32[]{:S(2)}, u32[]{:S(2)}) %collective-permute-start.44) | collective-permute-done | bytes 544 | tf_op jit(solution)/shard_map/ppermute | solution.py:1053
  182.8 1.7 adam.1
  (192 shorter events, 25.6 us)
Async XLA Ops:
  2.6 13.1 %collective-permute-start = (bf16[64,512]{1,0:T(8,128)(2,1)}, bf16[64,512]{1,0:T(8,128)(2,1)S(1)}, u32[]{:S(2)}, u32[]{:S(2)}) collective-permute-start(bf16[64,512]{1,0:T(8,128)(2,1)} %get-tuple-element.179), channel_id=1, source_target_pairs={{0,16},{1,17},{2,18},{3,19},{4,20},{5,21},{6,22},{7,23},{8,24},{9,... | collective-permute-start | bytes 196616 | tf_op jit(solution)/shard_map/ppermute | solution.py:874
  15.7 5.0 %collective-permute-start.1 = (bf16[2,64,512]{2,1,0:T(8,128)(2,1)S(1)}, bf16[2,64,512]{2,1,0:T(8,128)(2,1)S(1)}, u32[]{:S(2)}, u32[]{:S(2)}) collective-permute-start(bf16[2,64,512]{2,1,0:T(8,128)(2,1)S(1)} %get-tuple-element.337), channel_id=1, source_target_pairs={{0,8},{1,9},{2,10},{3,11},{4,12},{5,13},{6,14},{7,15},{8,0},{9,1},... | collective-permute-start | bytes 393224 | tf_op jit(solution)/shard_map/ppermute | solution.py:874
  21.5 8.3 %collective-permute-start.3 = (bf16[64,1152]{1,0:T(8,128)(2,1)S(1)}, bf16[64,1152]{1,0:T(8,128)(2,1)S(1)}, u32[]{:S(2)}, u32[]{:S(2)}) collective-permute-start(bf16[64,1152]{1,0:T(8,128)(2,1)S(1)} %copy-done.43), channel_id=1, source_target_pairs={{0,16},{1,17},{2,18},{3,19},{4,20},{5,21},{6,22},{7,23},{8,24},{9,... | collective-permute-start | bytes 442376 | tf_op jit(solution)/shard_map/ppermute | solution.py:874
  21.9 8.0 %collective-permute-start.2 = (bf16[2,2,64,512]{3,2,1,0:T(8,128)(2,1)S(1)}, bf16[2,2,64,512]{3,2,1,0:T(8,128)(2,1)S(1)}, u32[]{:S(2)}, u32[]{:S(2)}) collective-permute-start(bf16[2,2,64,512]{3,2,1,0:T(8,128)(2,1)S(1)} %pad_maximum_fusion.5), channel_id=1, source_target_pairs={{0,4},{1,5},{2,6},{3,7},{4,0},{5,1},{6,2},{7,3},{8,12},{9,13},{10,... | collective-permute-start | bytes 786440 | tf_op jit(solution)/shard_map/ppermute | solution.py:874
  29.9 11.4 %collective-permute-start.4 = (bf16[2,64,1152]{2,1,0:T(8,128)(2,1)S(1)}, bf16[2,64,1152]{2,1,0:T(8,128)(2,1)S(1)}, u32[]{:S(2)}, u32[]{:S(2)}) collective-permute-start(bf16[2,64,1152]{2,1,0:T(8,128)(2,1)S(1)} %pad_maximum_fusion.3), channel_id=1, source_target_pairs={{0,8},{1,9},{2,10},{3,11},{4,12},{5,13},{6,14},{7,15},{8,0},{9,1},... | collective-permute-start | bytes 884744 | tf_op jit(solution)/shard_map/ppermute | solution.py:874
  30.0 14.1 %collective-permute-start.5 = (bf16[2,2,2,64,512]{4,3,2,1,0:T(8,128)(2,1)S(1)}, bf16[2,2,2,64,512]{4,3,2,1,0:T(8,128)(2,1)S(1)}, u32[]{:S(2)}, u32[]{:S(2)}) collective-permute-start(bf16[2,2,2,64,512]{4,3,2,1,0:T(8,128)(2,1)S(1)} %pad_maximum_fusion.1), channel_id=1, source_target_pairs={{0,2},{1,3},{2,0},{3,1},{4,6},{5,7},{6,4},{7,5},{8,10},{9,11},{10,... | collective-permute-start | bytes 1572872 | tf_op jit(solution)/shard_map/ppermute | solution.py:874
  31.6 9.8 %collective-permute-start.7 = (bf16[256,512]{1,0:T(8,128)(2,1)S(1)}, bf16[256,512]{1,0:T(8,128)(2,1)S(1)}, u32[]{:S(2)}, u32[]{:S(2)}) collective-permute-start(bf16[256,512]{1,0:T(8,128)(2,1)S(1)} %convert_element_type.9), channel_id=1, source_target_pairs={{4,0},{8,4},{12,8},{16,12},{20,16},{24,20},{28,24},{0,28},{5,1},{9... | collective-permute-start | bytes 786440 | tf_op jit(solution)/shard_map/ppermute | solution.py:1133
  35.0 9.1 %collective-permute-start.6 = (bf16[256,512]{1,0:T(8,128)(2,1)S(1)}, bf16[256,512]{1,0:T(8,128)(2,1)S(1)}, u32[]{:S(2)}, u32[]{:S(2)}) collective-permute-start(bf16[256,512]{1,0:T(8,128)(2,1)S(1)} %convert_element_type.9), channel_id=1, source_target_pairs={{0,4},{4,8},{8,12},{12,16},{16,20},{20,24},{24,28},{28,0},{1,5},{5... | collective-permute-start | bytes 786440 | tf_op jit(solution)/shard_map/ppermute | solution.py:1133
  35.0 12.6 %collective-permute-start.10 = (bf16[8,64,512]{2,1,0:T(8,128)(2,1)S(1)}, bf16[8,64,512]{2,1,0:T(8,128)(2,1)}, u32[]{:S(2)}, u32[]{:S(2)}) collective-permute-start(bf16[8,64,512]{2,1,0:T(8,128)(2,1)S(1)} %bitcast.74), channel_id=1, source_target_pairs={{0,1},{1,0},{2,3},{3,2},{4,5},{5,4},{6,7},{7,6},{8,9},{9,8},{10,11... | collective-permute-start | bytes 1572872 | tf_op jit(solution)/shard_map/ppermute | solution.py:874
  44.1 3.5 %collective-permute-start.11 = (bf16[8,64,512]{2,1,0:T(8,128)(2,1)S(1)}, bf16[8,64,512]{2,1,0:T(8,128)(2,1)S(1)}, u32[]{:S(2)}, u32[]{:S(2)}) collective-permute-start(bf16[8,64,512]{2,1,0:T(8,128)(2,1)S(1)} %bitcast.87), channel_id=1, source_target_pairs={{0,1},{1,0},{2,3},{3,2},{4,5},{5,4},{6,7},{7,6},{8,9},{9,8},{10,11... | collective-permute-start | bytes 1572872 | tf_op jit(solution)/shard_map/ppermute | solution.py:874
  44.2 10.2 %collective-permute-start.8 = (bf16[2,2,64,640]{3,2,1,0:T(8,128)(2,1)S(1)}, bf16[2,2,64,640]{3,2,1,0:T(8,128)(2,1)S(1)}, u32[]{:S(2)}, u32[]{:S(2)}) collective-permute-start(bf16[2,2,64,640]{3,2,1,0:T(8,128)(2,1)S(1)} %fusion.3), channel_id=1, source_target_pairs={{0,4},{1,5},{2,6},{3,7},{4,0},{5,1},{6,2},{7,3},{8,12},{9,13},{10,... | collective-permute-start | bytes 983048 | tf_op jit(solution)/shard_map/ppermute | solution.py:874
  46.0 8.4 %collective-permute-start.9 = (bf16[2,2,64,512]{3,2,1,0:T(8,128)(2,1)S(1)}, bf16[2,2,64,512]{3,2,1,0:T(8,128)(2,1)S(1)}, u32[]{:S(2)}, u32[]{:S(2)}) collective-permute-start(bf16[2,2,64,512]{3,2,1,0:T(8,128)(2,1)S(1)} %pad_maximum_fusion.4), channel_id=1, source_target_pairs={{0,2},{1,3},{2,0},{3,1},{4,6},{5,7},{6,4},{7,5},{8,10},{9,11},{10,... | collective-permute-start | bytes 786440 | tf_op jit(solution)/shard_map/ppermute | solution.py:874
  54.5 17.0 %collective-permute-start.14 = (bf16[8,64,640]{2,1,0:T(8,128)(2,1)S(1)}, bf16[8,64,640]{2,1,0:T(8,128)(2,1)S(1)}, u32[]{:S(2)}, u32[]{:S(2)}) collective-permute-start(bf16[8,64,640]{2,1,0:T(8,128)(2,1)S(1)} %bitcast.70), channel_id=1, source_target_pairs={{0,1},{1,0},{2,3},{3,2},{4,5},{5,4},{6,7},{7,6},{8,9},{9,8},{10,11... | collective-permute-start | bytes 1966088 | tf_op jit(solution)/shard_map/ppermute | solution.py:874
  54.6 17.1 %collective-permute-start.12 = (bf16[2,2,2,64,640]{4,3,2,1,0:T(8,128)(2,1)S(1)}, bf16[2,2,2,64,640]{4,3,2,1,0:T(8,128)(2,1)S(1)}, u32[]{:S(2)}, u32[]{:S(2)}) collective-permute-start(bf16[2,2,2,64,640]{4,3,2,1,0:T(8,128)(2,1)S(1)} %pad_maximum_fusion), channel_id=1, source_target_pairs={{0,2},{1,3},{2,0},{3,1},{4,6},{5,7},{6,4},{7,5},{8,10},{9,11},{10,... | collective-permute-start | bytes 1966088 | tf_op jit(solution)/shard_map/ppermute | solution.py:874
  55.9 15.5 %collective-permute-start.15 = (bf16[8,64,512]{2,1,0:T(8,128)(2,1)S(1)}, bf16[8,64,512]{2,1,0:T(8,128)(2,1)S(1)}, u32[]{:S(2)}, u32[]{:S(2)}) collective-permute-start(bf16[8,64,512]{2,1,0:T(8,128)(2,1)S(1)} %bitcast.72), channel_id=1, source_target_pairs={{0,1},{1,0},{2,3},{3,2},{4,5},{5,4},{6,7},{7,6},{8,9},{9,8},{10,11... | collective-permute-start | bytes 1572872 | tf_op jit(solution)/shard_map/ppermute | solution.py:874
  56.1 15.4 %collective-permute-start.13 = (bf16[2,2,2,64,512]{4,3,2,1,0:T(8,128)(2,1)S(1)}, bf16[2,2,2,64,512]{4,3,2,1,0:T(8,128)(2,1)S(1)}, u32[]{:S(2)}, u32[]{:S(2)}) collective-permute-start(bf16[2,2,2,64,512]{4,3,2,1,0:T(8,128)(2,1)S(1)} %pad_maximum_fusion.2), channel_id=1, source_target_pairs={{0,4},{1,5},{2,6},{3,7},{4,0},{5,1},{6,2},{7,3},{8,12},{9,13},{10,... | collective-permute-start | bytes 1572872 | tf_op jit(solution)/shard_map/ppermute | solution.py:874
  71.7 2.9 %collective-permute-start.16 = (bf16[8,64,640]{2,1,0:T(8,128)(2,1)S(1)}, bf16[8,64,640]{2,1,0:T(8,128)(2,1)S(1)}, u32[]{:S(2)}, u32[]{:S(2)}) collective-permute-start(bf16[8,64,640]{2,1,0:T(8,128)(2,1)S(1)} %bitcast.83), channel_id=1, source_target_pairs={{0,1},{1,0},{2,3},{3,2},{4,5},{5,4},{6,7},{7,6},{8,9},{9,8},{10,11... | collective-permute-start | bytes 1966088 | tf_op jit(solution)/shard_map/ppermute | solution.py:874
  71.7 2.8 %collective-permute-start.17 = (bf16[8,64,512]{2,1,0:T(8,128)(2,1)S(1)}, bf16[8,64,512]{2,1,0:T(8,128)(2,1)S(1)}, u32[]{:S(2)}, u32[]{:S(2)}) collective-permute-start(bf16[8,64,512]{2,1,0:T(8,128)(2,1)S(1)} %bitcast.85), channel_id=1, source_target_pairs={{0,1},{1,0},{2,3},{3,2},{4,5},{5,4},{6,7},{7,6},{8,9},{9,8},{10,11... | collective-permute-start | bytes 1572872 | tf_op jit(solution)/shard_map/ppermute | solution.py:874
  95.5 5.3 %collective-permute-start.18 = (bf16[16,64,384]{2,1,0:T(8,128)(2,1)}, bf16[16,64,384]{2,1,0:T(8,128)(2,1)S(1)}, u32[]{:S(2)}, u32[]{:S(2)}) collective-permute-start(bf16[16,64,384]{2,1,0:T(8,128)(2,1)} %get-tuple-element.223), channel_id=1, source_target_pairs={{0,1},{1,0},{2,3},{3,2},{4,5},{5,4},{6,7},{7,6},{8,9},{9,8},{10,11... | collective-permute-start | bytes 2359304 | tf_op jit(solution)/shard_map/ppermute | solution.py:874
  95.7 5.1 %collective-permute-start.19 = (bf16[16,64,384]{2,1,0:T(8,128)(2,1)}, bf16[16,64,384]{2,1,0:T(8,128)(2,1)S(1)}, u32[]{:S(2)}, u32[]{:S(2)}) collective-permute-start(bf16[16,64,384]{2,1,0:T(8,128)(2,1)} %get-tuple-element.225), channel_id=1, source_target_pairs={{0,1},{1,0},{2,3},{3,2},{4,5},{5,4},{6,7},{7,6},{8,9},{9,8},{10,11... | collective-permute-start | bytes 2359304 | tf_op jit(solution)/shard_map/ppermute | solution.py:874
  96.1 4.8 %collective-permute-start.20 = (bf16[16,64,384]{2,1,0:T(8,128)(2,1)}, bf16[16,64,384]{2,1,0:T(8,128)(2,1)}, u32[]{:S(2)}, u32[]{:S(2)}) collective-permute-start(bf16[16,64,384]{2,1,0:T(8,128)(2,1)} %get-tuple-element.227), channel_id=1, source_target_pairs={{0,1},{1,0},{2,3},{3,2},{4,5},{5,4},{6,7},{7,6},{8,9},{9,8},{10,11... | collective-permute-start | bytes 2359304 | tf_op jit(solution)/shard_map/ppermute | solution.py:874
  103.8 11.8 %collective-permute-start.21 = (bf16[8,64,384]{2,1,0:T(8,128)(2,1)}, bf16[8,64,384]{2,1,0:T(8,128)(2,1)}, u32[]{:S(2)}, u32[]{:S(2)}) collective-permute-start(bf16[8,64,384]{2,1,0:T(8,128)(2,1)} %get-tuple-element.239), channel_id=1, source_target_pairs={{0,2},{1,3},{2,0},{3,1},{4,6},{5,7},{6,4},{7,5},{8,10},{9,11},{10,... | collective-permute-start | bytes 1179656 | tf_op jit(solution)/shard_map/ppermute | solution.py:874
  105.2 11.4 %collective-permute-start.22 = (bf16[8,64,384]{2,1,0:T(8,128)(2,1)}, bf16[8,64,384]{2,1,0:T(8,128)(2,1)}, u32[]{:S(2)}, u32[]{:S(2)}) collective-permute-start(bf16[8,64,384]{2,1,0:T(8,128)(2,1)} %get-tuple-element.240), channel_id=1, source_target_pairs={{0,4},{1,5},{2,6},{3,7},{4,0},{5,1},{6,2},{7,3},{8,12},{9,13},{10,... | collective-permute-start | bytes 1179656 | tf_op jit(solution)/shard_map/ppermute | solution.py:874
  106.6 11.1 %collective-permute-start.23 = (bf16[8,64,384]{2,1,0:T(8,128)(2,1)}, bf16[8,64,384]{2,1,0:T(8,128)(2,1)}, u32[]{:S(2)}, u32[]{:S(2)}) collective-permute-start(bf16[8,64,384]{2,1,0:T(8,128)(2,1)} %get-tuple-element.241), channel_id=1, source_target_pairs={{0,8},{1,9},{2,10},{3,11},{4,12},{5,13},{6,14},{7,15},{8,0},{9,1},... | collective-permute-start | bytes 1179656 | tf_op jit(solution)/shard_map/ppermute | solution.py:874
  122.3 11.9 %collective-permute-start.24 = (bf16[4,64,384]{2,1,0:T(8,128)(2,1)S(1)}, bf16[4,64,384]{2,1,0:T(8,128)(2,1)S(1)}, u32[]{:S(2)}, u32[]{:S(2)}) collective-permute-start(bf16[4,64,384]{2,1,0:T(8,128)(2,1)S(1)} %get-tuple-element.249), channel_id=1, source_target_pairs={{0,4},{1,5},{2,6},{3,7},{4,0},{5,1},{6,2},{7,3},{8,12},{9,13},{10,... | collective-permute-start | bytes 589832 | tf_op jit(solution)/shard_map/ppermute | solution.py:874
  122.9 11.3 %collective-permute-start.25 = (bf16[4,64,384]{2,1,0:T(8,128)(2,1)S(1)}, bf16[4,64,384]{2,1,0:T(8,128)(2,1)S(1)}, u32[]{:S(2)}, u32[]{:S(2)}) collective-permute-start(bf16[4,64,384]{2,1,0:T(8,128)(2,1)S(1)} %get-tuple-element.250), channel_id=1, source_target_pairs={{0,8},{1,9},{2,10},{3,11},{4,12},{5,13},{6,14},{7,15},{8,0},{9,1},... | collective-permute-start | bytes 589832 | tf_op jit(solution)/shard_map/ppermute | solution.py:874
  123.2 11.0 %collective-permute-start.26 = (bf16[4,64,384]{2,1,0:T(8,128)(2,1)S(1)}, bf16[4,64,384]{2,1,0:T(8,128)(2,1)S(1)}, u32[]{:S(2)}, u32[]{:S(2)}) collective-permute-start(bf16[4,64,384]{2,1,0:T(8,128)(2,1)S(1)} %get-tuple-element.251), channel_id=1, source_target_pairs={{0,2},{1,3},{2,0},{3,1},{4,6},{5,7},{6,4},{7,5},{8,10},{9,11},{10,... | collective-permute-start | bytes 589832 | tf_op jit(solution)/shard_map/ppermute | solution.py:874
  134.2 2.0 %collective-permute-start.27 = (bf16[16,64,256]{2,1,0:T(8,128)(2,1)S(1)}, bf16[16,64,256]{2,1,0:T(8,128)(2,1)S(1)}, u32[]{:S(2)}, u32[]{:S(2)}) collective-permute-start(bf16[16,64,256]{2,1,0:T(8,128)(2,1)S(1)} %get-tuple-element.264), channel_id=1, source_target_pairs={{0,1},{1,0},{2,3},{3,2},{4,5},{5,4},{6,7},{7,6},{8,9},{9,8},{10,11... | collective-permute-start | bytes 1572872 | tf_op jit(solution)/shard_map/ppermute | solution.py:874
  134.3 2.6 %collective-permute-start.28 = (bf16[16,64,256]{2,1,0:T(8,128)(2,1)S(1)}, bf16[16,64,256]{2,1,0:T(8,128)(2,1)S(1)}, u32[]{:S(2)}, u32[]{:S(2)}) collective-permute-start(bf16[16,64,256]{2,1,0:T(8,128)(2,1)S(1)} %get-tuple-element.266), channel_id=1, source_target_pairs={{0,1},{1,0},{2,3},{3,2},{4,5},{5,4},{6,7},{7,6},{8,9},{9,8},{10,11... | collective-permute-start | bytes 1572872 | tf_op jit(solution)/shard_map/ppermute | solution.py:874
  137.2 9.2 %collective-permute-start.29 = (bf16[8,64,256]{2,1,0:T(8,128)(2,1)S(1)}, bf16[8,64,256]{2,1,0:T(8,128)(2,1)S(1)}, u32[]{:S(2)}, u32[]{:S(2)}) collective-permute-start(bf16[8,64,256]{2,1,0:T(8,128)(2,1)S(1)} %get-tuple-element.276), channel_id=1, source_target_pairs={{0,2},{1,3},{2,0},{3,1},{4,6},{5,7},{6,4},{7,5},{8,10},{9,11},{10,... | collective-permute-start | bytes 786440 | tf_op jit(solution)/shard_map/ppermute | solution.py:874
  138.5 9.1 %collective-permute-start.30 = (bf16[8,64,256]{2,1,0:T(8,128)(2,1)S(1)}, bf16[8,64,256]{2,1,0:T(8,128)(2,1)S(1)}, u32[]{:S(2)}, u32[]{:S(2)}) collective-permute-start(bf16[8,64,256]{2,1,0:T(8,128)(2,1)S(1)} %get-tuple-element.278), channel_id=1, source_target_pairs={{0,4},{1,5},{2,6},{3,7},{4,0},{5,1},{6,2},{7,3},{8,12},{9,13},{10,... | collective-permute-start | bytes 786440 | tf_op jit(solution)/shard_map/ppermute | solution.py:874
  140.0 7.8 %collective-permute-start.31 = (bf16[2,64,384]{2,1,0:T(8,128)(2,1)S(1)}, bf16[2,64,384]{2,1,0:T(8,128)(2,1)S(1)}, u32[]{:S(2)}, u32[]{:S(2)}) collective-permute-start(bf16[2,64,384]{2,1,0:T(8,128)(2,1)S(1)} %get-tuple-element.292), channel_id=1, source_target_pairs={{0,8},{1,9},{2,10},{3,11},{4,12},{5,13},{6,14},{7,15},{8,0},{9,1},... | collective-permute-start | bytes 294920 | tf_op jit(solution)/shard_map/ppermute | solution.py:874
  141.8 6.1 %collective-permute-start.32 = (bf16[2,64,384]{2,1,0:T(8,128)(2,1)S(1)}, bf16[2,64,384]{2,1,0:T(8,128)(2,1)S(1)}, u32[]{:S(2)}, u32[]{:S(2)}) collective-permute-start(bf16[2,64,384]{2,1,0:T(8,128)(2,1)S(1)} %get-tuple-element.294), channel_id=1, source_target_pairs={{0,2},{1,3},{2,0},{3,1},{4,6},{5,7},{6,4},{7,5},{8,10},{9,11},{10,... | collective-permute-start | bytes 294920 | tf_op jit(solution)/shard_map/ppermute | solution.py:874
  142.8 5.9 %collective-permute-start.33 = (bf16[2,64,384]{2,1,0:T(8,128)(2,1)S(1)}, bf16[2,64,384]{2,1,0:T(8,128)(2,1)S(1)}, u32[]{:S(2)}, u32[]{:S(2)}) collective-permute-start(bf16[2,64,384]{2,1,0:T(8,128)(2,1)S(1)} %get-tuple-element.296), channel_id=1, source_target_pairs={{0,4},{1,5},{2,6},{3,7},{4,0},{5,1},{6,2},{7,3},{8,12},{9,13},{10,... | collective-permute-start | bytes 294920 | tf_op jit(solution)/shard_map/ppermute | solution.py:874
  147.7 34.9 %copy-start.11 = (f32[64,896]{1,0:T(8,128)S(1)}, f32[64,896]{1,0:T(8,128)}, u32[]{:S(2)}) copy-start(f32[64,896]{1,0:T(8,128)} %refs_4_.1) | copy-start | bytes 688132
  147.7 34.9 %copy-start.12 = (f32[640,64]{0,1:T(8,128)S(1)}, f32[640,64]{0,1:T(8,128)}, u32[]{:S(2)}) copy-start(f32[640,64]{0,1:T(8,128)} %param.36) | copy-start | bytes 491524
  147.7 34.9 %copy-start.14 = (f32[64,896]{1,0:T(8,128)S(1)}, f32[64,896]{1,0:T(8,128)}, u32[]{:S(2)}) copy-start(f32[64,896]{1,0:T(8,128)} %refs_5_.1) | copy-start | bytes 688132
  148.7 5.0 %collective-permute-start.34 = (bf16[4,64,256]{2,1,0:T(8,128)(2,1)S(1)}, bf16[4,64,256]{2,1,0:T(8,128)(2,1)S(1)}, u32[]{:S(2)}, u32[]{:S(2)}) collective-permute-start(bf16[4,64,256]{2,1,0:T(8,128)(2,1)S(1)} %get-tuple-element.297), channel_id=1, source_target_pairs={{0,4},{1,5},{2,6},{3,7},{4,0},{5,1},{6,2},{7,3},{8,12},{9,13},{10,... | collective-permute-start | bytes 393224 | tf_op jit(solution)/shard_map/ppermute | solution.py:874
  150.1 5.0 %collective-permute-start.35 = (bf16[4,64,256]{2,1,0:T(8,128)(2,1)S(1)}, bf16[4,64,256]{2,1,0:T(8,128)(2,1)S(1)}, u32[]{:S(2)}, u32[]{:S(2)}) collective-permute-start(bf16[4,64,256]{2,1,0:T(8,128)(2,1)S(1)} %get-tuple-element.299), channel_id=1, source_target_pairs={{0,2},{1,3},{2,0},{3,1},{4,6},{5,7},{6,4},{7,5},{8,10},{9,11},{10,... | collective-permute-start | bytes 393224 | tf_op jit(solution)/shard_map/ppermute | solution.py:874
  155.1 5.0 %collective-permute-start.36 = (bf16[2,64,512]{2,1,0:T(8,128)(2,1)S(1)}, bf16[2,64,512]{2,1,0:T(8,128)(2,1)S(1)}, u32[]{:S(2)}, u32[]{:S(2)}) collective-permute-start(bf16[2,64,512]{2,1,0:T(8,128)(2,1)S(1)} %get-tuple-element.301), channel_id=1, source_target_pairs={{0,8},{1,9},{2,10},{3,11},{4,12},{5,13},{6,14},{7,15},{8,0},{9,1},... | collective-permute-start | bytes 393224 | tf_op jit(solution)/shard_map/ppermute | solution.py:874
  157.0 8.9 %collective-permute-start.38 = (bf16[1,64,1152]{2,1,0:T(8,128)(2,1)S(1)}, bf16[1,64,1152]{2,1,0:T(8,128)(2,1)S(1)}, u32[]{:S(2)}, u32[]{:S(2)}) collective-permute-start(bf16[1,64,1152]{2,1,0:T(8,128)(2,1)S(1)} %get-tuple-element.311), channel_id=1, source_target_pairs={{0,16},{1,17},{2,18},{3,19},{4,20},{5,21},{6,22},{7,23},{8,24},{9,... | collective-permute-start | bytes 442376 | tf_op jit(solution)/shard_map/ppermute | solution.py:874
  160.2 7.0 %collective-permute-start.37 = (bf16[1,64,512]{2,1,0:T(8,128)(2,1)S(1)}, bf16[1,64,512]{2,1,0:T(8,128)(2,1)S(1)}, u32[]{:S(2)}, u32[]{:S(2)}) collective-permute-start(bf16[1,64,512]{2,1,0:T(8,128)(2,1)S(1)} %get-tuple-element.303), channel_id=1, source_target_pairs={{0,16},{1,17},{2,18},{3,19},{4,20},{5,21},{6,22},{7,23},{8,24},{9,... | collective-permute-start | bytes 196616 | tf_op jit(solution)/shard_map/ppermute | solution.py:874
  167.5 1.2 collective-permute-start.39
  168.7 4.4 %collective-permute-start.42 = (f32[1,128]{1,0:T(1,128)S(1)}, f32[1,128]{1,0:T(1,128)S(1)}, u32[]{:S(2)}, u32[]{:S(2)}) collective-permute-start(f32[1,128]{1,0:T(1,128)S(1)} %add.63), channel_id=1, source_target_pairs={{0,6},{1,7},{2,4},{3,5},{4,2},{5,3},{6,0},{7,1},{8,14},{9,15},{10,... | collective-permute-start | bytes 1544 | tf_op jit(solution)/shard_map/ppermute | solution.py:1053
  168.7 4.4 %collective-permute-start.41 = (f32[1,128]{1,0:T(1,128)S(1)}, f32[1,128]{1,0:T(1,128)S(1)}, u32[]{:S(2)}, u32[]{:S(2)}) collective-permute-start(f32[1,128]{1,0:T(1,128)S(1)} %add.63), channel_id=1, source_target_pairs={{0,4},{1,5},{2,6},{3,7},{4,0},{5,1},{6,2},{7,3},{8,12},{9,13},{10,... | collective-permute-start | bytes 1544 | tf_op jit(solution)/shard_map/ppermute | solution.py:1053
  171.1 3.5 %collective-permute-start.40 = (f32[1,128]{1,0:T(1,128)S(1)}, f32[1,128]{1,0:T(1,128)S(1)}, u32[]{:S(2)}, u32[]{:S(2)}) collective-permute-start(f32[1,128]{1,0:T(1,128)S(1)} %add.63), channel_id=1, source_target_pairs={{0,2},{1,3},{2,0},{3,1},{4,6},{5,7},{6,4},{7,5},{8,10},{9,11},{10,... | collective-permute-start | bytes 1544 | tf_op jit(solution)/shard_map/ppermute | solution.py:1053
  174.7 3.5 %collective-permute-start.43 = (f32[1,128]{1,0:T(1,128)S(1)}, f32[1,128]{1,0:T(1,128)S(1)}, u32[]{:S(2)}, u32[]{:S(2)}) collective-permute-start(f32[1,128]{1,0:T(1,128)S(1)} %add_add_fusion), channel_id=1, source_target_pairs={{0,8},{1,9},{2,10},{3,11},{4,12},{5,13},{6,14},{7,15},{8,0},{9,1},... | collective-permute-start | bytes 1544 | tf_op jit(solution)/shard_map/ppermute | solution.py:1053
  178.2 4.4 %collective-permute-start.44 = (f32[1,128]{1,0:T(1,128)S(1)}, f32[1,128]{1,0:T(1,128)S(1)}, u32[]{:S(2)}, u32[]{:S(2)}) collective-permute-start(f32[1,128]{1,0:T(1,128)S(1)} %add.67), channel_id=1, source_target_pairs={{0,16},{1,17},{2,18},{3,19},{4,20},{5,21},{6,22},{7,23},{8,24},{9,... | collective-permute-start | bytes 1544 | tf_op jit(solution)/shard_map/ppermute | solution.py:1053
  (47 other events, 744.0 us)
